TPU v7x, 256 devices: a whole 4x4x8 slice. The times are simulated.
256 devices in a mesh: dp: 8 (over x_lo, y), tensor: 32 (over z, x_hi, core).
Axes of the slice: x: 4 (x_hi: 2, x_lo: 2; x = x_hi * 2 + x_lo), y: 4, z: 8, core: 2. Of those that a mesh axis runs over, the one named last changes fastest.
Arguments:
- tokens: bfloat16 [4096, 4096], P(('dp', 'tensor')), may hold values from -24 to 24
- weight: bfloat16 [4096, 28672], P(None, 'tensor'), may hold values from -0.125 to 0.125
- block_mask: int32 [64, 448], replicated, may hold values from 0 to 1, as said below
- act_grad: bfloat16 [4096, 28672], P('dp', 'tensor'), may hold values from -6 to 6
Outputs:
- act: bfloat16 [4096, 28672], P('dp', 'tensor')
- x_grad: bfloat16 [4096, 4096], P(('dp', 'tensor'))
- weight_grad: float32 [4096, 28672], P('dp', 'tensor')
Inputs may be any that keep to these rules, and one draw needn't show every extreme that they name: `block_mask`: split block rows into 8 equal consecutive groups and block columns into 32; each such region keeps at most 70 blocks, and some region keeps exactly 70.
All inputs are finite; a program needn't handle non-finite values.
Results may differ from a plain program's by a relative error of at most 0.015.
Values may be sent and summed in bfloat16 or wider, within the bound.
No kernel may reach another device: no remote copies, remote signals or barrier semaphores. Data moves between devices by JAX's collectives and lax.ppermute only.
A program may use at most 128 MiB of HBM per device.

v0:
```python
import functools

import jax
import jax.numpy as jnp
from jax import lax
from jax.experimental import pallas as pl
from jax.experimental.pallas import tpu as pltpu
from jax.sharding import PartitionSpec as P


BLOCK = 64
CAP = 70
PAIRS = CAP // 2
NZ = 8
NY = 4
F32 = jnp.float32
BF16 = jnp.bfloat16


VMEM = pl.BlockSpec(memory_space=pltpu.VMEM)
SMEM = pl.BlockSpec(memory_space=pltpu.SMEM)


def tensor_perm(dz, dx, dc, split=False):
    pairs = []
    for z in range(NZ):
        for xh in range(2):
            for core in range(2):
                shift = -dz if split and core else dz
                source = (z * 2 + xh) * 2 + core
                target = (((z + shift) % NZ) * 2 + (xh ^ dx)) * 2 + (core ^ dc)
                pairs.append((source, target))
    return pairs


def dp_perm(dx, dy):
    return [
        (xl * NY + y, (xl ^ dx) * NY + (y + dy) % NY) for xl in range(2) for y in range(NY)
    ]


def move(x, dz=0, dx=0, dc=0):
    return lax.ppermute(x, "tensor", tensor_perm(dz, dx, dc, split=True))


def move_dp(x, dx, dy):
    return lax.ppermute(x, "dp", dp_perm(dx, dy))


def call(kernel, n_scalar, out_shape, args, flops, scratch=(), after=(), limit=12):
    n_args, n_after = len(args), len(after)

    def run(*refs):
        kernel(*refs[:n_args], *refs[n_args + n_after :])

    n_out = len(out_shape) if isinstance(out_shape, (tuple, list)) else 1
    out_specs = [VMEM] * n_out if isinstance(out_shape, (tuple, list)) else VMEM
    moved = sum(a.size * a.dtype.itemsize for a in args)
    return pl.pallas_call(
        run,
        out_shape=out_shape,
        in_specs=[SMEM] * n_scalar
        + [VMEM] * (n_args - n_scalar)
        + [pl.BlockSpec(memory_space=pl.ANY)] * n_after,
        out_specs=out_specs,
        scratch_shapes=list(scratch),
        compiler_params=pltpu.CompilerParams(vmem_limit_bytes=limit << 20),
        cost_estimate=pl.CostEstimate(flops=flops, bytes_accessed=moved, transcendentals=0),
    )(*args, *after)


def tick_kernel(x_ref, o_ref):
    o_ref[...] = jnp.full(o_ref.shape, x_ref[0], F32)


def mask_kernel(t_ref, w_ref, m_ref, o_ref, e_ref):
    n_rows, blocks = m_ref.shape
    width = w_ref.shape[1]
    rows = lax.broadcasted_iota(jnp.int32, (blocks, width), 0)
    cols = lax.broadcasted_iota(jnp.int32, (blocks, width), 1)
    pick = (rows == t_ref[0] + lax.div(cols, BLOCK)).astype(BF16)
    e_ref[...] = jnp.dot(m_ref[...].astype(F32).astype(BF16), pick, preferred_element_type=F32)

    @pl.loop(0, n_rows // 8)
    def _(g):
        eight = e_ref[pl.ds(pl.multiple_of(g * 8, 8), 8), :]
        for i in range(8):
            at = pl.ds(pl.multiple_of(g * 512 + i * BLOCK, BLOCK), BLOCK)
            row = jnp.broadcast_to(eight[i : i + 1, :], (BLOCK, width)).astype(BF16)
            o_ref[at, :] = w_ref[at, :] * row


def forward_kernel(first, count, idx_ref, xa, xb, w_ref, g_ref, *rest):
    act_ref, p_ref, pt_ref, acc_ref = rest[-4:]
    d = w_ref.shape[0]
    kb = 1024

    def product(s):
        cols = pl.ds(pl.multiple_of(s * kb, kb), kb)
        x = jnp.concatenate([xa[:, cols], xb[:, cols]], axis=0)
        return jnp.dot(x, w_ref[cols, :], preferred_element_type=F32)

    acc_ref[...] = product(0)

    @pl.loop(1, d // kb)
    def _(s):
        acc_ref[...] += product(s)

    @pl.loop(0, count)
    def _(n):
        at = idx_ref[first + n]
        rows = pl.ds(pl.multiple_of(n * 16, 16), 16)
        pre = acc_ref[rows, :]
        s = jax.nn.sigmoid(pre)
        act = (pre * s).astype(BF16)
        if first:
            act_ref[at] = act
            act_ref[idx_ref[n]] = rest[0][n]
        else:
            act_ref[n] = act
        grad = g_ref[at].astype(F32) * s * (1.0 + pre * (1.0 - s))
        acc_ref[rows, :] = grad
        p_ref[rows, :] = grad.astype(BF16)

    for c in range(7):
        cols = slice(c * 128, (c + 1) * 128)
        pt_ref[cols, :] = jnp.transpose(acc_ref[:, cols]).astype(BF16)


def forward(first, idx, xa, xb, masked, act_grad, acts=(), after=()):
    d, width = masked.shape
    blocks = 32 if first else 16
    return call(
        functools.partial(forward_kernel, first, 16),
        1,
        (
            jax.ShapeDtypeStruct((blocks, 16, width), BF16),
            jax.ShapeDtypeStruct((256, width), BF16),
            jax.ShapeDtypeStruct((width, 256), BF16),
        ),
        (idx, xa, xb, masked, act_grad, *acts),
        2 * 256 * d * width,
        scratch=(pltpu.VMEM((256, width), F32),),
        after=after,
    )


def xgrad_kernel(p_ref, w_ref, own_ref, other_ref):
    @pl.loop(0, w_ref.shape[0] // 512)
    def _(s):
        cols = pl.ds(pl.multiple_of(s * 512, 512), 512)
        part = lax.dot_general(
            p_ref[...], w_ref[cols, :], (((1,), (1,)), ((), ())), preferred_element_type=F32
        )
        own_ref[:, cols] = part[:128, :]
        other_ref[:, cols] = part[128:, :].astype(BF16)


def xgrad(p, masked, after=()):
    d, width = masked.shape
    return call(
        xgrad_kernel,
        0,
        (jax.ShapeDtypeStruct((128, d), F32), jax.ShapeDtypeStruct((128, d), BF16)),
        (p, masked),
        2 * 256 * d * width,
        after=after,
    )


def mix_kernel(own_ref, r_ref, near1, near2, near3, far, home):
    @pl.loop(0, own_ref.shape[1] // 512)
    def _(s):
        cols = pl.ds(pl.multiple_of(s * 512, 512), 512)
        total = (own_ref[:, cols] + r_ref[:, cols].astype(F32)).astype(BF16)
        home[:, cols] = total[0:16, :]
        far[:, cols] = total[16:32, :]
        near1[:, cols] = total[32:64, :]
        near2[:, cols] = total[64:96, :]
        near3[:, cols] = total[96:128, :]


def send_back(own, other, after):
    d = own.shape[1]
    near1, near2, near3, far, home = call(
        mix_kernel,
        0,
        [jax.ShapeDtypeStruct((32, d), BF16)] * 3 + [jax.ShapeDtypeStruct((16, d), BF16)] * 2,
        (own, move(other, dc=1)),
        128 * d,
        after=after,
    )
    back = []
    for k, v in ((3, near3), (2, near2), (1, near1), (4, far)):
        back.append(move(v, dz=NZ - k))
    return near1, [*back, home]


def sum_kernel(*refs):
    halves, to_core, kept = (refs[0:5], refs[5:10]), refs[10], refs[11]

    @pl.loop(0, kept.shape[1] // 512)
    def _(s):
        cols = pl.ds(pl.multiple_of(s * 512, 512), 512)
        for q, (*nears, far, home) in enumerate(halves):
            rows = slice(q * 16, q * 16 + 16)
            total = home[:, cols].astype(F32) + far[:, cols].astype(F32)
            away = jnp.zeros_like(total)
            for near in nears:
                total = total + near[0:16, cols].astype(F32)
                away = away + near[16:32, cols].astype(F32)
            to_core[rows, cols] = away.astype(BF16)
            kept[rows, cols] = total


def sum_core_kernel(kept, received, to_x, out):
    @pl.loop(0, kept.shape[1] // 512)
    def _(s):
        cols = pl.ds(pl.multiple_of(s * 512, 512), 512)
        total = kept[:, cols] + received[:, cols].astype(F32)
        out[:, cols] = total[0:16, :]
        to_x[:, cols] = total[16:32, :].astype(BF16)


def place_of(code):
    return (
        pl.multiple_of(code & 1023, BLOCK),
        pl.multiple_of((code >> 10) & 1023, 128),
        code >> 20,
    )


def wgrad_kernel(first, dest_ref, code_ref, odd_ref, pa, pb, x0, x1, x2, x3, *rest):
    outs, acc_ref = rest[:-1], rest[-1]
    last = acc_ref.shape[0] - BLOCK
    left = lax.broadcasted_iota(jnp.int32, (BLOCK, 128), 1) < BLOCK
    for n, out in enumerate(outs):
        dest = dest_ref[first + n]
        cols = pl.ds(pl.multiple_of(dest * 512, 512), 512)
        xa = jnp.concatenate([x0[:, cols], x2[:, cols]], axis=0)
        xb = jnp.concatenate([x1[:, cols], x3[:, cols]], axis=0)
        acc_ref[...] = jnp.dot(pa[...], xa, preferred_element_type=F32) + jnp.dot(
            pb[...], xb, preferred_element_type=F32
        )

        def tiles(s):
            row, lane, h = place_of(code_ref[dest, s])
            row = pl.multiple_of(jnp.minimum(row, last), BLOCK)
            row2, lane2, h2 = place_of(code_ref[dest, PAIRS + s])
            row2 = pl.multiple_of(jnp.minimum(row2, last), BLOCK)
            return (
                acc_ref[pl.ds(row, BLOCK), pl.ds(lane, 128)],
                acc_ref[pl.ds(row2, BLOCK), pl.ds(lane2, 128)],
                h,
                h2,
            )

        def pack(s, carry):
            one, two, _, _ = tiles(s)
            out[s] = jnp.where(left, one, two).astype(BF16)
            return carry

        def repack(n, carry):
            s = PAIRS - 1 - n
            one, two, h, h2 = tiles(s)
            one = pltpu.roll(one, h * BLOCK, 1)
            two = pltpu.roll(two, (1 - h2) * BLOCK, 1)
            out[s] = jnp.where(left, one, two).astype(BF16)
            return carry

        lax.fori_loop(0, PAIRS, pack, 0, unroll=5)
        lax.fori_loop(0, odd_ref[dest], repack, 0)


def wgrad(first, count, scalars, pa, pb, xs, after):
    width = pa.shape[0]
    return call(
        functools.partial(wgrad_kernel, first),
        3,
        [jax.ShapeDtypeStruct((PAIRS, BLOCK, 128), BF16)] * count,
        (*scalars, pa, pb, *xs),
        2 * 512 * 512 * width * count,
        scratch=(pltpu.VMEM((width, 512), F32),),
        after=after,
    )


def unpack_kernel(own_ref, code_ref, *refs):
    parts, out, buf = refs[:8], refs[8], refs[9]
    own = own_ref[0]
    width = out.shape[1]
    buf[...] = jnp.zeros_like(buf)
    half = lax.broadcasted_iota(jnp.int32, (BLOCK, 128), 1) // BLOCK

    def place(s, carry):
        total = parts[0][s].astype(F32)
        for part in parts[1:]:
            total = total + part[s].astype(F32)
        row, lane, h = place_of(code_ref[own, s])
        at = buf.at[pl.ds(row, BLOCK), pl.ds(lane, 128)]
        at[...] = jnp.where(half == h, pltpu.roll(total, h * BLOCK, 1), at[...])
        row, lane, h = place_of(code_ref[own, PAIRS + s])
        at = buf.at[pl.ds(row, BLOCK), pl.ds(lane, 128)]
        at[...] = jnp.where(half == h, pltpu.roll(total, (1 - h) * BLOCK, 1), at[...])
        return carry

    lax.fori_loop(0, PAIRS, place, 0)
    for c in range(4):
        lanes = slice(c * 128, (c + 1) * 128)
        out[lanes, :] = jnp.transpose(buf[0:width, lanes])


def kept_codes(block_mask, t, width):
    mask = lax.dynamic_slice(block_mask, (0, t * 14), (64, 14)).reshape(8, 112)
    kept = mask != 0
    at = jnp.arange(112, dtype=jnp.int32)
    i = jnp.array([b // 14 for b in range(112)], jnp.int32)
    j = at - i * 14
    h = i & 1
    before = (at[:, None] <= at[None, :]) & (h[:, None] == h[None, :])
    rank = jnp.dot(kept.astype(BF16), before.astype(BF16), preferred_element_type=F32)
    rank = rank.astype(jnp.int32) - 1
    extra = rank >= PAIRS
    slot = jnp.where(extra, 3 * PAIRS - 1 - PAIRS * h - rank, rank + PAIRS * h)
    hit = kept[:, None, :] & (slot[:, None, :] == jnp.arange(CAP, dtype=jnp.int32)[None, :, None])
    code = j * BLOCK + (i >> 1) * (128 << 10) + (h << 20) - width
    code = jnp.sum(jnp.where(hit, code[None, None, :], 0), axis=2, dtype=jnp.int32) + width
    odd = jnp.sum((kept & extra).astype(jnp.int32), axis=1, dtype=jnp.int32)
    return code, odd


def layer(tokens, weight, block_mask, act_grad):
    d, width = weight.shape
    t = lax.axis_index("tensor").astype(jnp.int32)
    g = lax.axis_index("dp").astype(jnp.int32)
    z, xh, core = t >> 2, (t >> 1) & 1, t & 1
    xl, y = g >> 2, g & 3

    partner = move(tokens, dc=1)
    home = move(tokens, dx=1)
    chip = jnp.concatenate([tokens, partner], axis=0)
    t, chip = lax.optimization_barrier((t, chip))
    near = [move(chip, dz=k) for k in (1, 2, 3)]
    far = move(chip[:16], dz=4)

    masked = call(
        mask_kernel,
        1,
        jax.ShapeDtypeStruct((d, width), BF16),
        ((t * 14).reshape(1), weight, block_mask),
        d * width,
        scratch=(pltpu.VMEM((64, width), F32),),
    )
    code, odd = kept_codes(block_mask, t, width)

    n = jnp.arange(32, dtype=jnp.int32)
    slot = n & 7
    dist = jnp.where(slot == 0, 0, jnp.where(slot == 1, 4, slot >> 1))
    flip = jnp.where(slot > 1, slot & 1, 0)
    gather_core = core ^ ((n >> 3) & 1)
    zk = (z - (1 - 2 * gather_core) * dist) & (NZ - 1)
    idx = zk * 4 + (xh ^ (n >> 4)) * 2 + (gather_core ^ flip)
    order = [(1, 2), (0, 2), (1, 1), (0, 3), (1, 3), (0, 1), (1, 0), (0, 0)]
    dx = jnp.array([o[0] for o in order], jnp.int32)
    dy = jnp.array([o[1] for o in order], jnp.int32)
    dests = (xl ^ dx) * NY + ((y + dy) & (NY - 1))

    near[0], masked, code, odd, idx, dests = lax.optimization_barrier(
        (near[0], masked, code, odd, idx, dests)
    )
    scalars = (dests, code, odd)

    tick = call(tick_kernel, 1, jax.ShapeDtypeStruct((8, 128), F32), (dests,), 0)
    near_x = [move(near[k], dx=1) for k in range(3)]
    far_x = move(far, dx=1)
    x0 = jnp.concatenate([tokens, far, *near], axis=0)
    x2 = move(x0, dc=1)
    x1 = jnp.concatenate([home, far_x, *near_x], axis=0)
    x3 = move(x1, dc=1)
    xs = (x0, x1, x2, x3)

    grads = act_grad.reshape(32, 16, width)
    act, p, pa = forward(0, idx, x0, x2, masked, grads, after=(tick,))
    own_a, other_a = xgrad(p, masked)
    act, p, pb = forward(16, idx, x1, x3, masked, grads, (act,), (other_a,))

    parts = []

    def pack_two(first, after):
        packed = wgrad(first, 2, scalars, pa, pb, xs, after)
        for v, o in zip(packed, order[first : first + 2]):
            parts.append(v if o == (0, 0) else move_dp(v, *o))
        return (packed[0],)

    done = pack_two(0, ())
    done, back_a = send_back(own_a, other_a, done)
    done = pack_two(2, (done,))
    own_b, other_b = xgrad(p, masked, done)
    done = pack_two(4, (other_b,))
    done, back_b = send_back(own_b, other_b, done)
    pack_two(6, (done,))

    to_core, kept = call(
        sum_kernel,
        0,
        (jax.ShapeDtypeStruct((32, d), BF16), jax.ShapeDtypeStruct((32, d), F32)),
        (*back_a, *back_b),
        10 * 32 * d,
    )
    to_x, kept = call(
        sum_core_kernel,
        0,
        (jax.ShapeDtypeStruct((16, d), BF16), jax.ShapeDtypeStruct((16, d), F32)),
        (kept, move(to_core, dc=1)),
        32 * d,
    )
    x_grad = (kept + move(to_x, dx=1).astype(F32)).astype(BF16)

    weight_grad = call(
        unpack_kernel,
        2,
        jax.ShapeDtypeStruct((512, width), F32),
        (g.reshape(1), code, *parts),
        8 * CAP * 4096,
        scratch=(pltpu.VMEM((width + BLOCK, 512), F32),),
    )
    return (act.reshape(512, width), x_grad, weight_grad)


def solution(mesh):
    return jax.shard_map(
        layer,
        mesh=mesh,
        in_specs=(P(("dp", "tensor"), None), P(None, "tensor"), P(), P("dp", "tensor")),
        out_specs=(P("dp", "tensor"), P(("dp", "tensor"), None), P("dp", "tensor")),
        check_vma=False,
    )
```

profile of v0, /device:TPU:8, one launch (start us, length us, event | category | flops | bytes accessed | tf_op | source)
XLA Modules:
  0.0 186.1 jit_solution(7832887752952455744)
XLA Ops:
  0.7 3.1 %collective-permute-start.2 = (bf16[16,4096]{1,0:T(8,128)(2,1)}, bf16[16,4096]{1,0:T(8,128)(2,1)S(1)}, u32[]{:S(2)}, u32[]{:S(2)}) collective-permute-start(bf16[16,4096]{1,0:T(8,128)(2,1)} %param.7), channel_id=1, source_target_pairs={{0,2},{1,3},{2,0},{3,1},{4,6},{5,7},{6,4},{7,5},{8,10},{9,11},{10,... | collective-permute-start | bytes 393224 | tf_op jit(solution)/shard_map/ppermute | solution.py:43
  3.8 0.9 constant_dynamic-update-slice_fusion.9
  4.8 0.7 and_add_fusion.refs_0_
  5.5 0.9 pad_maximum_fusion
  6.4 4.7 %collective-permute-start.8 = (bf16[32,4096]{1,0:T(8,128)(2,1)S(1)}, bf16[32,4096]{1,0:T(8,128)(2,1)S(1)}, u32[]{:S(2)}, u32[]{:S(2)}) collective-permute-start(bf16[32,4096]{1,0:T(8,128)(2,1)S(1)} %pad_maximum_fusion), channel_id=1, source_target_pairs={{0,12},{1,21},{2,14},{3,23},{4,16},{5,25},{6,18},{7,27},{8,20},{9,... | collective-permute-start | bytes 786440 | tf_op jit(solution)/shard_map/ppermute | solution.py:43
  11.1 3.6 %collective-permute-start.6 = (bf16[32,4096]{1,0:T(8,128)(2,1)S(1)}, bf16[32,4096]{1,0:T(8,128)(2,1)S(1)}, u32[]{:S(2)}, u32[]{:S(2)}) collective-permute-start(bf16[32,4096]{1,0:T(8,128)(2,1)S(1)} %pad_maximum_fusion), channel_id=1, source_target_pairs={{0,8},{1,25},{2,10},{3,27},{4,12},{5,29},{6,14},{7,31},{8,16},{9,1... | collective-permute-start | bytes 786440 | tf_op jit(solution)/shard_map/ppermute | solution.py:43
  14.7 1.0 collective-permute-start.1
  15.8 0.9 dynamic-slice_compare_fusion
  16.8 1.0 convert_reduce_fusion
  17.8 1.9 %select_reduce_fusion = s32[8,70]{0,1:T(8,128)S(1)} fusion(s32[112]{0:T(128)} %constant.75, s32[8,112]{1,0:T(8,128)S(1)} %get-tuple-element.84, pred[8,112]{1,0:T(8,128)(4,1)S(1)} %ne.15), kind=kLoop, calls=%fused_computation.2 | loop fusion | flops 250320 | bytes 7168 | tf_op jit(solution)/shard_map/reduce_sum | solution.py:327
  20.4 3.1 %copy-done = bf16[4096,896]{1,0:T(8,128)(2,1)S(1)} copy-done((bf16[4096,896]{1,0:T(8,128)(2,1)S(1)}, bf16[4096,896]{1,0:T(8,128)(2,1)}, u32[]{:S(2)}) %copy-start) | copy-done | bytes 7340056
  23.5 0.9 copy-done.2
  24.4 1.4 shard_map.94.refs_3_.refs_1_
  25.8 12.5 %collective-permute-done.3 = bf16[16,4096]{1,0:T(8,128)(2,1)S(1)} collective-permute-done((bf16[16,4096]{1,0:T(8,128)(2,1)S(1)}, bf16[16,4096]{1,0:T(8,128)(2,1)S(1)}, u32[]{:S(2)}, u32[]{:S(2)}) %collective-permute-start.3) | collective-permute-done | bytes 131104 | tf_op jit(solution)/shard_map/ppermute | solution.py:43
  38.8 3.1 %collective-permute-start.5 = (bf16[32,4096]{1,0:T(8,128)(2,1)S(1)}, bf16[32,4096]{1,0:T(8,128)(2,1)S(1)}, u32[]{:S(2)}, u32[]{:S(2)}) collective-permute-start(bf16[32,4096]{1,0:T(8,128)(2,1)S(1)} %collective-permute-done.1), channel_id=1, source_target_pairs={{0,2},{1,3},{2,0},{3,1},{4,6},{5,7},{6,4},{7,5},{8,10},{9,11},{10,... | collective-permute-start | bytes 786440 | tf_op jit(solution)/shard_map/ppermute | solution.py:43
  43.3 3.0 %collective-permute-start.7 = (bf16[32,4096]{1,0:T(8,128)(2,1)S(1)}, bf16[32,4096]{1,0:T(8,128)(2,1)S(1)}, u32[]{:S(2)}, u32[]{:S(2)}) collective-permute-start(bf16[32,4096]{1,0:T(8,128)(2,1)S(1)} %collective-permute-done.6), channel_id=1, source_target_pairs={{0,2},{1,3},{2,0},{3,1},{4,6},{5,7},{6,4},{7,5},{8,10},{9,11},{10,... | collective-permute-start | bytes 786440 | tf_op jit(solution)/shard_map/ppermute | solution.py:43
  46.3 1.5 collective-permute-done.5
  47.9 10.9 %collective-permute-done.7 = bf16[32,4096]{1,0:T(8,128)(2,1)S(1)} collective-permute-done((bf16[32,4096]{1,0:T(8,128)(2,1)S(1)}, bf16[32,4096]{1,0:T(8,128)(2,1)S(1)}, u32[]{:S(2)}, u32[]{:S(2)}) %collective-permute-start.7) | collective-permute-done | bytes 262176 | tf_op jit(solution)/shard_map/ppermute | solution.py:43
  59.0 4.1 %shard_map.96 = (bf16[16,16,896]{2,1,0:T(8,128)(2,1)S(1)}, bf16[256,896]{1,0:T(8,128)(2,1)S(1)}, bf16[896,256]{1,0:T(8,128)(2,1)S(1)}) custom-call(s32[32]{0:T(128)S(1)} %fusion.9.refs_0_, bf16[128,4096]{1,0:T(8,128)(2,1)S(1)} %constant_dynamic-update-slice_fusion.5.refs_1_.refs_5_, bf16[128,4096]{1,0:T(8,128)(2,1)S(1)} %collective-permute-done.11.refs_2_.refs_7_, ...), custom_call_target="tpu_custom_call" | custom-call | flops 1879048192 | bytes 10354816 | tf_op jit(solution)/shard_map/pallas_call | solution.py:59
  63.1 3.8 %shard_map.97 = (f32[128,4096]{1,0:T(8,128)S(1)}, bf16[128,4096]{1,0:T(8,128)(2,1)S(1)}) custom-call(bf16[256,896]{1,0:T(8,128)(2,1)S(1)} %get-tuple-element.50.refs_0_, bf16[4096,896]{1,0:T(8,128)(2,1)S(1)} %shard_map.94.refs_3_.refs_1_), custom_call_target="tpu_custom_call" | custom-call | flops 1879048192 | bytes 7798784 | tf_op jit(solution)/shard_map/pallas_call | solution.py:59
  66.8 0.8 collective-permute-start.12
  67.6 4.8 %shard_map.98 = (bf16[32,16,896]{2,1,0:T(8,128)(2,1)}, bf16[256,896]{1,0:T(8,128)(2,1)S(1)}, bf16[896,256]{1,0:T(8,128)(2,1)S(1)}) custom-call(s32[32]{0:T(128)S(1)} %fusion.9.refs_0_, bf16[128,4096]{1,0:T(8,128)(2,1)S(1)} %constant_dynamic-update-slice_fusion.refs_1_.refs_6_, bf16[128,4096]{1,0:T(8,128)(2,1)S(1)} %collective-permute-done.10.refs_2_.refs_8_, ...), custom_call_target="tpu_custom_call" | custom-call | flops 1879048192 | bytes 10813568 | tf_op jit(solution)/shard_map/pallas_call | solution.py:59
  72.4 2.7 %shard_map.99 = (bf16[35,64,128]{2,1,0:T(8,128)(2,1)S(1)}, bf16[35,64,128]{2,1,0:T(8,128)(2,1)S(1)}) custom-call(s32[8]{0:T(128)S(1)} %and_add_fusion.refs_0_, s32[8,70]{1,0:T(8,128)S(1)} %broadcast_add_fusion.refs_1_, s32[8]{0:T(128)S(1)} %get-tuple-element.55.refs_2_, bf16[896,256]{1,0:T(8,128)(2,1)S(1)} %get-tuple-element.56.refs_3_, ...), custom_call_target="tpu_custom_call" | custom-call | flops 939524096 | bytes 5114112 | tf_op jit(solution)/shard_map/pallas_call | solution.py:59
  75.4 2.7 %shard_map.101 = (bf16[35,64,128]{2,1,0:T(8,128)(2,1)S(1)}, bf16[35,64,128]{2,1,0:T(8,128)(2,1)S(1)}) custom-call(s32[8]{0:T(128)S(1)} %and_add_fusion.refs_0_, s32[8,70]{1,0:T(8,128)S(1)} %broadcast_add_fusion.refs_1_, s32[8]{0:T(128)S(1)} %get-tuple-element.55.refs_2_, bf16[896,256]{1,0:T(8,128)(2,1)S(1)} %get-tuple-element.56.refs_3_, ...), custom_call_target="tpu_custom_call" | custom-call | flops 939524096 | bytes 5114112 | tf_op jit(solution)/shard_map/pallas_call | solution.py:59
  78.2 3.8 %shard_map.102 = (f32[128,4096]{1,0:T(8,128)S(1)}, bf16[128,4096]{1,0:T(8,128)(2,1)S(1)}) custom-call(bf16[256,896]{1,0:T(8,128)(2,1)S(1)} %get-tuple-element.64.refs_0_, bf16[4096,896]{1,0:T(8,128)(2,1)S(1)} %shard_map.94.refs_3_.refs_1_, bf16[35,64,128]{2,1,0:T(8,128)(2,1)S(1)} %get-tuple-element.65.refs_2_), custom_call_target="tpu_custom_call" | custom-call | flops 1879048192 | bytes 7798784 | tf_op jit(solution)/shard_map/pallas_call | solution.py:59
  82.0 2.0 %collective-permute-start.13 = (bf16[32,4096]{1,0:T(8,128)(2,1)S(1)}, bf16[32,4096]{1,0:T(8,128)(2,1)S(1)}, u32[]{:S(2)}, u32[]{:S(2)}) collective-permute-start(bf16[32,4096]{1,0:T(8,128)(2,1)S(1)} %get-tuple-element.59), channel_id=1, source_target_pairs={{0,20},{1,13},{2,22},{3,15},{4,24},{5,17},{6,26},{7,19},{8,28},{9,... | collective-permute-start | bytes 786440 | tf_op jit(solution)/shard_map/ppermute | solution.py:43
  84.0 3.8 %collective-permute-start.14 = (bf16[32,4096]{1,0:T(8,128)(2,1)S(1)}, bf16[32,4096]{1,0:T(8,128)(2,1)S(1)}, u32[]{:S(2)}, u32[]{:S(2)}) collective-permute-start(bf16[32,4096]{1,0:T(8,128)(2,1)S(1)} %get-tuple-element.60), channel_id=1, source_target_pairs={{0,24},{1,9},{2,26},{3,11},{4,28},{5,13},{6,30},{7,15},{8,0},{9,17... | collective-permute-start | bytes 786440 | tf_op jit(solution)/shard_map/ppermute | solution.py:43
  87.8 4.3 %collective-permute-start.16 = (bf16[16,4096]{1,0:T(8,128)(2,1)S(1)}, bf16[16,4096]{1,0:T(8,128)(2,1)S(1)}, u32[]{:S(2)}, u32[]{:S(2)}) collective-permute-start(bf16[16,4096]{1,0:T(8,128)(2,1)S(1)} %get-tuple-element.62), channel_id=1, source_target_pairs={{0,16},{1,17},{2,18},{3,19},{4,20},{5,21},{6,22},{7,23},{8,24},{9,... | collective-permute-start | bytes 393224 | tf_op jit(solution)/shard_map/ppermute | solution.py:43
  92.1 2.7 %shard_map.103 = (bf16[35,64,128]{2,1,0:T(8,128)(2,1)S(1)}, bf16[35,64,128]{2,1,0:T(8,128)(2,1)S(1)}) custom-call(s32[8]{0:T(128)S(1)} %and_add_fusion.refs_0_, s32[8,70]{1,0:T(8,128)S(1)} %broadcast_add_fusion.refs_1_, s32[8]{0:T(128)S(1)} %get-tuple-element.55.refs_2_, bf16[896,256]{1,0:T(8,128)(2,1)S(1)} %get-tuple-element.56.refs_3_, ...), custom_call_target="tpu_custom_call" | custom-call | flops 939524096 | bytes 5114112 | tf_op jit(solution)/shard_map/pallas_call | solution.py:59
  95.0 1.7 collective-permute-start.21
  96.8 3.3 %collective-permute-done.16.refs_3_ = bf16[16,4096]{1,0:T(8,128)(2,1)S(1)} collective-permute-done((bf16[16,4096]{1,0:T(8,128)(2,1)S(1)}, bf16[16,4096]{1,0:T(8,128)(2,1)S(1)}, u32[]{:S(2)}, u32[]{:S(2)}) %collective-permute-start.16) | collective-permute-done | bytes 131104 | tf_op jit(solution)/shard_map/ppermute | solution.py:43
  100.0 2.4 %collective-permute-start.25 = (bf16[35,64,128]{2,1,0:T(8,128)(2,1)S(1)}, bf16[35,64,128]{2,1,0:T(8,128)(2,1)S(1)}, u32[]{:S(2)}, u32[]{:S(2)}) collective-permute-start(bf16[35,64,128]{2,1,0:T(8,128)(2,1)S(1)} %get-tuple-element.78), channel_id=1, source_target_pairs={{0,64},{32,96},{64,0},{96,32},{128,192},{160,224},{192,128},{224,1... | collective-permute-start | bytes 1720328 | tf_op jit(solution)/shard_map/ppermute | solution.py:47
  102.4 0.9 collective-permute-start.24
  103.3 16.1 %collective-permute-start.18 = (bf16[32,4096]{1,0:T(8,128)(2,1)S(1)}, bf16[32,4096]{1,0:T(8,128)(2,1)S(1)}, u32[]{:S(2)}, u32[]{:S(2)}) collective-permute-start(bf16[32,4096]{1,0:T(8,128)(2,1)S(1)} %get-tuple-element.69), channel_id=1, source_target_pairs={{0,20},{1,13},{2,22},{3,15},{4,24},{5,17},{6,26},{7,19},{8,28},{9,... | collective-permute-start | bytes 786440 | tf_op jit(solution)/shard_map/ppermute | solution.py:43
  119.4 2.5 %collective-permute-start.19 = (bf16[32,4096]{1,0:T(8,128)(2,1)S(1)}, bf16[32,4096]{1,0:T(8,128)(2,1)S(1)}, u32[]{:S(2)}, u32[]{:S(2)}) collective-permute-start(bf16[32,4096]{1,0:T(8,128)(2,1)S(1)} %get-tuple-element.70), channel_id=1, source_target_pairs={{0,24},{1,9},{2,26},{3,11},{4,28},{5,13},{6,30},{7,15},{8,0},{9,17... | collective-permute-start | bytes 786440 | tf_op jit(solution)/shard_map/ppermute | solution.py:43
  121.9 5.6 %collective-permute-done.18.refs_5_ = bf16[32,4096]{1,0:T(8,128)(2,1)S(1)} collective-permute-done((bf16[32,4096]{1,0:T(8,128)(2,1)S(1)}, bf16[32,4096]{1,0:T(8,128)(2,1)S(1)}, u32[]{:S(2)}, u32[]{:S(2)}) %collective-permute-start.18) | collective-permute-done | bytes 262176 | tf_op jit(solution)/shard_map/ppermute | solution.py:43
  127.6 8.9 %collective-permute-done.19.refs_6_ = bf16[32,4096]{1,0:T(8,128)(2,1)S(1)} collective-permute-done((bf16[32,4096]{1,0:T(8,128)(2,1)S(1)}, bf16[32,4096]{1,0:T(8,128)(2,1)S(1)}, u32[]{:S(2)}, u32[]{:S(2)}) %collective-permute-start.19) | collective-permute-done | bytes 262176 | tf_op jit(solution)/shard_map/ppermute | solution.py:43
  137.6 3.9 %collective-permute-start.26 = (bf16[35,64,128]{2,1,0:T(8,128)(2,1)S(1)}, bf16[35,64,128]{2,1,0:T(8,128)(2,1)S(1)}, u32[]{:S(2)}, u32[]{:S(2)}) collective-permute-start(bf16[35,64,128]{2,1,0:T(8,128)(2,1)S(1)} %get-tuple-element.65.refs_2_), channel_id=1, source_target_pairs={{0,160},{32,192},{64,224},{96,128},{128,32},{160,64},{192,96},{224... | collective-permute-start | bytes 1720328 | tf_op jit(solution)/shard_map/ppermute | solution.py:47
  141.5 2.7 %shard_map.107 = (bf16[35,64,128]{2,1,0:T(8,128)(2,1)S(1)}, bf16[35,64,128]{2,1,0:T(8,128)(2,1)S(1)}) custom-call(s32[8]{0:T(128)S(1)} %and_add_fusion.refs_0_, s32[8,70]{1,0:T(8,128)S(1)} %broadcast_add_fusion.refs_1_, s32[8]{0:T(128)S(1)} %get-tuple-element.55.refs_2_, bf16[896,256]{1,0:T(8,128)(2,1)S(1)} %get-tuple-element.56.refs_3_, ...), custom_call_target="tpu_custom_call" | custom-call | flops 939524096 | bytes 5114112 | tf_op jit(solution)/shard_map/pallas_call | solution.py:59
  144.3 0.9 collective-permute-start.28
  145.2 2.7 %collective-permute-start.30 = (bf16[35,64,128]{2,1,0:T(8,128)(2,1)S(1)}, bf16[35,64,128]{2,1,0:T(8,128)(2,1)S(1)}, u32[]{:S(2)}, u32[]{:S(2)}) collective-permute-start(bf16[35,64,128]{2,1,0:T(8,128)(2,1)S(1)} %get-tuple-element.81), channel_id=1, source_target_pairs={{0,128},{32,160},{64,192},{96,224},{128,0},{160,32},{192,64},{224,... | collective-permute-start | bytes 1720328 | tf_op jit(solution)/shard_map/ppermute | solution.py:47
  148.0 4.5 %collective-permute-done.27.refs_5_ = bf16[35,64,128]{2,1,0:T(8,128)(2,1)S(1)} collective-permute-done((bf16[35,64,128]{2,1,0:T(8,128)(2,1)S(1)}, bf16[35,64,128]{2,1,0:T(8,128)(2,1)S(1)}, u32[]{:S(2)}, u32[]{:S(2)}) %collective-permute-start.27) | collective-permute-done | bytes 573472 | tf_op jit(solution)/shard_map/ppermute | solution.py:47
  152.5 2.6 %collective-permute-start.23 = (bf16[16,4096]{1,0:T(8,128)(2,1)S(1)}, bf16[16,4096]{1,0:T(8,128)(2,1)S(1)}, u32[]{:S(2)}, u32[]{:S(2)}) collective-permute-start(bf16[16,4096]{1,0:T(8,128)(2,1)S(1)} %get-tuple-element.77), channel_id=1, source_target_pairs={{0,2},{1,3},{2,0},{3,1},{4,6},{5,7},{6,4},{7,5},{8,10},{9,11},{10,... | collective-permute-start | bytes 393224 | tf_op jit(solution)/shard_map/ppermute | solution.py:43
  155.1 1.1 collective-permute-done.26.refs_4_
  156.2 11.4 %collective-permute-done.29.refs_7_ = bf16[35,64,128]{2,1,0:T(8,128)(2,1)S(1)} collective-permute-done((bf16[35,64,128]{2,1,0:T(8,128)(2,1)S(1)}, bf16[35,64,128]{2,1,0:T(8,128)(2,1)S(1)}, u32[]{:S(2)}, u32[]{:S(2)}) %collective-permute-start.29) | collective-permute-done | bytes 573472 | tf_op jit(solution)/shard_map/ppermute | solution.py:47
  167.9 11.7 %collective-permute-done.30.refs_8_ = bf16[35,64,128]{2,1,0:T(8,128)(2,1)S(1)} collective-permute-done((bf16[35,64,128]{2,1,0:T(8,128)(2,1)S(1)}, bf16[35,64,128]{2,1,0:T(8,128)(2,1)S(1)}, u32[]{:S(2)}, u32[]{:S(2)}) %collective-permute-start.30) | collective-permute-done | bytes 573472 | tf_op jit(solution)/shard_map/ppermute | solution.py:47
  179.5 5.9 %shard_map.108 = f32[512,896]{1,0:T(8,128)} custom-call(s32[1]{0:T(128)} %bitcast.3.refs_0_, s32[8,70]{1,0:T(8,128)S(1)} %broadcast_add_fusion.refs_1_, bf16[35,64,128]{2,1,0:T(8,128)(2,1)S(1)} %collective-permute-done.24.refs_2_, bf16[35,64,128]{2,1,0:T(8,128)(2,1)S(1)} %collective-permute-done.25.refs_3_, ...), custom_call_target="tpu_custom_call" | custom-call | flops 2293760 | bytes 4589764 | tf_op jit(solution)/shard_map/pallas_call | solution.py:59
  185.5 0.7 add_convert_fusion
  (56 shorter events, 5.0 us)
Async XLA Ops:
  0.6 4.9 %collective-permute-start = (bf16[16,4096]{1,0:T(8,128)(2,1)}, bf16[16,4096]{1,0:T(8,128)(2,1)S(1)}, u32[]{:S(2)}, u32[]{:S(2)}) collective-permute-start(bf16[16,4096]{1,0:T(8,128)(2,1)} %param.7), channel_id=1, source_target_pairs={{0,1},{1,0},{2,3},{3,2},{4,5},{5,4},{6,7},{7,6},{8,9},{9,8},{10,11... | collective-permute-start | bytes 393224 | tf_op jit(solution)/shard_map/ppermute | solution.py:43
  0.7 25.1 %collective-permute-start.2 = (bf16[16,4096]{1,0:T(8,128)(2,1)}, bf16[16,4096]{1,0:T(8,128)(2,1)S(1)}, u32[]{:S(2)}, u32[]{:S(2)}) collective-permute-start(bf16[16,4096]{1,0:T(8,128)(2,1)} %param.7), channel_id=1, source_target_pairs={{0,2},{1,3},{2,0},{3,1},{4,6},{5,7},{6,4},{7,5},{8,10},{9,11},{10,... | collective-permute-start | bytes 393224 | tf_op jit(solution)/shard_map/ppermute | solution.py:43
  6.4 35.5 %collective-permute-start.8 = (bf16[32,4096]{1,0:T(8,128)(2,1)S(1)}, bf16[32,4096]{1,0:T(8,128)(2,1)S(1)}, u32[]{:S(2)}, u32[]{:S(2)}) collective-permute-start(bf16[32,4096]{1,0:T(8,128)(2,1)S(1)} %pad_maximum_fusion), channel_id=1, source_target_pairs={{0,12},{1,21},{2,14},{3,23},{4,16},{5,25},{6,18},{7,27},{8,20},{9,... | collective-permute-start | bytes 786440 | tf_op jit(solution)/shard_map/ppermute | solution.py:43
  11.1 30.8 %collective-permute-start.6 = (bf16[32,4096]{1,0:T(8,128)(2,1)S(1)}, bf16[32,4096]{1,0:T(8,128)(2,1)S(1)}, u32[]{:S(2)}, u32[]{:S(2)}) collective-permute-start(bf16[32,4096]{1,0:T(8,128)(2,1)S(1)} %pad_maximum_fusion), channel_id=1, source_target_pairs={{0,8},{1,25},{2,10},{3,27},{4,12},{5,29},{6,14},{7,31},{8,16},{9,1... | collective-permute-start | bytes 786440 | tf_op jit(solution)/shard_map/ppermute | solution.py:43
  14.7 24.1 %collective-permute-start.1 = (bf16[32,4096]{1,0:T(8,128)(2,1)S(1)}, bf16[32,4096]{1,0:T(8,128)(2,1)S(1)}, u32[]{:S(2)}, u32[]{:S(2)}) collective-permute-start(bf16[32,4096]{1,0:T(8,128)(2,1)S(1)} %pad_maximum_fusion), channel_id=1, source_target_pairs={{0,4},{1,29},{2,6},{3,31},{4,8},{5,1},{6,10},{7,3},{8,12},{9,5},{1... | collective-permute-start | bytes 786440 | tf_op jit(solution)/shard_map/ppermute | solution.py:43
  19.8 18.5 %collective-permute-start.3 = (bf16[16,4096]{1,0:T(8,128)(2,1)S(1)}, bf16[16,4096]{1,0:T(8,128)(2,1)S(1)}, u32[]{:S(2)}, u32[]{:S(2)}) collective-permute-start(bf16[16,4096]{1,0:T(8,128)(2,1)S(1)} %slice.3), channel_id=1, source_target_pairs={{0,16},{1,17},{2,18},{3,19},{4,20},{5,21},{6,22},{7,23},{8,24},{9,... | collective-permute-start | bytes 393224 | tf_op jit(solution)/shard_map/ppermute | solution.py:43
  20.4 3.1 %copy-start = (bf16[4096,896]{1,0:T(8,128)(2,1)S(1)}, bf16[4096,896]{1,0:T(8,128)(2,1)}, u32[]{:S(2)}) copy-start(bf16[4096,896]{1,0:T(8,128)(2,1)} %refs_1_.1) | copy-start | bytes 22020100
  23.5 0.9 copy-start.2
  25.8 33.2 %copy-start.1 = (bf16[512,896]{1,0:T(8,128)(2,1)S(1)}, bf16[512,896]{1,0:T(8,128)(2,1)}, u32[]{:S(2)}) copy-start(bf16[512,896]{1,0:T(8,128)(2,1)} %param.10) | copy-start | bytes 2752516
  38.3 8.0 %collective-permute-start.4 = (bf16[16,4096]{1,0:T(8,128)(2,1)S(1)}, bf16[16,4096]{1,0:T(8,128)(2,1)S(1)}, u32[]{:S(2)}, u32[]{:S(2)}) collective-permute-start(bf16[16,4096]{1,0:T(8,128)(2,1)S(1)} %collective-permute-done.3), channel_id=1, source_target_pairs={{0,2},{1,3},{2,0},{3,1},{4,6},{5,7},{6,4},{7,5},{8,10},{9,11},{10,... | collective-permute-start | bytes 393224 | tf_op jit(solution)/shard_map/ppermute | solution.py:43
  38.8 9.0 %collective-permute-start.5 = (bf16[32,4096]{1,0:T(8,128)(2,1)S(1)}, bf16[32,4096]{1,0:T(8,128)(2,1)S(1)}, u32[]{:S(2)}, u32[]{:S(2)}) collective-permute-start(bf16[32,4096]{1,0:T(8,128)(2,1)S(1)} %collective-permute-done.1), channel_id=1, source_target_pairs={{0,2},{1,3},{2,0},{3,1},{4,6},{5,7},{6,4},{7,5},{8,10},{9,11},{10,... | collective-permute-start | bytes 786440 | tf_op jit(solution)/shard_map/ppermute | solution.py:43
  42.6 16.4 %collective-permute-start.11 = (bf16[128,4096]{1,0:T(8,128)(2,1)S(1)}, bf16[128,4096]{1,0:T(8,128)(2,1)S(1)}, u32[]{:S(2)}, u32[]{:S(2)}) collective-permute-start(bf16[128,4096]{1,0:T(8,128)(2,1)S(1)} %constant_dynamic-update-slice_fusion.5.refs_1_.refs_5_), channel_id=1, source_target_pairs={{0,1},{1,0},{2,3},{3,2},{4,5},{5,4},{6,7},{7,6},{8,9},{9,8},{10,11... | collective-permute-start | bytes 3145736 | tf_op jit(solution)/shard_map/ppermute | solution.py:43
  42.7 16.1 %collective-permute-start.9 = (bf16[32,4096]{1,0:T(8,128)(2,1)S(1)}, bf16[32,4096]{1,0:T(8,128)(2,1)S(1)}, u32[]{:S(2)}, u32[]{:S(2)}) collective-permute-start(bf16[32,4096]{1,0:T(8,128)(2,1)S(1)} %collective-permute-done.8), channel_id=1, source_target_pairs={{0,2},{1,3},{2,0},{3,1},{4,6},{5,7},{6,4},{7,5},{8,10},{9,11},{10,... | collective-permute-start | bytes 786440 | tf_op jit(solution)/shard_map/ppermute | solution.py:43
  43.3 15.5 %collective-permute-start.7 = (bf16[32,4096]{1,0:T(8,128)(2,1)S(1)}, bf16[32,4096]{1,0:T(8,128)(2,1)S(1)}, u32[]{:S(2)}, u32[]{:S(2)}) collective-permute-start(bf16[32,4096]{1,0:T(8,128)(2,1)S(1)} %collective-permute-done.6), channel_id=1, source_target_pairs={{0,2},{1,3},{2,0},{3,1},{4,6},{5,7},{6,4},{7,5},{8,10},{9,11},{10,... | collective-permute-start | bytes 786440 | tf_op jit(solution)/shard_map/ppermute | solution.py:43
  58.9 8.8 %collective-permute-start.10 = (bf16[128,4096]{1,0:T(8,128)(2,1)S(1)}, bf16[128,4096]{1,0:T(8,128)(2,1)S(1)}, u32[]{:S(2)}, u32[]{:S(2)}) collective-permute-start(bf16[128,4096]{1,0:T(8,128)(2,1)S(1)} %constant_dynamic-update-slice_fusion.refs_1_.refs_6_), channel_id=1, source_target_pairs={{0,1},{1,0},{2,3},{3,2},{4,5},{5,4},{6,7},{7,6},{8,9},{9,8},{10,11... | collective-permute-start | bytes 3145736 | tf_op jit(solution)/shard_map/ppermute | solution.py:43
  66.8 8.3 %collective-permute-start.12 = (bf16[128,4096]{1,0:T(8,128)(2,1)S(1)}, bf16[128,4096]{1,0:T(8,128)(2,1)S(1)}, u32[]{:S(2)}, u32[]{:S(2)}) collective-permute-start(bf16[128,4096]{1,0:T(8,128)(2,1)S(1)} %get-tuple-element.51.refs_6_), channel_id=1, source_target_pairs={{0,1},{1,0},{2,3},{3,2},{4,5},{5,4},{6,7},{7,6},{8,9},{9,8},{10,11... | collective-permute-start | bytes 3145736 | tf_op jit(solution)/shard_map/ppermute | solution.py:43
  81.9 12.9 %collective-permute-start.17 = (bf16[128,4096]{1,0:T(8,128)(2,1)S(1)}, bf16[128,4096]{1,0:T(8,128)(2,1)S(1)}, u32[]{:S(2)}, u32[]{:S(2)}) collective-permute-start(bf16[128,4096]{1,0:T(8,128)(2,1)S(1)} %get-tuple-element.67.refs_9_), channel_id=1, source_target_pairs={{0,1},{1,0},{2,3},{3,2},{4,5},{5,4},{6,7},{7,6},{8,9},{9,8},{10,11... | collective-permute-start | bytes 3145736 | tf_op jit(solution)/shard_map/ppermute | solution.py:43
  82.0 20.4 %collective-permute-start.13 = (bf16[32,4096]{1,0:T(8,128)(2,1)S(1)}, bf16[32,4096]{1,0:T(8,128)(2,1)S(1)}, u32[]{:S(2)}, u32[]{:S(2)}) collective-permute-start(bf16[32,4096]{1,0:T(8,128)(2,1)S(1)} %get-tuple-element.59), channel_id=1, source_target_pairs={{0,20},{1,13},{2,22},{3,15},{4,24},{5,17},{6,26},{7,19},{8,28},{9,... | collective-permute-start | bytes 786440 | tf_op jit(solution)/shard_map/ppermute | solution.py:43
  84.0 19.3 %collective-permute-start.14 = (bf16[32,4096]{1,0:T(8,128)(2,1)S(1)}, bf16[32,4096]{1,0:T(8,128)(2,1)S(1)}, u32[]{:S(2)}, u32[]{:S(2)}) collective-permute-start(bf16[32,4096]{1,0:T(8,128)(2,1)S(1)} %get-tuple-element.60), channel_id=1, source_target_pairs={{0,24},{1,9},{2,26},{3,11},{4,28},{5,13},{6,30},{7,15},{8,0},{9,17... | collective-permute-start | bytes 786440 | tf_op jit(solution)/shard_map/ppermute | solution.py:43
  87.8 31.6 %collective-permute-start.15 = (bf16[32,4096]{1,0:T(8,128)(2,1)S(1)}, bf16[32,4096]{1,0:T(8,128)(2,1)S(1)}, u32[]{:S(2)}, u32[]{:S(2)}) collective-permute-start(bf16[32,4096]{1,0:T(8,128)(2,1)S(1)} %get-tuple-element.61.refs_9_), channel_id=1, source_target_pairs={{0,28},{1,5},{2,30},{3,7},{4,0},{5,9},{6,2},{7,11},{8,4},{9,13},{1... | collective-permute-start | bytes 786440 | tf_op jit(solution)/shard_map/ppermute | solution.py:43
  87.8 12.3 %collective-permute-start.16 = (bf16[16,4096]{1,0:T(8,128)(2,1)S(1)}, bf16[16,4096]{1,0:T(8,128)(2,1)S(1)}, u32[]{:S(2)}, u32[]{:S(2)}) collective-permute-start(bf16[16,4096]{1,0:T(8,128)(2,1)S(1)} %get-tuple-element.62), channel_id=1, source_target_pairs={{0,16},{1,17},{2,18},{3,19},{4,20},{5,21},{6,22},{7,23},{8,24},{9,... | collective-permute-start | bytes 393224 | tf_op jit(solution)/shard_map/ppermute | solution.py:43
  95.0 26.9 %collective-permute-start.21 = (bf16[16,4096]{1,0:T(8,128)(2,1)S(1)}, bf16[16,4096]{1,0:T(8,128)(2,1)S(1)}, u32[]{:S(2)}, u32[]{:S(2)}) collective-permute-start(bf16[16,4096]{1,0:T(8,128)(2,1)S(1)} %get-tuple-element.72), channel_id=1, source_target_pairs={{0,16},{1,17},{2,18},{3,19},{4,20},{5,21},{6,22},{7,23},{8,24},{9,... | collective-permute-start | bytes 393224 | tf_op jit(solution)/shard_map/ppermute | solution.py:43
  100.0 44.2 %collective-permute-start.25 = (bf16[35,64,128]{2,1,0:T(8,128)(2,1)S(1)}, bf16[35,64,128]{2,1,0:T(8,128)(2,1)S(1)}, u32[]{:S(2)}, u32[]{:S(2)}) collective-permute-start(bf16[35,64,128]{2,1,0:T(8,128)(2,1)S(1)} %get-tuple-element.78), channel_id=1, source_target_pairs={{0,64},{32,96},{64,0},{96,32},{128,192},{160,224},{192,128},{224,1... | collective-permute-start | bytes 1720328 | tf_op jit(solution)/shard_map/ppermute | solution.py:47
  102.4 42.7 %collective-permute-start.24 = (bf16[35,64,128]{2,1,0:T(8,128)(2,1)S(1)}, bf16[35,64,128]{2,1,0:T(8,128)(2,1)S(1)}, u32[]{:S(2)}, u32[]{:S(2)}) collective-permute-start(bf16[35,64,128]{2,1,0:T(8,128)(2,1)S(1)} %get-tuple-element.58.refs_2_), channel_id=1, source_target_pairs={{0,192},{32,224},{64,128},{96,160},{128,64},{160,96},{192,0},{224,... | collective-permute-start | bytes 1720328 | tf_op jit(solution)/shard_map/ppermute | solution.py:47
  103.3 24.2 %collective-permute-start.18 = (bf16[32,4096]{1,0:T(8,128)(2,1)S(1)}, bf16[32,4096]{1,0:T(8,128)(2,1)S(1)}, u32[]{:S(2)}, u32[]{:S(2)}) collective-permute-start(bf16[32,4096]{1,0:T(8,128)(2,1)S(1)} %get-tuple-element.69), channel_id=1, source_target_pairs={{0,20},{1,13},{2,22},{3,15},{4,24},{5,17},{6,26},{7,19},{8,28},{9,... | collective-permute-start | bytes 786440 | tf_op jit(solution)/shard_map/ppermute | solution.py:43
  119.4 17.0 %collective-permute-start.19 = (bf16[32,4096]{1,0:T(8,128)(2,1)S(1)}, bf16[32,4096]{1,0:T(8,128)(2,1)S(1)}, u32[]{:S(2)}, u32[]{:S(2)}) collective-permute-start(bf16[32,4096]{1,0:T(8,128)(2,1)S(1)} %get-tuple-element.70), channel_id=1, source_target_pairs={{0,24},{1,9},{2,26},{3,11},{4,28},{5,13},{6,30},{7,15},{8,0},{9,17... | collective-permute-start | bytes 786440 | tf_op jit(solution)/shard_map/ppermute | solution.py:43
  121.9 14.5 %collective-permute-start.20 = (bf16[32,4096]{1,0:T(8,128)(2,1)S(1)}, bf16[32,4096]{1,0:T(8,128)(2,1)S(1)}, u32[]{:S(2)}, u32[]{:S(2)}) collective-permute-start(bf16[32,4096]{1,0:T(8,128)(2,1)S(1)} %get-tuple-element.71.refs_9_), channel_id=1, source_target_pairs={{0,28},{1,5},{2,30},{3,7},{4,0},{5,9},{6,2},{7,11},{8,4},{9,13},{1... | collective-permute-start | bytes 786440 | tf_op jit(solution)/shard_map/ppermute | solution.py:43
  136.8 8.4 %collective-permute-start.22 = (bf16[32,4096]{1,0:T(8,128)(2,1)S(1)}, bf16[32,4096]{1,0:T(8,128)(2,1)S(1)}, u32[]{:S(2)}, u32[]{:S(2)}) collective-permute-start(bf16[32,4096]{1,0:T(8,128)(2,1)S(1)} %get-tuple-element.75), channel_id=1, source_target_pairs={{0,1},{1,0},{2,3},{3,2},{4,5},{5,4},{6,7},{7,6},{8,9},{9,8},{10,11... | collective-permute-start | bytes 786440 | tf_op jit(solution)/shard_map/ppermute | solution.py:43
  137.1 15.4 %collective-permute-start.27 = (bf16[35,64,128]{2,1,0:T(8,128)(2,1)S(1)}, bf16[35,64,128]{2,1,0:T(8,128)(2,1)S(1)}, u32[]{:S(2)}, u32[]{:S(2)}) collective-permute-start(bf16[35,64,128]{2,1,0:T(8,128)(2,1)S(1)} %get-tuple-element.79), channel_id=1, source_target_pairs={{0,96},{32,0},{64,32},{96,64},{128,224},{160,128},{192,160},{224,1... | collective-permute-start | bytes 1720328 | tf_op jit(solution)/shard_map/ppermute | solution.py:47
  137.6 18.6 %collective-permute-start.26 = (bf16[35,64,128]{2,1,0:T(8,128)(2,1)S(1)}, bf16[35,64,128]{2,1,0:T(8,128)(2,1)S(1)}, u32[]{:S(2)}, u32[]{:S(2)}) collective-permute-start(bf16[35,64,128]{2,1,0:T(8,128)(2,1)S(1)} %get-tuple-element.65.refs_2_), channel_id=1, source_target_pairs={{0,160},{32,192},{64,224},{96,128},{128,32},{160,64},{192,96},{224... | collective-permute-start | bytes 1720328 | tf_op jit(solution)/shard_map/ppermute | solution.py:47
  144.3 23.6 %collective-permute-start.28 = (bf16[35,64,128]{2,1,0:T(8,128)(2,1)S(1)}, bf16[35,64,128]{2,1,0:T(8,128)(2,1)S(1)}, u32[]{:S(2)}, u32[]{:S(2)}) collective-permute-start(bf16[35,64,128]{2,1,0:T(8,128)(2,1)S(1)} %get-tuple-element.68.refs_2_), channel_id=1, source_target_pairs={{0,224},{32,128},{64,160},{96,192},{128,96},{160,0},{192,32},{224,... | collective-permute-start | bytes 1720328 | tf_op jit(solution)/shard_map/ppermute | solution.py:47
  145.2 22.4 %collective-permute-start.29 = (bf16[35,64,128]{2,1,0:T(8,128)(2,1)S(1)}, bf16[35,64,128]{2,1,0:T(8,128)(2,1)S(1)}, u32[]{:S(2)}, u32[]{:S(2)}) collective-permute-start(bf16[35,64,128]{2,1,0:T(8,128)(2,1)S(1)} %get-tuple-element.80), channel_id=1, source_target_pairs={{0,32},{32,64},{64,96},{96,0},{128,160},{160,192},{192,224},{224,1... | collective-permute-start | bytes 1720328 | tf_op jit(solution)/shard_map/ppermute | solution.py:47
  145.2 34.3 %collective-permute-start.30 = (bf16[35,64,128]{2,1,0:T(8,128)(2,1)S(1)}, bf16[35,64,128]{2,1,0:T(8,128)(2,1)S(1)}, u32[]{:S(2)}, u32[]{:S(2)}) collective-permute-start(bf16[35,64,128]{2,1,0:T(8,128)(2,1)S(1)} %get-tuple-element.81), channel_id=1, source_target_pairs={{0,128},{32,160},{64,192},{96,224},{128,0},{160,32},{192,64},{224,... | collective-permute-start | bytes 1720328 | tf_op jit(solution)/shard_map/ppermute | solution.py:47
  152.5 33.0 %collective-permute-start.23 = (bf16[16,4096]{1,0:T(8,128)(2,1)S(1)}, bf16[16,4096]{1,0:T(8,128)(2,1)S(1)}, u32[]{:S(2)}, u32[]{:S(2)}) collective-permute-start(bf16[16,4096]{1,0:T(8,128)(2,1)S(1)} %get-tuple-element.77), channel_id=1, source_target_pairs={{0,2},{1,3},{2,0},{3,1},{4,6},{5,7},{6,4},{7,5},{8,10},{9,11},{10,... | collective-permute-start | bytes 393224 | tf_op jit(solution)/shard_map/ppermute | solution.py:43
where the time goes:
time: 188 us; the launch traced here: 186 us
  waiting for transfers between devices  71.7 us (38%)
  starting transfers between devices  66 us (35%)
  Pallas kernels  36 us (19%)
  local copies, waits for them, and re-layouts  5.25 us (3%)
  other arithmetic  5.14 us (3%)
    ppermute x24, starting transfers between devices, move(): return lax.ppermute(x, 'tensor', tensor_perm(dz, dx, dc, split=True))  54.7 us
    ppermute x24, waiting for transfers between devices, move(): return lax.ppermute(x, 'tensor', tensor_perm(dz, dx, dc, split=True))  42.8 us
    pallas_call x15, Pallas kernels, call(): pl.pallas_call(run, out_shape=out_shape, in_specs=[SMEM] * n_scalar + [VM...  36 us
    ppermute x7, waiting for transfers between devices, move_dp(): return lax.ppermute(x, 'dp', dp_perm(dx, dy))  29 us
    ppermute x7, starting transfers between devices, move_dp(): return lax.ppermute(x, 'dp', dp_perm(dx, dy))  11.3 us
    unnamed x14, local copies, waits for them, and re-layouts  5.04 us
  transfers between devices with their start and end apart: 31, of which 11 were waited for; matrix products, arithmetic and copies ran while one was open for 4% of the time, Pallas kernels for 16%

commit v1 on v0

--- a/solution.py
+++ b/solution.py
@@ -47,14 +47,14 @@
     return lax.ppermute(x, "dp", dp_perm(dx, dy))
 
 
-def call(kernel, n_scalar, out_shape, args, flops, scratch=(), after=(), limit=12):
+def call(kernel, n_scalar, out_shape, args, flops, scratch=(), after=(), limit=12, out_space=VMEM):
     n_args, n_after = len(args), len(after)
 
     def run(*refs):
         kernel(*refs[:n_args], *refs[n_args + n_after :])
 
     n_out = len(out_shape) if isinstance(out_shape, (tuple, list)) else 1
-    out_specs = [VMEM] * n_out if isinstance(out_shape, (tuple, list)) else VMEM
+    out_specs = [VMEM] * n_out if isinstance(out_shape, (tuple, list)) else out_space
     moved = sum(a.size * a.dtype.itemsize for a in args)
     return pl.pallas_call(
         run,
@@ -69,8 +69,13 @@
     )(*args, *after)
 
 
-def tick_kernel(x_ref, o_ref):
-    o_ref[...] = jnp.full(o_ref.shape, x_ref[0], F32)
+def tick_kernel(o_ref):
+    o_ref[...] = jnp.zeros_like(o_ref)
+
+
+def join_kernel(a_ref, b_ref, o_ref):
+    o_ref[0:16, :] = a_ref[...]
+    o_ref[16:32, :] = b_ref[...]
 
 
 def mask_kernel(t_ref, w_ref, m_ref, o_ref, e_ref):
@@ -285,15 +290,26 @@
     )
 
 
+def presum_kernel(*refs):
+    parts, out = refs[:-1], refs[-1]
+
+    @pl.loop(0, PAIRS)
+    def _(s):
+        total = parts[0][s].astype(F32)
+        for part in parts[1:]:
+            total = total + part[s].astype(F32)
+        out[s] = total
+
+
 def unpack_kernel(own_ref, code_ref, *refs):
-    parts, out, buf = refs[:8], refs[8], refs[9]
+    parts, (out, buf, turned, sems) = refs[:-4], refs[-4:]
     own = own_ref[0]
-    width = out.shape[1]
+    width = turned.shape[1]
     buf[...] = jnp.zeros_like(buf)
     half = lax.broadcasted_iota(jnp.int32, (BLOCK, 128), 1) // BLOCK
 
     def place(s, carry):
-        total = parts[0][s].astype(F32)
+        total = parts[0][s]
         for part in parts[1:]:
             total = total + part[s].astype(F32)
         row, lane, h = place_of(code_ref[own, s])
@@ -305,9 +321,14 @@
         return carry
 
     lax.fori_loop(0, PAIRS, place, 0)
+    copies = []
     for c in range(4):
         lanes = slice(c * 128, (c + 1) * 128)
-        out[lanes, :] = jnp.transpose(buf[0:width, lanes])
+        turned[lanes, :] = jnp.transpose(buf[0:width, lanes])
+        copies.append(pltpu.make_async_copy(turned.at[lanes], out.at[lanes], sems.at[c]))
+        copies[-1].start()
+    for copy in copies:
+        copy.wait()
 
 
 def kept_codes(block_mask, t, width):
@@ -333,25 +354,15 @@
     d, width = weight.shape
     t = lax.axis_index("tensor").astype(jnp.int32)
     g = lax.axis_index("dp").astype(jnp.int32)
+
+    partner = move(tokens, dc=1)
+    home = move(tokens, dx=1)
+    chip = call(join_kernel, 0, jax.ShapeDtypeStruct((32, d), BF16), (tokens, partner), 0)
+    t, g, chip = lax.optimization_barrier((t, g, chip))
     z, xh, core = t >> 2, (t >> 1) & 1, t & 1
     xl, y = g >> 2, g & 3
-
-    partner = move(tokens, dc=1)
-    home = move(tokens, dx=1)
-    chip = jnp.concatenate([tokens, partner], axis=0)
-    t, chip = lax.optimization_barrier((t, chip))
     near = [move(chip, dz=k) for k in (1, 2, 3)]
     far = move(chip[:16], dz=4)
-
-    masked = call(
-        mask_kernel,
-        1,
-        jax.ShapeDtypeStruct((d, width), BF16),
-        ((t * 14).reshape(1), weight, block_mask),
-        d * width,
-        scratch=(pltpu.VMEM((64, width), F32),),
-    )
-    code, odd = kept_codes(block_mask, t, width)
 
     n = jnp.arange(32, dtype=jnp.int32)
     slot = n & 7
@@ -365,12 +376,23 @@
     dy = jnp.array([o[1] for o in order], jnp.int32)
     dests = (xl ^ dx) * NY + ((y + dy) & (NY - 1))
 
-    near[0], masked, code, odd, idx, dests = lax.optimization_barrier(
-        (near[0], masked, code, odd, idx, dests)
+    ticks = [call(tick_kernel, 0, jax.ShapeDtypeStruct((8, 128), F32), (), 0) for _ in range(3)]
+    t_mask, ticks[2] = lax.optimization_barrier((t, ticks[2]))
+    t_list, ticks[1] = lax.optimization_barrier((t, ticks[1]))
+    masked = call(
+        mask_kernel,
+        1,
+        jax.ShapeDtypeStruct((d, width), BF16),
+        ((t_mask * 14).reshape(1), weight, block_mask),
+        d * width,
+        scratch=(pltpu.VMEM((64, width), F32),),
+    )
+    code, odd = kept_codes(block_mask, t_list, width)
+    near[2], masked, code, odd, idx, dests = lax.optimization_barrier(
+        (near[2], masked, code, odd, idx, dests)
     )
     scalars = (dests, code, odd)
 
-    tick = call(tick_kernel, 1, jax.ShapeDtypeStruct((8, 128), F32), (dests,), 0)
     near_x = [move(near[k], dx=1) for k in range(3)]
     far_x = move(far, dx=1)
     x0 = jnp.concatenate([tokens, far, *near], axis=0)
@@ -380,7 +402,7 @@
     xs = (x0, x1, x2, x3)
 
     grads = act_grad.reshape(32, 16, width)
-    act, p, pa = forward(0, idx, x0, x2, masked, grads, after=(tick,))
+    act, p, pa = forward(0, idx, x0, x2, masked, grads, after=ticks)
     own_a, other_a = xgrad(p, masked)
     act, p, pb = forward(16, idx, x1, x3, masked, grads, (act,), (other_a,))
 
@@ -400,12 +422,20 @@
     done, back_b = send_back(own_b, other_b, done)
     pack_two(6, (done,))
 
+    early = call(
+        presum_kernel,
+        0,
+        jax.ShapeDtypeStruct((PAIRS, BLOCK, 128), F32),
+        (parts[7], *parts[:4]),
+        5 * CAP * 4096,
+    )
     to_core, kept = call(
         sum_kernel,
         0,
         (jax.ShapeDtypeStruct((32, d), BF16), jax.ShapeDtypeStruct((32, d), F32)),
         (*back_a, *back_b),
         10 * 32 * d,
+        after=(early,),
     )
     to_x, kept = call(
         sum_core_kernel,
@@ -420,9 +450,14 @@
         unpack_kernel,
         2,
         jax.ShapeDtypeStruct((512, width), F32),
-        (g.reshape(1), code, *parts),
+        (g.reshape(1), code, early, *parts[4:7]),
         8 * CAP * 4096,
-        scratch=(pltpu.VMEM((width + BLOCK, 512), F32),),
+        scratch=(
+            pltpu.VMEM((width + BLOCK, 512), F32),
+            pltpu.VMEM((512, width), F32),
+            pltpu.SemaphoreType.DMA((4,)),
+        ),
+        out_space=pl.BlockSpec(memory_space=pl.ANY),
     )
     return (act.reshape(512, width), x_grad, weight_grad)
 

time: 188 us -> 193 us (1.027)
  the two profiles are of different devices: /device:TPU:8 before, /device:TPU:31 now
where the time goes in v1:
time: 193 us; the launch traced here: 192 us
  starting transfers between devices  82.4 us (43%)
  waiting for transfers between devices  60.6 us (31%)
  Pallas kernels  35.9 us (19%)
  local copies, waits for them, and re-layouts  7.09 us (4%)
  other arithmetic  4.22 us (2%)
    ppermute x24, starting transfers between devices, move(): return lax.ppermute(x, 'tensor', tensor_perm(dz, dx, dc, split=True))  53.3 us
    pallas_call x19, Pallas kernels, call(): pl.pallas_call(run, out_shape=out_shape, in_specs=[SMEM] * n_scalar + [VM...  35.9 us
    ppermute x7, waiting for transfers between devices, move_dp(): return lax.ppermute(x, 'dp', dp_perm(dx, dy))  33.4 us
    ppermute x7, starting transfers between devices, move_dp(): return lax.ppermute(x, 'dp', dp_perm(dx, dy))  29.1 us
    ppermute x24, waiting for transfers between devices, move(): return lax.ppermute(x, 'tensor', tensor_perm(dz, dx, dc, split=True))  27.2 us
    unnamed x16, local copies, waits for them, and re-layouts  6.88 us
  transfers between devices with their start and end apart: 31, of which 9 were waited for; matrix products, arithmetic and copies ran while one was open for 4% of the time, Pallas kernels for 15%

profile of v1, /device:TPU:31, one launch (start us, length us, event | category | flops | bytes accessed | tf_op | source)
XLA Modules:
  0.0 192.2 jit_solution(6439373643514516441)
XLA Ops:
  0.6 0.8 collective-permute-start
  1.4 1.1 collective-permute-start.2
  2.5 0.9 constant_dynamic-update-slice_fusion.9
  3.5 0.9 copy-done.2
  4.5 6.1 %collective-permute-start.7 = (bf16[32,4096]{1,0:T(8,128)(2,1)S(1)}, bf16[32,4096]{1,0:T(8,128)(2,1)S(1)}, u32[]{:S(2)}, u32[]{:S(2)}) collective-permute-start(bf16[32,4096]{1,0:T(8,128)(2,1)S(1)} %shard_map.94), channel_id=1, source_target_pairs={{0,8},{1,25},{2,10},{3,27},{4,12},{5,29},{6,14},{7,31},{8,16},{9,1... | collective-permute-start | bytes 786440 | tf_op jit(solution)/shard_map/ppermute | solution.py:43
  10.6 0.7 collective-permute-start.5
  11.8 0.9 dynamic-slice_compare_fusion
  12.8 1.0 convert_reduce_fusion
  13.9 1.9 select_reduce_fusion
  15.9 4.4 %collective-permute-start.3 = (bf16[16,4096]{1,0:T(8,128)(2,1)S(1)}, bf16[16,4096]{1,0:T(8,128)(2,1)}, u32[]{:S(2)}, u32[]{:S(2)}) collective-permute-start(bf16[16,4096]{1,0:T(8,128)(2,1)S(1)} %slice.3), channel_id=1, source_target_pairs={{0,16},{1,17},{2,18},{3,19},{4,20},{5,21},{6,22},{7,23},{8,24},{9,... | collective-permute-start | bytes 393224 | tf_op jit(solution)/shard_map/ppermute | solution.py:43
  21.0 3.1 %copy-done = bf16[4096,896]{1,0:T(8,128)(2,1)S(1)} copy-done((bf16[4096,896]{1,0:T(8,128)(2,1)S(1)}, bf16[4096,896]{1,0:T(8,128)(2,1)}, u32[]{:S(2)}) %copy-start) | copy-done | bytes 7340056
  24.1 0.9 copy-done.3
  25.0 1.4 shard_map.96.refs_3_.refs_1_
  26.4 2.5 %collective-permute-done.3 = bf16[16,4096]{1,0:T(8,128)(2,1)} collective-permute-done((bf16[16,4096]{1,0:T(8,128)(2,1)S(1)}, bf16[16,4096]{1,0:T(8,128)(2,1)}, u32[]{:S(2)}, u32[]{:S(2)}) %collective-permute-start.3) | collective-permute-done | bytes 131104 | tf_op jit(solution)/shard_map/ppermute | solution.py:43
  29.0 1.8 collective-permute-start.4
  30.8 0.9 constant_dynamic-update-slice_fusion.8
  31.8 1.8 collective-permute-done.1
  33.5 1.8 collective-permute-start.9
  35.5 3.1 %collective-permute-start.11 = (bf16[128,4096]{1,0:T(8,128)(2,1)S(1)}, bf16[128,4096]{1,0:T(8,128)(2,1)S(1)}, u32[]{:S(2)}, u32[]{:S(2)}) collective-permute-start(bf16[128,4096]{1,0:T(8,128)(2,1)S(1)} %constant_dynamic-update-slice_fusion.5.refs_1_.refs_5_), channel_id=1, source_target_pairs={{0,1},{1,0},{2,3},{3,2},{4,5},{5,4},{6,7},{7,6},{8,9},{9,8},{10,11... | collective-permute-start | bytes 3145736 | tf_op jit(solution)/shard_map/ppermute | solution.py:43
  38.6 1.8 collective-permute-start.8
  40.5 1.1 collective-permute-start.6
  41.6 12.5 %collective-permute-done.6 = bf16[32,4096]{1,0:T(8,128)(2,1)S(1)} collective-permute-done((bf16[32,4096]{1,0:T(8,128)(2,1)S(1)}, bf16[32,4096]{1,0:T(8,128)(2,1)S(1)}, u32[]{:S(2)}, u32[]{:S(2)}) %collective-permute-start.6) | collective-permute-done | bytes 262176 | tf_op jit(solution)/shard_map/ppermute | solution.py:43
  54.2 2.4 %collective-permute-start.10 = (bf16[128,4096]{1,0:T(8,128)(2,1)S(1)}, bf16[128,4096]{1,0:T(8,128)(2,1)S(1)}, u32[]{:S(2)}, u32[]{:S(2)}) collective-permute-start(bf16[128,4096]{1,0:T(8,128)(2,1)S(1)} %constant_dynamic-update-slice_fusion.refs_1_.refs_6_), channel_id=1, source_target_pairs={{0,1},{1,0},{2,3},{3,2},{4,5},{5,4},{6,7},{7,6},{8,9},{9,8},{10,11... | collective-permute-start | bytes 3145736 | tf_op jit(solution)/shard_map/ppermute | solution.py:43
  56.6 4.1 %shard_map.99 = (bf16[16,16,896]{2,1,0:T(8,128)(2,1)S(1)}, bf16[256,896]{1,0:T(8,128)(2,1)S(1)}, bf16[896,256]{1,0:T(8,128)(2,1)S(1)}) custom-call(s32[32]{0:T(128)S(1)} %fusion.9.refs_0_, bf16[128,4096]{1,0:T(8,128)(2,1)S(1)} %constant_dynamic-update-slice_fusion.5.refs_1_.refs_5_, bf16[128,4096]{1,0:T(8,128)(2,1)S(1)} %collective-permute-done.11.refs_2_.refs_7_, ...), custom_call_target="tpu_custom_call" | custom-call | flops 1879048192 | bytes 10354816 | tf_op jit(solution)/shard_map/pallas_call | solution.py:59
  60.7 3.8 %shard_map.100 = (f32[128,4096]{1,0:T(8,128)S(1)}, bf16[128,4096]{1,0:T(8,128)(2,1)S(1)}) custom-call(bf16[256,896]{1,0:T(8,128)(2,1)S(1)} %get-tuple-element.59.refs_0_, bf16[4096,896]{1,0:T(8,128)(2,1)S(1)} %shard_map.96.refs_3_.refs_1_), custom_call_target="tpu_custom_call" | custom-call | flops 1879048192 | bytes 7798784 | tf_op jit(solution)/shard_map/pallas_call | solution.py:59
  64.8 4.8 %shard_map.101 = (bf16[32,16,896]{2,1,0:T(8,128)(2,1)}, bf16[256,896]{1,0:T(8,128)(2,1)S(1)}, bf16[896,256]{1,0:T(8,128)(2,1)S(1)}) custom-call(s32[32]{0:T(128)S(1)} %fusion.9.refs_0_, bf16[128,4096]{1,0:T(8,128)(2,1)S(1)} %constant_dynamic-update-slice_fusion.refs_1_.refs_6_, bf16[128,4096]{1,0:T(8,128)(2,1)S(1)} %collective-permute-done.10.refs_2_.refs_8_, ...), custom_call_target="tpu_custom_call" | custom-call | flops 1879048192 | bytes 10813568 | tf_op jit(solution)/shard_map/pallas_call | solution.py:59
  69.6 2.7 %shard_map.102 = (bf16[35,64,128]{2,1,0:T(8,128)(2,1)S(1)}, bf16[35,64,128]{2,1,0:T(8,128)(2,1)S(1)}) custom-call(s32[8]{0:T(128)S(1)} %and_add_fusion.refs_0_, s32[8,70]{1,0:T(8,128)S(1)} %broadcast_add_fusion.refs_1_, s32[8]{0:T(128)S(1)} %get-tuple-element.65.refs_2_, bf16[896,256]{1,0:T(8,128)(2,1)S(1)} %get-tuple-element.66.refs_3_, ...), custom_call_target="tpu_custom_call" | custom-call | flops 939524096 | bytes 5114112 | tf_op jit(solution)/shard_map/pallas_call | solution.py:59
  72.6 2.7 %shard_map.104 = (bf16[35,64,128]{2,1,0:T(8,128)(2,1)S(1)}, bf16[35,64,128]{2,1,0:T(8,128)(2,1)S(1)}) custom-call(s32[8]{0:T(128)S(1)} %and_add_fusion.refs_0_, s32[8,70]{1,0:T(8,128)S(1)} %broadcast_add_fusion.refs_1_, s32[8]{0:T(128)S(1)} %get-tuple-element.65.refs_2_, bf16[896,256]{1,0:T(8,128)(2,1)S(1)} %get-tuple-element.66.refs_3_, ...), custom_call_target="tpu_custom_call" | custom-call | flops 939524096 | bytes 5114112 | tf_op jit(solution)/shard_map/pallas_call | solution.py:59
  75.3 3.8 %shard_map.105 = (f32[128,4096]{1,0:T(8,128)S(1)}, bf16[128,4096]{1,0:T(8,128)(2,1)S(1)}) custom-call(bf16[256,896]{1,0:T(8,128)(2,1)S(1)} %get-tuple-element.74.refs_0_, bf16[4096,896]{1,0:T(8,128)(2,1)S(1)} %shard_map.96.refs_3_.refs_1_, bf16[35,64,128]{2,1,0:T(8,128)(2,1)S(1)} %get-tuple-element.75.refs_2_), custom_call_target="tpu_custom_call" | custom-call | flops 1879048192 | bytes 7798784 | tf_op jit(solution)/shard_map/pallas_call | solution.py:59
  79.1 1.0 collective-permute-start.17
  80.7 2.4 %collective-permute-start.22 = (bf16[35,64,128]{2,1,0:T(8,128)(2,1)S(1)}, bf16[35,64,128]{2,1,0:T(8,128)(2,1)S(1)}, u32[]{:S(2)}, u32[]{:S(2)}) collective-permute-start(bf16[35,64,128]{2,1,0:T(8,128)(2,1)S(1)} %get-tuple-element.68.refs_2_), channel_id=1, source_target_pairs={{0,192},{32,224},{64,128},{96,160},{128,64},{160,96},{192,0},{224,... | collective-permute-start | bytes 1720328 | tf_op jit(solution)/shard_map/ppermute | solution.py:47
  83.4 3.2 %collective-permute-start.24 = (bf16[35,64,128]{2,1,0:T(8,128)(2,1)S(1)}, bf16[35,64,128]{2,1,0:T(8,128)(2,1)S(1)}, u32[]{:S(2)}, u32[]{:S(2)}) collective-permute-start(bf16[35,64,128]{2,1,0:T(8,128)(2,1)S(1)} %get-tuple-element.75.refs_2_), channel_id=1, source_target_pairs={{0,160},{32,192},{64,224},{96,128},{128,32},{160,64},{192,96},{224... | collective-permute-start | bytes 1720328 | tf_op jit(solution)/shard_map/ppermute | solution.py:47
  86.6 21.7 %collective-permute-done.23.refs_2_ = bf16[35,64,128]{2,1,0:T(8,128)(2,1)S(1)} collective-permute-done((bf16[35,64,128]{2,1,0:T(8,128)(2,1)S(1)}, bf16[35,64,128]{2,1,0:T(8,128)(2,1)S(1)}, u32[]{:S(2)}, u32[]{:S(2)}) %collective-permute-start.23) | collective-permute-done | bytes 573472 | tf_op jit(solution)/shard_map/ppermute | solution.py:47
  108.3 4.8 %collective-permute-start.16 = (bf16[16,4096]{1,0:T(8,128)(2,1)S(1)}, bf16[16,4096]{1,0:T(8,128)(2,1)S(1)}, u32[]{:S(2)}, u32[]{:S(2)}) collective-permute-start(bf16[16,4096]{1,0:T(8,128)(2,1)S(1)} %get-tuple-element.72), channel_id=1, source_target_pairs={{0,16},{1,17},{2,18},{3,19},{4,20},{5,21},{6,22},{7,23},{8,24},{9,... | collective-permute-start | bytes 393224 | tf_op jit(solution)/shard_map/ppermute | solution.py:43
  113.1 3.0 %collective-permute-done.16.refs_3_ = bf16[16,4096]{1,0:T(8,128)(2,1)S(1)} collective-permute-done((bf16[16,4096]{1,0:T(8,128)(2,1)S(1)}, bf16[16,4096]{1,0:T(8,128)(2,1)S(1)}, u32[]{:S(2)}, u32[]{:S(2)}) %collective-permute-start.16) | collective-permute-done | bytes 131104 | tf_op jit(solution)/shard_map/ppermute | solution.py:43
  116.2 11.0 %collective-permute-start.14 = (bf16[32,4096]{1,0:T(8,128)(2,1)S(1)}, bf16[32,4096]{1,0:T(8,128)(2,1)S(1)}, u32[]{:S(2)}, u32[]{:S(2)}) collective-permute-start(bf16[32,4096]{1,0:T(8,128)(2,1)S(1)} %get-tuple-element.70), channel_id=1, source_target_pairs={{0,24},{1,9},{2,26},{3,11},{4,28},{5,13},{6,30},{7,15},{8,0},{9,17... | collective-permute-start | bytes 786440 | tf_op jit(solution)/shard_map/ppermute | solution.py:43
  127.1 2.8 %shard_map.106 = (bf16[35,64,128]{2,1,0:T(8,128)(2,1)S(1)}, bf16[35,64,128]{2,1,0:T(8,128)(2,1)S(1)}) custom-call(s32[8]{0:T(128)S(1)} %and_add_fusion.refs_0_, s32[8,70]{1,0:T(8,128)S(1)} %broadcast_add_fusion.refs_1_, s32[8]{0:T(128)S(1)} %get-tuple-element.65.refs_2_, bf16[896,256]{1,0:T(8,128)(2,1)S(1)} %get-tuple-element.66.refs_3_, ...), custom_call_target="tpu_custom_call" | custom-call | flops 939524096 | bytes 5114112 | tf_op jit(solution)/shard_map/pallas_call | solution.py:59
  130.2 4.2 %collective-permute-start.18 = (bf16[32,4096]{1,0:T(8,128)(2,1)S(1)}, bf16[32,4096]{1,0:T(8,128)(2,1)S(1)}, u32[]{:S(2)}, u32[]{:S(2)}) collective-permute-start(bf16[32,4096]{1,0:T(8,128)(2,1)S(1)} %get-tuple-element.79), channel_id=1, source_target_pairs={{0,20},{1,13},{2,22},{3,15},{4,24},{5,17},{6,26},{7,19},{8,28},{9,... | collective-permute-start | bytes 786440 | tf_op jit(solution)/shard_map/ppermute | solution.py:43
  134.5 4.4 %collective-permute-start.21 = (bf16[16,4096]{1,0:T(8,128)(2,1)S(1)}, bf16[16,4096]{1,0:T(8,128)(2,1)S(1)}, u32[]{:S(2)}, u32[]{:S(2)}) collective-permute-start(bf16[16,4096]{1,0:T(8,128)(2,1)S(1)} %get-tuple-element.82), channel_id=1, source_target_pairs={{0,16},{1,17},{2,18},{3,19},{4,20},{5,21},{6,22},{7,23},{8,24},{9,... | collective-permute-start | bytes 393224 | tf_op jit(solution)/shard_map/ppermute | solution.py:43
  138.9 5.8 %collective-permute-done.15.refs_2_ = bf16[32,4096]{1,0:T(8,128)(2,1)S(1)} collective-permute-done((bf16[32,4096]{1,0:T(8,128)(2,1)S(1)}, bf16[32,4096]{1,0:T(8,128)(2,1)S(1)}, u32[]{:S(2)}, u32[]{:S(2)}) %collective-permute-start.15) | collective-permute-done | bytes 262176 | tf_op jit(solution)/shard_map/ppermute | solution.py:43
  144.7 3.1 %shard_map.108 = (bf16[35,64,128]{2,1,0:T(8,128)(2,1)S(1)}, bf16[35,64,128]{2,1,0:T(8,128)(2,1)S(1)}) custom-call(s32[8]{0:T(128)S(1)} %and_add_fusion.refs_0_, s32[8,70]{1,0:T(8,128)S(1)} %broadcast_add_fusion.refs_1_, s32[8]{0:T(128)S(1)} %get-tuple-element.65.refs_2_, bf16[896,256]{1,0:T(8,128)(2,1)S(1)} %get-tuple-element.66.refs_3_, ...), custom_call_target="tpu_custom_call" | custom-call | flops 939524096 | bytes 5114112 | tf_op jit(solution)/shard_map/pallas_call | solution.py:59
  147.8 15.1 %collective-permute-start.28 = (bf16[35,64,128]{2,1,0:T(8,128)(2,1)S(1)}, bf16[35,64,128]{2,1,0:T(8,128)(2,1)S(1)}, u32[]{:S(2)}, u32[]{:S(2)}) collective-permute-start(bf16[35,64,128]{2,1,0:T(8,128)(2,1)S(1)} %get-tuple-element.78.refs_2_), channel_id=1, source_target_pairs={{0,224},{32,128},{64,160},{96,192},{128,96},{160,0},{192,32},{224,... | collective-permute-start | bytes 1720328 | tf_op jit(solution)/shard_map/ppermute | solution.py:47
  162.9 7.4 %collective-permute-start.29 = (bf16[35,64,128]{2,1,0:T(8,128)(2,1)S(1)}, bf16[35,64,128]{2,1,0:T(8,128)(2,1)S(1)}, u32[]{:S(2)}, u32[]{:S(2)}) collective-permute-start(bf16[35,64,128]{2,1,0:T(8,128)(2,1)S(1)} %get-tuple-element.91), channel_id=1, source_target_pairs={{0,32},{32,64},{64,96},{96,0},{128,160},{160,192},{192,224},{224,1... | collective-permute-start | bytes 1720328 | tf_op jit(solution)/shard_map/ppermute | solution.py:47
  171.3 1.5 collective-permute-done.26.refs_1_
  172.9 1.6 collective-permute-start.27
  174.5 2.5 %collective-permute-done.29.refs_4_ = bf16[35,64,128]{2,1,0:T(8,128)(2,1)S(1)} collective-permute-done((bf16[35,64,128]{2,1,0:T(8,128)(2,1)S(1)}, bf16[35,64,128]{2,1,0:T(8,128)(2,1)S(1)}, u32[]{:S(2)}, u32[]{:S(2)}) %collective-permute-start.29) | collective-permute-done | bytes 573472 | tf_op jit(solution)/shard_map/ppermute | solution.py:47
  177.0 9.2 %collective-permute-done.30.refs_5_ = bf16[35,64,128]{2,1,0:T(8,128)(2,1)S(1)} collective-permute-done((bf16[35,64,128]{2,1,0:T(8,128)(2,1)S(1)}, bf16[35,64,128]{2,1,0:T(8,128)(2,1)S(1)}, u32[]{:S(2)}, u32[]{:S(2)}) %collective-permute-start.30) | collective-permute-done | bytes 573472 | tf_op jit(solution)/shard_map/ppermute | solution.py:47
  186.2 5.4 %shard_map.112 = f32[512,896]{1,0:T(8,128)} custom-call(s32[1]{0:T(128)} %bitcast.3.refs_0_, s32[8,70]{1,0:T(8,128)S(1)} %broadcast_add_fusion.refs_1_, f32[35,64,128]{2,1,0:T(8,128)S(1)} %shard_map.109.refs_10_.refs_2_, bf16[35,64,128]{2,1,0:T(8,128)(2,1)S(1)} %collective-permute-done.28.refs_3_, bf16[35,64,128]{2,1,0:T(8,128)(2,1)S(1)} %collective-permute-done.29.refs_4_, ...), custom_call_target="tpu_custom_call" | custom-call | flops 2293760 | bytes 2869444 | tf_op jit(solution)/shard_map/pallas_call | solution.py:59
  (61 shorter events, 5.1 us)
Async XLA Ops:
  0.6 2.9 %collective-permute-start = (bf16[16,4096]{1,0:T(8,128)(2,1)}, bf16[16,4096]{1,0:T(8,128)(2,1)S(1)}, u32[]{:S(2)}, u32[]{:S(2)}) collective-permute-start(bf16[16,4096]{1,0:T(8,128)(2,1)} %refs_0_.1), channel_id=1, source_target_pairs={{0,1},{1,0},{2,3},{3,2},{4,5},{5,4},{6,7},{7,6},{8,9},{9,8},{10,11... | collective-permute-start | bytes 393224 | tf_op jit(solution)/shard_map/ppermute | solution.py:43
  1.4 18.9 %collective-permute-start.2 = (bf16[16,4096]{1,0:T(8,128)(2,1)}, bf16[16,4096]{1,0:T(8,128)(2,1)S(1)}, u32[]{:S(2)}, u32[]{:S(2)}) collective-permute-start(bf16[16,4096]{1,0:T(8,128)(2,1)} %refs_0_.1), channel_id=1, source_target_pairs={{0,2},{1,3},{2,0},{3,1},{4,6},{5,7},{6,4},{7,5},{8,10},{9,11},{10,... | collective-permute-start | bytes 393224 | tf_op jit(solution)/shard_map/ppermute | solution.py:43
  3.5 0.9 copy-start.2
  4.5 31.0 %collective-permute-start.7 = (bf16[32,4096]{1,0:T(8,128)(2,1)S(1)}, bf16[32,4096]{1,0:T(8,128)(2,1)S(1)}, u32[]{:S(2)}, u32[]{:S(2)}) collective-permute-start(bf16[32,4096]{1,0:T(8,128)(2,1)S(1)} %shard_map.94), channel_id=1, source_target_pairs={{0,8},{1,25},{2,10},{3,27},{4,12},{5,29},{6,14},{7,31},{8,16},{9,1... | collective-permute-start | bytes 786440 | tf_op jit(solution)/shard_map/ppermute | solution.py:43
  10.6 24.8 %collective-permute-start.5 = (bf16[32,4096]{1,0:T(8,128)(2,1)S(1)}, bf16[32,4096]{1,0:T(8,128)(2,1)S(1)}, u32[]{:S(2)}, u32[]{:S(2)}) collective-permute-start(bf16[32,4096]{1,0:T(8,128)(2,1)S(1)} %shard_map.94), channel_id=1, source_target_pairs={{0,4},{1,29},{2,6},{3,31},{4,8},{5,1},{6,10},{7,3},{8,12},{9,5},{1... | collective-permute-start | bytes 786440 | tf_op jit(solution)/shard_map/ppermute | solution.py:43
  11.3 22.3 %collective-permute-start.1 = (bf16[32,4096]{1,0:T(8,128)(2,1)S(1)}, bf16[32,4096]{1,0:T(8,128)(2,1)S(1)}, u32[]{:S(2)}, u32[]{:S(2)}) collective-permute-start(bf16[32,4096]{1,0:T(8,128)(2,1)S(1)} %shard_map.94), channel_id=1, source_target_pairs={{0,12},{1,21},{2,14},{3,23},{4,16},{5,25},{6,18},{7,27},{8,20},{9,... | collective-permute-start | bytes 786440 | tf_op jit(solution)/shard_map/ppermute | solution.py:43
  15.9 13.1 %collective-permute-start.3 = (bf16[16,4096]{1,0:T(8,128)(2,1)S(1)}, bf16[16,4096]{1,0:T(8,128)(2,1)}, u32[]{:S(2)}, u32[]{:S(2)}) collective-permute-start(bf16[16,4096]{1,0:T(8,128)(2,1)S(1)} %slice.3), channel_id=1, source_target_pairs={{0,16},{1,17},{2,18},{3,19},{4,20},{5,21},{6,22},{7,23},{8,24},{9,... | collective-permute-start | bytes 393224 | tf_op jit(solution)/shard_map/ppermute | solution.py:43
  21.0 3.1 %copy-start = (bf16[4096,896]{1,0:T(8,128)(2,1)S(1)}, bf16[4096,896]{1,0:T(8,128)(2,1)}, u32[]{:S(2)}) copy-start(bf16[4096,896]{1,0:T(8,128)(2,1)} %refs_1_.1) | copy-start | bytes 22020100
  24.1 0.9 copy-start.3
  26.4 30.2 %copy-start.1 = (bf16[512,896]{1,0:T(8,128)(2,1)S(1)}, bf16[512,896]{1,0:T(8,128)(2,1)}, u32[]{:S(2)}) copy-start(bf16[512,896]{1,0:T(8,128)(2,1)} %param.10) | copy-start | bytes 2752516
  29.0 12.6 %collective-permute-start.4 = (bf16[16,4096]{1,0:T(8,128)(2,1)}, bf16[16,4096]{1,0:T(8,128)(2,1)S(1)}, u32[]{:S(2)}, u32[]{:S(2)}) collective-permute-start(bf16[16,4096]{1,0:T(8,128)(2,1)} %collective-permute-done.3), channel_id=1, source_target_pairs={{0,2},{1,3},{2,0},{3,1},{4,6},{5,7},{6,4},{7,5},{8,10},{9,11},{10,... | collective-permute-start | bytes 393224 | tf_op jit(solution)/shard_map/ppermute | solution.py:43
  33.5 20.6 %collective-permute-start.9 = (bf16[32,4096]{1,0:T(8,128)(2,1)S(1)}, bf16[32,4096]{1,0:T(8,128)(2,1)S(1)}, u32[]{:S(2)}, u32[]{:S(2)}) collective-permute-start(bf16[32,4096]{1,0:T(8,128)(2,1)S(1)} %collective-permute-done.1), channel_id=1, source_target_pairs={{0,2},{1,3},{2,0},{3,1},{4,6},{5,7},{6,4},{7,5},{8,10},{9,11},{10,... | collective-permute-start | bytes 786440 | tf_op jit(solution)/shard_map/ppermute | solution.py:43
  35.5 21.1 %collective-permute-start.11 = (bf16[128,4096]{1,0:T(8,128)(2,1)S(1)}, bf16[128,4096]{1,0:T(8,128)(2,1)S(1)}, u32[]{:S(2)}, u32[]{:S(2)}) collective-permute-start(bf16[128,4096]{1,0:T(8,128)(2,1)S(1)} %constant_dynamic-update-slice_fusion.5.refs_1_.refs_5_), channel_id=1, source_target_pairs={{0,1},{1,0},{2,3},{3,2},{4,5},{5,4},{6,7},{7,6},{8,9},{9,8},{10,11... | collective-permute-start | bytes 3145736 | tf_op jit(solution)/shard_map/ppermute | solution.py:43
  38.6 15.5 %collective-permute-start.8 = (bf16[32,4096]{1,0:T(8,128)(2,1)S(1)}, bf16[32,4096]{1,0:T(8,128)(2,1)S(1)}, u32[]{:S(2)}, u32[]{:S(2)}) collective-permute-start(bf16[32,4096]{1,0:T(8,128)(2,1)S(1)} %collective-permute-done.7), channel_id=1, source_target_pairs={{0,2},{1,3},{2,0},{3,1},{4,6},{5,7},{6,4},{7,5},{8,10},{9,11},{10,... | collective-permute-start | bytes 786440 | tf_op jit(solution)/shard_map/ppermute | solution.py:43
  40.5 13.6 %collective-permute-start.6 = (bf16[32,4096]{1,0:T(8,128)(2,1)S(1)}, bf16[32,4096]{1,0:T(8,128)(2,1)S(1)}, u32[]{:S(2)}, u32[]{:S(2)}) collective-permute-start(bf16[32,4096]{1,0:T(8,128)(2,1)S(1)} %collective-permute-done.5), channel_id=1, source_target_pairs={{0,2},{1,3},{2,0},{3,1},{4,6},{5,7},{6,4},{7,5},{8,10},{9,11},{10,... | collective-permute-start | bytes 786440 | tf_op jit(solution)/shard_map/ppermute | solution.py:43
  54.2 10.6 %collective-permute-start.10 = (bf16[128,4096]{1,0:T(8,128)(2,1)S(1)}, bf16[128,4096]{1,0:T(8,128)(2,1)S(1)}, u32[]{:S(2)}, u32[]{:S(2)}) collective-permute-start(bf16[128,4096]{1,0:T(8,128)(2,1)S(1)} %constant_dynamic-update-slice_fusion.refs_1_.refs_6_), channel_id=1, source_target_pairs={{0,1},{1,0},{2,3},{3,2},{4,5},{5,4},{6,7},{7,6},{8,9},{9,8},{10,11... | collective-permute-start | bytes 3145736 | tf_op jit(solution)/shard_map/ppermute | solution.py:43
  64.5 7.9 %collective-permute-start.12 = (bf16[128,4096]{1,0:T(8,128)(2,1)S(1)}, bf16[128,4096]{1,0:T(8,128)(2,1)S(1)}, u32[]{:S(2)}, u32[]{:S(2)}) collective-permute-start(bf16[128,4096]{1,0:T(8,128)(2,1)S(1)} %get-tuple-element.60.refs_6_), channel_id=1, source_target_pairs={{0,1},{1,0},{2,3},{3,2},{4,5},{5,4},{6,7},{7,6},{8,9},{9,8},{10,11... | collective-permute-start | bytes 3145736 | tf_op jit(solution)/shard_map/ppermute | solution.py:43
  79.1 48.0 %collective-permute-start.17 = (bf16[128,4096]{1,0:T(8,128)(2,1)S(1)}, bf16[128,4096]{1,0:T(8,128)(2,1)S(1)}, u32[]{:S(2)}, u32[]{:S(2)}) collective-permute-start(bf16[128,4096]{1,0:T(8,128)(2,1)S(1)} %get-tuple-element.77.refs_9_), channel_id=1, source_target_pairs={{0,1},{1,0},{2,3},{3,2},{4,5},{5,4},{6,7},{7,6},{8,9},{9,8},{10,11... | collective-permute-start | bytes 3145736 | tf_op jit(solution)/shard_map/ppermute | solution.py:43
  80.1 28.3 %collective-permute-start.23 = (bf16[35,64,128]{2,1,0:T(8,128)(2,1)S(1)}, bf16[35,64,128]{2,1,0:T(8,128)(2,1)S(1)}, u32[]{:S(2)}, u32[]{:S(2)}) collective-permute-start(bf16[35,64,128]{2,1,0:T(8,128)(2,1)S(1)} %get-tuple-element.85), channel_id=1, source_target_pairs={{0,64},{32,96},{64,0},{96,32},{128,192},{160,224},{192,128},{224,1... | collective-permute-start | bytes 1720328 | tf_op jit(solution)/shard_map/ppermute | solution.py:47
  80.7 32.5 %collective-permute-start.22 = (bf16[35,64,128]{2,1,0:T(8,128)(2,1)S(1)}, bf16[35,64,128]{2,1,0:T(8,128)(2,1)S(1)}, u32[]{:S(2)}, u32[]{:S(2)}) collective-permute-start(bf16[35,64,128]{2,1,0:T(8,128)(2,1)S(1)} %get-tuple-element.68.refs_2_), channel_id=1, source_target_pairs={{0,192},{32,224},{64,128},{96,160},{128,64},{160,96},{192,0},{224,... | collective-permute-start | bytes 1720328 | tf_op jit(solution)/shard_map/ppermute | solution.py:47
  83.0 61.7 %collective-permute-start.25 = (bf16[35,64,128]{2,1,0:T(8,128)(2,1)S(1)}, bf16[35,64,128]{2,1,0:T(8,128)(2,1)S(1)}, u32[]{:S(2)}, u32[]{:S(2)}) collective-permute-start(bf16[35,64,128]{2,1,0:T(8,128)(2,1)S(1)} %get-tuple-element.86), channel_id=1, source_target_pairs={{0,96},{32,0},{64,32},{96,64},{128,224},{160,128},{192,160},{224,1... | collective-permute-start | bytes 1720328 | tf_op jit(solution)/shard_map/ppermute | solution.py:47
  83.4 64.4 %collective-permute-start.24 = (bf16[35,64,128]{2,1,0:T(8,128)(2,1)S(1)}, bf16[35,64,128]{2,1,0:T(8,128)(2,1)S(1)}, u32[]{:S(2)}, u32[]{:S(2)}) collective-permute-start(bf16[35,64,128]{2,1,0:T(8,128)(2,1)S(1)} %get-tuple-element.75.refs_2_), channel_id=1, source_target_pairs={{0,160},{32,192},{64,224},{96,128},{128,32},{160,64},{192,96},{224... | collective-permute-start | bytes 1720328 | tf_op jit(solution)/shard_map/ppermute | solution.py:47
  108.3 7.8 %collective-permute-start.16 = (bf16[16,4096]{1,0:T(8,128)(2,1)S(1)}, bf16[16,4096]{1,0:T(8,128)(2,1)S(1)}, u32[]{:S(2)}, u32[]{:S(2)}) collective-permute-start(bf16[16,4096]{1,0:T(8,128)(2,1)S(1)} %get-tuple-element.72), channel_id=1, source_target_pairs={{0,16},{1,17},{2,18},{3,19},{4,20},{5,21},{6,22},{7,23},{8,24},{9,... | collective-permute-start | bytes 393224 | tf_op jit(solution)/shard_map/ppermute | solution.py:43
  113.1 17.1 %collective-permute-start.13 = (bf16[32,4096]{1,0:T(8,128)(2,1)S(1)}, bf16[32,4096]{1,0:T(8,128)(2,1)S(1)}, u32[]{:S(2)}, u32[]{:S(2)}) collective-permute-start(bf16[32,4096]{1,0:T(8,128)(2,1)S(1)} %get-tuple-element.69), channel_id=1, source_target_pairs={{0,20},{1,13},{2,22},{3,15},{4,24},{5,17},{6,26},{7,19},{8,28},{9,... | collective-permute-start | bytes 786440 | tf_op jit(solution)/shard_map/ppermute | solution.py:43
  116.2 18.3 %collective-permute-start.14 = (bf16[32,4096]{1,0:T(8,128)(2,1)S(1)}, bf16[32,4096]{1,0:T(8,128)(2,1)S(1)}, u32[]{:S(2)}, u32[]{:S(2)}) collective-permute-start(bf16[32,4096]{1,0:T(8,128)(2,1)S(1)} %get-tuple-element.70), channel_id=1, source_target_pairs={{0,24},{1,9},{2,26},{3,11},{4,28},{5,13},{6,30},{7,15},{8,0},{9,17... | collective-permute-start | bytes 786440 | tf_op jit(solution)/shard_map/ppermute | solution.py:43
  127.1 17.6 %collective-permute-start.15 = (bf16[32,4096]{1,0:T(8,128)(2,1)S(1)}, bf16[32,4096]{1,0:T(8,128)(2,1)S(1)}, u32[]{:S(2)}, u32[]{:S(2)}) collective-permute-start(bf16[32,4096]{1,0:T(8,128)(2,1)S(1)} %get-tuple-element.71.refs_9_), channel_id=1, source_target_pairs={{0,28},{1,5},{2,30},{3,7},{4,0},{5,9},{6,2},{7,11},{8,4},{9,13},{1... | collective-permute-start | bytes 786440 | tf_op jit(solution)/shard_map/ppermute | solution.py:43
  130.2 40.2 %collective-permute-start.18 = (bf16[32,4096]{1,0:T(8,128)(2,1)S(1)}, bf16[32,4096]{1,0:T(8,128)(2,1)S(1)}, u32[]{:S(2)}, u32[]{:S(2)}) collective-permute-start(bf16[32,4096]{1,0:T(8,128)(2,1)S(1)} %get-tuple-element.79), channel_id=1, source_target_pairs={{0,20},{1,13},{2,22},{3,15},{4,24},{5,17},{6,26},{7,19},{8,28},{9,... | collective-permute-start | bytes 786440 | tf_op jit(solution)/shard_map/ppermute | solution.py:43
  134.5 28.5 %collective-permute-start.21 = (bf16[16,4096]{1,0:T(8,128)(2,1)S(1)}, bf16[16,4096]{1,0:T(8,128)(2,1)S(1)}, u32[]{:S(2)}, u32[]{:S(2)}) collective-permute-start(bf16[16,4096]{1,0:T(8,128)(2,1)S(1)} %get-tuple-element.82), channel_id=1, source_target_pairs={{0,16},{1,17},{2,18},{3,19},{4,20},{5,21},{6,22},{7,23},{8,24},{9,... | collective-permute-start | bytes 393224 | tf_op jit(solution)/shard_map/ppermute | solution.py:43
  144.7 26.1 %collective-permute-start.19 = (bf16[32,4096]{1,0:T(8,128)(2,1)S(1)}, bf16[32,4096]{1,0:T(8,128)(2,1)S(1)}, u32[]{:S(2)}, u32[]{:S(2)}) collective-permute-start(bf16[32,4096]{1,0:T(8,128)(2,1)S(1)} %get-tuple-element.80), channel_id=1, source_target_pairs={{0,24},{1,9},{2,26},{3,11},{4,28},{5,13},{6,30},{7,15},{8,0},{9,17... | collective-permute-start | bytes 786440 | tf_op jit(solution)/shard_map/ppermute | solution.py:43
  144.7 26.1 %collective-permute-start.20 = (bf16[32,4096]{1,0:T(8,128)(2,1)S(1)}, bf16[32,4096]{1,0:T(8,128)(2,1)S(1)}, u32[]{:S(2)}, u32[]{:S(2)}) collective-permute-start(bf16[32,4096]{1,0:T(8,128)(2,1)S(1)} %get-tuple-element.81.refs_9_), channel_id=1, source_target_pairs={{0,28},{1,5},{2,30},{3,7},{4,0},{5,9},{6,2},{7,11},{8,4},{9,13},{1... | collective-permute-start | bytes 786440 | tf_op jit(solution)/shard_map/ppermute | solution.py:43
  147.8 29.2 %collective-permute-start.28 = (bf16[35,64,128]{2,1,0:T(8,128)(2,1)S(1)}, bf16[35,64,128]{2,1,0:T(8,128)(2,1)S(1)}, u32[]{:S(2)}, u32[]{:S(2)}) collective-permute-start(bf16[35,64,128]{2,1,0:T(8,128)(2,1)S(1)} %get-tuple-element.78.refs_2_), channel_id=1, source_target_pairs={{0,224},{32,128},{64,160},{96,192},{128,96},{160,0},{192,32},{224,... | collective-permute-start | bytes 1720328 | tf_op jit(solution)/shard_map/ppermute | solution.py:47
  162.9 14.1 %collective-permute-start.29 = (bf16[35,64,128]{2,1,0:T(8,128)(2,1)S(1)}, bf16[35,64,128]{2,1,0:T(8,128)(2,1)S(1)}, u32[]{:S(2)}, u32[]{:S(2)}) collective-permute-start(bf16[35,64,128]{2,1,0:T(8,128)(2,1)S(1)} %get-tuple-element.91), channel_id=1, source_target_pairs={{0,32},{32,64},{64,96},{96,0},{128,160},{160,192},{192,224},{224,1... | collective-permute-start | bytes 1720328 | tf_op jit(solution)/shard_map/ppermute | solution.py:47
  170.4 15.8 %collective-permute-start.30 = (bf16[35,64,128]{2,1,0:T(8,128)(2,1)S(1)}, bf16[35,64,128]{2,1,0:T(8,128)(2,1)S(1)}, u32[]{:S(2)}, u32[]{:S(2)}) collective-permute-start(bf16[35,64,128]{2,1,0:T(8,128)(2,1)S(1)} %get-tuple-element.92), channel_id=1, source_target_pairs={{0,128},{32,160},{64,192},{96,224},{128,0},{160,32},{192,64},{224,... | collective-permute-start | bytes 1720328 | tf_op jit(solution)/shard_map/ppermute | solution.py:47
  171.2 1.6 collective-permute-start.26
  172.9 18.7 %collective-permute-start.27 = (bf16[16,4096]{1,0:T(8,128)(2,1)S(1)}, bf16[16,4096]{1,0:T(8,128)(2,1)S(1)}, u32[]{:S(2)}, u32[]{:S(2)}) collective-permute-start(bf16[16,4096]{1,0:T(8,128)(2,1)S(1)} %get-tuple-element.90), channel_id=1, source_target_pairs={{0,2},{1,3},{2,0},{3,1},{4,6},{5,7},{6,4},{7,5},{8,10},{9,11},{10,... | collective-permute-start | bytes 393224 | tf_op jit(solution)/shard_map/ppermute | solution.py:43

commit v2 on v1

--- a/solution.py
+++ b/solution.py
@@ -73,9 +73,18 @@
     o_ref[...] = jnp.zeros_like(o_ref)
 
 
-def join_kernel(a_ref, b_ref, o_ref):
-    o_ref[0:16, :] = a_ref[...]
-    o_ref[16:32, :] = b_ref[...]
+def join_kernel(*refs):
+    parts, out = refs[:-1], refs[-1]
+    at = 0
+    for part in parts:
+        out[at : at + part.shape[0], :] = part[...]
+        at += part.shape[0]
+
+
+def join(*parts):
+    rows = sum(part.shape[0] for part in parts)
+    shape = jax.ShapeDtypeStruct((rows, parts[0].shape[1]), BF16)
+    return call(join_kernel, 0, shape, parts, 0)
 
 
 def mask_kernel(t_ref, w_ref, m_ref, o_ref, e_ref):
@@ -96,7 +105,7 @@
 
 
 def forward_kernel(first, count, idx_ref, xa, xb, w_ref, g_ref, *rest):
-    act_ref, p_ref, pt_ref, acc_ref = rest[-4:]
+    act_ref, p_ref, acc_ref = rest[-3:]
     d = w_ref.shape[0]
     kb = 1024
 
@@ -124,12 +133,7 @@
         else:
             act_ref[n] = act
         grad = g_ref[at].astype(F32) * s * (1.0 + pre * (1.0 - s))
-        acc_ref[rows, :] = grad
         p_ref[rows, :] = grad.astype(BF16)
-
-    for c in range(7):
-        cols = slice(c * 128, (c + 1) * 128)
-        pt_ref[cols, :] = jnp.transpose(acc_ref[:, cols]).astype(BF16)
 
 
 def forward(first, idx, xa, xb, masked, act_grad, acts=(), after=()):
@@ -141,7 +145,6 @@
         (
             jax.ShapeDtypeStruct((blocks, 16, width), BF16),
             jax.ShapeDtypeStruct((256, width), BF16),
-            jax.ShapeDtypeStruct((width, 256), BF16),
         ),
         (idx, xa, xb, masked, act_grad, *acts),
         2 * 256 * d * width,
@@ -185,37 +188,41 @@
         near3[:, cols] = total[96:128, :]
 
 
-def send_back(own, other, after):
+def mix(own, received, after):
     d = own.shape[1]
-    near1, near2, near3, far, home = call(
+    return call(
         mix_kernel,
         0,
         [jax.ShapeDtypeStruct((32, d), BF16)] * 3 + [jax.ShapeDtypeStruct((16, d), BF16)] * 2,
-        (own, move(other, dc=1)),
+        (own, received),
         128 * d,
         after=after,
     )
-    back = []
-    for k, v in ((3, near3), (2, near2), (1, near1), (4, far)):
-        back.append(move(v, dz=NZ - k))
-    return near1, [*back, home]
+
+
+def hop_kernel(near, received, out):
+    @pl.loop(0, near.shape[1] // 512)
+    def _(s):
+        cols = pl.ds(pl.multiple_of(s * 512, 512), 512)
+        out[:, cols] = (near[:, cols].astype(F32) + received[:, cols].astype(F32)).astype(BF16)
+
+
+def hop(near, received, after):
+    shape = jax.ShapeDtypeStruct(near.shape, BF16)
+    return call(hop_kernel, 0, shape, (near, received), near.size, after=after)
 
 
 def sum_kernel(*refs):
-    halves, to_core, kept = (refs[0:5], refs[5:10]), refs[10], refs[11]
+    halves, to_core, kept = (refs[0:3], refs[3:6]), refs[6], refs[7]
 
     @pl.loop(0, kept.shape[1] // 512)
     def _(s):
         cols = pl.ds(pl.multiple_of(s * 512, 512), 512)
-        for q, (*nears, far, home) in enumerate(halves):
+        for q, (near, far, home) in enumerate(halves):
             rows = slice(q * 16, q * 16 + 16)
             total = home[:, cols].astype(F32) + far[:, cols].astype(F32)
-            away = jnp.zeros_like(total)
-            for near in nears:
-                total = total + near[0:16, cols].astype(F32)
-                away = away + near[16:32, cols].astype(F32)
-            to_core[rows, cols] = away.astype(BF16)
-            kept[rows, cols] = total
+            kept[rows, cols] = total + near[0:16, cols].astype(F32)
+            to_core[rows, cols] = near[16:32, cols]
 
 
 def sum_core_kernel(kept, received, to_x, out):
@@ -237,27 +244,25 @@
 
 def wgrad_kernel(first, dest_ref, code_ref, odd_ref, pa, pb, x0, x1, x2, x3, *rest):
     outs, acc_ref = rest[:-1], rest[-1]
-    last = acc_ref.shape[0] - BLOCK
     left = lax.broadcasted_iota(jnp.int32, (BLOCK, 128), 1) < BLOCK
+    over_rows = (((0,), (0,)), ((), ()))
     for n, out in enumerate(outs):
         dest = dest_ref[first + n]
         cols = pl.ds(pl.multiple_of(dest * 512, 512), 512)
         xa = jnp.concatenate([x0[:, cols], x2[:, cols]], axis=0)
         xb = jnp.concatenate([x1[:, cols], x3[:, cols]], axis=0)
-        acc_ref[...] = jnp.dot(pa[...], xa, preferred_element_type=F32) + jnp.dot(
-            pb[...], xb, preferred_element_type=F32
-        )
+        acc_ref[...] = lax.dot_general(
+            xa, pa[...], over_rows, preferred_element_type=F32
+        ) + lax.dot_general(xb, pb[...], over_rows, preferred_element_type=F32)
 
         def tiles(s):
             row, lane, h = place_of(code_ref[dest, s])
-            row = pl.multiple_of(jnp.minimum(row, last), BLOCK)
             row2, lane2, h2 = place_of(code_ref[dest, PAIRS + s])
-            row2 = pl.multiple_of(jnp.minimum(row2, last), BLOCK)
             return (
                 acc_ref[pl.ds(row, BLOCK), pl.ds(lane, 128)],
                 acc_ref[pl.ds(row2, BLOCK), pl.ds(lane2, 128)],
-                h,
-                h2,
+                h & 1,
+                h2 & 1,
             )
 
         def pack(s, carry):
@@ -278,14 +283,14 @@
 
 
 def wgrad(first, count, scalars, pa, pb, xs, after):
-    width = pa.shape[0]
+    width = pa.shape[1]
     return call(
         functools.partial(wgrad_kernel, first),
         3,
         [jax.ShapeDtypeStruct((PAIRS, BLOCK, 128), BF16)] * count,
         (*scalars, pa, pb, *xs),
         2 * 512 * 512 * width * count,
-        scratch=(pltpu.VMEM((width, 512), F32),),
+        scratch=(pltpu.VMEM((512, width), F32),),
         after=after,
     )
 
@@ -302,9 +307,8 @@
 
 
 def unpack_kernel(own_ref, code_ref, *refs):
-    parts, (out, buf, turned, sems) = refs[:-4], refs[-4:]
+    parts, (out, buf, sems) = refs[:-3], refs[-3:]
     own = own_ref[0]
-    width = turned.shape[1]
     buf[...] = jnp.zeros_like(buf)
     half = lax.broadcasted_iota(jnp.int32, (BLOCK, 128), 1) // BLOCK
 
@@ -314,38 +318,37 @@
             total = total + part[s].astype(F32)
         row, lane, h = place_of(code_ref[own, s])
         at = buf.at[pl.ds(row, BLOCK), pl.ds(lane, 128)]
-        at[...] = jnp.where(half == h, pltpu.roll(total, h * BLOCK, 1), at[...])
+        at[...] = jnp.where(half == h, pltpu.roll(total, (h & 1) * BLOCK, 1), at[...])
         row, lane, h = place_of(code_ref[own, PAIRS + s])
         at = buf.at[pl.ds(row, BLOCK), pl.ds(lane, 128)]
-        at[...] = jnp.where(half == h, pltpu.roll(total, (1 - h) * BLOCK, 1), at[...])
+        at[...] = jnp.where(half == h, pltpu.roll(total, (1 - (h & 1)) * BLOCK, 1), at[...])
         return carry
 
     lax.fori_loop(0, PAIRS, place, 0)
     copies = []
     for c in range(4):
-        lanes = slice(c * 128, (c + 1) * 128)
-        turned[lanes, :] = jnp.transpose(buf[0:width, lanes])
-        copies.append(pltpu.make_async_copy(turned.at[lanes], out.at[lanes], sems.at[c]))
+        rows = slice(c * 128, (c + 1) * 128)
+        copies.append(pltpu.make_async_copy(buf.at[rows], out.at[rows], sems.at[c]))
         copies[-1].start()
     for copy in copies:
         copy.wait()
 
 
-def kept_codes(block_mask, t, width):
+def kept_codes(block_mask, t):
     mask = lax.dynamic_slice(block_mask, (0, t * 14), (64, 14)).reshape(8, 112)
     kept = mask != 0
     at = jnp.arange(112, dtype=jnp.int32)
     i = jnp.array([b // 14 for b in range(112)], jnp.int32)
     j = at - i * 14
-    h = i & 1
+    h = j & 1
     before = (at[:, None] <= at[None, :]) & (h[:, None] == h[None, :])
     rank = jnp.dot(kept.astype(BF16), before.astype(BF16), preferred_element_type=F32)
     rank = rank.astype(jnp.int32) - 1
     extra = rank >= PAIRS
     slot = jnp.where(extra, 3 * PAIRS - 1 - PAIRS * h - rank, rank + PAIRS * h)
     hit = kept[:, None, :] & (slot[:, None, :] == jnp.arange(CAP, dtype=jnp.int32)[None, :, None])
-    code = j * BLOCK + (i >> 1) * (128 << 10) + (h << 20) - width
-    code = jnp.sum(jnp.where(hit, code[None, None, :], 0), axis=2, dtype=jnp.int32) + width
+    code = i * BLOCK + (j >> 1) * (128 << 10) + ((h - 2) << 20)
+    code = jnp.sum(jnp.where(hit, code[None, None, :], 0), axis=2, dtype=jnp.int32) + (2 << 20)
     odd = jnp.sum((kept & extra).astype(jnp.int32), axis=1, dtype=jnp.int32)
     return code, odd
 
@@ -357,12 +360,14 @@
 
     partner = move(tokens, dc=1)
     home = move(tokens, dx=1)
-    chip = call(join_kernel, 0, jax.ShapeDtypeStruct((32, d), BF16), (tokens, partner), 0)
+    chip = join(tokens, partner)
     t, g, chip = lax.optimization_barrier((t, g, chip))
     z, xh, core = t >> 2, (t >> 1) & 1, t & 1
     xl, y = g >> 2, g & 3
-    near = [move(chip, dz=k) for k in (1, 2, 3)]
-    far = move(chip[:16], dz=4)
+    near = [move(chip, dz=1)]
+    near.append(move(near[0], dz=1))
+    near.append(move(near[1], dz=1))
+    far = move(tokens, dz=4)
 
     n = jnp.arange(32, dtype=jnp.int32)
     slot = n & 7
@@ -371,14 +376,14 @@
     gather_core = core ^ ((n >> 3) & 1)
     zk = (z - (1 - 2 * gather_core) * dist) & (NZ - 1)
     idx = zk * 4 + (xh ^ (n >> 4)) * 2 + (gather_core ^ flip)
-    order = [(1, 2), (0, 2), (1, 1), (0, 3), (1, 3), (0, 1), (1, 0), (0, 0)]
+    order = [(1, 2), (1, 0), (1, 1), (0, 2), (1, 3), (0, 1), (0, 3), (0, 0)]
     dx = jnp.array([o[0] for o in order], jnp.int32)
     dy = jnp.array([o[1] for o in order], jnp.int32)
     dests = (xl ^ dx) * NY + ((y + dy) & (NY - 1))
 
-    ticks = [call(tick_kernel, 0, jax.ShapeDtypeStruct((8, 128), F32), (), 0) for _ in range(3)]
-    t_mask, ticks[2] = lax.optimization_barrier((t, ticks[2]))
-    t_list, ticks[1] = lax.optimization_barrier((t, ticks[1]))
+    ticks = [call(tick_kernel, 0, jax.ShapeDtypeStruct((8, 128), F32), (), 0) for _ in range(2)]
+    t_list, ticks[0] = lax.optimization_barrier((t, ticks[0]))
+    t_mask, ticks[1] = lax.optimization_barrier((t, ticks[1]))
     masked = call(
         mask_kernel,
         1,
@@ -387,24 +392,24 @@
         d * width,
         scratch=(pltpu.VMEM((64, width), F32),),
     )
-    code, odd = kept_codes(block_mask, t_list, width)
-    near[2], masked, code, odd, idx, dests = lax.optimization_barrier(
-        (near[2], masked, code, odd, idx, dests)
-    )
+    code, odd = kept_codes(block_mask, t_list)
+    code, odd, idx, dests, near[1] = lax.optimization_barrier((code, odd, idx, dests, near[1]))
+    near[2], masked = lax.optimization_barrier((near[2], masked))
     scalars = (dests, code, odd)
 
     near_x = [move(near[k], dx=1) for k in range(3)]
     far_x = move(far, dx=1)
-    x0 = jnp.concatenate([tokens, far, *near], axis=0)
+    x0 = join(tokens, far, *near)
     x2 = move(x0, dc=1)
-    x1 = jnp.concatenate([home, far_x, *near_x], axis=0)
+    x1 = join(home, far_x, *near_x)
     x3 = move(x1, dc=1)
     xs = (x0, x1, x2, x3)
 
     grads = act_grad.reshape(32, 16, width)
-    act, p, pa = forward(0, idx, x0, x2, masked, grads, after=ticks)
-    own_a, other_a = xgrad(p, masked)
-    act, p, pb = forward(16, idx, x1, x3, masked, grads, (act,), (other_a,))
+    act, pa = forward(0, idx, x0, x2, masked, grads, after=ticks)
+    own_a, other_a = xgrad(pa, masked)
+    received_a = move(other_a, dc=1)
+    act, pb = forward(16, idx, x1, x3, masked, grads, (act,), (other_a,))
 
     parts = []
 
@@ -412,15 +417,29 @@
         packed = wgrad(first, 2, scalars, pa, pb, xs, after)
         for v, o in zip(packed, order[first : first + 2]):
             parts.append(v if o == (0, 0) else move_dp(v, *o))
-        return (packed[0],)
+        return packed[0]
+
+    def back(x, hops=1):
+        return move(x, dz=NZ - hops)
 
     done = pack_two(0, ())
-    done, back_a = send_back(own_a, other_a, done)
-    done = pack_two(2, (done,))
-    own_b, other_b = xgrad(p, masked, done)
-    done = pack_two(4, (other_b,))
-    done, back_b = send_back(own_b, other_b, done)
-    pack_two(6, (done,))
+    a1, a2, a3, far_a, home_a = mix(own_a, received_a, (done,))
+    ring_a, far_a = back(a3), back(far_a, 4)
+    own_b, other_b = xgrad(pb, masked, (a3,))
+    received_b = move(other_b, dc=1)
+    done = pack_two(2, (other_b,))
+    done = hop(a2, ring_a, (done,))
+    ring_a = back(done)
+    b1, b2, b3, far_b, home_b = mix(own_b, received_b, (done,))
+    ring_b, far_b = back(b3), back(far_b, 4)
+    done = pack_two(4, (b3,))
+    done = hop(a1, ring_a, (done,))
+    ring_a = back(done)
+    done = hop(b2, ring_b, (done,))
+    ring_b = back(done)
+    done = pack_two(6, (done,))
+    done = hop(b1, ring_b, (done,))
+    ring_b = back(done)
 
     early = call(
         presum_kernel,
@@ -428,13 +447,14 @@
         jax.ShapeDtypeStruct((PAIRS, BLOCK, 128), F32),
         (parts[7], *parts[:4]),
         5 * CAP * 4096,
+        after=(done,),
     )
     to_core, kept = call(
         sum_kernel,
         0,
         (jax.ShapeDtypeStruct((32, d), BF16), jax.ShapeDtypeStruct((32, d), F32)),
-        (*back_a, *back_b),
-        10 * 32 * d,
+        (ring_a, far_a, home_a, ring_b, far_b, home_b),
+        6 * 32 * d,
         after=(early,),
     )
     to_x, kept = call(
@@ -453,7 +473,6 @@
         (g.reshape(1), code, early, *parts[4:7]),
         8 * CAP * 4096,
         scratch=(
-            pltpu.VMEM((width + BLOCK, 512), F32),
             pltpu.VMEM((512, width), F32),
             pltpu.SemaphoreType.DMA((4,)),
         ),

time: 193 us -> 169 us (0.88)
  the two profiles are of different devices: /device:TPU:31 before, /device:TPU:69 now
where the time goes in v2:
time: 169 us; the launch traced here: 168 us
  waiting for transfers between devices  81.2 us (48%)
  starting transfers between devices  39.9 us (24%)
  Pallas kernels  36.1 us (21%)
  local copies, waits for them, and re-layouts  5.08 us (3%)
  other arithmetic  4.21 us (2%)
    ppermute x7, waiting for transfers between devices, move_dp(): return lax.ppermute(x, 'dp', dp_perm(dx, dy))  47.7 us
    pallas_call x24, Pallas kernels, call(): pl.pallas_call(run, out_shape=out_shape, in_specs=[SMEM] * n_scalar + [VM...  36.1 us
    ppermute x24, waiting for transfers between devices, move(): return lax.ppermute(x, 'tensor', tensor_perm(dz, dx, dc, split=True))  33.6 us
    ppermute x24, starting transfers between devices, move(): return lax.ppermute(x, 'tensor', tensor_perm(dz, dx, dc, split=True))  30.8 us
    ppermute x7, starting transfers between devices, move_dp(): return lax.ppermute(x, 'dp', dp_perm(dx, dy))  9.12 us
    unnamed x10, local copies, waits for them, and re-layouts  4.92 us
  transfers between devices with their start and end apart: 31, of which 12 were waited for; matrix products, arithmetic and copies ran while one was open for 3% of the time, Pallas kernels for 19%

profile of v2, /device:TPU:69, one launch (start us, length us, event | category | flops | bytes accessed | tf_op | source)
XLA Modules:
  0.0 168.4 jit_solution(14241090937173878718)
XLA Ops:
  0.6 0.8 collective-permute-start
  1.4 5.1 %collective-permute-start.4 = (bf16[16,4096]{1,0:T(8,128)(2,1)}, bf16[16,4096]{1,0:T(8,128)(2,1)S(1)}, u32[]{:S(2)}, u32[]{:S(2)}) collective-permute-start(bf16[16,4096]{1,0:T(8,128)(2,1)} %refs_0_.3), channel_id=1, source_target_pairs={{0,16},{1,17},{2,18},{3,19},{4,20},{5,21},{6,22},{7,23},{8,24},{9,... | collective-permute-start | bytes 393224 | tf_op jit(solution)/shard_map/ppermute | solution.py:43
  6.5 0.9 copy-done.2
  7.5 0.8 collective-permute-start.1
  8.3 0.9 dynamic-slice_compare_fusion
  9.3 1.0 convert_reduce_fusion
  10.3 5.6 %collective-permute-done.1.refs_2_ = bf16[32,4096]{1,0:T(8,128)(2,1)S(1)} collective-permute-done((bf16[32,4096]{1,0:T(8,128)(2,1)S(1)}, bf16[32,4096]{1,0:T(8,128)(2,1)S(1)}, u32[]{:S(2)}, u32[]{:S(2)}) %collective-permute-start.1) | collective-permute-done | bytes 262176 | tf_op jit(solution)/shard_map/ppermute | solution.py:43
  15.9 1.2 collective-permute-start.2
  17.1 1.9 %select_reduce_fusion = s32[8,70]{0,1:T(8,128)S(1)} fusion(s32[112]{0:T(128)} %constant.75, s32[8,112]{1,0:T(8,128)S(1)} %get-tuple-element.92, pred[8,112]{1,0:T(8,128)(4,1)S(1)} %ne.15), kind=kLoop, calls=%fused_computation.2 | loop fusion | flops 250320 | bytes 7168 | tf_op jit(solution)/shard_map/reduce_sum | solution.py:351
  19.1 2.3 %collective-permute-done.2.refs_3_ = bf16[32,4096]{1,0:T(8,128)(2,1)S(1)} collective-permute-done((bf16[32,4096]{1,0:T(8,128)(2,1)S(1)}, bf16[32,4096]{1,0:T(8,128)(2,1)S(1)}, u32[]{:S(2)}, u32[]{:S(2)}) %collective-permute-start.2) | collective-permute-done | bytes 262176 | tf_op jit(solution)/shard_map/ppermute | solution.py:43
  21.4 1.2 collective-permute-start.8
  22.6 0.7 and_add_fusion.refs_0_
  23.3 3.1 %copy-done = bf16[4096,896]{1,0:T(8,128)(2,1)S(1)} copy-done((bf16[4096,896]{1,0:T(8,128)(2,1)S(1)}, bf16[4096,896]{1,0:T(8,128)(2,1)}, u32[]{:S(2)}) %copy-start) | copy-done | bytes 7340056
  26.4 0.9 copy-done.4
  27.3 1.4 shard_map.97.refs_3_.refs_1_
  28.9 2.5 %collective-permute-start.11 = (bf16[128,4096]{1,0:T(8,128)(2,1)S(1)}, bf16[128,4096]{1,0:T(8,128)(2,1)S(1)}, u32[]{:S(2)}, u32[]{:S(2)}) collective-permute-start(bf16[128,4096]{1,0:T(8,128)(2,1)S(1)} %shard_map.99.refs_1_.refs_5_), channel_id=1, source_target_pairs={{0,1},{1,0},{2,3},{3,2},{4,5},{5,4},{6,7},{7,6},{8,9},{9,8},{10,11... | collective-permute-start | bytes 3145736 | tf_op jit(solution)/shard_map/ppermute | solution.py:43
  31.6 2.7 %collective-permute-start.6 = (bf16[32,4096]{1,0:T(8,128)(2,1)S(1)}, bf16[32,4096]{1,0:T(8,128)(2,1)S(1)}, u32[]{:S(2)}, u32[]{:S(2)}) collective-permute-start(bf16[32,4096]{1,0:T(8,128)(2,1)S(1)} %collective-permute-done.1.refs_2_), channel_id=1, source_target_pairs={{0,2},{1,3},{2,0},{3,1},{4,6},{5,7},{6,4},{7,5},{8,10},{9,11},{10,... | collective-permute-start | bytes 786440 | tf_op jit(solution)/shard_map/ppermute | solution.py:43
  34.6 2.7 %collective-permute-start.9 = (bf16[32,4096]{1,0:T(8,128)(2,1)S(1)}, bf16[32,4096]{1,0:T(8,128)(2,1)S(1)}, u32[]{:S(2)}, u32[]{:S(2)}) collective-permute-start(bf16[32,4096]{1,0:T(8,128)(2,1)S(1)} %collective-permute-done.8.refs_4_), channel_id=1, source_target_pairs={{0,2},{1,3},{2,0},{3,1},{4,6},{5,7},{6,4},{7,5},{8,10},{9,11},{10,... | collective-permute-start | bytes 786440 | tf_op jit(solution)/shard_map/ppermute | solution.py:43
  38.1 19.4 %collective-permute-done.5.refs_1_ = bf16[16,4096]{1,0:T(8,128)(2,1)S(1)} collective-permute-done((bf16[16,4096]{1,0:T(8,128)(2,1)S(1)}, bf16[16,4096]{1,0:T(8,128)(2,1)S(1)}, u32[]{:S(2)}, u32[]{:S(2)}) %collective-permute-start.5) | collective-permute-done | bytes 131104 | tf_op jit(solution)/shard_map/ppermute | solution.py:43
  57.6 1.0 collective-permute-start.10
  58.7 3.9 %shard_map.100 = (bf16[16,16,896]{2,1,0:T(8,128)(2,1)S(1)}, bf16[256,896]{1,0:T(8,128)(2,1)S(1)}) custom-call(s32[32]{0:T(128)S(1)} %fusion.9.refs_0_, bf16[128,4096]{1,0:T(8,128)(2,1)S(1)} %shard_map.99.refs_1_.refs_5_, bf16[128,4096]{1,0:T(8,128)(2,1)S(1)} %collective-permute-done.11.refs_2_.refs_7_, bf16[4096,896]{1,0:T(8,128)(2,1)S(1)} %shard_map.97.refs_3_.refs_1_, ...), custom_call_target="tpu_custom_call" | custom-call | flops 1879048192 | bytes 10354816 | tf_op jit(solution)/shard_map/pallas_call | solution.py:59
  62.6 3.8 %shard_map.101 = (f32[128,4096]{1,0:T(8,128)S(1)}, bf16[128,4096]{1,0:T(8,128)(2,1)S(1)}) custom-call(bf16[256,896]{1,0:T(8,128)(2,1)S(1)} %get-tuple-element.59.refs_0_.refs_3_, bf16[4096,896]{1,0:T(8,128)(2,1)S(1)} %shard_map.97.refs_3_.refs_1_), custom_call_target="tpu_custom_call" | custom-call | flops 1879048192 | bytes 7798784 | tf_op jit(solution)/shard_map/pallas_call | solution.py:59
  66.7 4.8 %shard_map.102 = (bf16[32,16,896]{2,1,0:T(8,128)(2,1)}, bf16[256,896]{1,0:T(8,128)(2,1)S(1)}) custom-call(s32[32]{0:T(128)S(1)} %fusion.9.refs_0_, bf16[128,4096]{1,0:T(8,128)(2,1)S(1)} %shard_map.98.refs_1_.refs_6_, bf16[128,4096]{1,0:T(8,128)(2,1)S(1)} %collective-permute-done.10.refs_2_.refs_8_, bf16[4096,896]{1,0:T(8,128)(2,1)S(1)} %shard_map.97.refs_3_.refs_1_, ...), custom_call_target="tpu_custom_call" | custom-call | flops 1879048192 | bytes 10813568 | tf_op jit(solution)/shard_map/pallas_call | solution.py:59
  71.5 2.8 %shard_map.103 = (bf16[35,64,128]{2,1,0:T(8,128)(2,1)S(1)}, bf16[35,64,128]{2,1,0:T(8,128)(2,1)S(1)}) custom-call(s32[8]{0:T(128)S(1)} %and_add_fusion.refs_0_, s32[8,70]{1,0:T(8,128)S(1)} %broadcast_add_fusion.refs_1_, s32[8]{0:T(128)S(1)} %get-tuple-element.65.refs_2_, bf16[256,896]{1,0:T(8,128)(2,1)S(1)} %get-tuple-element.59.refs_0_.refs_3_, ...), custom_call_target="tpu_custom_call" | custom-call | flops 939524096 | bytes 5114112 | tf_op jit(solution)/shard_map/pallas_call | solution.py:59
  74.6 3.8 %shard_map.105 = (f32[128,4096]{1,0:T(8,128)S(1)}, bf16[128,4096]{1,0:T(8,128)(2,1)S(1)}) custom-call(bf16[256,896]{1,0:T(8,128)(2,1)S(1)} %get-tuple-element.66.refs_4_.refs_0_, bf16[4096,896]{1,0:T(8,128)(2,1)S(1)} %shard_map.97.refs_3_.refs_1_, bf16[32,4096]{1,0:T(8,128)(2,1)S(1)} %get-tuple-element.70.refs_2_), custom_call_target="tpu_custom_call" | custom-call | flops 1879048192 | bytes 7798784 | tf_op jit(solution)/shard_map/pallas_call | solution.py:59
  78.4 0.6 collective-permute-start.15
  78.9 3.4 %collective-permute-start.13 = (bf16[32,4096]{1,0:T(8,128)(2,1)S(1)}, bf16[32,4096]{1,0:T(8,128)(2,1)S(1)}, u32[]{:S(2)}, u32[]{:S(2)}) collective-permute-start(bf16[32,4096]{1,0:T(8,128)(2,1)S(1)} %get-tuple-element.70.refs_2_), channel_id=1, source_target_pairs={{0,28},{1,5},{2,30},{3,7},{4,0},{5,9},{6,2},{7,11},{8,4},{9,13},{1... | collective-permute-start | bytes 786440 | tf_op jit(solution)/shard_map/ppermute | solution.py:43
  82.3 2.8 %shard_map.106 = (bf16[35,64,128]{2,1,0:T(8,128)(2,1)S(1)}, bf16[35,64,128]{2,1,0:T(8,128)(2,1)S(1)}) custom-call(s32[8]{0:T(128)S(1)} %and_add_fusion.refs_0_, s32[8,70]{1,0:T(8,128)S(1)} %broadcast_add_fusion.refs_1_, s32[8]{0:T(128)S(1)} %get-tuple-element.65.refs_2_, bf16[256,896]{1,0:T(8,128)(2,1)S(1)} %get-tuple-element.59.refs_0_.refs_3_, ...), custom_call_target="tpu_custom_call" | custom-call | flops 939524096 | bytes 5114112 | tf_op jit(solution)/shard_map/pallas_call | solution.py:59
  85.7 2.3 %collective-permute-start.14 = (bf16[32,4096]{1,0:T(8,128)(2,1)S(1)}, bf16[32,4096]{1,0:T(8,128)(2,1)S(1)}, u32[]{:S(2)}, u32[]{:S(2)}) collective-permute-start(bf16[32,4096]{1,0:T(8,128)(2,1)S(1)} %shard_map.107.refs_2_), channel_id=1, source_target_pairs={{0,28},{1,5},{2,30},{3,7},{4,0},{5,9},{6,2},{7,11},{8,4},{9,13},{1... | collective-permute-start | bytes 786440 | tf_op jit(solution)/shard_map/ppermute | solution.py:43
  88.0 1.2 collective-permute-start.23
  89.4 2.1 %collective-permute-start.18 = (bf16[32,4096]{1,0:T(8,128)(2,1)S(1)}, bf16[32,4096]{1,0:T(8,128)(2,1)S(1)}, u32[]{:S(2)}, u32[]{:S(2)}) collective-permute-start(bf16[32,4096]{1,0:T(8,128)(2,1)S(1)} %get-tuple-element.74.refs_9_), channel_id=1, source_target_pairs={{0,28},{1,5},{2,30},{3,7},{4,0},{5,9},{6,2},{7,11},{8,4},{9,13},{1... | collective-permute-start | bytes 786440 | tf_op jit(solution)/shard_map/ppermute | solution.py:43
  91.4 3.0 %collective-permute-start.22 = (bf16[35,64,128]{2,1,0:T(8,128)(2,1)S(1)}, bf16[35,64,128]{2,1,0:T(8,128)(2,1)S(1)}, u32[]{:S(2)}, u32[]{:S(2)}) collective-permute-start(bf16[35,64,128]{2,1,0:T(8,128)(2,1)S(1)} %get-tuple-element.67.refs_2_), channel_id=1, source_target_pairs={{0,192},{32,224},{64,128},{96,160},{128,64},{160,96},{192,0},{224,... | collective-permute-start | bytes 1720328 | tf_op jit(solution)/shard_map/ppermute | solution.py:47
  94.5 2.2 %collective-permute-start.24 = (bf16[35,64,128]{2,1,0:T(8,128)(2,1)S(1)}, bf16[35,64,128]{2,1,0:T(8,128)(2,1)S(1)}, u32[]{:S(2)}, u32[]{:S(2)}) collective-permute-start(bf16[35,64,128]{2,1,0:T(8,128)(2,1)S(1)} %get-tuple-element.72.refs_2_), channel_id=1, source_target_pairs={{0,160},{32,192},{64,224},{96,128},{128,32},{160,64},{192,96},{224... | collective-permute-start | bytes 1720328 | tf_op jit(solution)/shard_map/ppermute | solution.py:47
  96.7 3.0 %shard_map.109 = (bf16[35,64,128]{2,1,0:T(8,128)(2,1)S(1)}, bf16[35,64,128]{2,1,0:T(8,128)(2,1)S(1)}) custom-call(s32[8]{0:T(128)S(1)} %and_add_fusion.refs_0_, s32[8,70]{1,0:T(8,128)S(1)} %broadcast_add_fusion.refs_1_, s32[8]{0:T(128)S(1)} %get-tuple-element.65.refs_2_, bf16[256,896]{1,0:T(8,128)(2,1)S(1)} %get-tuple-element.59.refs_0_.refs_3_, ...), custom_call_target="tpu_custom_call" | custom-call | flops 939524096 | bytes 5114112 | tf_op jit(solution)/shard_map/pallas_call | solution.py:59
  100.0 2.9 %collective-permute-done.23.refs_2_ = bf16[35,64,128]{2,1,0:T(8,128)(2,1)S(1)} collective-permute-done((bf16[35,64,128]{2,1,0:T(8,128)(2,1)S(1)}, bf16[35,64,128]{2,1,0:T(8,128)(2,1)S(1)}, u32[]{:S(2)}, u32[]{:S(2)}) %collective-permute-start.23) | collective-permute-done | bytes 573472 | tf_op jit(solution)/shard_map/ppermute | solution.py:47
  103.0 4.0 %collective-permute-done.19.refs_1_ = bf16[32,4096]{1,0:T(8,128)(2,1)S(1)} collective-permute-done((bf16[32,4096]{1,0:T(8,128)(2,1)S(1)}, bf16[32,4096]{1,0:T(8,128)(2,1)S(1)}, u32[]{:S(2)}, u32[]{:S(2)}) %collective-permute-start.19) | collective-permute-done | bytes 262176 | tf_op jit(solution)/shard_map/ppermute | solution.py:43
  106.9 1.4 collective-permute-start.21
  108.3 2.8 %shard_map.112 = (bf16[35,64,128]{2,1,0:T(8,128)(2,1)S(1)}, bf16[35,64,128]{2,1,0:T(8,128)(2,1)S(1)}) custom-call(s32[8]{0:T(128)S(1)} %and_add_fusion.refs_0_, s32[8,70]{1,0:T(8,128)S(1)} %broadcast_add_fusion.refs_1_, s32[8]{0:T(128)S(1)} %get-tuple-element.65.refs_2_, bf16[256,896]{1,0:T(8,128)(2,1)S(1)} %get-tuple-element.59.refs_0_.refs_3_, ...), custom_call_target="tpu_custom_call" | custom-call | flops 939524096 | bytes 5114112 | tf_op jit(solution)/shard_map/pallas_call | solution.py:59
  111.3 6.8 %collective-permute-done.22.refs_1_ = bf16[35,64,128]{2,1,0:T(8,128)(2,1)S(1)} collective-permute-done((bf16[35,64,128]{2,1,0:T(8,128)(2,1)S(1)}, bf16[35,64,128]{2,1,0:T(8,128)(2,1)S(1)}, u32[]{:S(2)}, u32[]{:S(2)}) %collective-permute-start.22) | collective-permute-done | bytes 573472 | tf_op jit(solution)/shard_map/ppermute | solution.py:47
  118.0 1.1 collective-permute-start.16
  119.2 15.3 %collective-permute-done.25.refs_4_ = bf16[35,64,128]{2,1,0:T(8,128)(2,1)S(1)} collective-permute-done((bf16[35,64,128]{2,1,0:T(8,128)(2,1)S(1)}, bf16[35,64,128]{2,1,0:T(8,128)(2,1)S(1)}, u32[]{:S(2)}, u32[]{:S(2)}) %collective-permute-start.25) | collective-permute-done | bytes 573472 | tf_op jit(solution)/shard_map/ppermute | solution.py:47
  134.4 2.1 %collective-permute-start.29 = (bf16[35,64,128]{2,1,0:T(8,128)(2,1)S(1)}, bf16[35,64,128]{2,1,0:T(8,128)(2,1)S(1)}, u32[]{:S(2)}, u32[]{:S(2)}) collective-permute-start(bf16[35,64,128]{2,1,0:T(8,128)(2,1)S(1)} %get-tuple-element.90), channel_id=1, source_target_pairs={{0,32},{32,64},{64,96},{96,0},{128,160},{160,192},{192,224},{224,1... | collective-permute-start | bytes 1720328 | tf_op jit(solution)/shard_map/ppermute | solution.py:47
  136.5 0.6 collective-permute-start.30
  138.3 1.2 collective-permute-done.26.refs_1_
  139.8 10.5 %collective-permute-done.29.refs_4_ = bf16[35,64,128]{2,1,0:T(8,128)(2,1)S(1)} collective-permute-done((bf16[35,64,128]{2,1,0:T(8,128)(2,1)S(1)}, bf16[35,64,128]{2,1,0:T(8,128)(2,1)S(1)}, u32[]{:S(2)}, u32[]{:S(2)}) %collective-permute-start.29) | collective-permute-done | bytes 573472 | tf_op jit(solution)/shard_map/ppermute | solution.py:47
  150.3 12.2 %collective-permute-done.30.refs_5_ = bf16[35,64,128]{2,1,0:T(8,128)(2,1)S(1)} collective-permute-done((bf16[35,64,128]{2,1,0:T(8,128)(2,1)S(1)}, bf16[35,64,128]{2,1,0:T(8,128)(2,1)S(1)}, u32[]{:S(2)}, u32[]{:S(2)}) %collective-permute-start.30) | collective-permute-done | bytes 573472 | tf_op jit(solution)/shard_map/ppermute | solution.py:47
  162.5 5.2 %shard_map.117 = f32[512,896]{1,0:T(8,128)} custom-call(s32[1]{0:T(128)} %bitcast.3.refs_0_, s32[8,70]{1,0:T(8,128)S(1)} %broadcast_add_fusion.refs_1_, f32[35,64,128]{2,1,0:T(8,128)S(1)} %shard_map.114.refs_6_.refs_2_, bf16[35,64,128]{2,1,0:T(8,128)(2,1)S(1)} %collective-permute-done.28.refs_3_, bf16[35,64,128]{2,1,0:T(8,128)(2,1)S(1)} %collective-permute-done.29.refs_4_, ...), custom_call_target="tpu_custom_call" | custom-call | flops 2293760 | bytes 2869444 | tf_op jit(solution)/shard_map/pallas_call | solution.py:59
  167.8 0.7 add_convert_fusion
  (57 shorter events, 4.9 us)
Async XLA Ops:
  0.6 5.9 %collective-permute-start = (bf16[16,4096]{1,0:T(8,128)(2,1)}, bf16[16,4096]{1,0:T(8,128)(2,1)S(1)}, u32[]{:S(2)}, u32[]{:S(2)}) collective-permute-start(bf16[16,4096]{1,0:T(8,128)(2,1)} %refs_0_.3), channel_id=1, source_target_pairs={{0,1},{1,0},{2,3},{3,2},{4,5},{5,4},{6,7},{7,6},{8,9},{9,8},{10,11... | collective-permute-start | bytes 393224 | tf_op jit(solution)/shard_map/ppermute | solution.py:43
  1.4 27.4 %collective-permute-start.4 = (bf16[16,4096]{1,0:T(8,128)(2,1)}, bf16[16,4096]{1,0:T(8,128)(2,1)S(1)}, u32[]{:S(2)}, u32[]{:S(2)}) collective-permute-start(bf16[16,4096]{1,0:T(8,128)(2,1)} %refs_0_.3), channel_id=1, source_target_pairs={{0,16},{1,17},{2,18},{3,19},{4,20},{5,21},{6,22},{7,23},{8,24},{9,... | collective-permute-start | bytes 393224 | tf_op jit(solution)/shard_map/ppermute | solution.py:43
  6.5 0.9 copy-start.2
  7.5 8.5 %collective-permute-start.1 = (bf16[32,4096]{1,0:T(8,128)(2,1)S(1)}, bf16[32,4096]{1,0:T(8,128)(2,1)S(1)}, u32[]{:S(2)}, u32[]{:S(2)}) collective-permute-start(bf16[32,4096]{1,0:T(8,128)(2,1)S(1)} %shard_map.94), channel_id=1, source_target_pairs={{0,4},{1,29},{2,6},{3,31},{4,8},{5,1},{6,10},{7,3},{8,12},{9,5},{1... | collective-permute-start | bytes 786440 | tf_op jit(solution)/shard_map/ppermute | solution.py:43
  15.9 5.5 %collective-permute-start.2 = (bf16[32,4096]{1,0:T(8,128)(2,1)S(1)}, bf16[32,4096]{1,0:T(8,128)(2,1)S(1)}, u32[]{:S(2)}, u32[]{:S(2)}) collective-permute-start(bf16[32,4096]{1,0:T(8,128)(2,1)S(1)} %collective-permute-done.1.refs_2_), channel_id=1, source_target_pairs={{0,4},{1,29},{2,6},{3,31},{4,8},{5,1},{6,10},{7,3},{8,12},{9,5},{1... | collective-permute-start | bytes 786440 | tf_op jit(solution)/shard_map/ppermute | solution.py:43
  21.4 7.3 %collective-permute-start.8 = (bf16[32,4096]{1,0:T(8,128)(2,1)S(1)}, bf16[32,4096]{1,0:T(8,128)(2,1)S(1)}, u32[]{:S(2)}, u32[]{:S(2)}) collective-permute-start(bf16[32,4096]{1,0:T(8,128)(2,1)S(1)} %collective-permute-done.2.refs_3_), channel_id=1, source_target_pairs={{0,4},{1,29},{2,6},{3,31},{4,8},{5,1},{6,10},{7,3},{8,12},{9,5},{1... | collective-permute-start | bytes 786440 | tf_op jit(solution)/shard_map/ppermute | solution.py:43
  23.3 3.1 %copy-start = (bf16[4096,896]{1,0:T(8,128)(2,1)S(1)}, bf16[4096,896]{1,0:T(8,128)(2,1)}, u32[]{:S(2)}) copy-start(bf16[4096,896]{1,0:T(8,128)(2,1)} %refs_1_.1) | copy-start | bytes 22020100
  26.4 0.9 copy-start.4
  27.3 1.5 copy-start.3
  28.7 29.9 %copy-start.1 = (bf16[512,896]{1,0:T(8,128)(2,1)S(1)}, bf16[512,896]{1,0:T(8,128)(2,1)}, u32[]{:S(2)}) copy-start(bf16[512,896]{1,0:T(8,128)(2,1)} %param.10) | copy-start | bytes 2752516
  28.9 29.8 %collective-permute-start.11 = (bf16[128,4096]{1,0:T(8,128)(2,1)S(1)}, bf16[128,4096]{1,0:T(8,128)(2,1)S(1)}, u32[]{:S(2)}, u32[]{:S(2)}) collective-permute-start(bf16[128,4096]{1,0:T(8,128)(2,1)S(1)} %shard_map.99.refs_1_.refs_5_), channel_id=1, source_target_pairs={{0,1},{1,0},{2,3},{3,2},{4,5},{5,4},{6,7},{7,6},{8,9},{9,8},{10,11... | collective-permute-start | bytes 3145736 | tf_op jit(solution)/shard_map/ppermute | solution.py:43
  31.4 6.5 %collective-permute-start.3 = (bf16[16,4096]{1,0:T(8,128)(2,1)S(1)}, bf16[16,4096]{1,0:T(8,128)(2,1)S(1)}, u32[]{:S(2)}, u32[]{:S(2)}) collective-permute-start(bf16[16,4096]{1,0:T(8,128)(2,1)S(1)} %copy-done.3), channel_id=1, source_target_pairs={{0,2},{1,3},{2,0},{3,1},{4,6},{5,7},{6,4},{7,5},{8,10},{9,11},{10,... | collective-permute-start | bytes 393224 | tf_op jit(solution)/shard_map/ppermute | solution.py:43
  31.6 25.9 %collective-permute-start.6 = (bf16[32,4096]{1,0:T(8,128)(2,1)S(1)}, bf16[32,4096]{1,0:T(8,128)(2,1)S(1)}, u32[]{:S(2)}, u32[]{:S(2)}) collective-permute-start(bf16[32,4096]{1,0:T(8,128)(2,1)S(1)} %collective-permute-done.1.refs_2_), channel_id=1, source_target_pairs={{0,2},{1,3},{2,0},{3,1},{4,6},{5,7},{6,4},{7,5},{8,10},{9,11},{10,... | collective-permute-start | bytes 786440 | tf_op jit(solution)/shard_map/ppermute | solution.py:43
  34.4 23.2 %collective-permute-start.7 = (bf16[32,4096]{1,0:T(8,128)(2,1)S(1)}, bf16[32,4096]{1,0:T(8,128)(2,1)S(1)}, u32[]{:S(2)}, u32[]{:S(2)}) collective-permute-start(bf16[32,4096]{1,0:T(8,128)(2,1)S(1)} %collective-permute-done.2.refs_3_), channel_id=1, source_target_pairs={{0,2},{1,3},{2,0},{3,1},{4,6},{5,7},{6,4},{7,5},{8,10},{9,11},{10,... | collective-permute-start | bytes 786440 | tf_op jit(solution)/shard_map/ppermute | solution.py:43
  34.6 22.9 %collective-permute-start.9 = (bf16[32,4096]{1,0:T(8,128)(2,1)S(1)}, bf16[32,4096]{1,0:T(8,128)(2,1)S(1)}, u32[]{:S(2)}, u32[]{:S(2)}) collective-permute-start(bf16[32,4096]{1,0:T(8,128)(2,1)S(1)} %collective-permute-done.8.refs_4_), channel_id=1, source_target_pairs={{0,2},{1,3},{2,0},{3,1},{4,6},{5,7},{6,4},{7,5},{8,10},{9,11},{10,... | collective-permute-start | bytes 786440 | tf_op jit(solution)/shard_map/ppermute | solution.py:43
  37.9 19.7 %collective-permute-start.5 = (bf16[16,4096]{1,0:T(8,128)(2,1)S(1)}, bf16[16,4096]{1,0:T(8,128)(2,1)S(1)}, u32[]{:S(2)}, u32[]{:S(2)}) collective-permute-start(bf16[16,4096]{1,0:T(8,128)(2,1)S(1)} %collective-permute-done.4.refs_1_), channel_id=1, source_target_pairs={{0,2},{1,3},{2,0},{3,1},{4,6},{5,7},{6,4},{7,5},{8,10},{9,11},{10,... | collective-permute-start | bytes 393224 | tf_op jit(solution)/shard_map/ppermute | solution.py:43
  57.6 9.1 %collective-permute-start.10 = (bf16[128,4096]{1,0:T(8,128)(2,1)S(1)}, bf16[128,4096]{1,0:T(8,128)(2,1)S(1)}, u32[]{:S(2)}, u32[]{:S(2)}) collective-permute-start(bf16[128,4096]{1,0:T(8,128)(2,1)S(1)} %shard_map.98.refs_1_.refs_6_), channel_id=1, source_target_pairs={{0,1},{1,0},{2,3},{3,2},{4,5},{5,4},{6,7},{7,6},{8,9},{9,8},{10,11... | collective-permute-start | bytes 3145736 | tf_op jit(solution)/shard_map/ppermute | solution.py:43
  66.4 7.9 %collective-permute-start.12 = (bf16[128,4096]{1,0:T(8,128)(2,1)S(1)}, bf16[128,4096]{1,0:T(8,128)(2,1)S(1)}, u32[]{:S(2)}, u32[]{:S(2)}) collective-permute-start(bf16[128,4096]{1,0:T(8,128)(2,1)S(1)} %get-tuple-element.60.refs_6_), channel_id=1, source_target_pairs={{0,1},{1,0},{2,3},{3,2},{4,5},{5,4},{6,7},{7,6},{8,9},{9,8},{10,11... | collective-permute-start | bytes 3145736 | tf_op jit(solution)/shard_map/ppermute | solution.py:43
  78.4 10.8 %collective-permute-start.15 = (bf16[128,4096]{1,0:T(8,128)(2,1)S(1)}, bf16[128,4096]{1,0:T(8,128)(2,1)S(1)}, u32[]{:S(2)}, u32[]{:S(2)}) collective-permute-start(bf16[128,4096]{1,0:T(8,128)(2,1)S(1)} %get-tuple-element.71.refs_9_), channel_id=1, source_target_pairs={{0,1},{1,0},{2,3},{3,2},{4,5},{5,4},{6,7},{7,6},{8,9},{9,8},{10,11... | collective-permute-start | bytes 3145736 | tf_op jit(solution)/shard_map/ppermute | solution.py:43
  78.9 6.7 %collective-permute-start.13 = (bf16[32,4096]{1,0:T(8,128)(2,1)S(1)}, bf16[32,4096]{1,0:T(8,128)(2,1)S(1)}, u32[]{:S(2)}, u32[]{:S(2)}) collective-permute-start(bf16[32,4096]{1,0:T(8,128)(2,1)S(1)} %get-tuple-element.70.refs_2_), channel_id=1, source_target_pairs={{0,28},{1,5},{2,30},{3,7},{4,0},{5,9},{6,2},{7,11},{8,4},{9,13},{1... | collective-permute-start | bytes 786440 | tf_op jit(solution)/shard_map/ppermute | solution.py:43
  85.7 8.8 %collective-permute-start.14 = (bf16[32,4096]{1,0:T(8,128)(2,1)S(1)}, bf16[32,4096]{1,0:T(8,128)(2,1)S(1)}, u32[]{:S(2)}, u32[]{:S(2)}) collective-permute-start(bf16[32,4096]{1,0:T(8,128)(2,1)S(1)} %shard_map.107.refs_2_), channel_id=1, source_target_pairs={{0,28},{1,5},{2,30},{3,7},{4,0},{5,9},{6,2},{7,11},{8,4},{9,13},{1... | collective-permute-start | bytes 786440 | tf_op jit(solution)/shard_map/ppermute | solution.py:43
  88.0 15.0 %collective-permute-start.23 = (bf16[35,64,128]{2,1,0:T(8,128)(2,1)S(1)}, bf16[35,64,128]{2,1,0:T(8,128)(2,1)S(1)}, u32[]{:S(2)}, u32[]{:S(2)}) collective-permute-start(bf16[35,64,128]{2,1,0:T(8,128)(2,1)S(1)} %get-tuple-element.84), channel_id=1, source_target_pairs={{0,128},{32,160},{64,192},{96,224},{128,0},{160,32},{192,64},{224,... | collective-permute-start | bytes 1720328 | tf_op jit(solution)/shard_map/ppermute | solution.py:47
  89.4 10.4 %collective-permute-start.18 = (bf16[32,4096]{1,0:T(8,128)(2,1)S(1)}, bf16[32,4096]{1,0:T(8,128)(2,1)S(1)}, u32[]{:S(2)}, u32[]{:S(2)}) collective-permute-start(bf16[32,4096]{1,0:T(8,128)(2,1)S(1)} %get-tuple-element.74.refs_9_), channel_id=1, source_target_pairs={{0,28},{1,5},{2,30},{3,7},{4,0},{5,9},{6,2},{7,11},{8,4},{9,13},{1... | collective-permute-start | bytes 786440 | tf_op jit(solution)/shard_map/ppermute | solution.py:43
  91.4 26.6 %collective-permute-start.22 = (bf16[35,64,128]{2,1,0:T(8,128)(2,1)S(1)}, bf16[35,64,128]{2,1,0:T(8,128)(2,1)S(1)}, u32[]{:S(2)}, u32[]{:S(2)}) collective-permute-start(bf16[35,64,128]{2,1,0:T(8,128)(2,1)S(1)} %get-tuple-element.67.refs_2_), channel_id=1, source_target_pairs={{0,192},{32,224},{64,128},{96,160},{128,64},{160,96},{192,0},{224,... | collective-permute-start | bytes 1720328 | tf_op jit(solution)/shard_map/ppermute | solution.py:47
  94.5 39.9 %collective-permute-start.25 = (bf16[35,64,128]{2,1,0:T(8,128)(2,1)S(1)}, bf16[35,64,128]{2,1,0:T(8,128)(2,1)S(1)}, u32[]{:S(2)}, u32[]{:S(2)}) collective-permute-start(bf16[35,64,128]{2,1,0:T(8,128)(2,1)S(1)} %get-tuple-element.85), channel_id=1, source_target_pairs={{0,64},{32,96},{64,0},{96,32},{128,192},{160,224},{192,128},{224,1... | collective-permute-start | bytes 1720328 | tf_op jit(solution)/shard_map/ppermute | solution.py:47
  94.5 39.9 %collective-permute-start.24 = (bf16[35,64,128]{2,1,0:T(8,128)(2,1)S(1)}, bf16[35,64,128]{2,1,0:T(8,128)(2,1)S(1)}, u32[]{:S(2)}, u32[]{:S(2)}) collective-permute-start(bf16[35,64,128]{2,1,0:T(8,128)(2,1)S(1)} %get-tuple-element.72.refs_2_), channel_id=1, source_target_pairs={{0,160},{32,192},{64,224},{96,128},{128,32},{160,64},{192,96},{224... | collective-permute-start | bytes 1720328 | tf_op jit(solution)/shard_map/ppermute | solution.py:47
  99.9 7.0 %collective-permute-start.19 = (bf16[32,4096]{1,0:T(8,128)(2,1)S(1)}, bf16[32,4096]{1,0:T(8,128)(2,1)S(1)}, u32[]{:S(2)}, u32[]{:S(2)}) collective-permute-start(bf16[32,4096]{1,0:T(8,128)(2,1)S(1)} %shard_map.111.refs_9_), channel_id=1, source_target_pairs={{0,28},{1,5},{2,30},{3,7},{4,0},{5,9},{6,2},{7,11},{8,4},{9,13},{1... | collective-permute-start | bytes 786440 | tf_op jit(solution)/shard_map/ppermute | solution.py:43
  103.0 16.2 %collective-permute-start.17 = (bf16[16,4096]{1,0:T(8,128)(2,1)S(1)}, bf16[16,4096]{1,0:T(8,128)(2,1)S(1)}, u32[]{:S(2)}, u32[]{:S(2)}) collective-permute-start(bf16[16,4096]{1,0:T(8,128)(2,1)S(1)} %get-tuple-element.76), channel_id=1, source_target_pairs={{0,16},{1,17},{2,18},{3,19},{4,20},{5,21},{6,22},{7,23},{8,24},{9,... | collective-permute-start | bytes 393224 | tf_op jit(solution)/shard_map/ppermute | solution.py:43
  106.9 29.6 %collective-permute-start.21 = (bf16[16,4096]{1,0:T(8,128)(2,1)S(1)}, bf16[16,4096]{1,0:T(8,128)(2,1)S(1)}, u32[]{:S(2)}, u32[]{:S(2)}) collective-permute-start(bf16[16,4096]{1,0:T(8,128)(2,1)S(1)} %get-tuple-element.81), channel_id=1, source_target_pairs={{0,16},{1,17},{2,18},{3,19},{4,20},{5,21},{6,22},{7,23},{8,24},{9,... | collective-permute-start | bytes 393224 | tf_op jit(solution)/shard_map/ppermute | solution.py:43
  118.0 19.6 %collective-permute-start.16 = (bf16[32,4096]{1,0:T(8,128)(2,1)S(1)}, bf16[32,4096]{1,0:T(8,128)(2,1)S(1)}, u32[]{:S(2)}, u32[]{:S(2)}) collective-permute-start(bf16[32,4096]{1,0:T(8,128)(2,1)S(1)} %shard_map.110.refs_2_), channel_id=1, source_target_pairs={{0,28},{1,5},{2,30},{3,7},{4,0},{5,9},{6,2},{7,11},{8,4},{9,13},{1... | collective-permute-start | bytes 786440 | tf_op jit(solution)/shard_map/ppermute | solution.py:43
  119.1 18.5 %collective-permute-start.20 = (bf16[32,4096]{1,0:T(8,128)(2,1)S(1)}, bf16[32,4096]{1,0:T(8,128)(2,1)S(1)}, u32[]{:S(2)}, u32[]{:S(2)}) collective-permute-start(bf16[32,4096]{1,0:T(8,128)(2,1)S(1)} %shard_map.113.refs_5_), channel_id=1, source_target_pairs={{0,28},{1,5},{2,30},{3,7},{4,0},{5,9},{6,2},{7,11},{8,4},{9,13},{1... | collective-permute-start | bytes 786440 | tf_op jit(solution)/shard_map/ppermute | solution.py:43
  134.4 15.9 %collective-permute-start.28 = (bf16[35,64,128]{2,1,0:T(8,128)(2,1)S(1)}, bf16[35,64,128]{2,1,0:T(8,128)(2,1)S(1)}, u32[]{:S(2)}, u32[]{:S(2)}) collective-permute-start(bf16[35,64,128]{2,1,0:T(8,128)(2,1)S(1)} %get-tuple-element.75.refs_2_), channel_id=1, source_target_pairs={{0,224},{32,128},{64,160},{96,192},{128,96},{160,0},{192,32},{224,... | collective-permute-start | bytes 1720328 | tf_op jit(solution)/shard_map/ppermute | solution.py:47
  134.4 15.9 %collective-permute-start.29 = (bf16[35,64,128]{2,1,0:T(8,128)(2,1)S(1)}, bf16[35,64,128]{2,1,0:T(8,128)(2,1)S(1)}, u32[]{:S(2)}, u32[]{:S(2)}) collective-permute-start(bf16[35,64,128]{2,1,0:T(8,128)(2,1)S(1)} %get-tuple-element.90), channel_id=1, source_target_pairs={{0,32},{32,64},{64,96},{96,0},{128,160},{160,192},{192,224},{224,1... | collective-permute-start | bytes 1720328 | tf_op jit(solution)/shard_map/ppermute | solution.py:47
  136.5 26.0 %collective-permute-start.30 = (bf16[35,64,128]{2,1,0:T(8,128)(2,1)S(1)}, bf16[35,64,128]{2,1,0:T(8,128)(2,1)S(1)}, u32[]{:S(2)}, u32[]{:S(2)}) collective-permute-start(bf16[35,64,128]{2,1,0:T(8,128)(2,1)S(1)} %get-tuple-element.80.refs_2_), channel_id=1, source_target_pairs={{0,96},{32,0},{64,32},{96,64},{128,224},{160,128},{192,160},{224,1... | collective-permute-start | bytes 1720328 | tf_op jit(solution)/shard_map/ppermute | solution.py:47
  137.8 1.7 collective-permute-start.26
  139.5 28.2 %collective-permute-start.27 = (bf16[16,4096]{1,0:T(8,128)(2,1)S(1)}, bf16[16,4096]{1,0:T(8,128)(2,1)S(1)}, u32[]{:S(2)}, u32[]{:S(2)}) collective-permute-start(bf16[16,4096]{1,0:T(8,128)(2,1)S(1)} %get-tuple-element.89), channel_id=1, source_target_pairs={{0,2},{1,3},{2,0},{3,1},{4,6},{5,7},{6,4},{7,5},{8,10},{9,11},{10,... | collective-permute-start | bytes 393224 | tf_op jit(solution)/shard_map/ppermute | solution.py:43

commit v3 on v2

--- a/solution.py
+++ b/solution.py
@@ -47,7 +47,10 @@
     return lax.ppermute(x, "dp", dp_perm(dx, dy))
 
 
-def call(kernel, n_scalar, out_shape, args, flops, scratch=(), after=(), limit=12, out_space=VMEM):
+def call(
+    kernel, n_scalar, out_shape, args, flops, scratch=(), after=(), limit=12, out_space=VMEM,
+    space=VMEM,
+):
     n_args, n_after = len(args), len(after)
 
     def run(*refs):
@@ -60,7 +63,7 @@
         run,
         out_shape=out_shape,
         in_specs=[SMEM] * n_scalar
-        + [VMEM] * (n_args - n_scalar)
+        + [space] * (n_args - n_scalar)
         + [pl.BlockSpec(memory_space=pl.ANY)] * n_after,
         out_specs=out_specs,
         scratch_shapes=list(scratch),
@@ -69,8 +72,8 @@
     )(*args, *after)
 
 
-def tick_kernel(o_ref):
-    o_ref[...] = jnp.zeros_like(o_ref)
+def tick_kernel(*refs):
+    refs[-1][...] = jnp.zeros_like(refs[-1])
 
 
 def join_kernel(*refs):
@@ -87,21 +90,37 @@
     return call(join_kernel, 0, shape, parts, 0)
 
 
-def mask_kernel(t_ref, w_ref, m_ref, o_ref, e_ref):
+def head_kernel(x_ref, o_ref):
+    o_ref[...] = x_ref[0 : o_ref.shape[0], :]
+
+
+def mask_kernel(t_ref, w_hbm, m_hbm, o_ref, m_ref, e_ref, sems):
     n_rows, blocks = m_ref.shape
-    width = w_ref.shape[1]
+    width = o_ref.shape[1]
+    groups = n_rows // 8
+
+    def part(g):
+        rows = pl.ds(pl.multiple_of(g * 512, 512), 512)
+        return pltpu.make_async_copy(w_hbm.at[rows], o_ref.at[rows], sems.at[g])
+
+    mask_copy = pltpu.make_async_copy(m_hbm, m_ref, sems.at[groups])
+    mask_copy.start()
+    for g in range(groups):
+        part(g).start()
     rows = lax.broadcasted_iota(jnp.int32, (blocks, width), 0)
     cols = lax.broadcasted_iota(jnp.int32, (blocks, width), 1)
     pick = (rows == t_ref[0] + lax.div(cols, BLOCK)).astype(BF16)
+    mask_copy.wait()
     e_ref[...] = jnp.dot(m_ref[...].astype(F32).astype(BF16), pick, preferred_element_type=F32)
 
-    @pl.loop(0, n_rows // 8)
+    @pl.loop(0, groups)
     def _(g):
+        part(g).wait()
         eight = e_ref[pl.ds(pl.multiple_of(g * 8, 8), 8), :]
         for i in range(8):
             at = pl.ds(pl.multiple_of(g * 512 + i * BLOCK, BLOCK), BLOCK)
             row = jnp.broadcast_to(eight[i : i + 1, :], (BLOCK, width)).astype(BF16)
-            o_ref[at, :] = w_ref[at, :] * row
+            o_ref[at, :] = o_ref[at, :] * row
 
 
 def forward_kernel(first, count, idx_ref, xa, xb, w_ref, g_ref, *rest):
@@ -207,21 +226,30 @@
         out[:, cols] = (near[:, cols].astype(F32) + received[:, cols].astype(F32)).astype(BF16)
 
 
+def hop_far_kernel(near, received, out):
+    @pl.loop(0, near.shape[1] // 512)
+    def _(s):
+        cols = pl.ds(pl.multiple_of(s * 512, 512), 512)
+        total = near[0:16, cols].astype(F32) + received[:, cols].astype(F32)
+        out[0:16, cols] = total.astype(BF16)
+        out[16:32, cols] = near[16:32, cols]
+
+
 def hop(near, received, after):
     shape = jax.ShapeDtypeStruct(near.shape, BF16)
-    return call(hop_kernel, 0, shape, (near, received), near.size, after=after)
+    kernel = hop_kernel if near.shape == received.shape else hop_far_kernel
+    return call(kernel, 0, shape, (near, received), near.size, after=after)
 
 
 def sum_kernel(*refs):
-    halves, to_core, kept = (refs[0:3], refs[3:6]), refs[6], refs[7]
+    halves, to_core, kept = (refs[0:2], refs[2:4]), refs[4], refs[5]
 
     @pl.loop(0, kept.shape[1] // 512)
     def _(s):
         cols = pl.ds(pl.multiple_of(s * 512, 512), 512)
-        for q, (near, far, home) in enumerate(halves):
+        for q, (near, home) in enumerate(halves):
             rows = slice(q * 16, q * 16 + 16)
-            total = home[:, cols].astype(F32) + far[:, cols].astype(F32)
-            kept[rows, cols] = total + near[0:16, cols].astype(F32)
+            kept[rows, cols] = home[:, cols].astype(F32) + near[0:16, cols].astype(F32)
             to_core[rows, cols] = near[16:32, cols]
 
 
@@ -316,15 +344,15 @@
         total = parts[0][s]
         for part in parts[1:]:
             total = total + part[s].astype(F32)
-        row, lane, h = place_of(code_ref[own, s])
-        at = buf.at[pl.ds(row, BLOCK), pl.ds(lane, 128)]
-        at[...] = jnp.where(half == h, pltpu.roll(total, (h & 1) * BLOCK, 1), at[...])
-        row, lane, h = place_of(code_ref[own, PAIRS + s])
-        at = buf.at[pl.ds(row, BLOCK), pl.ds(lane, 128)]
-        at[...] = jnp.where(half == h, pltpu.roll(total, (1 - (h & 1)) * BLOCK, 1), at[...])
+        other = pltpu.roll(total, BLOCK, 1)
+        for side in range(2):
+            row, lane, h = place_of(code_ref[own, side * PAIRS + s])
+            value = jnp.where(h == side, total, other)
+            at = buf.at[pl.ds(row, BLOCK), pl.ds(lane, 128)]
+            pltpu.store(at, value, mask=half == h)
         return carry
 
-    lax.fori_loop(0, PAIRS, place, 0)
+    lax.fori_loop(0, PAIRS, place, 0, unroll=5)
     copies = []
     for c in range(4):
         rows = slice(c * 128, (c + 1) * 128)
@@ -334,23 +362,26 @@
         copy.wait()
 
 
-def kept_codes(block_mask, t):
+def slots_of(block_mask, t):
     mask = lax.dynamic_slice(block_mask, (0, t * 14), (64, 14)).reshape(8, 112)
     kept = mask != 0
     at = jnp.arange(112, dtype=jnp.int32)
-    i = jnp.array([b // 14 for b in range(112)], jnp.int32)
-    j = at - i * 14
-    h = j & 1
+    h = jnp.array([b % 14 % 2 for b in range(112)], jnp.int32)
     before = (at[:, None] <= at[None, :]) & (h[:, None] == h[None, :])
     rank = jnp.dot(kept.astype(BF16), before.astype(BF16), preferred_element_type=F32)
     rank = rank.astype(jnp.int32) - 1
     extra = rank >= PAIRS
     slot = jnp.where(extra, 3 * PAIRS - 1 - PAIRS * h - rank, rank + PAIRS * h)
-    hit = kept[:, None, :] & (slot[:, None, :] == jnp.arange(CAP, dtype=jnp.int32)[None, :, None])
-    code = i * BLOCK + (j >> 1) * (128 << 10) + ((h - 2) << 20)
-    code = jnp.sum(jnp.where(hit, code[None, None, :], 0), axis=2, dtype=jnp.int32) + (2 << 20)
     odd = jnp.sum((kept & extra).astype(jnp.int32), axis=1, dtype=jnp.int32)
-    return code, odd
+    return jnp.where(kept, slot, -1), odd
+
+
+def codes_of(slot):
+    i = jnp.array([b // 14 for b in range(112)], jnp.int32)
+    j = jnp.array([b % 14 for b in range(112)], jnp.int32)
+    hit = slot[:, None, :] == jnp.arange(CAP, dtype=jnp.int32)[None, :, None]
+    code = i * BLOCK + (j >> 1) * (128 << 10) + (((j & 1) - 2) << 20)
+    return jnp.sum(jnp.where(hit, code[None, None, :], 0), axis=2, dtype=jnp.int32) + (2 << 20)
 
 
 def layer(tokens, weight, block_mask, act_grad):
@@ -364,10 +395,6 @@
     t, g, chip = lax.optimization_barrier((t, g, chip))
     z, xh, core = t >> 2, (t >> 1) & 1, t & 1
     xl, y = g >> 2, g & 3
-    near = [move(chip, dz=1)]
-    near.append(move(near[0], dz=1))
-    near.append(move(near[1], dz=1))
-    far = move(tokens, dz=4)
 
     n = jnp.arange(32, dtype=jnp.int32)
     slot = n & 7
@@ -376,32 +403,48 @@
     gather_core = core ^ ((n >> 3) & 1)
     zk = (z - (1 - 2 * gather_core) * dist) & (NZ - 1)
     idx = zk * 4 + (xh ^ (n >> 4)) * 2 + (gather_core ^ flip)
-    order = [(1, 2), (1, 0), (1, 1), (0, 2), (1, 3), (0, 1), (0, 3), (0, 0)]
+    order = [(1, 0), (0, 2), (1, 1), (1, 3), (1, 2), (0, 1), (0, 3), (0, 0)]
     dx = jnp.array([o[0] for o in order], jnp.int32)
     dy = jnp.array([o[1] for o in order], jnp.int32)
     dests = (xl ^ dx) * NY + ((y + dy) & (NY - 1))
 
-    ticks = [call(tick_kernel, 0, jax.ShapeDtypeStruct((8, 128), F32), (), 0) for _ in range(2)]
-    t_list, ticks[0] = lax.optimization_barrier((t, ticks[0]))
-    t_mask, ticks[1] = lax.optimization_barrier((t, ticks[1]))
+    def tick():
+        return call(tick_kernel, 0, jax.ShapeDtypeStruct((8, 128), F32), (), 0)
+
+    ticks = [tick() for _ in range(4)]
+    near1 = move(chip, dz=1)
+    t_slot, ticks[0] = lax.optimization_barrier((t, ticks[0]))
+    slot, odd = slots_of(block_mask, t_slot)
+    slot, odd, idx, dests, near1 = lax.optimization_barrier((slot, odd, idx, dests, near1))
+    near2 = move(near1, dz=1)
+    slot, ticks[1] = lax.optimization_barrier((slot, ticks[1]))
+    code, near2 = lax.optimization_barrier((codes_of(slot), near2))
+    scalars = (dests, code, odd)
+
+    near3 = move(near2, dz=1)
+    t_mask, ticks[2] = lax.optimization_barrier((t, ticks[2]))
     masked = call(
         mask_kernel,
         1,
         jax.ShapeDtypeStruct((d, width), BF16),
         ((t_mask * 14).reshape(1), weight, block_mask),
         d * width,
-        scratch=(pltpu.VMEM((64, width), F32),),
-    )
-    code, odd = kept_codes(block_mask, t_list)
-    code, odd, idx, dests, near[1] = lax.optimization_barrier((code, odd, idx, dests, near[1]))
-    near[2], masked = lax.optimization_barrier((near[2], masked))
-    scalars = (dests, code, odd)
-
-    near_x = [move(near[k], dx=1) for k in range(3)]
-    far_x = move(far, dx=1)
-    x0 = join(tokens, far, *near)
+        scratch=(
+            pltpu.VMEM(block_mask.shape, jnp.int32),
+            pltpu.VMEM((block_mask.shape[0], width), F32),
+            pltpu.SemaphoreType.DMA((9,)),
+        ),
+        space=pl.BlockSpec(memory_space=pl.ANY),
+        limit=44,
+    )
+    near3, masked = lax.optimization_barrier((near3, masked))
+
+    head = call(head_kernel, 0, jax.ShapeDtypeStruct((16, d), BF16), (near3,), 0)
+    far = move(head, dz=1)
+    cross = [move(v, dx=1) for v in (near1, near2, near3, far)]
+    x0 = join(tokens, far, near1, near2, near3)
     x2 = move(x0, dc=1)
-    x1 = join(home, far_x, *near_x)
+    x1 = join(home, cross[3], *cross[:3])
     x3 = move(x1, dc=1)
     xs = (x0, x1, x2, x3)
 
@@ -413,31 +456,36 @@
 
     parts = []
 
-    def pack_two(first, after):
-        packed = wgrad(first, 2, scalars, pa, pb, xs, after)
-        for v, o in zip(packed, order[first : first + 2]):
+    def pack(first, count, after):
+        packed = wgrad(first, count, scalars, pa, pb, xs, (after,))
+        for v, o in zip(packed, order[first : first + count]):
             parts.append(v if o == (0, 0) else move_dp(v, *o))
         return packed[0]
 
-    def back(x, hops=1):
-        return move(x, dz=NZ - hops)
-
-    done = pack_two(0, ())
-    a1, a2, a3, far_a, home_a = mix(own_a, received_a, (done,))
-    ring_a, far_a = back(a3), back(far_a, 4)
-    own_b, other_b = xgrad(pb, masked, (a3,))
+    def back(x):
+        return move(x, dz=NZ - 1)
+
+    done = pack(0, 1, other_a)
+    done = pack(1, 2, done)
+    a1, a2, a3, a4, home_a = mix(own_a, received_a, (done,))
+    ring_a = back(a4)
+    own_b, other_b = xgrad(pb, masked, (a4,))
     received_b = move(other_b, dc=1)
-    done = pack_two(2, (other_b,))
-    done = hop(a2, ring_a, (done,))
+    done = hop(a3, ring_a, (other_b,))
     ring_a = back(done)
-    b1, b2, b3, far_b, home_b = mix(own_b, received_b, (done,))
-    ring_b, far_b = back(b3), back(far_b, 4)
-    done = pack_two(4, (b3,))
+    done = pack(3, 2, done)
+    b1, b2, b3, b4, home_b = mix(own_b, received_b, (done,))
+    ring_b = back(b4)
+    done = hop(a2, ring_a, (b4,))
+    ring_a = back(done)
+    done = pack(5, 2, done)
+    done = hop(b3, ring_b, (done,))
+    ring_b = back(done)
     done = hop(a1, ring_a, (done,))
     ring_a = back(done)
+    done = pack(7, 1, done)
     done = hop(b2, ring_b, (done,))
     ring_b = back(done)
-    done = pack_two(6, (done,))
     done = hop(b1, ring_b, (done,))
     ring_b = back(done)
 
@@ -453,8 +501,8 @@
         sum_kernel,
         0,
         (jax.ShapeDtypeStruct((32, d), BF16), jax.ShapeDtypeStruct((32, d), F32)),
-        (ring_a, far_a, home_a, ring_b, far_b, home_b),
-        6 * 32 * d,
+        (ring_a, home_a, ring_b, home_b),
+        4 * 32 * d,
         after=(early,),
     )
     to_x, kept = call(

time: 169 us -> 168 us (level)
  the two profiles are of different devices: /device:TPU:69 before, /device:TPU:8 now
where the time goes in v3:
time: 168 us; the launch traced here: 166 us
  waiting for transfers between devices  76.2 us (45%)
  starting transfers between devices  44.9 us (27%)
  Pallas kernels  36.3 us (22%)
  other arithmetic  4.21 us (3%)
  local copies, waits for them, and re-layouts  1.98 us (1%)
    ppermute x24, waiting for transfers between devices, move(): return lax.ppermute(x, 'tensor', tensor_perm(dz, dx, dc, split=True))  54.1 us
    pallas_call x30, Pallas kernels, call(): pl.pallas_call(run, out_shape=out_shape, in_specs=[SMEM] * n_scalar + [sp...  36.3 us
    ppermute x24, starting transfers between devices, move(): return lax.ppermute(x, 'tensor', tensor_perm(dz, dx, dc, split=True))  26.4 us
    ppermute x7, waiting for transfers between devices, move_dp(): return lax.ppermute(x, 'dp', dp_perm(dx, dy))  22.2 us
    ppermute x7, starting transfers between devices, move_dp(): return lax.ppermute(x, 'dp', dp_perm(dx, dy))  18.5 us
  transfers between devices with their start and end apart: 31, of which 18 were waited for; matrix products, arithmetic and copies ran while one was open for 3% of the time, Pallas kernels for 19%

profile of v3, /device:TPU:8, one launch (start us, length us, event | category | flops | bytes accessed | tf_op | source)
XLA Modules:
  0.0 165.7 jit_solution(2911547745322493255)
XLA Ops:
  0.8 1.5 collective-permute-done.refs_1_
  2.3 0.9 copy-done.1
  3.2 2.0 %collective-permute-start.1 = (bf16[32,4096]{1,0:T(8,128)(2,1)S(1)}, bf16[32,4096]{1,0:T(8,128)(2,1)S(1)}, u32[]{:S(2)}, u32[]{:S(2)}) collective-permute-start(bf16[32,4096]{1,0:T(8,128)(2,1)S(1)} %shard_map.112), channel_id=1, source_target_pairs={{0,4},{1,29},{2,6},{3,31},{4,8},{5,1},{6,10},{7,3},{8,12},{9,5},{1... | collective-permute-start | bytes 786440 | tf_op jit(solution)/shard_map/ppermute | solution.py:43
  5.2 0.9 dynamic-slice_compare_fusion
  6.9 1.0 convert_reduce_fusion
  8.0 5.5 %collective-permute-done.1.refs_2_ = bf16[32,4096]{1,0:T(8,128)(2,1)S(1)} collective-permute-done((bf16[32,4096]{1,0:T(8,128)(2,1)S(1)}, bf16[32,4096]{1,0:T(8,128)(2,1)S(1)}, u32[]{:S(2)}, u32[]{:S(2)}) %collective-permute-start.1) | collective-permute-done | bytes 262176 | tf_op jit(solution)/shard_map/ppermute | solution.py:43
  13.5 1.9 %select_reduce_fusion = s32[8,70]{0,1:T(8,128)S(1)} fusion(s32[112]{0:T(128)} %constant.79, s32[8,112]{1,0:T(8,128)S(1)} %get-tuple-element.55), kind=kLoop, calls=%fused_computation.2 | loop fusion | flops 187600 | bytes 6272 | tf_op jit(solution)/shard_map/reduce_sum | solution.py:384
  15.5 5.6 %collective-permute-done.3.refs_3_ = bf16[32,4096]{1,0:T(8,128)(2,1)S(1)} collective-permute-done((bf16[32,4096]{1,0:T(8,128)(2,1)S(1)}, bf16[32,4096]{1,0:T(8,128)(2,1)S(1)}, u32[]{:S(2)}, u32[]{:S(2)}) %collective-permute-start.3) | collective-permute-done | bytes 262176 | tf_op jit(solution)/shard_map/ppermute | solution.py:43
  21.1 0.9 copy-done.3
  22.0 3.4 %shard_map.116.refs_3_.refs_1_ = bf16[4096,896]{1,0:T(8,128)(2,1)S(1)} custom-call(s32[1]{0:T(128)} %bitcast.refs_0_, bf16[4096,896]{1,0:T(8,128)(2,1)} %refs_1_.1, s32[64,448]{1,0:T(8,128)S(1)} %copy-done.3), custom_call_target="tpu_custom_call" | custom-call | flops 3670016 | bytes 7454724 | tf_op jit(solution)/shard_map/pallas_call | solution.py:62
  25.4 3.3 %collective-permute-done.4.refs_0_.refs_4_ = bf16[32,4096]{1,0:T(8,128)(2,1)S(1)} collective-permute-done((bf16[32,4096]{1,0:T(8,128)(2,1)S(1)}, bf16[32,4096]{1,0:T(8,128)(2,1)S(1)}, u32[]{:S(2)}, u32[]{:S(2)}) %collective-permute-start.4) | collective-permute-done | bytes 262176 | tf_op jit(solution)/shard_map/ppermute | solution.py:43
  28.8 6.2 %collective-permute-done.5.refs_1_ = bf16[16,4096]{1,0:T(8,128)(2,1)S(1)} collective-permute-done((bf16[16,4096]{1,0:T(8,128)(2,1)S(1)}, bf16[16,4096]{1,0:T(8,128)(2,1)S(1)}, u32[]{:S(2)}, u32[]{:S(2)}) %collective-permute-start.5) | collective-permute-done | bytes 131104 | tf_op jit(solution)/shard_map/ppermute | solution.py:43
  35.1 3.1 %collective-permute-start.2 = (bf16[16,4096]{1,0:T(8,128)(2,1)S(1)}, bf16[16,4096]{1,0:T(8,128)(2,1)S(1)}, u32[]{:S(2)}, u32[]{:S(2)}) collective-permute-start(bf16[16,4096]{1,0:T(8,128)(2,1)S(1)} %copy-done.2), channel_id=1, source_target_pairs={{0,2},{1,3},{2,0},{3,1},{4,6},{5,7},{6,4},{7,5},{8,10},{9,11},{10,... | collective-permute-start | bytes 393224 | tf_op jit(solution)/shard_map/ppermute | solution.py:43
  38.7 3.0 %collective-permute-start.8 = (bf16[32,4096]{1,0:T(8,128)(2,1)S(1)}, bf16[32,4096]{1,0:T(8,128)(2,1)S(1)}, u32[]{:S(2)}, u32[]{:S(2)}) collective-permute-start(bf16[32,4096]{1,0:T(8,128)(2,1)S(1)} %collective-permute-done.3.refs_3_), channel_id=1, source_target_pairs={{0,2},{1,3},{2,0},{3,1},{4,6},{5,7},{6,4},{7,5},{8,10},{9,11},{10,... | collective-permute-start | bytes 786440 | tf_op jit(solution)/shard_map/ppermute | solution.py:43
  42.6 3.5 %collective-permute-start.6 = (bf16[16,4096]{1,0:T(8,128)(2,1)S(1)}, bf16[16,4096]{1,0:T(8,128)(2,1)S(1)}, u32[]{:S(2)}, u32[]{:S(2)}) collective-permute-start(bf16[16,4096]{1,0:T(8,128)(2,1)S(1)} %collective-permute-done.5.refs_1_), channel_id=1, source_target_pairs={{0,2},{1,3},{2,0},{3,1},{4,6},{5,7},{6,4},{7,5},{8,10},{9,11},{10,... | collective-permute-start | bytes 393224 | tf_op jit(solution)/shard_map/ppermute | solution.py:43
  46.1 2.8 %collective-permute-done.7.refs_2_ = bf16[32,4096]{1,0:T(8,128)(2,1)S(1)} collective-permute-done((bf16[32,4096]{1,0:T(8,128)(2,1)S(1)}, bf16[32,4096]{1,0:T(8,128)(2,1)S(1)}, u32[]{:S(2)}, u32[]{:S(2)}) %collective-permute-start.7) | collective-permute-done | bytes 262176 | tf_op jit(solution)/shard_map/ppermute | solution.py:43
  48.9 5.6 %collective-permute-done.8.refs_3_ = bf16[32,4096]{1,0:T(8,128)(2,1)S(1)} collective-permute-done((bf16[32,4096]{1,0:T(8,128)(2,1)S(1)}, bf16[32,4096]{1,0:T(8,128)(2,1)S(1)}, u32[]{:S(2)}, u32[]{:S(2)}) %collective-permute-start.8) | collective-permute-done | bytes 262176 | tf_op jit(solution)/shard_map/ppermute | solution.py:43
  54.5 7.7 %collective-permute-done.6.refs_1_ = bf16[16,4096]{1,0:T(8,128)(2,1)S(1)} collective-permute-done((bf16[16,4096]{1,0:T(8,128)(2,1)S(1)}, bf16[16,4096]{1,0:T(8,128)(2,1)S(1)}, u32[]{:S(2)}, u32[]{:S(2)}) %collective-permute-start.6) | collective-permute-done | bytes 131104 | tf_op jit(solution)/shard_map/ppermute | solution.py:43
  62.4 3.9 %shard_map.121 = (bf16[16,16,896]{2,1,0:T(8,128)(2,1)S(1)}, bf16[256,896]{1,0:T(8,128)(2,1)S(1)}) custom-call(s32[32]{0:T(128)S(1)} %fusion.8.refs_0_, bf16[128,4096]{1,0:T(8,128)(2,1)S(1)} %shard_map.119.refs_1_.refs_5_, bf16[128,4096]{1,0:T(8,128)(2,1)S(1)} %collective-permute-done.11.refs_2_.refs_7_, bf16[4096,896]{1,0:T(8,128)(2,1)S(1)} %shard_map.116.refs_3_.refs_1_, ...), custom_call_target="tpu_custom_call" | custom-call | flops 1879048192 | bytes 10354816 | tf_op jit(solution)/shard_map/pallas_call | solution.py:62
  66.3 3.8 %shard_map.122 = (f32[128,4096]{1,0:T(8,128)S(1)}, bf16[128,4096]{1,0:T(8,128)(2,1)S(1)}) custom-call(bf16[256,896]{1,0:T(8,128)(2,1)S(1)} %get-tuple-element.65.refs_0_.refs_3_, bf16[4096,896]{1,0:T(8,128)(2,1)S(1)} %shard_map.116.refs_3_.refs_1_), custom_call_target="tpu_custom_call" | custom-call | flops 1879048192 | bytes 7798784 | tf_op jit(solution)/shard_map/pallas_call | solution.py:62
  70.8 4.8 %shard_map.123 = (bf16[32,16,896]{2,1,0:T(8,128)(2,1)}, bf16[256,896]{1,0:T(8,128)(2,1)S(1)}) custom-call(s32[32]{0:T(128)S(1)} %fusion.8.refs_0_, bf16[128,4096]{1,0:T(8,128)(2,1)S(1)} %shard_map.118.refs_1_.refs_6_, bf16[128,4096]{1,0:T(8,128)(2,1)S(1)} %collective-permute-done.10.refs_2_.refs_8_, bf16[4096,896]{1,0:T(8,128)(2,1)S(1)} %shard_map.116.refs_3_.refs_1_, ...), custom_call_target="tpu_custom_call" | custom-call | flops 1879048192 | bytes 10813568 | tf_op jit(solution)/shard_map/pallas_call | solution.py:62
  75.6 1.7 %shard_map.124.refs_9_ = bf16[35,64,128]{2,1,0:T(8,128)(2,1)S(1)} custom-call(s32[8]{0:T(128)S(1)} %and_add_fusion.refs_0_, s32[8,70]{1,0:T(8,128)S(1)} %broadcast_add_fusion.refs_1_, s32[8]{0:T(128)S(1)} %get-tuple-element.71.refs_2_, bf16[256,896]{1,0:T(8,128)(2,1)S(1)} %get-tuple-element.65.refs_0_.refs_3_, ...), custom_call_target="tpu_custom_call" | custom-call | flops 469762048 | bytes 5114112 | tf_op jit(solution)/shard_map/pallas_call | solution.py:62
  77.3 2.8 %shard_map.125 = (bf16[35,64,128]{2,1,0:T(8,128)(2,1)S(1)}, bf16[35,64,128]{2,1,0:T(8,128)(2,1)S(1)}) custom-call(s32[8]{0:T(128)S(1)} %and_add_fusion.refs_0_, s32[8,70]{1,0:T(8,128)S(1)} %broadcast_add_fusion.refs_1_, s32[8]{0:T(128)S(1)} %get-tuple-element.71.refs_2_, bf16[256,896]{1,0:T(8,128)(2,1)S(1)} %get-tuple-element.65.refs_0_.refs_3_, ...), custom_call_target="tpu_custom_call" | custom-call | flops 939524096 | bytes 5114112 | tf_op jit(solution)/shard_map/pallas_call | solution.py:62
  80.4 3.8 %shard_map.127 = (f32[128,4096]{1,0:T(8,128)S(1)}, bf16[128,4096]{1,0:T(8,128)(2,1)S(1)}) custom-call(bf16[256,896]{1,0:T(8,128)(2,1)S(1)} %get-tuple-element.72.refs_4_.refs_0_, bf16[4096,896]{1,0:T(8,128)(2,1)S(1)} %shard_map.116.refs_3_.refs_1_, bf16[16,4096]{1,0:T(8,128)(2,1)S(1)} %get-tuple-element.77.refs_2_), custom_call_target="tpu_custom_call" | custom-call | flops 1879048192 | bytes 7798784 | tf_op jit(solution)/shard_map/pallas_call | solution.py:62
  84.5 5.0 %collective-permute-done.13.refs_1_ = bf16[16,4096]{1,0:T(8,128)(2,1)S(1)} collective-permute-done((bf16[16,4096]{1,0:T(8,128)(2,1)S(1)}, bf16[16,4096]{1,0:T(8,128)(2,1)S(1)}, u32[]{:S(2)}, u32[]{:S(2)}) %collective-permute-start.13) | collective-permute-done | bytes 131104 | tf_op jit(solution)/shard_map/ppermute | solution.py:43
  89.5 1.3 collective-permute-start.14
  90.8 3.0 %shard_map.129 = (bf16[35,64,128]{2,1,0:T(8,128)(2,1)S(1)}, bf16[35,64,128]{2,1,0:T(8,128)(2,1)S(1)}) custom-call(s32[8]{0:T(128)S(1)} %and_add_fusion.refs_0_, s32[8,70]{1,0:T(8,128)S(1)} %broadcast_add_fusion.refs_1_, s32[8]{0:T(128)S(1)} %get-tuple-element.71.refs_2_, bf16[256,896]{1,0:T(8,128)(2,1)S(1)} %get-tuple-element.65.refs_0_.refs_3_, ...), custom_call_target="tpu_custom_call" | custom-call | flops 939524096 | bytes 5114112 | tf_op jit(solution)/shard_map/pallas_call | solution.py:62
  94.0 1.9 %collective-permute-done.14.refs_1_ = bf16[32,4096]{1,0:T(8,128)(2,1)S(1)} collective-permute-done((bf16[32,4096]{1,0:T(8,128)(2,1)S(1)}, bf16[32,4096]{1,0:T(8,128)(2,1)S(1)}, u32[]{:S(2)}, u32[]{:S(2)}) %collective-permute-start.14) | collective-permute-done | bytes 262176 | tf_op jit(solution)/shard_map/ppermute | solution.py:43
  96.1 2.5 %collective-permute-start.16 = (bf16[32,4096]{1,0:T(8,128)(2,1)S(1)}, bf16[32,4096]{1,0:T(8,128)(2,1)S(1)}, u32[]{:S(2)}, u32[]{:S(2)}) collective-permute-start(bf16[32,4096]{1,0:T(8,128)(2,1)S(1)} %shard_map.131.refs_9_), channel_id=1, source_target_pairs={{0,28},{1,5},{2,30},{3,7},{4,0},{5,9},{6,2},{7,11},{8,4},{9,13},{1... | collective-permute-start | bytes 786440 | tf_op jit(solution)/shard_map/ppermute | solution.py:43
  98.7 1.6 collective-permute-start.22
  100.2 2.8 %shard_map.132 = (bf16[35,64,128]{2,1,0:T(8,128)(2,1)S(1)}, bf16[35,64,128]{2,1,0:T(8,128)(2,1)S(1)}) custom-call(s32[8]{0:T(128)S(1)} %and_add_fusion.refs_0_, s32[8,70]{1,0:T(8,128)S(1)} %broadcast_add_fusion.refs_1_, s32[8]{0:T(128)S(1)} %get-tuple-element.71.refs_2_, bf16[256,896]{1,0:T(8,128)(2,1)S(1)} %get-tuple-element.65.refs_0_.refs_3_, ...), custom_call_target="tpu_custom_call" | custom-call | flops 939524096 | bytes 5114112 | tf_op jit(solution)/shard_map/pallas_call | solution.py:62
  104.0 3.7 %collective-permute-start.19 = (bf16[32,4096]{1,0:T(8,128)(2,1)S(1)}, bf16[32,4096]{1,0:T(8,128)(2,1)S(1)}, u32[]{:S(2)}, u32[]{:S(2)}) collective-permute-start(bf16[32,4096]{1,0:T(8,128)(2,1)S(1)} %shard_map.133.refs_2_), channel_id=1, source_target_pairs={{0,28},{1,5},{2,30},{3,7},{4,0},{5,9},{6,2},{7,11},{8,4},{9,13},{1... | collective-permute-start | bytes 786440 | tf_op jit(solution)/shard_map/ppermute | solution.py:43
  107.7 2.4 %collective-permute-start.24 = (bf16[35,64,128]{2,1,0:T(8,128)(2,1)S(1)}, bf16[35,64,128]{2,1,0:T(8,128)(2,1)S(1)}, u32[]{:S(2)}, u32[]{:S(2)}) collective-permute-start(bf16[35,64,128]{2,1,0:T(8,128)(2,1)S(1)} %get-tuple-element.88), channel_id=1, source_target_pairs={{0,160},{32,192},{64,224},{96,128},{128,32},{160,64},{192,96},{224... | collective-permute-start | bytes 1720328 | tf_op jit(solution)/shard_map/ppermute | solution.py:47
  110.1 1.0 collective-permute-start.23
  111.1 2.5 %collective-permute-start.25 = (bf16[35,64,128]{2,1,0:T(8,128)(2,1)S(1)}, bf16[35,64,128]{2,1,0:T(8,128)(2,1)S(1)}, u32[]{:S(2)}, u32[]{:S(2)}) collective-permute-start(bf16[35,64,128]{2,1,0:T(8,128)(2,1)S(1)} %get-tuple-element.80.refs_2_), channel_id=1, source_target_pairs={{0,224},{32,128},{64,160},{96,192},{128,96},{160,0},{192,32},{224,... | collective-permute-start | bytes 1720328 | tf_op jit(solution)/shard_map/ppermute | solution.py:47
  113.7 1.7 %shard_map.135.refs_2_.refs_0_ = bf16[35,64,128]{2,1,0:T(8,128)(2,1)S(1)} custom-call(s32[8]{0:T(128)S(1)} %and_add_fusion.refs_0_, s32[8,70]{1,0:T(8,128)S(1)} %broadcast_add_fusion.refs_1_, s32[8]{0:T(128)S(1)} %get-tuple-element.71.refs_2_, bf16[256,896]{1,0:T(8,128)(2,1)S(1)} %get-tuple-element.65.refs_0_.refs_3_, ...), custom_call_target="tpu_custom_call" | custom-call | flops 469762048 | bytes 5114112 | tf_op jit(solution)/shard_map/pallas_call | solution.py:62
  115.8 6.3 %collective-permute-done.20.refs_1_ = bf16[32,4096]{1,0:T(8,128)(2,1)S(1)} collective-permute-done((bf16[32,4096]{1,0:T(8,128)(2,1)S(1)}, bf16[32,4096]{1,0:T(8,128)(2,1)S(1)}, u32[]{:S(2)}, u32[]{:S(2)}) %collective-permute-start.20) | collective-permute-done | bytes 262176 | tf_op jit(solution)/shard_map/ppermute | solution.py:43
  122.0 1.3 collective-permute-start.18
  123.6 3.1 %collective-permute-done.24.refs_3_ = bf16[35,64,128]{2,1,0:T(8,128)(2,1)S(1)} collective-permute-done((bf16[35,64,128]{2,1,0:T(8,128)(2,1)S(1)}, bf16[35,64,128]{2,1,0:T(8,128)(2,1)S(1)}, u32[]{:S(2)}, u32[]{:S(2)}) %collective-permute-start.24) | collective-permute-done | bytes 573472 | tf_op jit(solution)/shard_map/ppermute | solution.py:47
  126.7 3.4 %collective-permute-start.28 = (bf16[35,64,128]{2,1,0:T(8,128)(2,1)S(1)}, bf16[35,64,128]{2,1,0:T(8,128)(2,1)S(1)}, u32[]{:S(2)}, u32[]{:S(2)}) collective-permute-start(bf16[35,64,128]{2,1,0:T(8,128)(2,1)S(1)} %get-tuple-element.93), channel_id=1, source_target_pairs={{0,192},{32,224},{64,128},{96,160},{128,64},{160,96},{192,0},{224,... | collective-permute-start | bytes 1720328 | tf_op jit(solution)/shard_map/ppermute | solution.py:47
  130.1 6.0 %collective-permute-start.30 = (bf16[35,64,128]{2,1,0:T(8,128)(2,1)S(1)}, bf16[35,64,128]{2,1,0:T(8,128)(2,1)S(1)}, u32[]{:S(2)}, u32[]{:S(2)}) collective-permute-start(bf16[35,64,128]{2,1,0:T(8,128)(2,1)S(1)} %get-tuple-element.94), channel_id=1, source_target_pairs={{0,96},{32,0},{64,32},{96,64},{128,224},{160,128},{192,160},{224,1... | collective-permute-start | bytes 1720328 | tf_op jit(solution)/shard_map/ppermute | solution.py:47
  136.2 4.1 %collective-permute-done.25.refs_4_ = bf16[35,64,128]{2,1,0:T(8,128)(2,1)S(1)} collective-permute-done((bf16[35,64,128]{2,1,0:T(8,128)(2,1)S(1)}, bf16[35,64,128]{2,1,0:T(8,128)(2,1)S(1)}, u32[]{:S(2)}, u32[]{:S(2)}) %collective-permute-start.25) | collective-permute-done | bytes 573472 | tf_op jit(solution)/shard_map/ppermute | solution.py:47
  140.3 1.5 collective-permute-start.29
  142.5 1.5 collective-permute-done.26.refs_1_
  144.1 3.1 %collective-permute-start.27 = (bf16[16,4096]{1,0:T(8,128)(2,1)S(1)}, bf16[16,4096]{1,0:T(8,128)(2,1)S(1)}, u32[]{:S(2)}, u32[]{:S(2)}) collective-permute-start(bf16[16,4096]{1,0:T(8,128)(2,1)S(1)} %get-tuple-element.92), channel_id=1, source_target_pairs={{0,2},{1,3},{2,0},{3,1},{4,6},{5,7},{6,4},{7,5},{8,10},{9,11},{10,... | collective-permute-start | bytes 393224 | tf_op jit(solution)/shard_map/ppermute | solution.py:43
  147.2 4.9 %collective-permute-done.28.refs_3_ = bf16[35,64,128]{2,1,0:T(8,128)(2,1)S(1)} collective-permute-done((bf16[35,64,128]{2,1,0:T(8,128)(2,1)S(1)}, bf16[35,64,128]{2,1,0:T(8,128)(2,1)S(1)}, u32[]{:S(2)}, u32[]{:S(2)}) %collective-permute-start.28) | collective-permute-done | bytes 573472 | tf_op jit(solution)/shard_map/ppermute | solution.py:47
  152.1 10.0 %collective-permute-done.30.refs_5_ = bf16[35,64,128]{2,1,0:T(8,128)(2,1)S(1)} collective-permute-done((bf16[35,64,128]{2,1,0:T(8,128)(2,1)S(1)}, bf16[35,64,128]{2,1,0:T(8,128)(2,1)S(1)}, u32[]{:S(2)}, u32[]{:S(2)}) %collective-permute-start.30) | collective-permute-done | bytes 573472 | tf_op jit(solution)/shard_map/ppermute | solution.py:47
  162.1 2.8 %shard_map.141 = f32[512,896]{1,0:T(8,128)} custom-call(s32[1]{0:T(128)} %bitcast.3.refs_0_, s32[8,70]{1,0:T(8,128)S(1)} %broadcast_add_fusion.refs_1_, f32[35,64,128]{2,1,0:T(8,128)S(1)} %shard_map.138.refs_4_.refs_2_, bf16[35,64,128]{2,1,0:T(8,128)(2,1)S(1)} %collective-permute-done.28.refs_3_, bf16[35,64,128]{2,1,0:T(8,128)(2,1)S(1)} %collective-permute-done.29.refs_4_, ...), custom_call_target="tpu_custom_call" | custom-call | flops 2293760 | bytes 2869444 | tf_op jit(solution)/shard_map/pallas_call | solution.py:62
  (61 shorter events, 7.5 us)
Async XLA Ops:
  0.6 1.6 collective-permute-start
  2.3 0.9 copy-start.1
  3.2 10.3 %collective-permute-start.1 = (bf16[32,4096]{1,0:T(8,128)(2,1)S(1)}, bf16[32,4096]{1,0:T(8,128)(2,1)S(1)}, u32[]{:S(2)}, u32[]{:S(2)}) collective-permute-start(bf16[32,4096]{1,0:T(8,128)(2,1)S(1)} %shard_map.112), channel_id=1, source_target_pairs={{0,4},{1,29},{2,6},{3,31},{4,8},{5,1},{6,10},{7,3},{8,12},{9,5},{1... | collective-permute-start | bytes 786440 | tf_op jit(solution)/shard_map/ppermute | solution.py:43
  13.5 7.6 %collective-permute-start.3 = (bf16[32,4096]{1,0:T(8,128)(2,1)S(1)}, bf16[32,4096]{1,0:T(8,128)(2,1)S(1)}, u32[]{:S(2)}, u32[]{:S(2)}) collective-permute-start(bf16[32,4096]{1,0:T(8,128)(2,1)S(1)} %collective-permute-done.1.refs_2_), channel_id=1, source_target_pairs={{0,4},{1,29},{2,6},{3,31},{4,8},{5,1},{6,10},{7,3},{8,12},{9,5},{1... | collective-permute-start | bytes 786440 | tf_op jit(solution)/shard_map/ppermute | solution.py:43
  21.1 7.6 %collective-permute-start.4 = (bf16[32,4096]{1,0:T(8,128)(2,1)S(1)}, bf16[32,4096]{1,0:T(8,128)(2,1)S(1)}, u32[]{:S(2)}, u32[]{:S(2)}) collective-permute-start(bf16[32,4096]{1,0:T(8,128)(2,1)S(1)} %collective-permute-done.3.refs_3_), channel_id=1, source_target_pairs={{0,4},{1,29},{2,6},{3,31},{4,8},{5,1},{6,10},{7,3},{8,12},{9,5},{1... | collective-permute-start | bytes 786440 | tf_op jit(solution)/shard_map/ppermute | solution.py:43
  21.1 0.9 copy-start.3
  22.0 13.0 %copy-start.2 = (bf16[16,4096]{1,0:T(8,128)(2,1)S(1)}, bf16[16,4096]{1,0:T(8,128)(2,1)}, u32[]{:S(2)}) copy-start(bf16[16,4096]{1,0:T(8,128)(2,1)} %refs_0_.3) | copy-start | bytes 393220
  28.7 33.7 %copy-start = (bf16[512,896]{1,0:T(8,128)(2,1)S(1)}, bf16[512,896]{1,0:T(8,128)(2,1)}, u32[]{:S(2)}) copy-start(bf16[512,896]{1,0:T(8,128)(2,1)} %param.12) | copy-start | bytes 2752516
  28.7 6.3 %collective-permute-start.5 = (bf16[16,4096]{1,0:T(8,128)(2,1)S(1)}, bf16[16,4096]{1,0:T(8,128)(2,1)S(1)}, u32[]{:S(2)}, u32[]{:S(2)}) collective-permute-start(bf16[16,4096]{1,0:T(8,128)(2,1)S(1)} %shard_map.117), channel_id=1, source_target_pairs={{0,4},{1,29},{2,6},{3,31},{4,8},{5,1},{6,10},{7,3},{8,12},{9,5},{1... | collective-permute-start | bytes 393224 | tf_op jit(solution)/shard_map/ppermute | solution.py:43
  35.0 27.3 %collective-permute-start.11 = (bf16[128,4096]{1,0:T(8,128)(2,1)S(1)}, bf16[128,4096]{1,0:T(8,128)(2,1)S(1)}, u32[]{:S(2)}, u32[]{:S(2)}) collective-permute-start(bf16[128,4096]{1,0:T(8,128)(2,1)S(1)} %shard_map.119.refs_1_.refs_5_), channel_id=1, source_target_pairs={{0,1},{1,0},{2,3},{3,2},{4,5},{5,4},{6,7},{7,6},{8,9},{9,8},{10,11... | collective-permute-start | bytes 3145736 | tf_op jit(solution)/shard_map/ppermute | solution.py:43
  35.1 7.5 %collective-permute-start.2 = (bf16[16,4096]{1,0:T(8,128)(2,1)S(1)}, bf16[16,4096]{1,0:T(8,128)(2,1)S(1)}, u32[]{:S(2)}, u32[]{:S(2)}) collective-permute-start(bf16[16,4096]{1,0:T(8,128)(2,1)S(1)} %copy-done.2), channel_id=1, source_target_pairs={{0,2},{1,3},{2,0},{3,1},{4,6},{5,7},{6,4},{7,5},{8,10},{9,11},{10,... | collective-permute-start | bytes 393224 | tf_op jit(solution)/shard_map/ppermute | solution.py:43
  38.2 10.7 %collective-permute-start.7 = (bf16[32,4096]{1,0:T(8,128)(2,1)S(1)}, bf16[32,4096]{1,0:T(8,128)(2,1)S(1)}, u32[]{:S(2)}, u32[]{:S(2)}) collective-permute-start(bf16[32,4096]{1,0:T(8,128)(2,1)S(1)} %collective-permute-done.1.refs_2_), channel_id=1, source_target_pairs={{0,2},{1,3},{2,0},{3,1},{4,6},{5,7},{6,4},{7,5},{8,10},{9,11},{10,... | collective-permute-start | bytes 786440 | tf_op jit(solution)/shard_map/ppermute | solution.py:43
  38.7 15.8 %collective-permute-start.8 = (bf16[32,4096]{1,0:T(8,128)(2,1)S(1)}, bf16[32,4096]{1,0:T(8,128)(2,1)S(1)}, u32[]{:S(2)}, u32[]{:S(2)}) collective-permute-start(bf16[32,4096]{1,0:T(8,128)(2,1)S(1)} %collective-permute-done.3.refs_3_), channel_id=1, source_target_pairs={{0,2},{1,3},{2,0},{3,1},{4,6},{5,7},{6,4},{7,5},{8,10},{9,11},{10,... | collective-permute-start | bytes 786440 | tf_op jit(solution)/shard_map/ppermute | solution.py:43
  41.8 20.4 %collective-permute-start.9 = (bf16[32,4096]{1,0:T(8,128)(2,1)S(1)}, bf16[32,4096]{1,0:T(8,128)(2,1)S(1)}, u32[]{:S(2)}, u32[]{:S(2)}) collective-permute-start(bf16[32,4096]{1,0:T(8,128)(2,1)S(1)} %collective-permute-done.4.refs_0_.refs_4_), channel_id=1, source_target_pairs={{0,2},{1,3},{2,0},{3,1},{4,6},{5,7},{6,4},{7,5},{8,10},{9,11},{10,... | collective-permute-start | bytes 786440 | tf_op jit(solution)/shard_map/ppermute | solution.py:43
  42.6 19.6 %collective-permute-start.6 = (bf16[16,4096]{1,0:T(8,128)(2,1)S(1)}, bf16[16,4096]{1,0:T(8,128)(2,1)S(1)}, u32[]{:S(2)}, u32[]{:S(2)}) collective-permute-start(bf16[16,4096]{1,0:T(8,128)(2,1)S(1)} %collective-permute-done.5.refs_1_), channel_id=1, source_target_pairs={{0,2},{1,3},{2,0},{3,1},{4,6},{5,7},{6,4},{7,5},{8,10},{9,11},{10,... | collective-permute-start | bytes 393224 | tf_op jit(solution)/shard_map/ppermute | solution.py:43
  62.3 8.6 %collective-permute-start.10 = (bf16[128,4096]{1,0:T(8,128)(2,1)S(1)}, bf16[128,4096]{1,0:T(8,128)(2,1)S(1)}, u32[]{:S(2)}, u32[]{:S(2)}) collective-permute-start(bf16[128,4096]{1,0:T(8,128)(2,1)S(1)} %shard_map.118.refs_1_.refs_6_), channel_id=1, source_target_pairs={{0,1},{1,0},{2,3},{3,2},{4,5},{5,4},{6,7},{7,6},{8,9},{9,8},{10,11... | collective-permute-start | bytes 3145736 | tf_op jit(solution)/shard_map/ppermute | solution.py:43
  70.1 10.1 %collective-permute-start.12 = (bf16[128,4096]{1,0:T(8,128)(2,1)S(1)}, bf16[128,4096]{1,0:T(8,128)(2,1)S(1)}, u32[]{:S(2)}, u32[]{:S(2)}) collective-permute-start(bf16[128,4096]{1,0:T(8,128)(2,1)S(1)} %get-tuple-element.66.refs_6_.refs_9_), channel_id=1, source_target_pairs={{0,1},{1,0},{2,3},{3,2},{4,5},{5,4},{6,7},{7,6},{8,9},{9,8},{10,11... | collective-permute-start | bytes 3145736 | tf_op jit(solution)/shard_map/ppermute | solution.py:43
  84.2 9.6 %collective-permute-start.15 = (bf16[128,4096]{1,0:T(8,128)(2,1)S(1)}, bf16[128,4096]{1,0:T(8,128)(2,1)S(1)}, u32[]{:S(2)}, u32[]{:S(2)}) collective-permute-start(bf16[128,4096]{1,0:T(8,128)(2,1)S(1)} %get-tuple-element.78.refs_2_), channel_id=1, source_target_pairs={{0,1},{1,0},{2,3},{3,2},{4,5},{5,4},{6,7},{7,6},{8,9},{9,8},{10,11... | collective-permute-start | bytes 3145736 | tf_op jit(solution)/shard_map/ppermute | solution.py:43
  84.5 5.0 %collective-permute-start.13 = (bf16[16,4096]{1,0:T(8,128)(2,1)S(1)}, bf16[16,4096]{1,0:T(8,128)(2,1)S(1)}, u32[]{:S(2)}, u32[]{:S(2)}) collective-permute-start(bf16[16,4096]{1,0:T(8,128)(2,1)S(1)} %get-tuple-element.77.refs_2_), channel_id=1, source_target_pairs={{0,28},{1,5},{2,30},{3,7},{4,0},{5,9},{6,2},{7,11},{8,4},{9,13},{1... | collective-permute-start | bytes 393224 | tf_op jit(solution)/shard_map/ppermute | solution.py:43
  89.5 6.5 %collective-permute-start.14 = (bf16[32,4096]{1,0:T(8,128)(2,1)S(1)}, bf16[32,4096]{1,0:T(8,128)(2,1)S(1)}, u32[]{:S(2)}, u32[]{:S(2)}) collective-permute-start(bf16[32,4096]{1,0:T(8,128)(2,1)S(1)} %shard_map.128.refs_9_), channel_id=1, source_target_pairs={{0,28},{1,5},{2,30},{3,7},{4,0},{5,9},{6,2},{7,11},{8,4},{9,13},{1... | collective-permute-start | bytes 786440 | tf_op jit(solution)/shard_map/ppermute | solution.py:43
  96.1 15.0 %collective-permute-start.16 = (bf16[32,4096]{1,0:T(8,128)(2,1)S(1)}, bf16[32,4096]{1,0:T(8,128)(2,1)S(1)}, u32[]{:S(2)}, u32[]{:S(2)}) collective-permute-start(bf16[32,4096]{1,0:T(8,128)(2,1)S(1)} %shard_map.131.refs_9_), channel_id=1, source_target_pairs={{0,28},{1,5},{2,30},{3,7},{4,0},{5,9},{6,2},{7,11},{8,4},{9,13},{1... | collective-permute-start | bytes 786440 | tf_op jit(solution)/shard_map/ppermute | solution.py:43
  98.6 5.4 %collective-permute-start.17 = (bf16[16,4096]{1,0:T(8,128)(2,1)S(1)}, bf16[16,4096]{1,0:T(8,128)(2,1)S(1)}, u32[]{:S(2)}, u32[]{:S(2)}) collective-permute-start(bf16[16,4096]{1,0:T(8,128)(2,1)S(1)} %get-tuple-element.81.refs_2_), channel_id=1, source_target_pairs={{0,28},{1,5},{2,30},{3,7},{4,0},{5,9},{6,2},{7,11},{8,4},{9,13},{1... | collective-permute-start | bytes 393224 | tf_op jit(solution)/shard_map/ppermute | solution.py:43
  98.7 24.8 %collective-permute-start.22 = (bf16[35,64,128]{2,1,0:T(8,128)(2,1)S(1)}, bf16[35,64,128]{2,1,0:T(8,128)(2,1)S(1)}, u32[]{:S(2)}, u32[]{:S(2)}) collective-permute-start(bf16[35,64,128]{2,1,0:T(8,128)(2,1)S(1)} %shard_map.124.refs_9_), channel_id=1, source_target_pairs={{0,128},{32,160},{64,192},{96,224},{128,0},{160,32},{192,64},{224,... | collective-permute-start | bytes 1720328 | tf_op jit(solution)/shard_map/ppermute | solution.py:47
  104.0 11.5 %collective-permute-start.19 = (bf16[32,4096]{1,0:T(8,128)(2,1)S(1)}, bf16[32,4096]{1,0:T(8,128)(2,1)S(1)}, u32[]{:S(2)}, u32[]{:S(2)}) collective-permute-start(bf16[32,4096]{1,0:T(8,128)(2,1)S(1)} %shard_map.133.refs_2_), channel_id=1, source_target_pairs={{0,28},{1,5},{2,30},{3,7},{4,0},{5,9},{6,2},{7,11},{8,4},{9,13},{1... | collective-permute-start | bytes 786440 | tf_op jit(solution)/shard_map/ppermute | solution.py:43
  107.7 19.0 %collective-permute-start.24 = (bf16[35,64,128]{2,1,0:T(8,128)(2,1)S(1)}, bf16[35,64,128]{2,1,0:T(8,128)(2,1)S(1)}, u32[]{:S(2)}, u32[]{:S(2)}) collective-permute-start(bf16[35,64,128]{2,1,0:T(8,128)(2,1)S(1)} %get-tuple-element.88), channel_id=1, source_target_pairs={{0,160},{32,192},{64,224},{96,128},{128,32},{160,64},{192,96},{224... | collective-permute-start | bytes 1720328 | tf_op jit(solution)/shard_map/ppermute | solution.py:47
  110.1 20.0 %collective-permute-start.23 = (bf16[35,64,128]{2,1,0:T(8,128)(2,1)S(1)}, bf16[35,64,128]{2,1,0:T(8,128)(2,1)S(1)}, u32[]{:S(2)}, u32[]{:S(2)}) collective-permute-start(bf16[35,64,128]{2,1,0:T(8,128)(2,1)S(1)} %get-tuple-element.73.refs_2_), channel_id=1, source_target_pairs={{0,64},{32,96},{64,0},{96,32},{128,192},{160,224},{192,128},{224,1... | collective-permute-start | bytes 1720328 | tf_op jit(solution)/shard_map/ppermute | solution.py:47
  111.1 29.2 %collective-permute-start.25 = (bf16[35,64,128]{2,1,0:T(8,128)(2,1)S(1)}, bf16[35,64,128]{2,1,0:T(8,128)(2,1)S(1)}, u32[]{:S(2)}, u32[]{:S(2)}) collective-permute-start(bf16[35,64,128]{2,1,0:T(8,128)(2,1)S(1)} %get-tuple-element.80.refs_2_), channel_id=1, source_target_pairs={{0,224},{32,128},{64,160},{96,192},{128,96},{160,0},{192,32},{224,... | collective-permute-start | bytes 1720328 | tf_op jit(solution)/shard_map/ppermute | solution.py:47
  115.6 6.5 %collective-permute-start.20 = (bf16[32,4096]{1,0:T(8,128)(2,1)S(1)}, bf16[32,4096]{1,0:T(8,128)(2,1)S(1)}, u32[]{:S(2)}, u32[]{:S(2)}) collective-permute-start(bf16[32,4096]{1,0:T(8,128)(2,1)S(1)} %shard_map.136.refs_2_), channel_id=1, source_target_pairs={{0,28},{1,5},{2,30},{3,7},{4,0},{5,9},{6,2},{7,11},{8,4},{9,13},{1... | collective-permute-start | bytes 786440 | tf_op jit(solution)/shard_map/ppermute | solution.py:43
  122.0 20.3 %collective-permute-start.18 = (bf16[32,4096]{1,0:T(8,128)(2,1)S(1)}, bf16[32,4096]{1,0:T(8,128)(2,1)S(1)}, u32[]{:S(2)}, u32[]{:S(2)}) collective-permute-start(bf16[32,4096]{1,0:T(8,128)(2,1)S(1)} %shard_map.134.refs_9_), channel_id=1, source_target_pairs={{0,28},{1,5},{2,30},{3,7},{4,0},{5,9},{6,2},{7,11},{8,4},{9,13},{1... | collective-permute-start | bytes 786440 | tf_op jit(solution)/shard_map/ppermute | solution.py:43
  123.5 18.9 %collective-permute-start.21 = (bf16[32,4096]{1,0:T(8,128)(2,1)S(1)}, bf16[32,4096]{1,0:T(8,128)(2,1)S(1)}, u32[]{:S(2)}, u32[]{:S(2)}) collective-permute-start(bf16[32,4096]{1,0:T(8,128)(2,1)S(1)} %shard_map.137.refs_5_), channel_id=1, source_target_pairs={{0,28},{1,5},{2,30},{3,7},{4,0},{5,9},{6,2},{7,11},{8,4},{9,13},{1... | collective-permute-start | bytes 786440 | tf_op jit(solution)/shard_map/ppermute | solution.py:43
  126.7 25.4 %collective-permute-start.28 = (bf16[35,64,128]{2,1,0:T(8,128)(2,1)S(1)}, bf16[35,64,128]{2,1,0:T(8,128)(2,1)S(1)}, u32[]{:S(2)}, u32[]{:S(2)}) collective-permute-start(bf16[35,64,128]{2,1,0:T(8,128)(2,1)S(1)} %get-tuple-element.93), channel_id=1, source_target_pairs={{0,192},{32,224},{64,128},{96,160},{128,64},{160,96},{192,0},{224,... | collective-permute-start | bytes 1720328 | tf_op jit(solution)/shard_map/ppermute | solution.py:47
  130.1 32.0 %collective-permute-start.30 = (bf16[35,64,128]{2,1,0:T(8,128)(2,1)S(1)}, bf16[35,64,128]{2,1,0:T(8,128)(2,1)S(1)}, u32[]{:S(2)}, u32[]{:S(2)}) collective-permute-start(bf16[35,64,128]{2,1,0:T(8,128)(2,1)S(1)} %get-tuple-element.94), channel_id=1, source_target_pairs={{0,96},{32,0},{64,32},{96,64},{128,224},{160,128},{192,160},{224,1... | collective-permute-start | bytes 1720328 | tf_op jit(solution)/shard_map/ppermute | solution.py:47
  140.3 21.8 %collective-permute-start.29 = (bf16[35,64,128]{2,1,0:T(8,128)(2,1)S(1)}, bf16[35,64,128]{2,1,0:T(8,128)(2,1)S(1)}, u32[]{:S(2)}, u32[]{:S(2)}) collective-permute-start(bf16[35,64,128]{2,1,0:T(8,128)(2,1)S(1)} %get-tuple-element.83.refs_2_), channel_id=1, source_target_pairs={{0,32},{32,64},{64,96},{96,0},{128,160},{160,192},{192,224},{224,1... | collective-permute-start | bytes 1720328 | tf_op jit(solution)/shard_map/ppermute | solution.py:47
  142.4 1.6 collective-permute-start.26
  144.1 20.8 %collective-permute-start.27 = (bf16[16,4096]{1,0:T(8,128)(2,1)S(1)}, bf16[16,4096]{1,0:T(8,128)(2,1)S(1)}, u32[]{:S(2)}, u32[]{:S(2)}) collective-permute-start(bf16[16,4096]{1,0:T(8,128)(2,1)S(1)} %get-tuple-element.92), channel_id=1, source_target_pairs={{0,2},{1,3},{2,0},{3,1},{4,6},{5,7},{6,4},{7,5},{8,10},{9,11},{10,... | collective-permute-start | bytes 393224 | tf_op jit(solution)/shard_map/ppermute | solution.py:43

commit v4 on v3

--- a/solution.py
+++ b/solution.py
@@ -123,8 +123,7 @@
             o_ref[at, :] = o_ref[at, :] * row
 
 
-def forward_kernel(first, count, idx_ref, xa, xb, w_ref, g_ref, *rest):
-    act_ref, p_ref, acc_ref = rest[-3:]
+def forward_kernel(first, idx_ref, xa, xb, w_ref, g_ref, act_ref, p_ref, acc_ref):
     d = w_ref.shape[0]
     kb = 1024
 
@@ -139,37 +138,46 @@
     def _(s):
         acc_ref[...] += product(s)
 
-    @pl.loop(0, count)
-    def _(n):
-        at = idx_ref[first + n]
+    def finish(n, carry):
         rows = pl.ds(pl.multiple_of(n * 16, 16), 16)
         pre = acc_ref[rows, :]
         s = jax.nn.sigmoid(pre)
-        act = (pre * s).astype(BF16)
-        if first:
-            act_ref[at] = act
-            act_ref[idx_ref[n]] = rest[0][n]
-        else:
-            act_ref[n] = act
-        grad = g_ref[at].astype(F32) * s * (1.0 + pre * (1.0 - s))
+        act_ref[n] = (pre * s).astype(BF16)
+        grad = g_ref[idx_ref[first + n]].astype(F32) * s * (1.0 + pre * (1.0 - s))
         p_ref[rows, :] = grad.astype(BF16)
-
-
-def forward(first, idx, xa, xb, masked, act_grad, acts=(), after=()):
+        return carry
+
+    lax.fori_loop(0, act_ref.shape[0], finish, 0, unroll=2)
+
+
+def forward(first, idx, xa, xb, masked, act_grad, after=()):
     d, width = masked.shape
-    blocks = 32 if first else 16
     return call(
-        functools.partial(forward_kernel, first, 16),
+        functools.partial(forward_kernel, first),
         1,
         (
-            jax.ShapeDtypeStruct((blocks, 16, width), BF16),
+            jax.ShapeDtypeStruct((16, 16, width), BF16),
             jax.ShapeDtypeStruct((256, width), BF16),
         ),
-        (idx, xa, xb, masked, act_grad, *acts),
+        (idx, xa, xb, masked, act_grad),
         2 * 256 * d * width,
         scratch=(pltpu.VMEM((256, width), F32),),
         after=after,
     )
+
+
+def act_join_kernel(idx_ref, a_ref, b_ref, out, tick):
+    tick[...] = jnp.zeros_like(tick)
+
+    @pl.loop(0, 16)
+    def _(n):
+        out[idx_ref[n]] = a_ref[n]
+        out[idx_ref[16 + n]] = b_ref[n]
+
+
+def last_kernel(kept, received, out, tick):
+    tick[...] = jnp.zeros_like(tick)
+    out[...] = (kept[...] + received[...].astype(F32)).astype(BF16)
 
 
 def xgrad_kernel(p_ref, w_ref, own_ref, other_ref):
@@ -403,7 +411,7 @@
     gather_core = core ^ ((n >> 3) & 1)
     zk = (z - (1 - 2 * gather_core) * dist) & (NZ - 1)
     idx = zk * 4 + (xh ^ (n >> 4)) * 2 + (gather_core ^ flip)
-    order = [(1, 0), (0, 2), (1, 1), (1, 3), (1, 2), (0, 1), (0, 3), (0, 0)]
+    order = [(1, 1), (0, 3), (1, 3), (0, 1), (1, 2), (1, 0), (0, 2), (0, 0)]
     dx = jnp.array([o[0] for o in order], jnp.int32)
     dy = jnp.array([o[1] for o in order], jnp.int32)
     dests = (xl ^ dx) * NY + ((y + dy) & (NY - 1))
@@ -412,16 +420,17 @@
         return call(tick_kernel, 0, jax.ShapeDtypeStruct((8, 128), F32), (), 0)
 
     ticks = [tick() for _ in range(4)]
-    near1 = move(chip, dz=1)
+    near1, near2 = move(chip, dz=1), move(chip, dz=2)
     t_slot, ticks[0] = lax.optimization_barrier((t, ticks[0]))
     slot, odd = slots_of(block_mask, t_slot)
     slot, odd, idx, dests, near1 = lax.optimization_barrier((slot, odd, idx, dests, near1))
-    near2 = move(near1, dz=1)
     slot, ticks[1] = lax.optimization_barrier((slot, ticks[1]))
     code, near2 = lax.optimization_barrier((codes_of(slot), near2))
     scalars = (dests, code, odd)
 
     near3 = move(near2, dz=1)
+    head = call(head_kernel, 0, jax.ShapeDtypeStruct((16, d), BF16), (near2,), 0)
+    far = move(head, dz=2)
     t_mask, ticks[2] = lax.optimization_barrier((t, ticks[2]))
     masked = call(
         mask_kernel,
@@ -439,8 +448,6 @@
     )
     near3, masked = lax.optimization_barrier((near3, masked))
 
-    head = call(head_kernel, 0, jax.ShapeDtypeStruct((16, d), BF16), (near3,), 0)
-    far = move(head, dz=1)
     cross = [move(v, dx=1) for v in (near1, near2, near3, far)]
     x0 = join(tokens, far, near1, near2, near3)
     x2 = move(x0, dc=1)
@@ -449,10 +456,10 @@
     xs = (x0, x1, x2, x3)
 
     grads = act_grad.reshape(32, 16, width)
-    act, pa = forward(0, idx, x0, x2, masked, grads, after=ticks)
+    act_a, pa = forward(0, idx, x0, x2, masked, grads, after=ticks)
     own_a, other_a = xgrad(pa, masked)
     received_a = move(other_a, dc=1)
-    act, pb = forward(16, idx, x1, x3, masked, grads, (act,), (other_a,))
+    act_b, pb = forward(16, idx, x1, x3, masked, grads, after=(other_a,))
 
     parts = []
 
@@ -469,25 +476,34 @@
     done = pack(1, 2, done)
     a1, a2, a3, a4, home_a = mix(own_a, received_a, (done,))
     ring_a = back(a4)
-    own_b, other_b = xgrad(pb, masked, (a4,))
+    done = pack(3, 2, a4)
+    done = hop(a3, ring_a, (done,))
+    ring_a = back(done)
+    own_b, other_b = xgrad(pb, masked, (done,))
     received_b = move(other_b, dc=1)
-    done = hop(a3, ring_a, (other_b,))
-    ring_a = back(done)
-    done = pack(3, 2, done)
+    done = pack(5, 2, other_b)
     b1, b2, b3, b4, home_b = mix(own_b, received_b, (done,))
     ring_b = back(b4)
     done = hop(a2, ring_a, (b4,))
     ring_a = back(done)
-    done = pack(5, 2, done)
     done = hop(b3, ring_b, (done,))
     ring_b = back(done)
     done = hop(a1, ring_a, (done,))
     ring_a = back(done)
-    done = pack(7, 1, done)
     done = hop(b2, ring_b, (done,))
     ring_b = back(done)
+    done = pack(7, 1, done)
     done = hop(b1, ring_b, (done,))
     ring_b = back(done)
+    order_after = jax.ShapeDtypeStruct((8, 128), F32)
+    act, done = call(
+        act_join_kernel,
+        1,
+        (jax.ShapeDtypeStruct((32, 16, width), BF16), order_after),
+        (idx, act_a, act_b),
+        0,
+        after=(done,),
+    )
 
     early = call(
         presum_kernel,
@@ -512,7 +528,13 @@
         (kept, move(to_core, dc=1)),
         32 * d,
     )
-    x_grad = (kept + move(to_x, dx=1).astype(F32)).astype(BF16)
+    x_grad, done = call(
+        last_kernel,
+        0,
+        (jax.ShapeDtypeStruct((16, d), BF16), order_after),
+        (kept, move(to_x, dx=1)),
+        16 * d,
+    )
 
     weight_grad = call(
         unpack_kernel,
@@ -524,6 +546,7 @@
             pltpu.VMEM((512, width), F32),
             pltpu.SemaphoreType.DMA((4,)),
         ),
+        after=(done,),
         out_space=pl.BlockSpec(memory_space=pl.ANY),
     )
     return (act.reshape(512, width), x_grad, weight_grad)

time: 168 us -> 166 us (0.988)
  waiting for transfers between devices: 76.2 us -> 61.4 us
  starting transfers between devices: 44.9 us -> 57.8 us
    ppermute x24, starting transfers between devices: 26.4 us -> 45.5 us  [move(): return lax.ppermute(x, 'tensor', tensor_perm(dz, dx, dc, split=True))]
    ppermute x24, waiting for transfers between devices: 54.1 us -> 42.1 us  [move(): return lax.ppermute(x, 'tensor', tensor_perm(dz, dx, dc, split=True))]
    ppermute x7, starting transfers between devices: 18.5 us -> 12.3 us  [move_dp(): return lax.ppermute(x, 'dp', dp_perm(dx, dy))]
    ppermute x7, waiting for transfers between devices: 22.2 us -> 19.3 us  [move_dp(): return lax.ppermute(x, 'dp', dp_perm(dx, dy))]
    pallas_call x30 -> x32, Pallas kernels: 36.3 us -> 37.6 us  [call(): pl.pallas_call(run, out_shape=out_shape, in_specs=[SMEM] * n_scalar + [sp...]
  transfers between devices with their start and end apart: 31 -> 31, of which waited for: 18 -> 12; matrix products, arithmetic and copies ran while one was open for 3% -> 3% of each run, Pallas kernels for 19% -> 19%
where the time goes in v4:
time: 166 us; the launch traced here: 164 us
  waiting for transfers between devices  61.4 us (37%)
  starting transfers between devices  57.8 us (35%)
  Pallas kernels  37.6 us (23%)
  other arithmetic  3.53 us (2%)
  local copies, waits for them, and re-layouts  1.98 us (1%)
    ppermute x24, starting transfers between devices, move(): return lax.ppermute(x, 'tensor', tensor_perm(dz, dx, dc, split=True))  45.5 us
    ppermute x24, waiting for transfers between devices, move(): return lax.ppermute(x, 'tensor', tensor_perm(dz, dx, dc, split=True))  42.1 us
    pallas_call x32, Pallas kernels, call(): pl.pallas_call(run, out_shape=out_shape, in_specs=[SMEM] * n_scalar + [sp...  37.6 us
    ppermute x7, waiting for transfers between devices, move_dp(): return lax.ppermute(x, 'dp', dp_perm(dx, dy))  19.3 us
    ppermute x7, starting transfers between devices, move_dp(): return lax.ppermute(x, 'dp', dp_perm(dx, dy))  12.3 us
  transfers between devices with their start and end apart: 31, of which 12 were waited for; matrix products, arithmetic and copies ran while one was open for 3% of the time, Pallas kernels for 19%

profile of v4, /device:TPU:8, one launch (start us, length us, event | category | flops | bytes accessed | tf_op | source)
XLA Modules:
  0.0 164.5 jit_solution(14416187399989766400)
XLA Ops:
  0.8 1.5 collective-permute-done.refs_1_
  2.3 0.9 copy-done.1
  3.2 3.3 %collective-permute-start.2 = (bf16[32,4096]{1,0:T(8,128)(2,1)S(1)}, bf16[32,4096]{1,0:T(8,128)(2,1)S(1)}, u32[]{:S(2)}, u32[]{:S(2)}) collective-permute-start(bf16[32,4096]{1,0:T(8,128)(2,1)S(1)} %shard_map.112), channel_id=1, source_target_pairs={{0,8},{1,25},{2,10},{3,27},{4,12},{5,29},{6,14},{7,31},{8,16},{9,1... | collective-permute-start | bytes 786440 | tf_op jit(solution)/shard_map/ppermute | solution.py:43
  6.6 1.9 %collective-permute-start.1 = (bf16[32,4096]{1,0:T(8,128)(2,1)S(1)}, bf16[32,4096]{1,0:T(8,128)(2,1)S(1)}, u32[]{:S(2)}, u32[]{:S(2)}) collective-permute-start(bf16[32,4096]{1,0:T(8,128)(2,1)S(1)} %shard_map.112), channel_id=1, source_target_pairs={{0,4},{1,29},{2,6},{3,31},{4,8},{5,1},{6,10},{7,3},{8,12},{9,5},{1... | collective-permute-start | bytes 786440 | tf_op jit(solution)/shard_map/ppermute | solution.py:43
  8.5 0.9 dynamic-slice_compare_fusion
  10.2 1.0 convert_reduce_fusion
  11.2 7.9 %collective-permute-done.1.refs_2_ = bf16[32,4096]{1,0:T(8,128)(2,1)S(1)} collective-permute-done((bf16[32,4096]{1,0:T(8,128)(2,1)S(1)}, bf16[32,4096]{1,0:T(8,128)(2,1)S(1)}, u32[]{:S(2)}, u32[]{:S(2)}) %collective-permute-start.1) | collective-permute-done | bytes 262176 | tf_op jit(solution)/shard_map/ppermute | solution.py:43
  19.1 1.9 %select_reduce_fusion = s32[8,70]{0,1:T(8,128)S(1)} fusion(s32[112]{0:T(128)} %constant.79, s32[8,112]{1,0:T(8,128)S(1)} %get-tuple-element.59), kind=kLoop, calls=%fused_computation.2 | loop fusion | flops 187600 | bytes 6272 | tf_op jit(solution)/shard_map/reduce_sum | solution.py:392
  21.2 3.9 %collective-permute-start.3 = (bf16[16,4096]{1,0:T(8,128)(2,1)S(1)}, bf16[16,4096]{1,0:T(8,128)(2,1)S(1)}, u32[]{:S(2)}, u32[]{:S(2)}) collective-permute-start(bf16[16,4096]{1,0:T(8,128)(2,1)S(1)} %shard_map.115), channel_id=1, source_target_pairs={{0,8},{1,25},{2,10},{3,27},{4,12},{5,29},{6,14},{7,31},{8,16},{9,1... | collective-permute-start | bytes 393224 | tf_op jit(solution)/shard_map/ppermute | solution.py:43
  25.1 0.9 copy-done.3
  26.0 3.4 %shard_map.117.refs_3_.refs_1_ = bf16[4096,896]{1,0:T(8,128)(2,1)S(1)} custom-call(s32[1]{0:T(128)} %bitcast.refs_0_, bf16[4096,896]{1,0:T(8,128)(2,1)} %refs_1_.1, s32[64,448]{1,0:T(8,128)S(1)} %copy-done.3), custom_call_target="tpu_custom_call" | custom-call | flops 3670016 | bytes 7454724 | tf_op jit(solution)/shard_map/pallas_call | solution.py:62
  29.4 0.7 collective-permute-done.4.refs_4_
  30.3 3.1 %collective-permute-start.6 = (bf16[16,4096]{1,0:T(8,128)(2,1)S(1)}, bf16[16,4096]{1,0:T(8,128)(2,1)S(1)}, u32[]{:S(2)}, u32[]{:S(2)}) collective-permute-start(bf16[16,4096]{1,0:T(8,128)(2,1)S(1)} %copy-done.2), channel_id=1, source_target_pairs={{0,2},{1,3},{2,0},{3,1},{4,6},{5,7},{6,4},{7,5},{8,10},{9,11},{10,... | collective-permute-start | bytes 393224 | tf_op jit(solution)/shard_map/ppermute | solution.py:43
  33.9 3.0 %collective-permute-start.8 = (bf16[32,4096]{1,0:T(8,128)(2,1)S(1)}, bf16[32,4096]{1,0:T(8,128)(2,1)S(1)}, u32[]{:S(2)}, u32[]{:S(2)}) collective-permute-start(bf16[32,4096]{1,0:T(8,128)(2,1)S(1)} %collective-permute-done.1.refs_2_), channel_id=1, source_target_pairs={{0,2},{1,3},{2,0},{3,1},{4,6},{5,7},{6,4},{7,5},{8,10},{9,11},{10,... | collective-permute-start | bytes 786440 | tf_op jit(solution)/shard_map/ppermute | solution.py:43
  37.8 3.5 %collective-permute-start.7 = (bf16[16,4096]{1,0:T(8,128)(2,1)S(1)}, bf16[16,4096]{1,0:T(8,128)(2,1)S(1)}, u32[]{:S(2)}, u32[]{:S(2)}) collective-permute-start(bf16[16,4096]{1,0:T(8,128)(2,1)S(1)} %collective-permute-done.3.refs_1_), channel_id=1, source_target_pairs={{0,2},{1,3},{2,0},{3,1},{4,6},{5,7},{6,4},{7,5},{8,10},{9,11},{10,... | collective-permute-start | bytes 393224 | tf_op jit(solution)/shard_map/ppermute | solution.py:43
  41.3 16.1 %collective-permute-done.7.refs_1_ = bf16[16,4096]{1,0:T(8,128)(2,1)S(1)} collective-permute-done((bf16[16,4096]{1,0:T(8,128)(2,1)S(1)}, bf16[16,4096]{1,0:T(8,128)(2,1)S(1)}, u32[]{:S(2)}, u32[]{:S(2)}) %collective-permute-start.7) | collective-permute-done | bytes 131104 | tf_op jit(solution)/shard_map/ppermute | solution.py:43
  57.6 3.9 %shard_map.120 = (bf16[16,16,896]{2,1,0:T(8,128)(2,1)S(1)}, bf16[256,896]{1,0:T(8,128)(2,1)S(1)}) custom-call(s32[32]{0:T(128)S(1)} %fusion.8.refs_0_, bf16[128,4096]{1,0:T(8,128)(2,1)S(1)} %shard_map.118.refs_1_.refs_5_, bf16[128,4096]{1,0:T(8,128)(2,1)S(1)} %collective-permute-done.5.refs_2_.refs_7_, bf16[4096,896]{1,0:T(8,128)(2,1)S(1)} %shard_map.117.refs_3_.refs_1_, ...), custom_call_target="tpu_custom_call" | custom-call | flops 1879048192 | bytes 10354816 | tf_op jit(solution)/shard_map/pallas_call | solution.py:62
  61.4 3.8 %shard_map.122 = (f32[128,4096]{1,0:T(8,128)S(1)}, bf16[128,4096]{1,0:T(8,128)(2,1)S(1)}) custom-call(bf16[256,896]{1,0:T(8,128)(2,1)S(1)} %get-tuple-element.69.refs_0_.refs_3_, bf16[4096,896]{1,0:T(8,128)(2,1)S(1)} %shard_map.117.refs_3_.refs_1_), custom_call_target="tpu_custom_call" | custom-call | flops 1879048192 | bytes 7798784 | tf_op jit(solution)/shard_map/pallas_call | solution.py:62
  65.2 0.7 collective-permute-start.12
  66.0 3.9 %shard_map.123 = (bf16[16,16,896]{2,1,0:T(8,128)(2,1)S(1)}, bf16[256,896]{1,0:T(8,128)(2,1)S(1)}) custom-call(s32[32]{0:T(128)S(1)} %fusion.8.refs_0_, bf16[128,4096]{1,0:T(8,128)(2,1)S(1)} %shard_map.121.refs_1_.refs_6_, bf16[128,4096]{1,0:T(8,128)(2,1)S(1)} %collective-permute-done.11.refs_2_.refs_8_, bf16[4096,896]{1,0:T(8,128)(2,1)S(1)} %shard_map.117.refs_3_.refs_1_, ...), custom_call_target="tpu_custom_call" | custom-call | flops 1879048192 | bytes 10354816 | tf_op jit(solution)/shard_map/pallas_call | solution.py:62
  69.8 1.7 %shard_map.124.refs_9_ = bf16[35,64,128]{2,1,0:T(8,128)(2,1)S(1)} custom-call(s32[8]{0:T(128)S(1)} %and_add_fusion.refs_0_, s32[8,70]{1,0:T(8,128)S(1)} %broadcast_add_fusion.refs_1_, s32[8]{0:T(128)S(1)} %get-tuple-element.76.refs_2_, bf16[256,896]{1,0:T(8,128)(2,1)S(1)} %get-tuple-element.69.refs_0_.refs_3_, ...), custom_call_target="tpu_custom_call" | custom-call | flops 469762048 | bytes 5114112 | tf_op jit(solution)/shard_map/pallas_call | solution.py:62
  71.5 2.8 %shard_map.125 = (bf16[35,64,128]{2,1,0:T(8,128)(2,1)S(1)}, bf16[35,64,128]{2,1,0:T(8,128)(2,1)S(1)}) custom-call(s32[8]{0:T(128)S(1)} %and_add_fusion.refs_0_, s32[8,70]{1,0:T(8,128)S(1)} %broadcast_add_fusion.refs_1_, s32[8]{0:T(128)S(1)} %get-tuple-element.76.refs_2_, bf16[256,896]{1,0:T(8,128)(2,1)S(1)} %get-tuple-element.69.refs_0_.refs_3_, ...), custom_call_target="tpu_custom_call" | custom-call | flops 939524096 | bytes 5114112 | tf_op jit(solution)/shard_map/pallas_call | solution.py:62
  74.6 3.2 %collective-permute-start.13 = (bf16[16,4096]{1,0:T(8,128)(2,1)S(1)}, bf16[16,4096]{1,0:T(8,128)(2,1)S(1)}, u32[]{:S(2)}, u32[]{:S(2)}) collective-permute-start(bf16[16,4096]{1,0:T(8,128)(2,1)S(1)} %get-tuple-element.79.refs_9_), channel_id=1, source_target_pairs={{0,28},{1,5},{2,30},{3,7},{4,0},{5,9},{6,2},{7,11},{8,4},{9,13},{1... | collective-permute-start | bytes 393224 | tf_op jit(solution)/shard_map/ppermute | solution.py:43
  77.8 3.0 %shard_map.127 = (bf16[35,64,128]{2,1,0:T(8,128)(2,1)S(1)}, bf16[35,64,128]{2,1,0:T(8,128)(2,1)S(1)}) custom-call(s32[8]{0:T(128)S(1)} %and_add_fusion.refs_0_, s32[8,70]{1,0:T(8,128)S(1)} %broadcast_add_fusion.refs_1_, s32[8]{0:T(128)S(1)} %get-tuple-element.76.refs_2_, bf16[256,896]{1,0:T(8,128)(2,1)S(1)} %get-tuple-element.69.refs_0_.refs_3_, ...), custom_call_target="tpu_custom_call" | custom-call | flops 939524096 | bytes 5114112 | tf_op jit(solution)/shard_map/pallas_call | solution.py:62
  80.8 3.8 %shard_map.129 = (f32[128,4096]{1,0:T(8,128)S(1)}, bf16[128,4096]{1,0:T(8,128)(2,1)S(1)}) custom-call(bf16[256,896]{1,0:T(8,128)(2,1)S(1)} %get-tuple-element.72.refs_4_.refs_0_, bf16[4096,896]{1,0:T(8,128)(2,1)S(1)} %shard_map.117.refs_3_.refs_1_, bf16[32,4096]{1,0:T(8,128)(2,1)S(1)} %shard_map.128.refs_2_), custom_call_target="tpu_custom_call" | custom-call | flops 1879048192 | bytes 7798784 | tf_op jit(solution)/shard_map/pallas_call | solution.py:62
  84.7 3.3 %collective-permute-start.16 = (bf16[32,4096]{1,0:T(8,128)(2,1)S(1)}, bf16[32,4096]{1,0:T(8,128)(2,1)S(1)}, u32[]{:S(2)}, u32[]{:S(2)}) collective-permute-start(bf16[32,4096]{1,0:T(8,128)(2,1)S(1)} %shard_map.128.refs_2_), channel_id=1, source_target_pairs={{0,28},{1,5},{2,30},{3,7},{4,0},{5,9},{6,2},{7,11},{8,4},{9,13},{1... | collective-permute-start | bytes 786440 | tf_op jit(solution)/shard_map/ppermute | solution.py:43
  88.0 2.8 %shard_map.130 = (bf16[35,64,128]{2,1,0:T(8,128)(2,1)S(1)}, bf16[35,64,128]{2,1,0:T(8,128)(2,1)S(1)}) custom-call(s32[8]{0:T(128)S(1)} %and_add_fusion.refs_0_, s32[8,70]{1,0:T(8,128)S(1)} %broadcast_add_fusion.refs_1_, s32[8]{0:T(128)S(1)} %get-tuple-element.76.refs_2_, bf16[256,896]{1,0:T(8,128)(2,1)S(1)} %get-tuple-element.69.refs_0_.refs_3_, ...), custom_call_target="tpu_custom_call" | custom-call | flops 939524096 | bytes 5114112 | tf_op jit(solution)/shard_map/pallas_call | solution.py:62
  91.0 0.8 collective-permute-done.16.refs_1_
  92.0 3.8 %collective-permute-start.18 = (bf16[32,4096]{1,0:T(8,128)(2,1)S(1)}, bf16[32,4096]{1,0:T(8,128)(2,1)S(1)}, u32[]{:S(2)}, u32[]{:S(2)}) collective-permute-start(bf16[32,4096]{1,0:T(8,128)(2,1)S(1)} %shard_map.132.refs_2_), channel_id=1, source_target_pairs={{0,28},{1,5},{2,30},{3,7},{4,0},{5,9},{6,2},{7,11},{8,4},{9,13},{1... | collective-permute-start | bytes 786440 | tf_op jit(solution)/shard_map/ppermute | solution.py:43
  95.8 2.6 %collective-permute-start.22 = (bf16[35,64,128]{2,1,0:T(8,128)(2,1)S(1)}, bf16[35,64,128]{2,1,0:T(8,128)(2,1)S(1)}, u32[]{:S(2)}, u32[]{:S(2)}) collective-permute-start(bf16[35,64,128]{2,1,0:T(8,128)(2,1)S(1)} %shard_map.124.refs_9_), channel_id=1, source_target_pairs={{0,160},{32,192},{64,224},{96,128},{128,32},{160,64},{192,96},{224... | collective-permute-start | bytes 1720328 | tf_op jit(solution)/shard_map/ppermute | solution.py:47
  98.5 2.6 %collective-permute-done.15.refs_1_ = bf16[16,4096]{1,0:T(8,128)(2,1)S(1)} collective-permute-done((bf16[16,4096]{1,0:T(8,128)(2,1)S(1)}, bf16[16,4096]{1,0:T(8,128)(2,1)S(1)}, u32[]{:S(2)}, u32[]{:S(2)}) %collective-permute-start.15) | collective-permute-done | bytes 131104 | tf_op jit(solution)/shard_map/ppermute | solution.py:43
  101.1 3.8 %collective-permute-start.17 = (bf16[32,4096]{1,0:T(8,128)(2,1)S(1)}, bf16[32,4096]{1,0:T(8,128)(2,1)S(1)}, u32[]{:S(2)}, u32[]{:S(2)}) collective-permute-start(bf16[32,4096]{1,0:T(8,128)(2,1)S(1)} %shard_map.133.refs_2_), channel_id=1, source_target_pairs={{0,28},{1,5},{2,30},{3,7},{4,0},{5,9},{6,2},{7,11},{8,4},{9,13},{1... | collective-permute-start | bytes 786440 | tf_op jit(solution)/shard_map/ppermute | solution.py:43
  104.9 1.4 collective-permute-start.24
  106.3 3.0 %collective-permute-start.23 = (bf16[35,64,128]{2,1,0:T(8,128)(2,1)S(1)}, bf16[35,64,128]{2,1,0:T(8,128)(2,1)S(1)}, u32[]{:S(2)}, u32[]{:S(2)}) collective-permute-start(bf16[35,64,128]{2,1,0:T(8,128)(2,1)S(1)} %get-tuple-element.77.refs_2_), channel_id=1, source_target_pairs={{0,96},{32,0},{64,32},{96,64},{128,224},{160,128},{192,160},{224,1... | collective-permute-start | bytes 1720328 | tf_op jit(solution)/shard_map/ppermute | solution.py:47
  109.5 3.1 %collective-permute-start.19 = (bf16[32,4096]{1,0:T(8,128)(2,1)S(1)}, bf16[32,4096]{1,0:T(8,128)(2,1)S(1)}, u32[]{:S(2)}, u32[]{:S(2)}) collective-permute-start(bf16[32,4096]{1,0:T(8,128)(2,1)S(1)} %shard_map.135.refs_9_), channel_id=1, source_target_pairs={{0,28},{1,5},{2,30},{3,7},{4,0},{5,9},{6,2},{7,11},{8,4},{9,13},{1... | collective-permute-start | bytes 786440 | tf_op jit(solution)/shard_map/ppermute | solution.py:43
  112.6 1.7 %shard_map.136.refs_2_.refs_0_ = bf16[35,64,128]{2,1,0:T(8,128)(2,1)S(1)} custom-call(s32[8]{0:T(128)S(1)} %and_add_fusion.refs_0_, s32[8,70]{1,0:T(8,128)S(1)} %broadcast_add_fusion.refs_1_, s32[8]{0:T(128)S(1)} %get-tuple-element.76.refs_2_, bf16[256,896]{1,0:T(8,128)(2,1)S(1)} %get-tuple-element.69.refs_0_.refs_3_, ...), custom_call_target="tpu_custom_call" | custom-call | flops 469762048 | bytes 5114112 | tf_op jit(solution)/shard_map/pallas_call | solution.py:62
  114.4 2.2 %collective-permute-done.19.refs_1_ = bf16[32,4096]{1,0:T(8,128)(2,1)S(1)} collective-permute-done((bf16[32,4096]{1,0:T(8,128)(2,1)S(1)}, bf16[32,4096]{1,0:T(8,128)(2,1)S(1)}, u32[]{:S(2)}, u32[]{:S(2)}) %collective-permute-start.19) | collective-permute-done | bytes 262176 | tf_op jit(solution)/shard_map/ppermute | solution.py:43
  116.5 3.7 %collective-permute-start.20 = (bf16[32,4096]{1,0:T(8,128)(2,1)S(1)}, bf16[32,4096]{1,0:T(8,128)(2,1)S(1)}, u32[]{:S(2)}, u32[]{:S(2)}) collective-permute-start(bf16[32,4096]{1,0:T(8,128)(2,1)S(1)} %shard_map.134.refs_2_), channel_id=1, source_target_pairs={{0,28},{1,5},{2,30},{3,7},{4,0},{5,9},{6,2},{7,11},{8,4},{9,13},{1... | collective-permute-start | bytes 786440 | tf_op jit(solution)/shard_map/ppermute | solution.py:43
  120.4 2.3 %collective-permute-done.24.refs_3_ = bf16[35,64,128]{2,1,0:T(8,128)(2,1)S(1)} collective-permute-done((bf16[35,64,128]{2,1,0:T(8,128)(2,1)S(1)}, bf16[35,64,128]{2,1,0:T(8,128)(2,1)S(1)}, u32[]{:S(2)}, u32[]{:S(2)}) %collective-permute-start.24) | collective-permute-done | bytes 573472 | tf_op jit(solution)/shard_map/ppermute | solution.py:47
  122.8 1.0 collective-permute-start.28
  123.7 17.0 %collective-permute-done.23.refs_2_ = bf16[35,64,128]{2,1,0:T(8,128)(2,1)S(1)} collective-permute-done((bf16[35,64,128]{2,1,0:T(8,128)(2,1)S(1)}, bf16[35,64,128]{2,1,0:T(8,128)(2,1)S(1)}, u32[]{:S(2)}, u32[]{:S(2)}) %collective-permute-start.23) | collective-permute-done | bytes 573472 | tf_op jit(solution)/shard_map/ppermute | solution.py:47
  140.7 3.5 %collective-permute-start.30 = (bf16[35,64,128]{2,1,0:T(8,128)(2,1)S(1)}, bf16[35,64,128]{2,1,0:T(8,128)(2,1)S(1)}, u32[]{:S(2)}, u32[]{:S(2)}) collective-permute-start(bf16[35,64,128]{2,1,0:T(8,128)(2,1)S(1)} %get-tuple-element.101), channel_id=1, source_target_pairs={{0,64},{32,96},{64,0},{96,32},{128,192},{160,224},{192,128},{224,1... | collective-permute-start | bytes 1720328 | tf_op jit(solution)/shard_map/ppermute | solution.py:47
  144.2 0.8 collective-permute-start.29
  145.1 1.6 shard_map.138
  147.4 1.5 collective-permute-done.26.refs_1_
  149.0 3.3 %collective-permute-start.27 = (bf16[16,4096]{1,0:T(8,128)(2,1)S(1)}, bf16[16,4096]{1,0:T(8,128)(2,1)S(1)}, u32[]{:S(2)}, u32[]{:S(2)}) collective-permute-start(bf16[16,4096]{1,0:T(8,128)(2,1)S(1)} %get-tuple-element.98), channel_id=1, source_target_pairs={{0,2},{1,3},{2,0},{3,1},{4,6},{5,7},{6,4},{7,5},{8,10},{9,11},{10,... | collective-permute-start | bytes 393224 | tf_op jit(solution)/shard_map/ppermute | solution.py:43
  152.3 8.5 %collective-permute-done.27.refs_1_ = bf16[16,4096]{1,0:T(8,128)(2,1)S(1)} collective-permute-done((bf16[16,4096]{1,0:T(8,128)(2,1)S(1)}, bf16[16,4096]{1,0:T(8,128)(2,1)S(1)}, u32[]{:S(2)}, u32[]{:S(2)}) %collective-permute-start.27) | collective-permute-done | bytes 131104 | tf_op jit(solution)/shard_map/ppermute | solution.py:43
  161.5 2.8 %shard_map.143 = f32[512,896]{1,0:T(8,128)} custom-call(s32[1]{0:T(128)} %bitcast.3.refs_0_, s32[8,70]{1,0:T(8,128)S(1)} %broadcast_add_fusion.refs_1_, f32[35,64,128]{2,1,0:T(8,128)S(1)} %shard_map.139.refs_4_.refs_2_, bf16[35,64,128]{2,1,0:T(8,128)(2,1)S(1)} %collective-permute-done.28.refs_3_, bf16[35,64,128]{2,1,0:T(8,128)(2,1)S(1)} %collective-permute-done.29.refs_4_, ...), custom_call_target="tpu_custom_call" | custom-call | flops 2293760 | bytes 2869444 | tf_op jit(solution)/shard_map/pallas_call | solution.py:62
  (62 shorter events, 5.5 us)
Async XLA Ops:
  0.6 1.6 %collective-permute-start = (bf16[16,4096]{1,0:T(8,128)(2,1)}, bf16[16,4096]{1,0:T(8,128)(2,1)S(1)}, u32[]{:S(2)}, u32[]{:S(2)}) collective-permute-start(bf16[16,4096]{1,0:T(8,128)(2,1)} %refs_0_.3), channel_id=1, source_target_pairs={{0,1},{1,0},{2,3},{3,2},{4,5},{5,4},{6,7},{7,6},{8,9},{9,8},{10,11... | collective-permute-start | bytes 393224 | tf_op jit(solution)/shard_map/ppermute | solution.py:43
  2.3 0.9 copy-start.1
  3.2 17.9 %collective-permute-start.2 = (bf16[32,4096]{1,0:T(8,128)(2,1)S(1)}, bf16[32,4096]{1,0:T(8,128)(2,1)S(1)}, u32[]{:S(2)}, u32[]{:S(2)}) collective-permute-start(bf16[32,4096]{1,0:T(8,128)(2,1)S(1)} %shard_map.112), channel_id=1, source_target_pairs={{0,8},{1,25},{2,10},{3,27},{4,12},{5,29},{6,14},{7,31},{8,16},{9,1... | collective-permute-start | bytes 786440 | tf_op jit(solution)/shard_map/ppermute | solution.py:43
  6.6 12.6 %collective-permute-start.1 = (bf16[32,4096]{1,0:T(8,128)(2,1)S(1)}, bf16[32,4096]{1,0:T(8,128)(2,1)S(1)}, u32[]{:S(2)}, u32[]{:S(2)}) collective-permute-start(bf16[32,4096]{1,0:T(8,128)(2,1)S(1)} %shard_map.112), channel_id=1, source_target_pairs={{0,4},{1,29},{2,6},{3,31},{4,8},{5,1},{6,10},{7,3},{8,12},{9,5},{1... | collective-permute-start | bytes 786440 | tf_op jit(solution)/shard_map/ppermute | solution.py:43
  21.1 9.0 %collective-permute-start.4 = (bf16[32,4096]{1,0:T(8,128)(2,1)S(1)}, bf16[32,4096]{1,0:T(8,128)(2,1)S(1)}, u32[]{:S(2)}, u32[]{:S(2)}) collective-permute-start(bf16[32,4096]{1,0:T(8,128)(2,1)S(1)} %collective-permute-done.2.refs_0_.refs_3_), channel_id=1, source_target_pairs={{0,4},{1,29},{2,6},{3,31},{4,8},{5,1},{6,10},{7,3},{8,12},{9,5},{1... | collective-permute-start | bytes 786440 | tf_op jit(solution)/shard_map/ppermute | solution.py:43
  21.2 9.0 %collective-permute-start.3 = (bf16[16,4096]{1,0:T(8,128)(2,1)S(1)}, bf16[16,4096]{1,0:T(8,128)(2,1)S(1)}, u32[]{:S(2)}, u32[]{:S(2)}) collective-permute-start(bf16[16,4096]{1,0:T(8,128)(2,1)S(1)} %shard_map.115), channel_id=1, source_target_pairs={{0,8},{1,25},{2,10},{3,27},{4,12},{5,29},{6,14},{7,31},{8,16},{9,1... | collective-permute-start | bytes 393224 | tf_op jit(solution)/shard_map/ppermute | solution.py:43
  25.1 0.9 copy-start.3
  26.0 4.1 %copy-start.2 = (bf16[16,4096]{1,0:T(8,128)(2,1)S(1)}, bf16[16,4096]{1,0:T(8,128)(2,1)}, u32[]{:S(2)}) copy-start(bf16[16,4096]{1,0:T(8,128)(2,1)} %refs_0_.3) | copy-start | bytes 393220
  29.4 28.2 %copy-start = (bf16[512,896]{1,0:T(8,128)(2,1)S(1)}, bf16[512,896]{1,0:T(8,128)(2,1)}, u32[]{:S(2)}) copy-start(bf16[512,896]{1,0:T(8,128)(2,1)} %param.12) | copy-start | bytes 2752516
  30.2 27.4 %collective-permute-start.5 = (bf16[128,4096]{1,0:T(8,128)(2,1)S(1)}, bf16[128,4096]{1,0:T(8,128)(2,1)S(1)}, u32[]{:S(2)}, u32[]{:S(2)}) collective-permute-start(bf16[128,4096]{1,0:T(8,128)(2,1)S(1)} %shard_map.118.refs_1_.refs_5_), channel_id=1, source_target_pairs={{0,1},{1,0},{2,3},{3,2},{4,5},{5,4},{6,7},{7,6},{8,9},{9,8},{10,11... | collective-permute-start | bytes 3145736 | tf_op jit(solution)/shard_map/ppermute | solution.py:43
  30.3 7.5 %collective-permute-start.6 = (bf16[16,4096]{1,0:T(8,128)(2,1)S(1)}, bf16[16,4096]{1,0:T(8,128)(2,1)S(1)}, u32[]{:S(2)}, u32[]{:S(2)}) collective-permute-start(bf16[16,4096]{1,0:T(8,128)(2,1)S(1)} %copy-done.2), channel_id=1, source_target_pairs={{0,2},{1,3},{2,0},{3,1},{4,6},{5,7},{6,4},{7,5},{8,10},{9,11},{10,... | collective-permute-start | bytes 393224 | tf_op jit(solution)/shard_map/ppermute | solution.py:43
  33.4 24.0 %collective-permute-start.9 = (bf16[32,4096]{1,0:T(8,128)(2,1)S(1)}, bf16[32,4096]{1,0:T(8,128)(2,1)S(1)}, u32[]{:S(2)}, u32[]{:S(2)}) collective-permute-start(bf16[32,4096]{1,0:T(8,128)(2,1)S(1)} %collective-permute-done.2.refs_0_.refs_3_), channel_id=1, source_target_pairs={{0,2},{1,3},{2,0},{3,1},{4,6},{5,7},{6,4},{7,5},{8,10},{9,11},{10,... | collective-permute-start | bytes 786440 | tf_op jit(solution)/shard_map/ppermute | solution.py:43
  33.9 23.5 %collective-permute-start.8 = (bf16[32,4096]{1,0:T(8,128)(2,1)S(1)}, bf16[32,4096]{1,0:T(8,128)(2,1)S(1)}, u32[]{:S(2)}, u32[]{:S(2)}) collective-permute-start(bf16[32,4096]{1,0:T(8,128)(2,1)S(1)} %collective-permute-done.1.refs_2_), channel_id=1, source_target_pairs={{0,2},{1,3},{2,0},{3,1},{4,6},{5,7},{6,4},{7,5},{8,10},{9,11},{10,... | collective-permute-start | bytes 786440 | tf_op jit(solution)/shard_map/ppermute | solution.py:43
  37.0 20.4 %collective-permute-start.10 = (bf16[32,4096]{1,0:T(8,128)(2,1)S(1)}, bf16[32,4096]{1,0:T(8,128)(2,1)S(1)}, u32[]{:S(2)}, u32[]{:S(2)}) collective-permute-start(bf16[32,4096]{1,0:T(8,128)(2,1)S(1)} %collective-permute-done.4.refs_4_), channel_id=1, source_target_pairs={{0,2},{1,3},{2,0},{3,1},{4,6},{5,7},{6,4},{7,5},{8,10},{9,11},{10,... | collective-permute-start | bytes 786440 | tf_op jit(solution)/shard_map/ppermute | solution.py:43
  37.8 19.6 %collective-permute-start.7 = (bf16[16,4096]{1,0:T(8,128)(2,1)S(1)}, bf16[16,4096]{1,0:T(8,128)(2,1)S(1)}, u32[]{:S(2)}, u32[]{:S(2)}) collective-permute-start(bf16[16,4096]{1,0:T(8,128)(2,1)S(1)} %collective-permute-done.3.refs_1_), channel_id=1, source_target_pairs={{0,2},{1,3},{2,0},{3,1},{4,6},{5,7},{6,4},{7,5},{8,10},{9,11},{10,... | collective-permute-start | bytes 393224 | tf_op jit(solution)/shard_map/ppermute | solution.py:43
  57.5 8.5 %collective-permute-start.11 = (bf16[128,4096]{1,0:T(8,128)(2,1)S(1)}, bf16[128,4096]{1,0:T(8,128)(2,1)S(1)}, u32[]{:S(2)}, u32[]{:S(2)}) collective-permute-start(bf16[128,4096]{1,0:T(8,128)(2,1)S(1)} %shard_map.121.refs_1_.refs_6_), channel_id=1, source_target_pairs={{0,1},{1,0},{2,3},{3,2},{4,5},{5,4},{6,7},{7,6},{8,9},{9,8},{10,11... | collective-permute-start | bytes 3145736 | tf_op jit(solution)/shard_map/ppermute | solution.py:43
  65.2 9.1 %collective-permute-start.12 = (bf16[128,4096]{1,0:T(8,128)(2,1)S(1)}, bf16[128,4096]{1,0:T(8,128)(2,1)S(1)}, u32[]{:S(2)}, u32[]{:S(2)}) collective-permute-start(bf16[128,4096]{1,0:T(8,128)(2,1)S(1)} %get-tuple-element.70.refs_5_.refs_9_), channel_id=1, source_target_pairs={{0,1},{1,0},{2,3},{3,2},{4,5},{5,4},{6,7},{7,6},{8,9},{9,8},{10,11... | collective-permute-start | bytes 3145736 | tf_op jit(solution)/shard_map/ppermute | solution.py:43
  74.6 6.2 %collective-permute-start.13 = (bf16[16,4096]{1,0:T(8,128)(2,1)S(1)}, bf16[16,4096]{1,0:T(8,128)(2,1)S(1)}, u32[]{:S(2)}, u32[]{:S(2)}) collective-permute-start(bf16[16,4096]{1,0:T(8,128)(2,1)S(1)} %get-tuple-element.79.refs_9_), channel_id=1, source_target_pairs={{0,28},{1,5},{2,30},{3,7},{4,0},{5,9},{6,2},{7,11},{8,4},{9,13},{1... | collective-permute-start | bytes 393224 | tf_op jit(solution)/shard_map/ppermute | solution.py:43
  84.6 6.2 %collective-permute-start.14 = (bf16[128,4096]{1,0:T(8,128)(2,1)S(1)}, bf16[128,4096]{1,0:T(8,128)(2,1)S(1)}, u32[]{:S(2)}, u32[]{:S(2)}) collective-permute-start(bf16[128,4096]{1,0:T(8,128)(2,1)S(1)} %get-tuple-element.82.refs_9_), channel_id=1, source_target_pairs={{0,1},{1,0},{2,3},{3,2},{4,5},{5,4},{6,7},{7,6},{8,9},{9,8},{10,11... | collective-permute-start | bytes 3145736 | tf_op jit(solution)/shard_map/ppermute | solution.py:43
  84.7 7.2 %collective-permute-start.16 = (bf16[32,4096]{1,0:T(8,128)(2,1)S(1)}, bf16[32,4096]{1,0:T(8,128)(2,1)S(1)}, u32[]{:S(2)}, u32[]{:S(2)}) collective-permute-start(bf16[32,4096]{1,0:T(8,128)(2,1)S(1)} %shard_map.128.refs_2_), channel_id=1, source_target_pairs={{0,28},{1,5},{2,30},{3,7},{4,0},{5,9},{6,2},{7,11},{8,4},{9,13},{1... | collective-permute-start | bytes 786440 | tf_op jit(solution)/shard_map/ppermute | solution.py:43
  92.0 17.3 %collective-permute-start.18 = (bf16[32,4096]{1,0:T(8,128)(2,1)S(1)}, bf16[32,4096]{1,0:T(8,128)(2,1)S(1)}, u32[]{:S(2)}, u32[]{:S(2)}) collective-permute-start(bf16[32,4096]{1,0:T(8,128)(2,1)S(1)} %shard_map.132.refs_2_), channel_id=1, source_target_pairs={{0,28},{1,5},{2,30},{3,7},{4,0},{5,9},{6,2},{7,11},{8,4},{9,13},{1... | collective-permute-start | bytes 786440 | tf_op jit(solution)/shard_map/ppermute | solution.py:43
  95.7 5.3 %collective-permute-start.15 = (bf16[16,4096]{1,0:T(8,128)(2,1)S(1)}, bf16[16,4096]{1,0:T(8,128)(2,1)S(1)}, u32[]{:S(2)}, u32[]{:S(2)}) collective-permute-start(bf16[16,4096]{1,0:T(8,128)(2,1)S(1)} %get-tuple-element.87.refs_2_), channel_id=1, source_target_pairs={{0,28},{1,5},{2,30},{3,7},{4,0},{5,9},{6,2},{7,11},{8,4},{9,13},{1... | collective-permute-start | bytes 393224 | tf_op jit(solution)/shard_map/ppermute | solution.py:43
  95.8 24.5 %collective-permute-start.22 = (bf16[35,64,128]{2,1,0:T(8,128)(2,1)S(1)}, bf16[35,64,128]{2,1,0:T(8,128)(2,1)S(1)}, u32[]{:S(2)}, u32[]{:S(2)}) collective-permute-start(bf16[35,64,128]{2,1,0:T(8,128)(2,1)S(1)} %shard_map.124.refs_9_), channel_id=1, source_target_pairs={{0,160},{32,192},{64,224},{96,128},{128,32},{160,64},{192,96},{224... | collective-permute-start | bytes 1720328 | tf_op jit(solution)/shard_map/ppermute | solution.py:47
  101.1 8.3 %collective-permute-start.17 = (bf16[32,4096]{1,0:T(8,128)(2,1)S(1)}, bf16[32,4096]{1,0:T(8,128)(2,1)S(1)}, u32[]{:S(2)}, u32[]{:S(2)}) collective-permute-start(bf16[32,4096]{1,0:T(8,128)(2,1)S(1)} %shard_map.133.refs_2_), channel_id=1, source_target_pairs={{0,28},{1,5},{2,30},{3,7},{4,0},{5,9},{6,2},{7,11},{8,4},{9,13},{1... | collective-permute-start | bytes 786440 | tf_op jit(solution)/shard_map/ppermute | solution.py:43
  104.9 17.9 %collective-permute-start.24 = (bf16[35,64,128]{2,1,0:T(8,128)(2,1)S(1)}, bf16[35,64,128]{2,1,0:T(8,128)(2,1)S(1)}, u32[]{:S(2)}, u32[]{:S(2)}) collective-permute-start(bf16[35,64,128]{2,1,0:T(8,128)(2,1)S(1)} %get-tuple-element.93), channel_id=1, source_target_pairs={{0,224},{32,128},{64,160},{96,192},{128,96},{160,0},{192,32},{224,... | collective-permute-start | bytes 1720328 | tf_op jit(solution)/shard_map/ppermute | solution.py:47
  106.3 34.4 %collective-permute-start.23 = (bf16[35,64,128]{2,1,0:T(8,128)(2,1)S(1)}, bf16[35,64,128]{2,1,0:T(8,128)(2,1)S(1)}, u32[]{:S(2)}, u32[]{:S(2)}) collective-permute-start(bf16[35,64,128]{2,1,0:T(8,128)(2,1)S(1)} %get-tuple-element.77.refs_2_), channel_id=1, source_target_pairs={{0,96},{32,0},{64,32},{96,64},{128,224},{160,128},{192,160},{224,1... | collective-permute-start | bytes 1720328 | tf_op jit(solution)/shard_map/ppermute | solution.py:47
  109.3 35.0 %collective-permute-start.25 = (bf16[35,64,128]{2,1,0:T(8,128)(2,1)S(1)}, bf16[35,64,128]{2,1,0:T(8,128)(2,1)S(1)}, u32[]{:S(2)}, u32[]{:S(2)}) collective-permute-start(bf16[35,64,128]{2,1,0:T(8,128)(2,1)S(1)} %get-tuple-element.80.refs_2_), channel_id=1, source_target_pairs={{0,32},{32,64},{64,96},{96,0},{128,160},{160,192},{192,224},{224,1... | collective-permute-start | bytes 1720328 | tf_op jit(solution)/shard_map/ppermute | solution.py:47
  109.5 7.0 %collective-permute-start.19 = (bf16[32,4096]{1,0:T(8,128)(2,1)S(1)}, bf16[32,4096]{1,0:T(8,128)(2,1)S(1)}, u32[]{:S(2)}, u32[]{:S(2)}) collective-permute-start(bf16[32,4096]{1,0:T(8,128)(2,1)S(1)} %shard_map.135.refs_9_), channel_id=1, source_target_pairs={{0,28},{1,5},{2,30},{3,7},{4,0},{5,9},{6,2},{7,11},{8,4},{9,13},{1... | collective-permute-start | bytes 786440 | tf_op jit(solution)/shard_map/ppermute | solution.py:43
  116.5 30.6 %collective-permute-start.20 = (bf16[32,4096]{1,0:T(8,128)(2,1)S(1)}, bf16[32,4096]{1,0:T(8,128)(2,1)S(1)}, u32[]{:S(2)}, u32[]{:S(2)}) collective-permute-start(bf16[32,4096]{1,0:T(8,128)(2,1)S(1)} %shard_map.134.refs_2_), channel_id=1, source_target_pairs={{0,28},{1,5},{2,30},{3,7},{4,0},{5,9},{6,2},{7,11},{8,4},{9,13},{1... | collective-permute-start | bytes 786440 | tf_op jit(solution)/shard_map/ppermute | solution.py:43
  120.3 26.9 %collective-permute-start.21 = (bf16[32,4096]{1,0:T(8,128)(2,1)S(1)}, bf16[32,4096]{1,0:T(8,128)(2,1)S(1)}, u32[]{:S(2)}, u32[]{:S(2)}) collective-permute-start(bf16[32,4096]{1,0:T(8,128)(2,1)S(1)} %shard_map.137.refs_3_), channel_id=1, source_target_pairs={{0,28},{1,5},{2,30},{3,7},{4,0},{5,9},{6,2},{7,11},{8,4},{9,13},{1... | collective-permute-start | bytes 786440 | tf_op jit(solution)/shard_map/ppermute | solution.py:43
  122.8 38.7 %collective-permute-start.28 = (bf16[35,64,128]{2,1,0:T(8,128)(2,1)S(1)}, bf16[35,64,128]{2,1,0:T(8,128)(2,1)S(1)}, u32[]{:S(2)}, u32[]{:S(2)}) collective-permute-start(bf16[35,64,128]{2,1,0:T(8,128)(2,1)S(1)} %get-tuple-element.100), channel_id=1, source_target_pairs={{0,192},{32,224},{64,128},{96,160},{128,64},{160,96},{192,0},{224,... | collective-permute-start | bytes 1720328 | tf_op jit(solution)/shard_map/ppermute | solution.py:47
  140.7 20.8 %collective-permute-start.30 = (bf16[35,64,128]{2,1,0:T(8,128)(2,1)S(1)}, bf16[35,64,128]{2,1,0:T(8,128)(2,1)S(1)}, u32[]{:S(2)}, u32[]{:S(2)}) collective-permute-start(bf16[35,64,128]{2,1,0:T(8,128)(2,1)S(1)} %get-tuple-element.101), channel_id=1, source_target_pairs={{0,64},{32,96},{64,0},{96,32},{128,192},{160,224},{192,128},{224,1... | collective-permute-start | bytes 1720328 | tf_op jit(solution)/shard_map/ppermute | solution.py:47
  144.2 17.3 %collective-permute-start.29 = (bf16[35,64,128]{2,1,0:T(8,128)(2,1)S(1)}, bf16[35,64,128]{2,1,0:T(8,128)(2,1)S(1)}, u32[]{:S(2)}, u32[]{:S(2)}) collective-permute-start(bf16[35,64,128]{2,1,0:T(8,128)(2,1)S(1)} %get-tuple-element.83.refs_2_), channel_id=1, source_target_pairs={{0,128},{32,160},{64,192},{96,224},{128,0},{160,32},{192,64},{224,... | collective-permute-start | bytes 1720328 | tf_op jit(solution)/shard_map/ppermute | solution.py:47
  147.3 1.6 collective-permute-start.26
  149.0 11.8 %collective-permute-start.27 = (bf16[16,4096]{1,0:T(8,128)(2,1)S(1)}, bf16[16,4096]{1,0:T(8,128)(2,1)S(1)}, u32[]{:S(2)}, u32[]{:S(2)}) collective-permute-start(bf16[16,4096]{1,0:T(8,128)(2,1)S(1)} %get-tuple-element.98), channel_id=1, source_target_pairs={{0,2},{1,3},{2,0},{3,1},{4,6},{5,7},{6,4},{7,5},{8,10},{9,11},{10,... | collective-permute-start | bytes 393224 | tf_op jit(solution)/shard_map/ppermute | solution.py:43

commit v5 on v4

--- a/solution.py
+++ b/solution.py
@@ -227,38 +227,31 @@
     )
 
 
-def hop_kernel(near, received, out):
+def hop_kernel(near, one, two, out):
     @pl.loop(0, near.shape[1] // 512)
     def _(s):
         cols = pl.ds(pl.multiple_of(s * 512, 512), 512)
-        out[:, cols] = (near[:, cols].astype(F32) + received[:, cols].astype(F32)).astype(BF16)
-
-
-def hop_far_kernel(near, received, out):
-    @pl.loop(0, near.shape[1] // 512)
+        total = near[:, cols].astype(F32) + one[:, cols].astype(F32)
+        out[0:16, cols] = (total[0:16] + two[:, cols].astype(F32)).astype(BF16)
+        out[16:32, cols] = total[16:32].astype(BF16)
+
+
+def hop(near, one, two, after):
+    shape = jax.ShapeDtypeStruct(near.shape, BF16)
+    return call(hop_kernel, 0, shape, (near, one, two), 2 * near.size, after=after)
+
+
+def sum_kernel(*refs):
+    halves, to_core, kept = (refs[0:3], refs[3:6]), refs[6], refs[7]
+
+    @pl.loop(0, kept.shape[1] // 512)
     def _(s):
         cols = pl.ds(pl.multiple_of(s * 512, 512), 512)
-        total = near[0:16, cols].astype(F32) + received[:, cols].astype(F32)
-        out[0:16, cols] = total.astype(BF16)
-        out[16:32, cols] = near[16:32, cols]
-
-
-def hop(near, received, after):
-    shape = jax.ShapeDtypeStruct(near.shape, BF16)
-    kernel = hop_kernel if near.shape == received.shape else hop_far_kernel
-    return call(kernel, 0, shape, (near, received), near.size, after=after)
-
-
-def sum_kernel(*refs):
-    halves, to_core, kept = (refs[0:2], refs[2:4]), refs[4], refs[5]
-
-    @pl.loop(0, kept.shape[1] // 512)
-    def _(s):
-        cols = pl.ds(pl.multiple_of(s * 512, 512), 512)
-        for q, (near, home) in enumerate(halves):
+        for q, (one, two, home) in enumerate(halves):
             rows = slice(q * 16, q * 16 + 16)
-            kept[rows, cols] = home[:, cols].astype(F32) + near[0:16, cols].astype(F32)
-            to_core[rows, cols] = near[16:32, cols]
+            total = one[:, cols].astype(F32) + two[:, cols].astype(F32)
+            kept[rows, cols] = home[:, cols].astype(F32) + total[0:16]
+            to_core[rows, cols] = total[16:32].astype(BF16)
 
 
 def sum_core_kernel(kept, received, to_x, out):
@@ -411,7 +404,7 @@
     gather_core = core ^ ((n >> 3) & 1)
     zk = (z - (1 - 2 * gather_core) * dist) & (NZ - 1)
     idx = zk * 4 + (xh ^ (n >> 4)) * 2 + (gather_core ^ flip)
-    order = [(1, 1), (0, 3), (1, 3), (0, 1), (1, 2), (1, 0), (0, 2), (0, 0)]
+    order = [(1, 1), (0, 3), (1, 2), (1, 3), (0, 1), (1, 0), (0, 2), (0, 0)]
     dx = jnp.array([o[0] for o in order], jnp.int32)
     dy = jnp.array([o[1] for o in order], jnp.int32)
     dests = (xl ^ dx) * NY + ((y + dy) & (NY - 1))
@@ -469,32 +462,25 @@
             parts.append(v if o == (0, 0) else move_dp(v, *o))
         return packed[0]
 
-    def back(x):
-        return move(x, dz=NZ - 1)
+    def back(x, hops):
+        return move(x, dz=NZ - hops)
 
     done = pack(0, 1, other_a)
     done = pack(1, 2, done)
     a1, a2, a3, a4, home_a = mix(own_a, received_a, (done,))
-    ring_a = back(a4)
-    done = pack(3, 2, a4)
-    done = hop(a3, ring_a, (done,))
-    ring_a = back(done)
-    own_b, other_b = xgrad(pb, masked, (done,))
+    from_a3, from_a4 = back(a3, 1), back(a4, 2)
+    own_b, other_b = xgrad(pb, masked, (a4,))
     received_b = move(other_b, dc=1)
-    done = pack(5, 2, other_b)
+    done = pack(3, 2, other_b)
     b1, b2, b3, b4, home_b = mix(own_b, received_b, (done,))
-    ring_b = back(b4)
-    done = hop(a2, ring_a, (b4,))
-    ring_a = back(done)
-    done = hop(b3, ring_b, (done,))
-    ring_b = back(done)
-    done = hop(a1, ring_a, (done,))
-    ring_a = back(done)
-    done = hop(b2, ring_b, (done,))
-    ring_b = back(done)
+    from_b3, from_b4, from_b1 = back(b3, 1), back(b4, 2), back(b1, 1)
+    done = hop(a2, from_a3, from_a4, (b4,))
+    from_a2 = back(done, 2)
+    done = pack(5, 2, done)
+    done = hop(b2, from_b3, from_b4, (done,))
+    a1, done = lax.optimization_barrier((a1, done))
+    from_b2, from_a1 = back(done, 2), back(a1, 1)
     done = pack(7, 1, done)
-    done = hop(b1, ring_b, (done,))
-    ring_b = back(done)
     order_after = jax.ShapeDtypeStruct((8, 128), F32)
     act, done = call(
         act_join_kernel,
@@ -517,9 +503,8 @@
         sum_kernel,
         0,
         (jax.ShapeDtypeStruct((32, d), BF16), jax.ShapeDtypeStruct((32, d), F32)),
-        (ring_a, home_a, ring_b, home_b),
-        4 * 32 * d,
-        after=(early,),
+        (from_a1, from_a2, home_a, from_b1, from_b2, home_b),
+        6 * 32 * d,
     )
     to_x, kept = call(
         sum_core_kernel,

time: 166 us -> 175 us (1.054)
  the two profiles are of different devices: /device:TPU:8 before, /device:TPU:30 now
where the time goes in v5:
time: 175 us
  waiting for transfers between devices  82.2 us (47%)
  starting transfers between devices  47.6 us (27%)
  Pallas kernels  37.6 us (21%)
  other arithmetic  3.53 us (2%)
  local copies, waits for them, and re-layouts  1.98 us (1%)
    ppermute x24, waiting for transfers between devices, move(): return lax.ppermute(x, 'tensor', tensor_perm(dz, dx, dc, split=True))  47.7 us
    pallas_call x28, Pallas kernels, call(): pl.pallas_call(run, out_shape=out_shape, in_specs=[SMEM] * n_scalar + [sp...  37.6 us
    ppermute x24, starting transfers between devices, move(): return lax.ppermute(x, 'tensor', tensor_perm(dz, dx, dc, split=True))  36.8 us
    ppermute x7, waiting for transfers between devices, move_dp(): return lax.ppermute(x, 'dp', dp_perm(dx, dy))  34.5 us
    ppermute x7, starting transfers between devices, move_dp(): return lax.ppermute(x, 'dp', dp_perm(dx, dy))  10.8 us
  transfers between devices with their start and end apart: 31, of which 10 were waited for; matrix products, arithmetic and copies ran while one was open for 3% of the time, Pallas kernels for 18%

profile of v5, /device:TPU:30, one launch (start us, length us, event | category | flops | bytes accessed | tf_op | source)
XLA Modules:
  0.0 175.1 jit_solution(11142559825519362537)
XLA Ops:
  0.8 1.5 collective-permute-done.refs_1_
  2.3 0.9 copy-done.1
  3.2 3.3 %collective-permute-start.2 = (bf16[32,4096]{1,0:T(8,128)(2,1)S(1)}, bf16[32,4096]{1,0:T(8,128)(2,1)S(1)}, u32[]{:S(2)}, u32[]{:S(2)}) collective-permute-start(bf16[32,4096]{1,0:T(8,128)(2,1)S(1)} %shard_map.112), channel_id=1, source_target_pairs={{0,8},{1,25},{2,10},{3,27},{4,12},{5,29},{6,14},{7,31},{8,16},{9,1... | collective-permute-start | bytes 786440 | tf_op jit(solution)/shard_map/ppermute | solution.py:43
  6.6 1.9 %collective-permute-start.1 = (bf16[32,4096]{1,0:T(8,128)(2,1)S(1)}, bf16[32,4096]{1,0:T(8,128)(2,1)S(1)}, u32[]{:S(2)}, u32[]{:S(2)}) collective-permute-start(bf16[32,4096]{1,0:T(8,128)(2,1)S(1)} %shard_map.112), channel_id=1, source_target_pairs={{0,4},{1,29},{2,6},{3,31},{4,8},{5,1},{6,10},{7,3},{8,12},{9,5},{1... | collective-permute-start | bytes 786440 | tf_op jit(solution)/shard_map/ppermute | solution.py:43
  8.5 0.9 dynamic-slice_compare_fusion
  10.2 1.0 convert_reduce_fusion
  11.2 7.9 %collective-permute-done.1.refs_2_ = bf16[32,4096]{1,0:T(8,128)(2,1)S(1)} collective-permute-done((bf16[32,4096]{1,0:T(8,128)(2,1)S(1)}, bf16[32,4096]{1,0:T(8,128)(2,1)S(1)}, u32[]{:S(2)}, u32[]{:S(2)}) %collective-permute-start.1) | collective-permute-done | bytes 262176 | tf_op jit(solution)/shard_map/ppermute | solution.py:43
  19.1 1.9 %select_reduce_fusion = s32[8,70]{0,1:T(8,128)S(1)} fusion(s32[112]{0:T(128)} %constant.79, s32[8,112]{1,0:T(8,128)S(1)} %get-tuple-element.61), kind=kLoop, calls=%fused_computation.2 | loop fusion | flops 187600 | bytes 6272 | tf_op jit(solution)/shard_map/reduce_sum | solution.py:385
  21.2 3.9 %collective-permute-start.3 = (bf16[16,4096]{1,0:T(8,128)(2,1)S(1)}, bf16[16,4096]{1,0:T(8,128)(2,1)S(1)}, u32[]{:S(2)}, u32[]{:S(2)}) collective-permute-start(bf16[16,4096]{1,0:T(8,128)(2,1)S(1)} %shard_map.115), channel_id=1, source_target_pairs={{0,8},{1,25},{2,10},{3,27},{4,12},{5,29},{6,14},{7,31},{8,16},{9,1... | collective-permute-start | bytes 393224 | tf_op jit(solution)/shard_map/ppermute | solution.py:43
  25.1 0.9 copy-done.3
  26.0 3.4 %shard_map.117.refs_3_.refs_1_ = bf16[4096,896]{1,0:T(8,128)(2,1)S(1)} custom-call(s32[1]{0:T(128)} %bitcast.refs_0_, bf16[4096,896]{1,0:T(8,128)(2,1)} %refs_1_.1, s32[64,448]{1,0:T(8,128)S(1)} %copy-done.3), custom_call_target="tpu_custom_call" | custom-call | flops 3670016 | bytes 7454724 | tf_op jit(solution)/shard_map/pallas_call | solution.py:62
  29.4 0.7 collective-permute-done.4.refs_4_
  30.3 1.5 collective-permute-start.6
  31.8 2.1 %collective-permute-start.9 = (bf16[32,4096]{1,0:T(8,128)(2,1)S(1)}, bf16[32,4096]{1,0:T(8,128)(2,1)S(1)}, u32[]{:S(2)}, u32[]{:S(2)}) collective-permute-start(bf16[32,4096]{1,0:T(8,128)(2,1)S(1)} %collective-permute-done.2.refs_0_.refs_3_), channel_id=1, source_target_pairs={{0,2},{1,3},{2,0},{3,1},{4,6},{5,7},{6,4},{7,5},{8,10},{9,11},{10,... | collective-permute-start | bytes 786440 | tf_op jit(solution)/shard_map/ppermute | solution.py:43
  33.9 1.4 collective-permute-start.8
  35.3 2.1 %collective-permute-start.10 = (bf16[32,4096]{1,0:T(8,128)(2,1)S(1)}, bf16[32,4096]{1,0:T(8,128)(2,1)S(1)}, u32[]{:S(2)}, u32[]{:S(2)}) collective-permute-start(bf16[32,4096]{1,0:T(8,128)(2,1)S(1)} %collective-permute-done.4.refs_4_), channel_id=1, source_target_pairs={{0,2},{1,3},{2,0},{3,1},{4,6},{5,7},{6,4},{7,5},{8,10},{9,11},{10,... | collective-permute-start | bytes 786440 | tf_op jit(solution)/shard_map/ppermute | solution.py:43
  37.5 0.8 collective-permute-done.6.refs_0_
  38.3 1.4 collective-permute-start.7
  39.7 17.7 %collective-permute-done.7.refs_1_ = bf16[16,4096]{1,0:T(8,128)(2,1)S(1)} collective-permute-done((bf16[16,4096]{1,0:T(8,128)(2,1)S(1)}, bf16[16,4096]{1,0:T(8,128)(2,1)S(1)}, u32[]{:S(2)}, u32[]{:S(2)}) %collective-permute-start.7) | collective-permute-done | bytes 131104 | tf_op jit(solution)/shard_map/ppermute | solution.py:43
  57.6 3.9 %shard_map.120 = (bf16[16,16,896]{2,1,0:T(8,128)(2,1)S(1)}, bf16[256,896]{1,0:T(8,128)(2,1)S(1)}) custom-call(s32[32]{0:T(128)S(1)} %fusion.8.refs_0_, bf16[128,4096]{1,0:T(8,128)(2,1)S(1)} %shard_map.118.refs_1_.refs_5_, bf16[128,4096]{1,0:T(8,128)(2,1)S(1)} %collective-permute-done.5.refs_2_.refs_7_, bf16[4096,896]{1,0:T(8,128)(2,1)S(1)} %shard_map.117.refs_3_.refs_1_, ...), custom_call_target="tpu_custom_call" | custom-call | flops 1879048192 | bytes 10354816 | tf_op jit(solution)/shard_map/pallas_call | solution.py:62
  61.5 3.8 %shard_map.122 = (f32[128,4096]{1,0:T(8,128)S(1)}, bf16[128,4096]{1,0:T(8,128)(2,1)S(1)}) custom-call(bf16[256,896]{1,0:T(8,128)(2,1)S(1)} %get-tuple-element.71.refs_0_.refs_3_, bf16[4096,896]{1,0:T(8,128)(2,1)S(1)} %shard_map.117.refs_3_.refs_1_), custom_call_target="tpu_custom_call" | custom-call | flops 1879048192 | bytes 7798784 | tf_op jit(solution)/shard_map/pallas_call | solution.py:62
  65.2 0.8 collective-permute-start.12
  66.0 3.9 %shard_map.123 = (bf16[16,16,896]{2,1,0:T(8,128)(2,1)S(1)}, bf16[256,896]{1,0:T(8,128)(2,1)S(1)}) custom-call(s32[32]{0:T(128)S(1)} %fusion.8.refs_0_, bf16[128,4096]{1,0:T(8,128)(2,1)S(1)} %shard_map.121.refs_1_.refs_6_, bf16[128,4096]{1,0:T(8,128)(2,1)S(1)} %collective-permute-done.11.refs_2_.refs_8_, bf16[4096,896]{1,0:T(8,128)(2,1)S(1)} %shard_map.117.refs_3_.refs_1_, ...), custom_call_target="tpu_custom_call" | custom-call | flops 1879048192 | bytes 10354816 | tf_op jit(solution)/shard_map/pallas_call | solution.py:62
  69.8 1.7 shard_map.124.refs_9_
  71.6 3.2 %shard_map.125 = (bf16[35,64,128]{2,1,0:T(8,128)(2,1)S(1)}, bf16[35,64,128]{2,1,0:T(8,128)(2,1)S(1)}) custom-call(s32[8]{0:T(128)S(1)} %and_add_fusion.refs_0_, s32[8,70]{1,0:T(8,128)S(1)} %broadcast_add_fusion.refs_1_, s32[8]{0:T(128)S(1)} %get-tuple-element.76.refs_2_, bf16[256,896]{1,0:T(8,128)(2,1)S(1)} %get-tuple-element.71.refs_0_.refs_3_, ...), custom_call_target="tpu_custom_call" | custom-call | flops 939524096 | bytes 5114112 | tf_op jit(solution)/shard_map/pallas_call | solution.py:62
  75.0 3.8 %shard_map.127 = (f32[128,4096]{1,0:T(8,128)S(1)}, bf16[128,4096]{1,0:T(8,128)(2,1)S(1)}) custom-call(bf16[256,896]{1,0:T(8,128)(2,1)S(1)} %get-tuple-element.77.refs_4_.refs_0_, bf16[4096,896]{1,0:T(8,128)(2,1)S(1)} %shard_map.117.refs_3_.refs_1_, bf16[16,4096]{1,0:T(8,128)(2,1)S(1)} %get-tuple-element.81.refs_2_), custom_call_target="tpu_custom_call" | custom-call | flops 1879048192 | bytes 7798784 | tf_op jit(solution)/shard_map/pallas_call | solution.py:62
  78.9 3.0 %collective-permute-start.16 = (bf16[32,4096]{1,0:T(8,128)(2,1)S(1)}, bf16[32,4096]{1,0:T(8,128)(2,1)S(1)}, u32[]{:S(2)}, u32[]{:S(2)}) collective-permute-start(bf16[32,4096]{1,0:T(8,128)(2,1)S(1)} %get-tuple-element.89), channel_id=1, source_target_pairs={{0,28},{1,5},{2,30},{3,7},{4,0},{5,9},{6,2},{7,11},{8,4},{9,13},{1... | collective-permute-start | bytes 786440 | tf_op jit(solution)/shard_map/ppermute | solution.py:43
  81.8 2.8 %shard_map.128 = (bf16[35,64,128]{2,1,0:T(8,128)(2,1)S(1)}, bf16[35,64,128]{2,1,0:T(8,128)(2,1)S(1)}) custom-call(s32[8]{0:T(128)S(1)} %and_add_fusion.refs_0_, s32[8,70]{1,0:T(8,128)S(1)} %broadcast_add_fusion.refs_1_, s32[8]{0:T(128)S(1)} %get-tuple-element.76.refs_2_, bf16[256,896]{1,0:T(8,128)(2,1)S(1)} %get-tuple-element.71.refs_0_.refs_3_, ...), custom_call_target="tpu_custom_call" | custom-call | flops 939524096 | bytes 5114112 | tf_op jit(solution)/shard_map/pallas_call | solution.py:62
  84.9 0.7 collective-permute-start.14
  85.6 3.6 %collective-permute-start.20 = (bf16[32,4096]{1,0:T(8,128)(2,1)S(1)}, bf16[32,4096]{1,0:T(8,128)(2,1)S(1)}, u32[]{:S(2)}, u32[]{:S(2)}) collective-permute-start(bf16[32,4096]{1,0:T(8,128)(2,1)S(1)} %get-tuple-element.95), channel_id=1, source_target_pairs={{0,28},{1,5},{2,30},{3,7},{4,0},{5,9},{6,2},{7,11},{8,4},{9,13},{1... | collective-permute-start | bytes 786440 | tf_op jit(solution)/shard_map/ppermute | solution.py:43
  89.2 1.4 collective-permute-start.15
  90.7 5.2 %collective-permute-done.17.refs_2_ = bf16[16,4096]{1,0:T(8,128)(2,1)S(1)} collective-permute-done((bf16[16,4096]{1,0:T(8,128)(2,1)S(1)}, bf16[16,4096]{1,0:T(8,128)(2,1)S(1)}, u32[]{:S(2)}, u32[]{:S(2)}) %collective-permute-start.17) | collective-permute-done | bytes 131104 | tf_op jit(solution)/shard_map/ppermute | solution.py:43
  96.5 3.5 %collective-permute-start.26 = (bf16[35,64,128]{2,1,0:T(8,128)(2,1)S(1)}, bf16[35,64,128]{2,1,0:T(8,128)(2,1)S(1)}, u32[]{:S(2)}, u32[]{:S(2)}) collective-permute-start(bf16[35,64,128]{2,1,0:T(8,128)(2,1)S(1)} %get-tuple-element.102), channel_id=1, source_target_pairs={{0,192},{32,224},{64,128},{96,160},{128,64},{160,96},{192,0},{224,... | collective-permute-start | bytes 1720328 | tf_op jit(solution)/shard_map/ppermute | solution.py:47
  100.1 2.8 %shard_map.131 = (bf16[35,64,128]{2,1,0:T(8,128)(2,1)S(1)}, bf16[35,64,128]{2,1,0:T(8,128)(2,1)S(1)}) custom-call(s32[8]{0:T(128)S(1)} %and_add_fusion.refs_0_, s32[8,70]{1,0:T(8,128)S(1)} %broadcast_add_fusion.refs_1_, s32[8]{0:T(128)S(1)} %get-tuple-element.76.refs_2_, bf16[256,896]{1,0:T(8,128)(2,1)S(1)} %get-tuple-element.71.refs_0_.refs_3_, ...), custom_call_target="tpu_custom_call" | custom-call | flops 939524096 | bytes 5114112 | tf_op jit(solution)/shard_map/pallas_call | solution.py:62
  103.0 3.3 %collective-permute-start.19 = (bf16[32,4096]{1,0:T(8,128)(2,1)S(1)}, bf16[32,4096]{1,0:T(8,128)(2,1)S(1)}, u32[]{:S(2)}, u32[]{:S(2)}) collective-permute-start(bf16[32,4096]{1,0:T(8,128)(2,1)S(1)} %shard_map.130.refs_9_), channel_id=1, source_target_pairs={{0,24},{1,9},{2,26},{3,11},{4,28},{5,13},{6,30},{7,15},{8,0},{9,17... | collective-permute-start | bytes 786440 | tf_op jit(solution)/shard_map/ppermute | solution.py:43
  106.4 4.5 %collective-permute-start.18 = (bf16[32,4096]{1,0:T(8,128)(2,1)S(1)}, bf16[32,4096]{1,0:T(8,128)(2,1)S(1)}, u32[]{:S(2)}, u32[]{:S(2)}) collective-permute-start(bf16[32,4096]{1,0:T(8,128)(2,1)S(1)} %get-tuple-element.93), channel_id=1, source_target_pairs={{0,28},{1,5},{2,30},{3,7},{4,0},{5,9},{6,2},{7,11},{8,4},{9,13},{1... | collective-permute-start | bytes 786440 | tf_op jit(solution)/shard_map/ppermute | solution.py:43
  110.9 1.2 collective-permute-start.21
  112.2 5.2 %collective-permute-done.18.refs_0_ = bf16[32,4096]{1,0:T(8,128)(2,1)S(1)} collective-permute-done((bf16[32,4096]{1,0:T(8,128)(2,1)S(1)}, bf16[32,4096]{1,0:T(8,128)(2,1)S(1)}, u32[]{:S(2)}, u32[]{:S(2)}) %collective-permute-start.18) | collective-permute-done | bytes 262176 | tf_op jit(solution)/shard_map/ppermute | solution.py:43
  117.3 6.1 %collective-permute-done.21.refs_4_ = bf16[32,4096]{1,0:T(8,128)(2,1)S(1)} collective-permute-done((bf16[32,4096]{1,0:T(8,128)(2,1)S(1)}, bf16[32,4096]{1,0:T(8,128)(2,1)S(1)}, u32[]{:S(2)}, u32[]{:S(2)}) %collective-permute-start.21) | collective-permute-done | bytes 262176 | tf_op jit(solution)/shard_map/ppermute | solution.py:43
  123.8 0.9 collective-permute-start.27
  124.7 2.5 %collective-permute-start.28 = (bf16[35,64,128]{2,1,0:T(8,128)(2,1)S(1)}, bf16[35,64,128]{2,1,0:T(8,128)(2,1)S(1)}, u32[]{:S(2)}, u32[]{:S(2)}) collective-permute-start(bf16[35,64,128]{2,1,0:T(8,128)(2,1)S(1)} %get-tuple-element.104), channel_id=1, source_target_pairs={{0,32},{32,64},{64,96},{96,0},{128,160},{160,192},{192,224},{224,1... | collective-permute-start | bytes 1720328 | tf_op jit(solution)/shard_map/ppermute | solution.py:47
  127.2 2.2 %collective-permute-start.30 = (bf16[35,64,128]{2,1,0:T(8,128)(2,1)S(1)}, bf16[35,64,128]{2,1,0:T(8,128)(2,1)S(1)}, u32[]{:S(2)}, u32[]{:S(2)}) collective-permute-start(bf16[35,64,128]{2,1,0:T(8,128)(2,1)S(1)} %get-tuple-element.105), channel_id=1, source_target_pairs={{0,64},{32,96},{64,0},{96,32},{128,192},{160,224},{192,128},{224,1... | collective-permute-start | bytes 1720328 | tf_op jit(solution)/shard_map/ppermute | solution.py:47
  129.4 0.9 collective-permute-start.29
  130.4 34.5 %collective-permute-done.25.refs_2_ = bf16[35,64,128]{2,1,0:T(8,128)(2,1)S(1)} collective-permute-done((bf16[35,64,128]{2,1,0:T(8,128)(2,1)S(1)}, bf16[35,64,128]{2,1,0:T(8,128)(2,1)S(1)}, u32[]{:S(2)}, u32[]{:S(2)}) %collective-permute-start.25) | collective-permute-done | bytes 573472 | tf_op jit(solution)/shard_map/ppermute | solution.py:47
  164.9 1.7 shard_map.133.refs_3_.refs_0_
  166.6 1.6 shard_map.134
  168.7 2.6 %collective-permute-done.23.refs_1_ = bf16[16,4096]{1,0:T(8,128)(2,1)S(1)} collective-permute-done((bf16[16,4096]{1,0:T(8,128)(2,1)S(1)}, bf16[16,4096]{1,0:T(8,128)(2,1)S(1)}, u32[]{:S(2)}, u32[]{:S(2)}) %collective-permute-start.23) | collective-permute-done | bytes 131104 | tf_op jit(solution)/shard_map/ppermute | solution.py:43
  172.0 2.8 %shard_map.139 = f32[512,896]{1,0:T(8,128)} custom-call(s32[1]{0:T(128)} %bitcast.3.refs_0_, s32[8,70]{1,0:T(8,128)S(1)} %broadcast_add_fusion.refs_1_, f32[35,64,128]{2,1,0:T(8,128)S(1)} %shard_map.138.refs_2_, bf16[35,64,128]{2,1,0:T(8,128)(2,1)S(1)} %collective-permute-done.28.refs_3_, bf16[35,64,128]{2,1,0:T(8,128)(2,1)S(1)} %collective-permute-done.29.refs_4_, ...), custom_call_target="tpu_custom_call" | custom-call | flops 2293760 | bytes 2869444 | tf_op jit(solution)/shard_map/pallas_call | solution.py:62
  (58 shorter events, 4.5 us)
Async XLA Ops:
  0.6 1.6 collective-permute-start
  2.3 0.9 copy-start.1
  3.2 17.9 %collective-permute-start.2 = (bf16[32,4096]{1,0:T(8,128)(2,1)S(1)}, bf16[32,4096]{1,0:T(8,128)(2,1)S(1)}, u32[]{:S(2)}, u32[]{:S(2)}) collective-permute-start(bf16[32,4096]{1,0:T(8,128)(2,1)S(1)} %shard_map.112), channel_id=1, source_target_pairs={{0,8},{1,25},{2,10},{3,27},{4,12},{5,29},{6,14},{7,31},{8,16},{9,1... | collective-permute-start | bytes 786440 | tf_op jit(solution)/shard_map/ppermute | solution.py:43
  6.6 12.6 %collective-permute-start.1 = (bf16[32,4096]{1,0:T(8,128)(2,1)S(1)}, bf16[32,4096]{1,0:T(8,128)(2,1)S(1)}, u32[]{:S(2)}, u32[]{:S(2)}) collective-permute-start(bf16[32,4096]{1,0:T(8,128)(2,1)S(1)} %shard_map.112), channel_id=1, source_target_pairs={{0,4},{1,29},{2,6},{3,31},{4,8},{5,1},{6,10},{7,3},{8,12},{9,5},{1... | collective-permute-start | bytes 786440 | tf_op jit(solution)/shard_map/ppermute | solution.py:43
  21.1 9.0 %collective-permute-start.4 = (bf16[32,4096]{1,0:T(8,128)(2,1)S(1)}, bf16[32,4096]{1,0:T(8,128)(2,1)S(1)}, u32[]{:S(2)}, u32[]{:S(2)}) collective-permute-start(bf16[32,4096]{1,0:T(8,128)(2,1)S(1)} %collective-permute-done.2.refs_0_.refs_3_), channel_id=1, source_target_pairs={{0,4},{1,29},{2,6},{3,31},{4,8},{5,1},{6,10},{7,3},{8,12},{9,5},{1... | collective-permute-start | bytes 786440 | tf_op jit(solution)/shard_map/ppermute | solution.py:43
  21.2 9.0 %collective-permute-start.3 = (bf16[16,4096]{1,0:T(8,128)(2,1)S(1)}, bf16[16,4096]{1,0:T(8,128)(2,1)S(1)}, u32[]{:S(2)}, u32[]{:S(2)}) collective-permute-start(bf16[16,4096]{1,0:T(8,128)(2,1)S(1)} %shard_map.115), channel_id=1, source_target_pairs={{0,8},{1,25},{2,10},{3,27},{4,12},{5,29},{6,14},{7,31},{8,16},{9,1... | collective-permute-start | bytes 393224 | tf_op jit(solution)/shard_map/ppermute | solution.py:43
  25.1 0.9 copy-start.3
  26.0 4.1 %copy-start.2 = (bf16[16,4096]{1,0:T(8,128)(2,1)S(1)}, bf16[16,4096]{1,0:T(8,128)(2,1)}, u32[]{:S(2)}) copy-start(bf16[16,4096]{1,0:T(8,128)(2,1)} %refs_0_.3) | copy-start | bytes 393220
  29.4 28.2 %copy-start = (bf16[512,896]{1,0:T(8,128)(2,1)S(1)}, bf16[512,896]{1,0:T(8,128)(2,1)}, u32[]{:S(2)}) copy-start(bf16[512,896]{1,0:T(8,128)(2,1)} %param.12) | copy-start | bytes 2752516
  30.2 27.4 %collective-permute-start.5 = (bf16[128,4096]{1,0:T(8,128)(2,1)S(1)}, bf16[128,4096]{1,0:T(8,128)(2,1)S(1)}, u32[]{:S(2)}, u32[]{:S(2)}) collective-permute-start(bf16[128,4096]{1,0:T(8,128)(2,1)S(1)} %shard_map.118.refs_1_.refs_5_), channel_id=1, source_target_pairs={{0,1},{1,0},{2,3},{3,2},{4,5},{5,4},{6,7},{7,6},{8,9},{9,8},{10,11... | collective-permute-start | bytes 3145736 | tf_op jit(solution)/shard_map/ppermute | solution.py:43
  30.3 8.0 %collective-permute-start.6 = (bf16[16,4096]{1,0:T(8,128)(2,1)S(1)}, bf16[16,4096]{1,0:T(8,128)(2,1)S(1)}, u32[]{:S(2)}, u32[]{:S(2)}) collective-permute-start(bf16[16,4096]{1,0:T(8,128)(2,1)S(1)} %copy-done.2), channel_id=1, source_target_pairs={{0,2},{1,3},{2,0},{3,1},{4,6},{5,7},{6,4},{7,5},{8,10},{9,11},{10,... | collective-permute-start | bytes 393224 | tf_op jit(solution)/shard_map/ppermute | solution.py:43
  31.8 25.6 %collective-permute-start.9 = (bf16[32,4096]{1,0:T(8,128)(2,1)S(1)}, bf16[32,4096]{1,0:T(8,128)(2,1)S(1)}, u32[]{:S(2)}, u32[]{:S(2)}) collective-permute-start(bf16[32,4096]{1,0:T(8,128)(2,1)S(1)} %collective-permute-done.2.refs_0_.refs_3_), channel_id=1, source_target_pairs={{0,2},{1,3},{2,0},{3,1},{4,6},{5,7},{6,4},{7,5},{8,10},{9,11},{10,... | collective-permute-start | bytes 786440 | tf_op jit(solution)/shard_map/ppermute | solution.py:43
  33.9 23.5 %collective-permute-start.8 = (bf16[32,4096]{1,0:T(8,128)(2,1)S(1)}, bf16[32,4096]{1,0:T(8,128)(2,1)S(1)}, u32[]{:S(2)}, u32[]{:S(2)}) collective-permute-start(bf16[32,4096]{1,0:T(8,128)(2,1)S(1)} %collective-permute-done.1.refs_2_), channel_id=1, source_target_pairs={{0,2},{1,3},{2,0},{3,1},{4,6},{5,7},{6,4},{7,5},{8,10},{9,11},{10,... | collective-permute-start | bytes 786440 | tf_op jit(solution)/shard_map/ppermute | solution.py:43
  35.3 22.1 %collective-permute-start.10 = (bf16[32,4096]{1,0:T(8,128)(2,1)S(1)}, bf16[32,4096]{1,0:T(8,128)(2,1)S(1)}, u32[]{:S(2)}, u32[]{:S(2)}) collective-permute-start(bf16[32,4096]{1,0:T(8,128)(2,1)S(1)} %collective-permute-done.4.refs_4_), channel_id=1, source_target_pairs={{0,2},{1,3},{2,0},{3,1},{4,6},{5,7},{6,4},{7,5},{8,10},{9,11},{10,... | collective-permute-start | bytes 786440 | tf_op jit(solution)/shard_map/ppermute | solution.py:43
  38.3 19.1 %collective-permute-start.7 = (bf16[16,4096]{1,0:T(8,128)(2,1)S(1)}, bf16[16,4096]{1,0:T(8,128)(2,1)S(1)}, u32[]{:S(2)}, u32[]{:S(2)}) collective-permute-start(bf16[16,4096]{1,0:T(8,128)(2,1)S(1)} %collective-permute-done.3.refs_1_), channel_id=1, source_target_pairs={{0,2},{1,3},{2,0},{3,1},{4,6},{5,7},{6,4},{7,5},{8,10},{9,11},{10,... | collective-permute-start | bytes 393224 | tf_op jit(solution)/shard_map/ppermute | solution.py:43
  57.5 8.5 %collective-permute-start.11 = (bf16[128,4096]{1,0:T(8,128)(2,1)S(1)}, bf16[128,4096]{1,0:T(8,128)(2,1)S(1)}, u32[]{:S(2)}, u32[]{:S(2)}) collective-permute-start(bf16[128,4096]{1,0:T(8,128)(2,1)S(1)} %shard_map.121.refs_1_.refs_6_), channel_id=1, source_target_pairs={{0,1},{1,0},{2,3},{3,2},{4,5},{5,4},{6,7},{7,6},{8,9},{9,8},{10,11... | collective-permute-start | bytes 3145736 | tf_op jit(solution)/shard_map/ppermute | solution.py:43
  65.2 9.5 %collective-permute-start.12 = (bf16[128,4096]{1,0:T(8,128)(2,1)S(1)}, bf16[128,4096]{1,0:T(8,128)(2,1)S(1)}, u32[]{:S(2)}, u32[]{:S(2)}) collective-permute-start(bf16[128,4096]{1,0:T(8,128)(2,1)S(1)} %get-tuple-element.72.refs_5_.refs_9_), channel_id=1, source_target_pairs={{0,1},{1,0},{2,3},{3,2},{4,5},{5,4},{6,7},{7,6},{8,9},{9,8},{10,11... | collective-permute-start | bytes 3145736 | tf_op jit(solution)/shard_map/ppermute | solution.py:43
  78.8 5.9 %collective-permute-start.13 = (bf16[128,4096]{1,0:T(8,128)(2,1)S(1)}, bf16[128,4096]{1,0:T(8,128)(2,1)S(1)}, u32[]{:S(2)}, u32[]{:S(2)}) collective-permute-start(bf16[128,4096]{1,0:T(8,128)(2,1)S(1)} %get-tuple-element.83.refs_9_), channel_id=1, source_target_pairs={{0,1},{1,0},{2,3},{3,2},{4,5},{5,4},{6,7},{7,6},{8,9},{9,8},{10,11... | collective-permute-start | bytes 3145736 | tf_op jit(solution)/shard_map/ppermute | solution.py:43
  78.9 17.6 %collective-permute-start.16 = (bf16[32,4096]{1,0:T(8,128)(2,1)S(1)}, bf16[32,4096]{1,0:T(8,128)(2,1)S(1)}, u32[]{:S(2)}, u32[]{:S(2)}) collective-permute-start(bf16[32,4096]{1,0:T(8,128)(2,1)S(1)} %get-tuple-element.89), channel_id=1, source_target_pairs={{0,28},{1,5},{2,30},{3,7},{4,0},{5,9},{6,2},{7,11},{8,4},{9,13},{1... | collective-permute-start | bytes 786440 | tf_op jit(solution)/shard_map/ppermute | solution.py:43
  84.9 21.4 %collective-permute-start.14 = (bf16[32,4096]{1,0:T(8,128)(2,1)S(1)}, bf16[32,4096]{1,0:T(8,128)(2,1)S(1)}, u32[]{:S(2)}, u32[]{:S(2)}) collective-permute-start(bf16[32,4096]{1,0:T(8,128)(2,1)S(1)} %get-tuple-element.86), channel_id=1, source_target_pairs={{0,28},{1,5},{2,30},{3,7},{4,0},{5,9},{6,2},{7,11},{8,4},{9,13},{1... | collective-permute-start | bytes 786440 | tf_op jit(solution)/shard_map/ppermute | solution.py:43
  85.6 25.3 %collective-permute-start.20 = (bf16[32,4096]{1,0:T(8,128)(2,1)S(1)}, bf16[32,4096]{1,0:T(8,128)(2,1)S(1)}, u32[]{:S(2)}, u32[]{:S(2)}) collective-permute-start(bf16[32,4096]{1,0:T(8,128)(2,1)S(1)} %get-tuple-element.95), channel_id=1, source_target_pairs={{0,28},{1,5},{2,30},{3,7},{4,0},{5,9},{6,2},{7,11},{8,4},{9,13},{1... | collective-permute-start | bytes 786440 | tf_op jit(solution)/shard_map/ppermute | solution.py:43
  89.2 6.6 %collective-permute-start.17 = (bf16[16,4096]{1,0:T(8,128)(2,1)S(1)}, bf16[16,4096]{1,0:T(8,128)(2,1)S(1)}, u32[]{:S(2)}, u32[]{:S(2)}) collective-permute-start(bf16[16,4096]{1,0:T(8,128)(2,1)S(1)} %get-tuple-element.81.refs_2_), channel_id=1, source_target_pairs={{0,24},{1,9},{2,26},{3,11},{4,28},{5,13},{6,30},{7,15},{8,0},{9,17... | collective-permute-start | bytes 393224 | tf_op jit(solution)/shard_map/ppermute | solution.py:43
  89.2 13.7 %collective-permute-start.15 = (bf16[16,4096]{1,0:T(8,128)(2,1)S(1)}, bf16[16,4096]{1,0:T(8,128)(2,1)S(1)}, u32[]{:S(2)}, u32[]{:S(2)}) collective-permute-start(bf16[16,4096]{1,0:T(8,128)(2,1)S(1)} %get-tuple-element.87.refs_3_), channel_id=1, source_target_pairs={{0,24},{1,9},{2,26},{3,11},{4,28},{5,13},{6,30},{7,15},{8,0},{9,17... | collective-permute-start | bytes 393224 | tf_op jit(solution)/shard_map/ppermute | solution.py:43
  95.8 28.9 %collective-permute-start.24 = (bf16[35,64,128]{2,1,0:T(8,128)(2,1)S(1)}, bf16[35,64,128]{2,1,0:T(8,128)(2,1)S(1)}, u32[]{:S(2)}, u32[]{:S(2)}) collective-permute-start(bf16[35,64,128]{2,1,0:T(8,128)(2,1)S(1)} %shard_map.124.refs_9_), channel_id=1, source_target_pairs={{0,160},{32,192},{64,224},{96,128},{128,32},{160,64},{192,96},{224... | collective-permute-start | bytes 1720328 | tf_op jit(solution)/shard_map/ppermute | solution.py:47
  96.5 30.7 %collective-permute-start.26 = (bf16[35,64,128]{2,1,0:T(8,128)(2,1)S(1)}, bf16[35,64,128]{2,1,0:T(8,128)(2,1)S(1)}, u32[]{:S(2)}, u32[]{:S(2)}) collective-permute-start(bf16[35,64,128]{2,1,0:T(8,128)(2,1)S(1)} %get-tuple-element.102), channel_id=1, source_target_pairs={{0,192},{32,224},{64,128},{96,160},{128,64},{160,96},{192,0},{224,... | collective-permute-start | bytes 1720328 | tf_op jit(solution)/shard_map/ppermute | solution.py:47
  103.0 9.2 %collective-permute-start.19 = (bf16[32,4096]{1,0:T(8,128)(2,1)S(1)}, bf16[32,4096]{1,0:T(8,128)(2,1)S(1)}, u32[]{:S(2)}, u32[]{:S(2)}) collective-permute-start(bf16[32,4096]{1,0:T(8,128)(2,1)S(1)} %shard_map.130.refs_9_), channel_id=1, source_target_pairs={{0,24},{1,9},{2,26},{3,11},{4,28},{5,13},{6,30},{7,15},{8,0},{9,17... | collective-permute-start | bytes 786440 | tf_op jit(solution)/shard_map/ppermute | solution.py:43
  106.4 10.9 %collective-permute-start.18 = (bf16[32,4096]{1,0:T(8,128)(2,1)S(1)}, bf16[32,4096]{1,0:T(8,128)(2,1)S(1)}, u32[]{:S(2)}, u32[]{:S(2)}) collective-permute-start(bf16[32,4096]{1,0:T(8,128)(2,1)S(1)} %get-tuple-element.93), channel_id=1, source_target_pairs={{0,28},{1,5},{2,30},{3,7},{4,0},{5,9},{6,2},{7,11},{8,4},{9,13},{1... | collective-permute-start | bytes 786440 | tf_op jit(solution)/shard_map/ppermute | solution.py:43
  110.9 12.5 %collective-permute-start.21 = (bf16[32,4096]{1,0:T(8,128)(2,1)S(1)}, bf16[32,4096]{1,0:T(8,128)(2,1)S(1)}, u32[]{:S(2)}, u32[]{:S(2)}) collective-permute-start(bf16[32,4096]{1,0:T(8,128)(2,1)S(1)} %shard_map.132.refs_9_), channel_id=1, source_target_pairs={{0,24},{1,9},{2,26},{3,11},{4,28},{5,13},{6,30},{7,15},{8,0},{9,17... | collective-permute-start | bytes 786440 | tf_op jit(solution)/shard_map/ppermute | solution.py:43
  123.6 5.8 %collective-permute-start.22 = (bf16[32,4096]{1,0:T(8,128)(2,1)S(1)}, bf16[32,4096]{1,0:T(8,128)(2,1)S(1)}, u32[]{:S(2)}, u32[]{:S(2)}) collective-permute-start(bf16[32,4096]{1,0:T(8,128)(2,1)S(1)} %get-tuple-element.98), channel_id=1, source_target_pairs={{0,1},{1,0},{2,3},{3,2},{4,5},{5,4},{6,7},{7,6},{8,9},{9,8},{10,11... | collective-permute-start | bytes 786440 | tf_op jit(solution)/shard_map/ppermute | solution.py:43
  123.7 41.2 %collective-permute-start.25 = (bf16[35,64,128]{2,1,0:T(8,128)(2,1)S(1)}, bf16[35,64,128]{2,1,0:T(8,128)(2,1)S(1)}, u32[]{:S(2)}, u32[]{:S(2)}) collective-permute-start(bf16[35,64,128]{2,1,0:T(8,128)(2,1)S(1)} %get-tuple-element.79.refs_2_), channel_id=1, source_target_pairs={{0,96},{32,0},{64,32},{96,64},{128,224},{160,128},{192,160},{224,1... | collective-permute-start | bytes 1720328 | tf_op jit(solution)/shard_map/ppermute | solution.py:47
  123.8 44.4 %collective-permute-start.27 = (bf16[35,64,128]{2,1,0:T(8,128)(2,1)S(1)}, bf16[35,64,128]{2,1,0:T(8,128)(2,1)S(1)}, u32[]{:S(2)}, u32[]{:S(2)}) collective-permute-start(bf16[35,64,128]{2,1,0:T(8,128)(2,1)S(1)} %get-tuple-element.84.refs_2_), channel_id=1, source_target_pairs={{0,224},{32,128},{64,160},{96,192},{128,96},{160,0},{192,32},{224,... | collective-permute-start | bytes 1720328 | tf_op jit(solution)/shard_map/ppermute | solution.py:47
  124.7 47.3 %collective-permute-start.28 = (bf16[35,64,128]{2,1,0:T(8,128)(2,1)S(1)}, bf16[35,64,128]{2,1,0:T(8,128)(2,1)S(1)}, u32[]{:S(2)}, u32[]{:S(2)}) collective-permute-start(bf16[35,64,128]{2,1,0:T(8,128)(2,1)S(1)} %get-tuple-element.104), channel_id=1, source_target_pairs={{0,32},{32,64},{64,96},{96,0},{128,160},{160,192},{192,224},{224,1... | collective-permute-start | bytes 1720328 | tf_op jit(solution)/shard_map/ppermute | solution.py:47
  127.2 44.8 %collective-permute-start.30 = (bf16[35,64,128]{2,1,0:T(8,128)(2,1)S(1)}, bf16[35,64,128]{2,1,0:T(8,128)(2,1)S(1)}, u32[]{:S(2)}, u32[]{:S(2)}) collective-permute-start(bf16[35,64,128]{2,1,0:T(8,128)(2,1)S(1)} %get-tuple-element.105), channel_id=1, source_target_pairs={{0,64},{32,96},{64,0},{96,32},{128,192},{160,224},{192,128},{224,1... | collective-permute-start | bytes 1720328 | tf_op jit(solution)/shard_map/ppermute | solution.py:47
  129.4 42.6 %collective-permute-start.29 = (bf16[35,64,128]{2,1,0:T(8,128)(2,1)S(1)}, bf16[35,64,128]{2,1,0:T(8,128)(2,1)S(1)}, u32[]{:S(2)}, u32[]{:S(2)}) collective-permute-start(bf16[35,64,128]{2,1,0:T(8,128)(2,1)S(1)} %get-tuple-element.90.refs_3_), channel_id=1, source_target_pairs={{0,128},{32,160},{64,192},{96,224},{128,0},{160,32},{192,64},{224,... | collective-permute-start | bytes 1720328 | tf_op jit(solution)/shard_map/ppermute | solution.py:47
  164.9 6.5 %collective-permute-start.23 = (bf16[16,4096]{1,0:T(8,128)(2,1)S(1)}, bf16[16,4096]{1,0:T(8,128)(2,1)S(1)}, u32[]{:S(2)}, u32[]{:S(2)}) collective-permute-start(bf16[16,4096]{1,0:T(8,128)(2,1)S(1)} %get-tuple-element.100), channel_id=1, source_target_pairs={{0,2},{1,3},{2,0},{3,1},{4,6},{5,7},{6,4},{7,5},{8,10},{9,11},{10,... | collective-permute-start | bytes 393224 | tf_op jit(solution)/shard_map/ppermute | solution.py:43

commit v6 on v5

--- a/solution.py
+++ b/solution.py
@@ -175,8 +175,7 @@
         out[idx_ref[16 + n]] = b_ref[n]
 
 
-def last_kernel(kept, received, out, tick):
-    tick[...] = jnp.zeros_like(tick)
+def last_kernel(kept, received, out):
     out[...] = (kept[...] + received[...].astype(F32)).astype(BF16)
 
 
@@ -468,18 +467,18 @@
     done = pack(0, 1, other_a)
     done = pack(1, 2, done)
     a1, a2, a3, a4, home_a = mix(own_a, received_a, (done,))
-    from_a3, from_a4 = back(a3, 1), back(a4, 2)
+    from_a3, from_a4, from_a1 = back(a3, 1), back(a4, 2), back(a1, 1)
     own_b, other_b = xgrad(pb, masked, (a4,))
     received_b = move(other_b, dc=1)
-    done = pack(3, 2, other_b)
+    done = hop(a2, from_a3, from_a4, (other_b,))
+    from_a2 = back(done, 2)
+    done = pack(3, 2, done)
     b1, b2, b3, b4, home_b = mix(own_b, received_b, (done,))
-    from_b3, from_b4, from_b1 = back(b3, 1), back(b4, 2), back(b1, 1)
-    done = hop(a2, from_a3, from_a4, (b4,))
-    from_a2 = back(done, 2)
-    done = pack(5, 2, done)
+    from_b3, from_b4 = back(b3, 1), back(b4, 2)
+    done = pack(5, 2, b4)
     done = hop(b2, from_b3, from_b4, (done,))
-    a1, done = lax.optimization_barrier((a1, done))
-    from_b2, from_a1 = back(done, 2), back(a1, 1)
+    b1, done = lax.optimization_barrier((b1, done))
+    from_b2, from_b1 = back(done, 2), back(b1, 1)
     done = pack(7, 1, done)
     order_after = jax.ShapeDtypeStruct((8, 128), F32)
     act, done = call(
@@ -513,12 +512,8 @@
         (kept, move(to_core, dc=1)),
         32 * d,
     )
-    x_grad, done = call(
-        last_kernel,
-        0,
-        (jax.ShapeDtypeStruct((16, d), BF16), order_after),
-        (kept, move(to_x, dx=1)),
-        16 * d,
+    x_grad = call(
+        last_kernel, 0, jax.ShapeDtypeStruct((16, d), BF16), (kept, move(to_x, dx=1)), 16 * d
     )
 
     weight_grad = call(
@@ -531,7 +526,6 @@
             pltpu.VMEM((512, width), F32),
             pltpu.SemaphoreType.DMA((4,)),
         ),
-        after=(done,),
         out_space=pl.BlockSpec(memory_space=pl.ANY),
     )
     return (act.reshape(512, width), x_grad, weight_grad)

time: 175 us -> 177 us (1.011)
  the two profiles are of different devices: /device:TPU:30 before, /device:TPU:24 now
where the time goes in v6:
time: 177 us; the launch traced here: 176 us
  waiting for transfers between devices  74.7 us (42%)
  starting transfers between devices  56.8 us (32%)
  Pallas kernels  37.4 us (21%)
  other arithmetic  3.53 us (2%)
  local copies, waits for them, and re-layouts  1.98 us (1%)
    ppermute x24, starting transfers between devices, move(): return lax.ppermute(x, 'tensor', tensor_perm(dz, dx, dc, split=True))  46.7 us
    ppermute x24, waiting for transfers between devices, move(): return lax.ppermute(x, 'tensor', tensor_perm(dz, dx, dc, split=True))  40.4 us
    pallas_call x28, Pallas kernels, call(): pl.pallas_call(run, out_shape=out_shape, in_specs=[SMEM] * n_scalar + [sp...  37.4 us
    ppermute x7, waiting for transfers between devices, move_dp(): return lax.ppermute(x, 'dp', dp_perm(dx, dy))  34.3 us
    ppermute x7, starting transfers between devices, move_dp(): return lax.ppermute(x, 'dp', dp_perm(dx, dy))  10.2 us
  transfers between devices with their start and end apart: 31, of which 10 were waited for; matrix products, arithmetic and copies ran while one was open for 3% of the time, Pallas kernels for 18%

profile of v6, /device:TPU:24, one launch (start us, length us, event | category | flops | bytes accessed | tf_op | source)
XLA Modules:
  0.0 176.5 jit_solution(252912639057380481)
XLA Ops:
  0.8 1.5 collective-permute-done.refs_1_
  2.3 0.9 copy-done.1
  3.2 3.3 %collective-permute-start.2 = (bf16[32,4096]{1,0:T(8,128)(2,1)S(1)}, bf16[32,4096]{1,0:T(8,128)(2,1)S(1)}, u32[]{:S(2)}, u32[]{:S(2)}) collective-permute-start(bf16[32,4096]{1,0:T(8,128)(2,1)S(1)} %shard_map.112), channel_id=1, source_target_pairs={{0,8},{1,25},{2,10},{3,27},{4,12},{5,29},{6,14},{7,31},{8,16},{9,1... | collective-permute-start | bytes 786440 | tf_op jit(solution)/shard_map/ppermute | solution.py:43
  6.6 1.9 %collective-permute-start.1 = (bf16[32,4096]{1,0:T(8,128)(2,1)S(1)}, bf16[32,4096]{1,0:T(8,128)(2,1)S(1)}, u32[]{:S(2)}, u32[]{:S(2)}) collective-permute-start(bf16[32,4096]{1,0:T(8,128)(2,1)S(1)} %shard_map.112), channel_id=1, source_target_pairs={{0,4},{1,29},{2,6},{3,31},{4,8},{5,1},{6,10},{7,3},{8,12},{9,5},{1... | collective-permute-start | bytes 786440 | tf_op jit(solution)/shard_map/ppermute | solution.py:43
  8.5 0.9 dynamic-slice_compare_fusion
  9.4 0.7 and_add_fusion.refs_0_
  10.2 1.0 convert_reduce_fusion
  11.2 7.9 %collective-permute-done.1.refs_2_ = bf16[32,4096]{1,0:T(8,128)(2,1)S(1)} collective-permute-done((bf16[32,4096]{1,0:T(8,128)(2,1)S(1)}, bf16[32,4096]{1,0:T(8,128)(2,1)S(1)}, u32[]{:S(2)}, u32[]{:S(2)}) %collective-permute-start.1) | collective-permute-done | bytes 262176 | tf_op jit(solution)/shard_map/ppermute | solution.py:43
  19.1 1.9 %select_reduce_fusion = s32[8,70]{0,1:T(8,128)S(1)} fusion(s32[112]{0:T(128)} %constant.79, s32[8,112]{1,0:T(8,128)S(1)} %get-tuple-element.59), kind=kLoop, calls=%fused_computation.2 | loop fusion | flops 187600 | bytes 6272 | tf_op jit(solution)/shard_map/reduce_sum | solution.py:384
  21.2 3.9 %collective-permute-start.3 = (bf16[16,4096]{1,0:T(8,128)(2,1)S(1)}, bf16[16,4096]{1,0:T(8,128)(2,1)S(1)}, u32[]{:S(2)}, u32[]{:S(2)}) collective-permute-start(bf16[16,4096]{1,0:T(8,128)(2,1)S(1)} %shard_map.115), channel_id=1, source_target_pairs={{0,8},{1,25},{2,10},{3,27},{4,12},{5,29},{6,14},{7,31},{8,16},{9,1... | collective-permute-start | bytes 393224 | tf_op jit(solution)/shard_map/ppermute | solution.py:43
  25.1 0.9 copy-done.3
  26.0 3.4 %shard_map.117.refs_3_.refs_1_ = bf16[4096,896]{1,0:T(8,128)(2,1)S(1)} custom-call(s32[1]{0:T(128)} %bitcast.refs_0_, bf16[4096,896]{1,0:T(8,128)(2,1)} %refs_1_.1, s32[64,448]{1,0:T(8,128)S(1)} %copy-done.3), custom_call_target="tpu_custom_call" | custom-call | flops 3670016 | bytes 7454724 | tf_op jit(solution)/shard_map/pallas_call | solution.py:62
  29.4 0.7 collective-permute-done.4.refs_4_
  30.3 3.1 %collective-permute-start.6 = (bf16[16,4096]{1,0:T(8,128)(2,1)S(1)}, bf16[16,4096]{1,0:T(8,128)(2,1)S(1)}, u32[]{:S(2)}, u32[]{:S(2)}) collective-permute-start(bf16[16,4096]{1,0:T(8,128)(2,1)S(1)} %copy-done.2), channel_id=1, source_target_pairs={{0,2},{1,3},{2,0},{3,1},{4,6},{5,7},{6,4},{7,5},{8,10},{9,11},{10,... | collective-permute-start | bytes 393224 | tf_op jit(solution)/shard_map/ppermute | solution.py:43
  33.9 3.0 %collective-permute-start.8 = (bf16[32,4096]{1,0:T(8,128)(2,1)S(1)}, bf16[32,4096]{1,0:T(8,128)(2,1)S(1)}, u32[]{:S(2)}, u32[]{:S(2)}) collective-permute-start(bf16[32,4096]{1,0:T(8,128)(2,1)S(1)} %collective-permute-done.1.refs_2_), channel_id=1, source_target_pairs={{0,2},{1,3},{2,0},{3,1},{4,6},{5,7},{6,4},{7,5},{8,10},{9,11},{10,... | collective-permute-start | bytes 786440 | tf_op jit(solution)/shard_map/ppermute | solution.py:43
  37.8 3.5 %collective-permute-start.7 = (bf16[16,4096]{1,0:T(8,128)(2,1)S(1)}, bf16[16,4096]{1,0:T(8,128)(2,1)S(1)}, u32[]{:S(2)}, u32[]{:S(2)}) collective-permute-start(bf16[16,4096]{1,0:T(8,128)(2,1)S(1)} %collective-permute-done.3.refs_1_), channel_id=1, source_target_pairs={{0,2},{1,3},{2,0},{3,1},{4,6},{5,7},{6,4},{7,5},{8,10},{9,11},{10,... | collective-permute-start | bytes 393224 | tf_op jit(solution)/shard_map/ppermute | solution.py:43
  41.3 16.1 %collective-permute-done.7.refs_1_ = bf16[16,4096]{1,0:T(8,128)(2,1)S(1)} collective-permute-done((bf16[16,4096]{1,0:T(8,128)(2,1)S(1)}, bf16[16,4096]{1,0:T(8,128)(2,1)S(1)}, u32[]{:S(2)}, u32[]{:S(2)}) %collective-permute-start.7) | collective-permute-done | bytes 131104 | tf_op jit(solution)/shard_map/ppermute | solution.py:43
  57.6 3.9 %shard_map.120 = (bf16[16,16,896]{2,1,0:T(8,128)(2,1)S(1)}, bf16[256,896]{1,0:T(8,128)(2,1)S(1)}) custom-call(s32[32]{0:T(128)S(1)} %fusion.8.refs_0_, bf16[128,4096]{1,0:T(8,128)(2,1)S(1)} %shard_map.118.refs_1_.refs_5_, bf16[128,4096]{1,0:T(8,128)(2,1)S(1)} %collective-permute-done.5.refs_2_.refs_7_, bf16[4096,896]{1,0:T(8,128)(2,1)S(1)} %shard_map.117.refs_3_.refs_1_, ...), custom_call_target="tpu_custom_call" | custom-call | flops 1879048192 | bytes 10354816 | tf_op jit(solution)/shard_map/pallas_call | solution.py:62
  61.4 3.8 %shard_map.122 = (f32[128,4096]{1,0:T(8,128)S(1)}, bf16[128,4096]{1,0:T(8,128)(2,1)S(1)}) custom-call(bf16[256,896]{1,0:T(8,128)(2,1)S(1)} %get-tuple-element.69.refs_0_.refs_3_, bf16[4096,896]{1,0:T(8,128)(2,1)S(1)} %shard_map.117.refs_3_.refs_1_), custom_call_target="tpu_custom_call" | custom-call | flops 1879048192 | bytes 7798784 | tf_op jit(solution)/shard_map/pallas_call | solution.py:62
  65.2 0.7 collective-permute-start.12
  66.0 3.9 %shard_map.123 = (bf16[16,16,896]{2,1,0:T(8,128)(2,1)S(1)}, bf16[256,896]{1,0:T(8,128)(2,1)S(1)}) custom-call(s32[32]{0:T(128)S(1)} %fusion.8.refs_0_, bf16[128,4096]{1,0:T(8,128)(2,1)S(1)} %shard_map.121.refs_1_.refs_6_, bf16[128,4096]{1,0:T(8,128)(2,1)S(1)} %collective-permute-done.11.refs_2_.refs_8_, bf16[4096,896]{1,0:T(8,128)(2,1)S(1)} %shard_map.117.refs_3_.refs_1_, ...), custom_call_target="tpu_custom_call" | custom-call | flops 1879048192 | bytes 10354816 | tf_op jit(solution)/shard_map/pallas_call | solution.py:62
  69.8 1.7 shard_map.124.refs_9_
  71.6 2.8 %shard_map.125 = (bf16[35,64,128]{2,1,0:T(8,128)(2,1)S(1)}, bf16[35,64,128]{2,1,0:T(8,128)(2,1)S(1)}) custom-call(s32[8]{0:T(128)S(1)} %and_add_fusion.refs_0_, s32[8,70]{1,0:T(8,128)S(1)} %broadcast_add_fusion.refs_1_, s32[8]{0:T(128)S(1)} %get-tuple-element.74.refs_2_, bf16[256,896]{1,0:T(8,128)(2,1)S(1)} %get-tuple-element.69.refs_0_.refs_3_, ...), custom_call_target="tpu_custom_call" | custom-call | flops 939524096 | bytes 5114112 | tf_op jit(solution)/shard_map/pallas_call | solution.py:62
  74.6 3.8 %shard_map.127 = (f32[128,4096]{1,0:T(8,128)S(1)}, bf16[128,4096]{1,0:T(8,128)(2,1)S(1)}) custom-call(bf16[256,896]{1,0:T(8,128)(2,1)S(1)} %get-tuple-element.75.refs_4_.refs_0_, bf16[4096,896]{1,0:T(8,128)(2,1)S(1)} %shard_map.117.refs_3_.refs_1_, bf16[16,4096]{1,0:T(8,128)(2,1)S(1)} %get-tuple-element.78.refs_2_), custom_call_target="tpu_custom_call" | custom-call | flops 1879048192 | bytes 7798784 | tf_op jit(solution)/shard_map/pallas_call | solution.py:62
  78.7 3.0 %collective-permute-start.14 = (bf16[32,4096]{1,0:T(8,128)(2,1)S(1)}, bf16[32,4096]{1,0:T(8,128)(2,1)S(1)}, u32[]{:S(2)}, u32[]{:S(2)}) collective-permute-start(bf16[32,4096]{1,0:T(8,128)(2,1)S(1)} %get-tuple-element.82), channel_id=1, source_target_pairs={{0,28},{1,5},{2,30},{3,7},{4,0},{5,9},{6,2},{7,11},{8,4},{9,13},{1... | collective-permute-start | bytes 786440 | tf_op jit(solution)/shard_map/ppermute | solution.py:43
  81.7 4.2 %collective-permute-start.15 = (bf16[16,4096]{1,0:T(8,128)(2,1)S(1)}, bf16[16,4096]{1,0:T(8,128)(2,1)S(1)}, u32[]{:S(2)}, u32[]{:S(2)}) collective-permute-start(bf16[16,4096]{1,0:T(8,128)(2,1)S(1)} %get-tuple-element.78.refs_2_), channel_id=1, source_target_pairs={{0,24},{1,9},{2,26},{3,11},{4,28},{5,13},{6,30},{7,15},{8,0},{9,17... | collective-permute-start | bytes 393224 | tf_op jit(solution)/shard_map/ppermute | solution.py:43
  85.9 4.2 %collective-permute-done.15.refs_2_ = bf16[16,4096]{1,0:T(8,128)(2,1)S(1)} collective-permute-done((bf16[16,4096]{1,0:T(8,128)(2,1)S(1)}, bf16[16,4096]{1,0:T(8,128)(2,1)S(1)}, u32[]{:S(2)}, u32[]{:S(2)}) %collective-permute-start.15) | collective-permute-done | bytes 131104 | tf_op jit(solution)/shard_map/ppermute | solution.py:43
  90.2 2.8 %shard_map.129 = (bf16[35,64,128]{2,1,0:T(8,128)(2,1)S(1)}, bf16[35,64,128]{2,1,0:T(8,128)(2,1)S(1)}) custom-call(s32[8]{0:T(128)S(1)} %and_add_fusion.refs_0_, s32[8,70]{1,0:T(8,128)S(1)} %broadcast_add_fusion.refs_1_, s32[8]{0:T(128)S(1)} %get-tuple-element.74.refs_2_, bf16[256,896]{1,0:T(8,128)(2,1)S(1)} %get-tuple-element.69.refs_0_.refs_3_, ...), custom_call_target="tpu_custom_call" | custom-call | flops 939524096 | bytes 5114112 | tf_op jit(solution)/shard_map/pallas_call | solution.py:62
  93.2 0.7 collective-permute-start.16
  93.9 2.9 %collective-permute-start.18 = (bf16[32,4096]{1,0:T(8,128)(2,1)S(1)}, bf16[32,4096]{1,0:T(8,128)(2,1)S(1)}, u32[]{:S(2)}, u32[]{:S(2)}) collective-permute-start(bf16[32,4096]{1,0:T(8,128)(2,1)S(1)} %get-tuple-element.91), channel_id=1, source_target_pairs={{0,28},{1,5},{2,30},{3,7},{4,0},{5,9},{6,2},{7,11},{8,4},{9,13},{1... | collective-permute-start | bytes 786440 | tf_op jit(solution)/shard_map/ppermute | solution.py:43
  96.8 3.0 %collective-permute-start.17 = (bf16[16,4096]{1,0:T(8,128)(2,1)S(1)}, bf16[16,4096]{1,0:T(8,128)(2,1)S(1)}, u32[]{:S(2)}, u32[]{:S(2)}) collective-permute-start(bf16[16,4096]{1,0:T(8,128)(2,1)S(1)} %get-tuple-element.87.refs_9_), channel_id=1, source_target_pairs={{0,24},{1,9},{2,26},{3,11},{4,28},{5,13},{6,30},{7,15},{8,0},{9,17... | collective-permute-start | bytes 393224 | tf_op jit(solution)/shard_map/ppermute | solution.py:43
  99.8 0.9 collective-permute-start.24
  100.6 2.6 %collective-permute-start.26 = (bf16[35,64,128]{2,1,0:T(8,128)(2,1)S(1)}, bf16[35,64,128]{2,1,0:T(8,128)(2,1)S(1)}, u32[]{:S(2)}, u32[]{:S(2)}) collective-permute-start(bf16[35,64,128]{2,1,0:T(8,128)(2,1)S(1)} %get-tuple-element.99), channel_id=1, source_target_pairs={{0,192},{32,224},{64,128},{96,160},{128,64},{160,96},{192,0},{224,... | collective-permute-start | bytes 1720328 | tf_op jit(solution)/shard_map/ppermute | solution.py:47
  103.2 3.0 %shard_map.131 = (bf16[35,64,128]{2,1,0:T(8,128)(2,1)S(1)}, bf16[35,64,128]{2,1,0:T(8,128)(2,1)S(1)}) custom-call(s32[8]{0:T(128)S(1)} %and_add_fusion.refs_0_, s32[8,70]{1,0:T(8,128)S(1)} %broadcast_add_fusion.refs_1_, s32[8]{0:T(128)S(1)} %get-tuple-element.74.refs_2_, bf16[256,896]{1,0:T(8,128)(2,1)S(1)} %get-tuple-element.69.refs_0_.refs_3_, ...), custom_call_target="tpu_custom_call" | custom-call | flops 939524096 | bytes 5114112 | tf_op jit(solution)/shard_map/pallas_call | solution.py:62
  106.2 0.8 collective-permute-start.19
  107.1 3.0 %collective-permute-start.20 = (bf16[32,4096]{1,0:T(8,128)(2,1)S(1)}, bf16[32,4096]{1,0:T(8,128)(2,1)S(1)}, u32[]{:S(2)}, u32[]{:S(2)}) collective-permute-start(bf16[32,4096]{1,0:T(8,128)(2,1)S(1)} %get-tuple-element.93), channel_id=1, source_target_pairs={{0,28},{1,5},{2,30},{3,7},{4,0},{5,9},{6,2},{7,11},{8,4},{9,13},{1... | collective-permute-start | bytes 786440 | tf_op jit(solution)/shard_map/ppermute | solution.py:43
  110.1 4.2 %collective-permute-start.21 = (bf16[32,4096]{1,0:T(8,128)(2,1)S(1)}, bf16[32,4096]{1,0:T(8,128)(2,1)S(1)}, u32[]{:S(2)}, u32[]{:S(2)}) collective-permute-start(bf16[32,4096]{1,0:T(8,128)(2,1)S(1)} %shard_map.132.refs_9_), channel_id=1, source_target_pairs={{0,24},{1,9},{2,26},{3,11},{4,28},{5,13},{6,30},{7,15},{8,0},{9,17... | collective-permute-start | bytes 786440 | tf_op jit(solution)/shard_map/ppermute | solution.py:43
  114.5 4.7 %collective-permute-done.20.refs_3_ = bf16[32,4096]{1,0:T(8,128)(2,1)S(1)} collective-permute-done((bf16[32,4096]{1,0:T(8,128)(2,1)S(1)}, bf16[32,4096]{1,0:T(8,128)(2,1)S(1)}, u32[]{:S(2)}, u32[]{:S(2)}) %collective-permute-start.20) | collective-permute-done | bytes 262176 | tf_op jit(solution)/shard_map/ppermute | solution.py:43
  119.2 4.8 %collective-permute-done.21.refs_4_ = bf16[32,4096]{1,0:T(8,128)(2,1)S(1)} collective-permute-done((bf16[32,4096]{1,0:T(8,128)(2,1)S(1)}, bf16[32,4096]{1,0:T(8,128)(2,1)S(1)}, u32[]{:S(2)}, u32[]{:S(2)}) %collective-permute-start.21) | collective-permute-done | bytes 262176 | tf_op jit(solution)/shard_map/ppermute | solution.py:43
  124.4 2.0 %collective-permute-start.27 = (bf16[35,64,128]{2,1,0:T(8,128)(2,1)S(1)}, bf16[35,64,128]{2,1,0:T(8,128)(2,1)S(1)}, u32[]{:S(2)}, u32[]{:S(2)}) collective-permute-start(bf16[35,64,128]{2,1,0:T(8,128)(2,1)S(1)} %get-tuple-element.83.refs_2_), channel_id=1, source_target_pairs={{0,224},{32,128},{64,160},{96,192},{128,96},{160,0},{192,32},{224,... | collective-permute-start | bytes 1720328 | tf_op jit(solution)/shard_map/ppermute | solution.py:47
  126.4 2.7 %collective-permute-start.28 = (bf16[35,64,128]{2,1,0:T(8,128)(2,1)S(1)}, bf16[35,64,128]{2,1,0:T(8,128)(2,1)S(1)}, u32[]{:S(2)}, u32[]{:S(2)}) collective-permute-start(bf16[35,64,128]{2,1,0:T(8,128)(2,1)S(1)} %get-tuple-element.101), channel_id=1, source_target_pairs={{0,32},{32,64},{64,96},{96,0},{128,160},{160,192},{192,224},{224,1... | collective-permute-start | bytes 1720328 | tf_op jit(solution)/shard_map/ppermute | solution.py:47
  129.1 1.9 %collective-permute-start.30 = (bf16[35,64,128]{2,1,0:T(8,128)(2,1)S(1)}, bf16[35,64,128]{2,1,0:T(8,128)(2,1)S(1)}, u32[]{:S(2)}, u32[]{:S(2)}) collective-permute-start(bf16[35,64,128]{2,1,0:T(8,128)(2,1)S(1)} %get-tuple-element.102), channel_id=1, source_target_pairs={{0,64},{32,96},{64,0},{96,32},{128,192},{160,224},{192,128},{224,1... | collective-permute-start | bytes 1720328 | tf_op jit(solution)/shard_map/ppermute | solution.py:47
  131.1 34.3 %collective-permute-done.25.refs_2_ = bf16[35,64,128]{2,1,0:T(8,128)(2,1)S(1)} collective-permute-done((bf16[35,64,128]{2,1,0:T(8,128)(2,1)S(1)}, bf16[35,64,128]{2,1,0:T(8,128)(2,1)S(1)}, u32[]{:S(2)}, u32[]{:S(2)}) %collective-permute-start.25) | collective-permute-done | bytes 573472 | tf_op jit(solution)/shard_map/ppermute | solution.py:47
  165.4 3.6 %collective-permute-start.23 = (bf16[16,4096]{1,0:T(8,128)(2,1)S(1)}, bf16[16,4096]{1,0:T(8,128)(2,1)S(1)}, u32[]{:S(2)}, u32[]{:S(2)}) collective-permute-start(bf16[16,4096]{1,0:T(8,128)(2,1)S(1)} %get-tuple-element.98), channel_id=1, source_target_pairs={{0,2},{1,3},{2,0},{3,1},{4,6},{5,7},{6,4},{7,5},{8,10},{9,11},{10,... | collective-permute-start | bytes 393224 | tf_op jit(solution)/shard_map/ppermute | solution.py:43
  169.1 1.7 shard_map.133.refs_3_.refs_0_
  170.8 1.6 shard_map.134
  173.0 2.8 %shard_map.139 = f32[512,896]{1,0:T(8,128)} custom-call(s32[1]{0:T(128)} %bitcast.3.refs_0_, s32[8,70]{1,0:T(8,128)S(1)} %broadcast_add_fusion.refs_1_, f32[35,64,128]{2,1,0:T(8,128)S(1)} %shard_map.138.refs_2_, bf16[35,64,128]{2,1,0:T(8,128)(2,1)S(1)} %collective-permute-done.28.refs_3_, bf16[35,64,128]{2,1,0:T(8,128)(2,1)S(1)} %collective-permute-done.29.refs_4_, ...), custom_call_target="tpu_custom_call" | custom-call | flops 2293760 | bytes 2869444 | tf_op jit(solution)/shard_map/pallas_call | solution.py:62
  175.8 0.7 shard_map.137
  (58 shorter events, 4.1 us)
Async XLA Ops:
  0.6 1.6 collective-permute-start
  2.3 0.9 copy-start.1
  3.2 17.9 %collective-permute-start.2 = (bf16[32,4096]{1,0:T(8,128)(2,1)S(1)}, bf16[32,4096]{1,0:T(8,128)(2,1)S(1)}, u32[]{:S(2)}, u32[]{:S(2)}) collective-permute-start(bf16[32,4096]{1,0:T(8,128)(2,1)S(1)} %shard_map.112), channel_id=1, source_target_pairs={{0,8},{1,25},{2,10},{3,27},{4,12},{5,29},{6,14},{7,31},{8,16},{9,1... | collective-permute-start | bytes 786440 | tf_op jit(solution)/shard_map/ppermute | solution.py:43
  6.6 12.6 %collective-permute-start.1 = (bf16[32,4096]{1,0:T(8,128)(2,1)S(1)}, bf16[32,4096]{1,0:T(8,128)(2,1)S(1)}, u32[]{:S(2)}, u32[]{:S(2)}) collective-permute-start(bf16[32,4096]{1,0:T(8,128)(2,1)S(1)} %shard_map.112), channel_id=1, source_target_pairs={{0,4},{1,29},{2,6},{3,31},{4,8},{5,1},{6,10},{7,3},{8,12},{9,5},{1... | collective-permute-start | bytes 786440 | tf_op jit(solution)/shard_map/ppermute | solution.py:43
  21.1 9.0 %collective-permute-start.4 = (bf16[32,4096]{1,0:T(8,128)(2,1)S(1)}, bf16[32,4096]{1,0:T(8,128)(2,1)S(1)}, u32[]{:S(2)}, u32[]{:S(2)}) collective-permute-start(bf16[32,4096]{1,0:T(8,128)(2,1)S(1)} %collective-permute-done.2.refs_0_.refs_3_), channel_id=1, source_target_pairs={{0,4},{1,29},{2,6},{3,31},{4,8},{5,1},{6,10},{7,3},{8,12},{9,5},{1... | collective-permute-start | bytes 786440 | tf_op jit(solution)/shard_map/ppermute | solution.py:43
  21.2 9.0 %collective-permute-start.3 = (bf16[16,4096]{1,0:T(8,128)(2,1)S(1)}, bf16[16,4096]{1,0:T(8,128)(2,1)S(1)}, u32[]{:S(2)}, u32[]{:S(2)}) collective-permute-start(bf16[16,4096]{1,0:T(8,128)(2,1)S(1)} %shard_map.115), channel_id=1, source_target_pairs={{0,8},{1,25},{2,10},{3,27},{4,12},{5,29},{6,14},{7,31},{8,16},{9,1... | collective-permute-start | bytes 393224 | tf_op jit(solution)/shard_map/ppermute | solution.py:43
  25.1 0.9 copy-start.3
  26.0 4.1 %copy-start.2 = (bf16[16,4096]{1,0:T(8,128)(2,1)S(1)}, bf16[16,4096]{1,0:T(8,128)(2,1)}, u32[]{:S(2)}) copy-start(bf16[16,4096]{1,0:T(8,128)(2,1)} %refs_0_.3) | copy-start | bytes 393220
  29.4 28.2 %copy-start = (bf16[512,896]{1,0:T(8,128)(2,1)S(1)}, bf16[512,896]{1,0:T(8,128)(2,1)}, u32[]{:S(2)}) copy-start(bf16[512,896]{1,0:T(8,128)(2,1)} %param.12) | copy-start | bytes 2752516
  30.2 27.4 %collective-permute-start.5 = (bf16[128,4096]{1,0:T(8,128)(2,1)S(1)}, bf16[128,4096]{1,0:T(8,128)(2,1)S(1)}, u32[]{:S(2)}, u32[]{:S(2)}) collective-permute-start(bf16[128,4096]{1,0:T(8,128)(2,1)S(1)} %shard_map.118.refs_1_.refs_5_), channel_id=1, source_target_pairs={{0,1},{1,0},{2,3},{3,2},{4,5},{5,4},{6,7},{7,6},{8,9},{9,8},{10,11... | collective-permute-start | bytes 3145736 | tf_op jit(solution)/shard_map/ppermute | solution.py:43
  30.3 7.5 %collective-permute-start.6 = (bf16[16,4096]{1,0:T(8,128)(2,1)S(1)}, bf16[16,4096]{1,0:T(8,128)(2,1)S(1)}, u32[]{:S(2)}, u32[]{:S(2)}) collective-permute-start(bf16[16,4096]{1,0:T(8,128)(2,1)S(1)} %copy-done.2), channel_id=1, source_target_pairs={{0,2},{1,3},{2,0},{3,1},{4,6},{5,7},{6,4},{7,5},{8,10},{9,11},{10,... | collective-permute-start | bytes 393224 | tf_op jit(solution)/shard_map/ppermute | solution.py:43
  33.4 24.0 %collective-permute-start.9 = (bf16[32,4096]{1,0:T(8,128)(2,1)S(1)}, bf16[32,4096]{1,0:T(8,128)(2,1)S(1)}, u32[]{:S(2)}, u32[]{:S(2)}) collective-permute-start(bf16[32,4096]{1,0:T(8,128)(2,1)S(1)} %collective-permute-done.2.refs_0_.refs_3_), channel_id=1, source_target_pairs={{0,2},{1,3},{2,0},{3,1},{4,6},{5,7},{6,4},{7,5},{8,10},{9,11},{10,... | collective-permute-start | bytes 786440 | tf_op jit(solution)/shard_map/ppermute | solution.py:43
  33.9 23.5 %collective-permute-start.8 = (bf16[32,4096]{1,0:T(8,128)(2,1)S(1)}, bf16[32,4096]{1,0:T(8,128)(2,1)S(1)}, u32[]{:S(2)}, u32[]{:S(2)}) collective-permute-start(bf16[32,4096]{1,0:T(8,128)(2,1)S(1)} %collective-permute-done.1.refs_2_), channel_id=1, source_target_pairs={{0,2},{1,3},{2,0},{3,1},{4,6},{5,7},{6,4},{7,5},{8,10},{9,11},{10,... | collective-permute-start | bytes 786440 | tf_op jit(solution)/shard_map/ppermute | solution.py:43
  36.9 20.4 %collective-permute-start.10 = (bf16[32,4096]{1,0:T(8,128)(2,1)S(1)}, bf16[32,4096]{1,0:T(8,128)(2,1)S(1)}, u32[]{:S(2)}, u32[]{:S(2)}) collective-permute-start(bf16[32,4096]{1,0:T(8,128)(2,1)S(1)} %collective-permute-done.4.refs_4_), channel_id=1, source_target_pairs={{0,2},{1,3},{2,0},{3,1},{4,6},{5,7},{6,4},{7,5},{8,10},{9,11},{10,... | collective-permute-start | bytes 786440 | tf_op jit(solution)/shard_map/ppermute | solution.py:43
  37.8 19.6 %collective-permute-start.7 = (bf16[16,4096]{1,0:T(8,128)(2,1)S(1)}, bf16[16,4096]{1,0:T(8,128)(2,1)S(1)}, u32[]{:S(2)}, u32[]{:S(2)}) collective-permute-start(bf16[16,4096]{1,0:T(8,128)(2,1)S(1)} %collective-permute-done.3.refs_1_), channel_id=1, source_target_pairs={{0,2},{1,3},{2,0},{3,1},{4,6},{5,7},{6,4},{7,5},{8,10},{9,11},{10,... | collective-permute-start | bytes 393224 | tf_op jit(solution)/shard_map/ppermute | solution.py:43
  57.5 8.5 %collective-permute-start.11 = (bf16[128,4096]{1,0:T(8,128)(2,1)S(1)}, bf16[128,4096]{1,0:T(8,128)(2,1)S(1)}, u32[]{:S(2)}, u32[]{:S(2)}) collective-permute-start(bf16[128,4096]{1,0:T(8,128)(2,1)S(1)} %shard_map.121.refs_1_.refs_6_), channel_id=1, source_target_pairs={{0,1},{1,0},{2,3},{3,2},{4,5},{5,4},{6,7},{7,6},{8,9},{9,8},{10,11... | collective-permute-start | bytes 3145736 | tf_op jit(solution)/shard_map/ppermute | solution.py:43
  65.2 9.1 %collective-permute-start.12 = (bf16[128,4096]{1,0:T(8,128)(2,1)S(1)}, bf16[128,4096]{1,0:T(8,128)(2,1)S(1)}, u32[]{:S(2)}, u32[]{:S(2)}) collective-permute-start(bf16[128,4096]{1,0:T(8,128)(2,1)S(1)} %get-tuple-element.70.refs_5_.refs_9_), channel_id=1, source_target_pairs={{0,1},{1,0},{2,3},{3,2},{4,5},{5,4},{6,7},{7,6},{8,9},{9,8},{10,11... | collective-permute-start | bytes 3145736 | tf_op jit(solution)/shard_map/ppermute | solution.py:43
  78.4 14.6 %collective-permute-start.13 = (bf16[128,4096]{1,0:T(8,128)(2,1)S(1)}, bf16[128,4096]{1,0:T(8,128)(2,1)S(1)}, u32[]{:S(2)}, u32[]{:S(2)}) collective-permute-start(bf16[128,4096]{1,0:T(8,128)(2,1)S(1)} %get-tuple-element.80.refs_3_), channel_id=1, source_target_pairs={{0,1},{1,0},{2,3},{3,2},{4,5},{5,4},{6,7},{7,6},{8,9},{9,8},{10,11... | collective-permute-start | bytes 3145736 | tf_op jit(solution)/shard_map/ppermute | solution.py:43
  78.7 11.4 %collective-permute-start.14 = (bf16[32,4096]{1,0:T(8,128)(2,1)S(1)}, bf16[32,4096]{1,0:T(8,128)(2,1)S(1)}, u32[]{:S(2)}, u32[]{:S(2)}) collective-permute-start(bf16[32,4096]{1,0:T(8,128)(2,1)S(1)} %get-tuple-element.82), channel_id=1, source_target_pairs={{0,28},{1,5},{2,30},{3,7},{4,0},{5,9},{6,2},{7,11},{8,4},{9,13},{1... | collective-permute-start | bytes 786440 | tf_op jit(solution)/shard_map/ppermute | solution.py:43
  81.7 8.4 %collective-permute-start.15 = (bf16[16,4096]{1,0:T(8,128)(2,1)S(1)}, bf16[16,4096]{1,0:T(8,128)(2,1)S(1)}, u32[]{:S(2)}, u32[]{:S(2)}) collective-permute-start(bf16[16,4096]{1,0:T(8,128)(2,1)S(1)} %get-tuple-element.78.refs_2_), channel_id=1, source_target_pairs={{0,24},{1,9},{2,26},{3,11},{4,28},{5,13},{6,30},{7,15},{8,0},{9,17... | collective-permute-start | bytes 393224 | tf_op jit(solution)/shard_map/ppermute | solution.py:43
  93.2 13.7 %collective-permute-start.16 = (bf16[32,4096]{1,0:T(8,128)(2,1)S(1)}, bf16[32,4096]{1,0:T(8,128)(2,1)S(1)}, u32[]{:S(2)}, u32[]{:S(2)}) collective-permute-start(bf16[32,4096]{1,0:T(8,128)(2,1)S(1)} %get-tuple-element.86), channel_id=1, source_target_pairs={{0,28},{1,5},{2,30},{3,7},{4,0},{5,9},{6,2},{7,11},{8,4},{9,13},{1... | collective-permute-start | bytes 786440 | tf_op jit(solution)/shard_map/ppermute | solution.py:43
  93.9 16.2 %collective-permute-start.18 = (bf16[32,4096]{1,0:T(8,128)(2,1)S(1)}, bf16[32,4096]{1,0:T(8,128)(2,1)S(1)}, u32[]{:S(2)}, u32[]{:S(2)}) collective-permute-start(bf16[32,4096]{1,0:T(8,128)(2,1)S(1)} %get-tuple-element.91), channel_id=1, source_target_pairs={{0,28},{1,5},{2,30},{3,7},{4,0},{5,9},{6,2},{7,11},{8,4},{9,13},{1... | collective-permute-start | bytes 786440 | tf_op jit(solution)/shard_map/ppermute | solution.py:43
  96.8 9.4 %collective-permute-start.17 = (bf16[16,4096]{1,0:T(8,128)(2,1)S(1)}, bf16[16,4096]{1,0:T(8,128)(2,1)S(1)}, u32[]{:S(2)}, u32[]{:S(2)}) collective-permute-start(bf16[16,4096]{1,0:T(8,128)(2,1)S(1)} %get-tuple-element.87.refs_9_), channel_id=1, source_target_pairs={{0,24},{1,9},{2,26},{3,11},{4,28},{5,13},{6,30},{7,15},{8,0},{9,17... | collective-permute-start | bytes 393224 | tf_op jit(solution)/shard_map/ppermute | solution.py:43
  99.8 26.6 %collective-permute-start.24 = (bf16[35,64,128]{2,1,0:T(8,128)(2,1)S(1)}, bf16[35,64,128]{2,1,0:T(8,128)(2,1)S(1)}, u32[]{:S(2)}, u32[]{:S(2)}) collective-permute-start(bf16[35,64,128]{2,1,0:T(8,128)(2,1)S(1)} %shard_map.124.refs_9_), channel_id=1, source_target_pairs={{0,160},{32,192},{64,224},{96,128},{128,32},{160,64},{192,96},{224... | collective-permute-start | bytes 1720328 | tf_op jit(solution)/shard_map/ppermute | solution.py:47
  100.6 28.5 %collective-permute-start.26 = (bf16[35,64,128]{2,1,0:T(8,128)(2,1)S(1)}, bf16[35,64,128]{2,1,0:T(8,128)(2,1)S(1)}, u32[]{:S(2)}, u32[]{:S(2)}) collective-permute-start(bf16[35,64,128]{2,1,0:T(8,128)(2,1)S(1)} %get-tuple-element.99), channel_id=1, source_target_pairs={{0,192},{32,224},{64,128},{96,160},{128,64},{160,96},{192,0},{224,... | collective-permute-start | bytes 1720328 | tf_op jit(solution)/shard_map/ppermute | solution.py:47
  106.2 8.3 %collective-permute-start.19 = (bf16[32,4096]{1,0:T(8,128)(2,1)S(1)}, bf16[32,4096]{1,0:T(8,128)(2,1)S(1)}, u32[]{:S(2)}, u32[]{:S(2)}) collective-permute-start(bf16[32,4096]{1,0:T(8,128)(2,1)S(1)} %shard_map.128.refs_9_), channel_id=1, source_target_pairs={{0,24},{1,9},{2,26},{3,11},{4,28},{5,13},{6,30},{7,15},{8,0},{9,17... | collective-permute-start | bytes 786440 | tf_op jit(solution)/shard_map/ppermute | solution.py:43
  107.1 12.1 %collective-permute-start.20 = (bf16[32,4096]{1,0:T(8,128)(2,1)S(1)}, bf16[32,4096]{1,0:T(8,128)(2,1)S(1)}, u32[]{:S(2)}, u32[]{:S(2)}) collective-permute-start(bf16[32,4096]{1,0:T(8,128)(2,1)S(1)} %get-tuple-element.93), channel_id=1, source_target_pairs={{0,28},{1,5},{2,30},{3,7},{4,0},{5,9},{6,2},{7,11},{8,4},{9,13},{1... | collective-permute-start | bytes 786440 | tf_op jit(solution)/shard_map/ppermute | solution.py:43
  110.1 13.9 %collective-permute-start.21 = (bf16[32,4096]{1,0:T(8,128)(2,1)S(1)}, bf16[32,4096]{1,0:T(8,128)(2,1)S(1)}, u32[]{:S(2)}, u32[]{:S(2)}) collective-permute-start(bf16[32,4096]{1,0:T(8,128)(2,1)S(1)} %shard_map.132.refs_9_), channel_id=1, source_target_pairs={{0,24},{1,9},{2,26},{3,11},{4,28},{5,13},{6,30},{7,15},{8,0},{9,17... | collective-permute-start | bytes 786440 | tf_op jit(solution)/shard_map/ppermute | solution.py:43
  124.2 6.9 %collective-permute-start.22 = (bf16[32,4096]{1,0:T(8,128)(2,1)S(1)}, bf16[32,4096]{1,0:T(8,128)(2,1)S(1)}, u32[]{:S(2)}, u32[]{:S(2)}) collective-permute-start(bf16[32,4096]{1,0:T(8,128)(2,1)S(1)} %get-tuple-element.96), channel_id=1, source_target_pairs={{0,1},{1,0},{2,3},{3,2},{4,5},{5,4},{6,7},{7,6},{8,9},{9,8},{10,11... | collective-permute-start | bytes 786440 | tf_op jit(solution)/shard_map/ppermute | solution.py:43
  124.3 41.2 %collective-permute-start.25 = (bf16[35,64,128]{2,1,0:T(8,128)(2,1)S(1)}, bf16[35,64,128]{2,1,0:T(8,128)(2,1)S(1)}, u32[]{:S(2)}, u32[]{:S(2)}) collective-permute-start(bf16[35,64,128]{2,1,0:T(8,128)(2,1)S(1)} %get-tuple-element.77.refs_2_), channel_id=1, source_target_pairs={{0,96},{32,0},{64,32},{96,64},{128,224},{160,128},{192,160},{224,1... | collective-permute-start | bytes 1720328 | tf_op jit(solution)/shard_map/ppermute | solution.py:47
  124.4 48.1 %collective-permute-start.27 = (bf16[35,64,128]{2,1,0:T(8,128)(2,1)S(1)}, bf16[35,64,128]{2,1,0:T(8,128)(2,1)S(1)}, u32[]{:S(2)}, u32[]{:S(2)}) collective-permute-start(bf16[35,64,128]{2,1,0:T(8,128)(2,1)S(1)} %get-tuple-element.83.refs_2_), channel_id=1, source_target_pairs={{0,224},{32,128},{64,160},{96,192},{128,96},{160,0},{192,32},{224,... | collective-permute-start | bytes 1720328 | tf_op jit(solution)/shard_map/ppermute | solution.py:47
  126.4 46.6 %collective-permute-start.28 = (bf16[35,64,128]{2,1,0:T(8,128)(2,1)S(1)}, bf16[35,64,128]{2,1,0:T(8,128)(2,1)S(1)}, u32[]{:S(2)}, u32[]{:S(2)}) collective-permute-start(bf16[35,64,128]{2,1,0:T(8,128)(2,1)S(1)} %get-tuple-element.101), channel_id=1, source_target_pairs={{0,32},{32,64},{64,96},{96,0},{128,160},{160,192},{192,224},{224,1... | collective-permute-start | bytes 1720328 | tf_op jit(solution)/shard_map/ppermute | solution.py:47
  129.1 43.8 %collective-permute-start.30 = (bf16[35,64,128]{2,1,0:T(8,128)(2,1)S(1)}, bf16[35,64,128]{2,1,0:T(8,128)(2,1)S(1)}, u32[]{:S(2)}, u32[]{:S(2)}) collective-permute-start(bf16[35,64,128]{2,1,0:T(8,128)(2,1)S(1)} %get-tuple-element.102), channel_id=1, source_target_pairs={{0,64},{32,96},{64,0},{96,32},{128,192},{160,224},{192,128},{224,1... | collective-permute-start | bytes 1720328 | tf_op jit(solution)/shard_map/ppermute | solution.py:47
  131.0 41.9 %collective-permute-start.29 = (bf16[35,64,128]{2,1,0:T(8,128)(2,1)S(1)}, bf16[35,64,128]{2,1,0:T(8,128)(2,1)S(1)}, u32[]{:S(2)}, u32[]{:S(2)}) collective-permute-start(bf16[35,64,128]{2,1,0:T(8,128)(2,1)S(1)} %get-tuple-element.88.refs_3_), channel_id=1, source_target_pairs={{0,128},{32,160},{64,192},{96,224},{128,0},{160,32},{192,64},{224,... | collective-permute-start | bytes 1720328 | tf_op jit(solution)/shard_map/ppermute | solution.py:47
  165.4 10.4 %collective-permute-start.23 = (bf16[16,4096]{1,0:T(8,128)(2,1)S(1)}, bf16[16,4096]{1,0:T(8,128)(2,1)S(1)}, u32[]{:S(2)}, u32[]{:S(2)}) collective-permute-start(bf16[16,4096]{1,0:T(8,128)(2,1)S(1)} %get-tuple-element.98), channel_id=1, source_target_pairs={{0,2},{1,3},{2,0},{3,1},{4,6},{5,7},{6,4},{7,5},{8,10},{9,11},{10,... | collective-permute-start | bytes 393224 | tf_op jit(solution)/shard_map/ppermute | solution.py:43

commit v7 on v5

--- a/solution.py
+++ b/solution.py
@@ -175,8 +175,7 @@
         out[idx_ref[16 + n]] = b_ref[n]
 
 
-def last_kernel(kept, received, out, tick):
-    tick[...] = jnp.zeros_like(tick)
+def last_kernel(kept, received, out):
     out[...] = (kept[...] + received[...].astype(F32)).astype(BF16)
 
 
@@ -513,12 +512,8 @@
         (kept, move(to_core, dc=1)),
         32 * d,
     )
-    x_grad, done = call(
-        last_kernel,
-        0,
-        (jax.ShapeDtypeStruct((16, d), BF16), order_after),
-        (kept, move(to_x, dx=1)),
-        16 * d,
+    x_grad = call(
+        last_kernel, 0, jax.ShapeDtypeStruct((16, d), BF16), (kept, move(to_x, dx=1)), 16 * d
     )
 
     weight_grad = call(
@@ -531,7 +526,6 @@
             pltpu.VMEM((512, width), F32),
             pltpu.SemaphoreType.DMA((4,)),
         ),
-        after=(done,),
         out_space=pl.BlockSpec(memory_space=pl.ANY),
     )
     return (act.reshape(512, width), x_grad, weight_grad)

time: 175 us -> 175 us (level)
  the two profiles are of different devices: /device:TPU:30 before, /device:TPU:26 now
where the time goes in v7:
time: 175 us
  waiting for transfers between devices  65 us (37%)
  starting transfers between devices  64.6 us (37%)
  Pallas kernels  37.4 us (21%)
  other arithmetic  3.53 us (2%)
  local copies, waits for them, and re-layouts  1.98 us (1%)
    ppermute x24, starting transfers between devices, move(): return lax.ppermute(x, 'tensor', tensor_perm(dz, dx, dc, split=True))  52.7 us
    ppermute x24, waiting for transfers between devices, move(): return lax.ppermute(x, 'tensor', tensor_perm(dz, dx, dc, split=True))  44.2 us
    pallas_call x28, Pallas kernels, call(): pl.pallas_call(run, out_shape=out_shape, in_specs=[SMEM] * n_scalar + [sp...  37.4 us
    ppermute x7, waiting for transfers between devices, move_dp(): return lax.ppermute(x, 'dp', dp_perm(dx, dy))  20.8 us
    ppermute x7, starting transfers between devices, move_dp(): return lax.ppermute(x, 'dp', dp_perm(dx, dy))  11.9 us
  transfers between devices with their start and end apart: 31, of which 10 were waited for; matrix products, arithmetic and copies ran while one was open for 3% of the time, Pallas kernels for 19%

profile of v7, /device:TPU:26, one launch (start us, length us, event | category | flops | bytes accessed | tf_op | source)
XLA Modules:
  0.0 174.6 jit_solution(17088676341533612750)
XLA Ops:
  0.8 1.5 collective-permute-done.refs_1_
  2.3 0.9 copy-done.1
  3.2 3.3 %collective-permute-start.2 = (bf16[32,4096]{1,0:T(8,128)(2,1)S(1)}, bf16[32,4096]{1,0:T(8,128)(2,1)S(1)}, u32[]{:S(2)}, u32[]{:S(2)}) collective-permute-start(bf16[32,4096]{1,0:T(8,128)(2,1)S(1)} %shard_map.112), channel_id=1, source_target_pairs={{0,8},{1,25},{2,10},{3,27},{4,12},{5,29},{6,14},{7,31},{8,16},{9,1... | collective-permute-start | bytes 786440 | tf_op jit(solution)/shard_map/ppermute | solution.py:43
  6.6 1.9 %collective-permute-start.1 = (bf16[32,4096]{1,0:T(8,128)(2,1)S(1)}, bf16[32,4096]{1,0:T(8,128)(2,1)S(1)}, u32[]{:S(2)}, u32[]{:S(2)}) collective-permute-start(bf16[32,4096]{1,0:T(8,128)(2,1)S(1)} %shard_map.112), channel_id=1, source_target_pairs={{0,4},{1,29},{2,6},{3,31},{4,8},{5,1},{6,10},{7,3},{8,12},{9,5},{1... | collective-permute-start | bytes 786440 | tf_op jit(solution)/shard_map/ppermute | solution.py:43
  8.5 0.9 dynamic-slice_compare_fusion
  10.2 1.0 convert_reduce_fusion
  11.2 7.9 %collective-permute-done.1.refs_2_ = bf16[32,4096]{1,0:T(8,128)(2,1)S(1)} collective-permute-done((bf16[32,4096]{1,0:T(8,128)(2,1)S(1)}, bf16[32,4096]{1,0:T(8,128)(2,1)S(1)}, u32[]{:S(2)}, u32[]{:S(2)}) %collective-permute-start.1) | collective-permute-done | bytes 262176 | tf_op jit(solution)/shard_map/ppermute | solution.py:43
  19.1 1.9 %select_reduce_fusion = s32[8,70]{0,1:T(8,128)S(1)} fusion(s32[112]{0:T(128)} %constant.79, s32[8,112]{1,0:T(8,128)S(1)} %get-tuple-element.59), kind=kLoop, calls=%fused_computation.2 | loop fusion | flops 187600 | bytes 6272 | tf_op jit(solution)/shard_map/reduce_sum | solution.py:384
  21.2 3.9 %collective-permute-start.3 = (bf16[16,4096]{1,0:T(8,128)(2,1)S(1)}, bf16[16,4096]{1,0:T(8,128)(2,1)S(1)}, u32[]{:S(2)}, u32[]{:S(2)}) collective-permute-start(bf16[16,4096]{1,0:T(8,128)(2,1)S(1)} %shard_map.115), channel_id=1, source_target_pairs={{0,8},{1,25},{2,10},{3,27},{4,12},{5,29},{6,14},{7,31},{8,16},{9,1... | collective-permute-start | bytes 393224 | tf_op jit(solution)/shard_map/ppermute | solution.py:43
  25.1 0.9 copy-done.3
  26.0 3.4 %shard_map.117.refs_3_.refs_1_ = bf16[4096,896]{1,0:T(8,128)(2,1)S(1)} custom-call(s32[1]{0:T(128)} %bitcast.refs_0_, bf16[4096,896]{1,0:T(8,128)(2,1)} %refs_1_.1, s32[64,448]{1,0:T(8,128)S(1)} %copy-done.3), custom_call_target="tpu_custom_call" | custom-call | flops 3670016 | bytes 7454724 | tf_op jit(solution)/shard_map/pallas_call | solution.py:62
  29.4 0.7 collective-permute-done.4.refs_4_
  30.3 2.2 %collective-permute-start.6 = (bf16[16,4096]{1,0:T(8,128)(2,1)S(1)}, bf16[16,4096]{1,0:T(8,128)(2,1)S(1)}, u32[]{:S(2)}, u32[]{:S(2)}) collective-permute-start(bf16[16,4096]{1,0:T(8,128)(2,1)S(1)} %copy-done.2), channel_id=1, source_target_pairs={{0,2},{1,3},{2,0},{3,1},{4,6},{5,7},{6,4},{7,5},{8,10},{9,11},{10,... | collective-permute-start | bytes 393224 | tf_op jit(solution)/shard_map/ppermute | solution.py:43
  32.5 1.4 collective-permute-start.9
  33.9 2.1 %collective-permute-start.8 = (bf16[32,4096]{1,0:T(8,128)(2,1)S(1)}, bf16[32,4096]{1,0:T(8,128)(2,1)S(1)}, u32[]{:S(2)}, u32[]{:S(2)}) collective-permute-start(bf16[32,4096]{1,0:T(8,128)(2,1)S(1)} %collective-permute-done.1.refs_2_), channel_id=1, source_target_pairs={{0,2},{1,3},{2,0},{3,1},{4,6},{5,7},{6,4},{7,5},{8,10},{9,11},{10,... | collective-permute-start | bytes 786440 | tf_op jit(solution)/shard_map/ppermute | solution.py:43
  36.0 1.4 collective-permute-start.10
  37.5 0.8 collective-permute-done.6.refs_0_
  38.3 2.1 %collective-permute-start.7 = (bf16[16,4096]{1,0:T(8,128)(2,1)S(1)}, bf16[16,4096]{1,0:T(8,128)(2,1)S(1)}, u32[]{:S(2)}, u32[]{:S(2)}) collective-permute-start(bf16[16,4096]{1,0:T(8,128)(2,1)S(1)} %collective-permute-done.3.refs_1_), channel_id=1, source_target_pairs={{0,2},{1,3},{2,0},{3,1},{4,6},{5,7},{6,4},{7,5},{8,10},{9,11},{10,... | collective-permute-start | bytes 393224 | tf_op jit(solution)/shard_map/ppermute | solution.py:43
  40.4 17.0 %collective-permute-done.7.refs_1_ = bf16[16,4096]{1,0:T(8,128)(2,1)S(1)} collective-permute-done((bf16[16,4096]{1,0:T(8,128)(2,1)S(1)}, bf16[16,4096]{1,0:T(8,128)(2,1)S(1)}, u32[]{:S(2)}, u32[]{:S(2)}) %collective-permute-start.7) | collective-permute-done | bytes 131104 | tf_op jit(solution)/shard_map/ppermute | solution.py:43
  57.6 3.9 %shard_map.120 = (bf16[16,16,896]{2,1,0:T(8,128)(2,1)S(1)}, bf16[256,896]{1,0:T(8,128)(2,1)S(1)}) custom-call(s32[32]{0:T(128)S(1)} %fusion.8.refs_0_, bf16[128,4096]{1,0:T(8,128)(2,1)S(1)} %shard_map.118.refs_1_.refs_5_, bf16[128,4096]{1,0:T(8,128)(2,1)S(1)} %collective-permute-done.5.refs_2_.refs_7_, bf16[4096,896]{1,0:T(8,128)(2,1)S(1)} %shard_map.117.refs_3_.refs_1_, ...), custom_call_target="tpu_custom_call" | custom-call | flops 1879048192 | bytes 10354816 | tf_op jit(solution)/shard_map/pallas_call | solution.py:62
  61.4 3.8 %shard_map.122 = (f32[128,4096]{1,0:T(8,128)S(1)}, bf16[128,4096]{1,0:T(8,128)(2,1)S(1)}) custom-call(bf16[256,896]{1,0:T(8,128)(2,1)S(1)} %get-tuple-element.69.refs_0_.refs_3_, bf16[4096,896]{1,0:T(8,128)(2,1)S(1)} %shard_map.117.refs_3_.refs_1_), custom_call_target="tpu_custom_call" | custom-call | flops 1879048192 | bytes 7798784 | tf_op jit(solution)/shard_map/pallas_call | solution.py:62
  65.2 0.7 collective-permute-start.12
  66.0 3.9 %shard_map.123 = (bf16[16,16,896]{2,1,0:T(8,128)(2,1)S(1)}, bf16[256,896]{1,0:T(8,128)(2,1)S(1)}) custom-call(s32[32]{0:T(128)S(1)} %fusion.8.refs_0_, bf16[128,4096]{1,0:T(8,128)(2,1)S(1)} %shard_map.121.refs_1_.refs_6_, bf16[128,4096]{1,0:T(8,128)(2,1)S(1)} %collective-permute-done.11.refs_2_.refs_8_, bf16[4096,896]{1,0:T(8,128)(2,1)S(1)} %shard_map.117.refs_3_.refs_1_, ...), custom_call_target="tpu_custom_call" | custom-call | flops 1879048192 | bytes 10354816 | tf_op jit(solution)/shard_map/pallas_call | solution.py:62
  69.8 1.7 shard_map.124.refs_9_
  71.5 2.8 %shard_map.125 = (bf16[35,64,128]{2,1,0:T(8,128)(2,1)S(1)}, bf16[35,64,128]{2,1,0:T(8,128)(2,1)S(1)}) custom-call(s32[8]{0:T(128)S(1)} %and_add_fusion.refs_0_, s32[8,70]{1,0:T(8,128)S(1)} %broadcast_add_fusion.refs_1_, s32[8]{0:T(128)S(1)} %get-tuple-element.74.refs_2_, bf16[256,896]{1,0:T(8,128)(2,1)S(1)} %get-tuple-element.69.refs_0_.refs_3_, ...), custom_call_target="tpu_custom_call" | custom-call | flops 939524096 | bytes 5114112 | tf_op jit(solution)/shard_map/pallas_call | solution.py:62
  74.6 3.8 %shard_map.127 = (f32[128,4096]{1,0:T(8,128)S(1)}, bf16[128,4096]{1,0:T(8,128)(2,1)S(1)}) custom-call(bf16[256,896]{1,0:T(8,128)(2,1)S(1)} %get-tuple-element.75.refs_4_.refs_0_, bf16[4096,896]{1,0:T(8,128)(2,1)S(1)} %shard_map.117.refs_3_.refs_1_, bf16[16,4096]{1,0:T(8,128)(2,1)S(1)} %get-tuple-element.79.refs_2_), custom_call_target="tpu_custom_call" | custom-call | flops 1879048192 | bytes 7798784 | tf_op jit(solution)/shard_map/pallas_call | solution.py:62
  78.6 3.1 %collective-permute-start.16 = (bf16[32,4096]{1,0:T(8,128)(2,1)S(1)}, bf16[32,4096]{1,0:T(8,128)(2,1)S(1)}, u32[]{:S(2)}, u32[]{:S(2)}) collective-permute-start(bf16[32,4096]{1,0:T(8,128)(2,1)S(1)} %get-tuple-element.87), channel_id=1, source_target_pairs={{0,28},{1,5},{2,30},{3,7},{4,0},{5,9},{6,2},{7,11},{8,4},{9,13},{1... | collective-permute-start | bytes 786440 | tf_op jit(solution)/shard_map/ppermute | solution.py:43
  81.6 2.8 %shard_map.128 = (bf16[35,64,128]{2,1,0:T(8,128)(2,1)S(1)}, bf16[35,64,128]{2,1,0:T(8,128)(2,1)S(1)}) custom-call(s32[8]{0:T(128)S(1)} %and_add_fusion.refs_0_, s32[8,70]{1,0:T(8,128)S(1)} %broadcast_add_fusion.refs_1_, s32[8]{0:T(128)S(1)} %get-tuple-element.74.refs_2_, bf16[256,896]{1,0:T(8,128)(2,1)S(1)} %get-tuple-element.69.refs_0_.refs_3_, ...), custom_call_target="tpu_custom_call" | custom-call | flops 939524096 | bytes 5114112 | tf_op jit(solution)/shard_map/pallas_call | solution.py:62
  84.7 1.5 collective-permute-start.14
  86.1 3.1 %collective-permute-start.20 = (bf16[32,4096]{1,0:T(8,128)(2,1)S(1)}, bf16[32,4096]{1,0:T(8,128)(2,1)S(1)}, u32[]{:S(2)}, u32[]{:S(2)}) collective-permute-start(bf16[32,4096]{1,0:T(8,128)(2,1)S(1)} %get-tuple-element.93), channel_id=1, source_target_pairs={{0,28},{1,5},{2,30},{3,7},{4,0},{5,9},{6,2},{7,11},{8,4},{9,13},{1... | collective-permute-start | bytes 786440 | tf_op jit(solution)/shard_map/ppermute | solution.py:43
  89.2 1.5 collective-permute-start.15
  90.7 5.1 %collective-permute-done.17.refs_2_ = bf16[16,4096]{1,0:T(8,128)(2,1)S(1)} collective-permute-done((bf16[16,4096]{1,0:T(8,128)(2,1)S(1)}, bf16[16,4096]{1,0:T(8,128)(2,1)S(1)}, u32[]{:S(2)}, u32[]{:S(2)}) %collective-permute-start.17) | collective-permute-done | bytes 131104 | tf_op jit(solution)/shard_map/ppermute | solution.py:43
  96.1 3.4 %collective-permute-start.26 = (bf16[35,64,128]{2,1,0:T(8,128)(2,1)S(1)}, bf16[35,64,128]{2,1,0:T(8,128)(2,1)S(1)}, u32[]{:S(2)}, u32[]{:S(2)}) collective-permute-start(bf16[35,64,128]{2,1,0:T(8,128)(2,1)S(1)} %get-tuple-element.99), channel_id=1, source_target_pairs={{0,192},{32,224},{64,128},{96,160},{128,64},{160,96},{192,0},{224,... | collective-permute-start | bytes 1720328 | tf_op jit(solution)/shard_map/ppermute | solution.py:47
  99.6 2.8 %shard_map.131 = (bf16[35,64,128]{2,1,0:T(8,128)(2,1)S(1)}, bf16[35,64,128]{2,1,0:T(8,128)(2,1)S(1)}) custom-call(s32[8]{0:T(128)S(1)} %and_add_fusion.refs_0_, s32[8,70]{1,0:T(8,128)S(1)} %broadcast_add_fusion.refs_1_, s32[8]{0:T(128)S(1)} %get-tuple-element.74.refs_2_, bf16[256,896]{1,0:T(8,128)(2,1)S(1)} %get-tuple-element.69.refs_0_.refs_3_, ...), custom_call_target="tpu_custom_call" | custom-call | flops 939524096 | bytes 5114112 | tf_op jit(solution)/shard_map/pallas_call | solution.py:62
  102.5 4.1 %collective-permute-start.19 = (bf16[32,4096]{1,0:T(8,128)(2,1)S(1)}, bf16[32,4096]{1,0:T(8,128)(2,1)S(1)}, u32[]{:S(2)}, u32[]{:S(2)}) collective-permute-start(bf16[32,4096]{1,0:T(8,128)(2,1)S(1)} %shard_map.130.refs_9_), channel_id=1, source_target_pairs={{0,24},{1,9},{2,26},{3,11},{4,28},{5,13},{6,30},{7,15},{8,0},{9,17... | collective-permute-start | bytes 786440 | tf_op jit(solution)/shard_map/ppermute | solution.py:43
  106.7 3.8 %collective-permute-start.18 = (bf16[32,4096]{1,0:T(8,128)(2,1)S(1)}, bf16[32,4096]{1,0:T(8,128)(2,1)S(1)}, u32[]{:S(2)}, u32[]{:S(2)}) collective-permute-start(bf16[32,4096]{1,0:T(8,128)(2,1)S(1)} %get-tuple-element.91), channel_id=1, source_target_pairs={{0,28},{1,5},{2,30},{3,7},{4,0},{5,9},{6,2},{7,11},{8,4},{9,13},{1... | collective-permute-start | bytes 786440 | tf_op jit(solution)/shard_map/ppermute | solution.py:43
  110.5 2.8 %collective-permute-done.19.refs_1_ = bf16[32,4096]{1,0:T(8,128)(2,1)S(1)} collective-permute-done((bf16[32,4096]{1,0:T(8,128)(2,1)S(1)}, bf16[32,4096]{1,0:T(8,128)(2,1)S(1)}, u32[]{:S(2)}, u32[]{:S(2)}) %collective-permute-start.19) | collective-permute-done | bytes 262176 | tf_op jit(solution)/shard_map/ppermute | solution.py:43
  113.4 4.5 %collective-permute-done.18.refs_0_ = bf16[32,4096]{1,0:T(8,128)(2,1)S(1)} collective-permute-done((bf16[32,4096]{1,0:T(8,128)(2,1)S(1)}, bf16[32,4096]{1,0:T(8,128)(2,1)S(1)}, u32[]{:S(2)}, u32[]{:S(2)}) %collective-permute-start.18) | collective-permute-done | bytes 262176 | tf_op jit(solution)/shard_map/ppermute | solution.py:43
  117.9 3.9 %collective-permute-done.21.refs_4_ = bf16[32,4096]{1,0:T(8,128)(2,1)S(1)} collective-permute-done((bf16[32,4096]{1,0:T(8,128)(2,1)S(1)}, bf16[32,4096]{1,0:T(8,128)(2,1)S(1)}, u32[]{:S(2)}, u32[]{:S(2)}) %collective-permute-start.21) | collective-permute-done | bytes 262176 | tf_op jit(solution)/shard_map/ppermute | solution.py:43
  122.2 1.1 collective-permute-start.27
  123.3 3.1 %collective-permute-start.28 = (bf16[35,64,128]{2,1,0:T(8,128)(2,1)S(1)}, bf16[35,64,128]{2,1,0:T(8,128)(2,1)S(1)}, u32[]{:S(2)}, u32[]{:S(2)}) collective-permute-start(bf16[35,64,128]{2,1,0:T(8,128)(2,1)S(1)} %get-tuple-element.101), channel_id=1, source_target_pairs={{0,32},{32,64},{64,96},{96,0},{128,160},{160,192},{192,224},{224,1... | collective-permute-start | bytes 1720328 | tf_op jit(solution)/shard_map/ppermute | solution.py:47
  126.5 1.5 collective-permute-start.30
  127.9 2.3 %collective-permute-start.29 = (bf16[35,64,128]{2,1,0:T(8,128)(2,1)S(1)}, bf16[35,64,128]{2,1,0:T(8,128)(2,1)S(1)}, u32[]{:S(2)}, u32[]{:S(2)}) collective-permute-start(bf16[35,64,128]{2,1,0:T(8,128)(2,1)S(1)} %get-tuple-element.88.refs_3_), channel_id=1, source_target_pairs={{0,128},{32,160},{64,192},{96,224},{128,0},{160,32},{192,64},{224,... | collective-permute-start | bytes 1720328 | tf_op jit(solution)/shard_map/ppermute | solution.py:47
  130.4 20.8 %collective-permute-done.25.refs_2_ = bf16[35,64,128]{2,1,0:T(8,128)(2,1)S(1)} collective-permute-done((bf16[35,64,128]{2,1,0:T(8,128)(2,1)S(1)}, bf16[35,64,128]{2,1,0:T(8,128)(2,1)S(1)}, u32[]{:S(2)}, u32[]{:S(2)}) %collective-permute-start.25) | collective-permute-done | bytes 573472 | tf_op jit(solution)/shard_map/ppermute | solution.py:47
  151.2 15.8 %collective-permute-start.23 = (bf16[16,4096]{1,0:T(8,128)(2,1)S(1)}, bf16[16,4096]{1,0:T(8,128)(2,1)S(1)}, u32[]{:S(2)}, u32[]{:S(2)}) collective-permute-start(bf16[16,4096]{1,0:T(8,128)(2,1)S(1)} %get-tuple-element.98), channel_id=1, source_target_pairs={{0,2},{1,3},{2,0},{3,1},{4,6},{5,7},{6,4},{7,5},{8,10},{9,11},{10,... | collective-permute-start | bytes 393224 | tf_op jit(solution)/shard_map/ppermute | solution.py:43
  167.0 1.9 %shard_map.133.refs_3_.refs_0_ = bf16[35,64,128]{2,1,0:T(8,128)(2,1)S(1)} custom-call(s32[8]{0:T(128)S(1)} %and_add_fusion.refs_0_, s32[8,70]{1,0:T(8,128)S(1)} %broadcast_add_fusion.refs_1_, s32[8]{0:T(128)S(1)} %get-tuple-element.74.refs_2_, bf16[256,896]{1,0:T(8,128)(2,1)S(1)} %get-tuple-element.69.refs_0_.refs_3_, ...), custom_call_target="tpu_custom_call" | custom-call | flops 469762048 | bytes 5114112 | tf_op jit(solution)/shard_map/pallas_call | solution.py:62
  168.9 1.6 shard_map.134
  171.0 2.8 %shard_map.139 = f32[512,896]{1,0:T(8,128)} custom-call(s32[1]{0:T(128)} %bitcast.3.refs_0_, s32[8,70]{1,0:T(8,128)S(1)} %broadcast_add_fusion.refs_1_, f32[35,64,128]{2,1,0:T(8,128)S(1)} %shard_map.138.refs_2_, bf16[35,64,128]{2,1,0:T(8,128)(2,1)S(1)} %collective-permute-done.28.refs_3_, bf16[35,64,128]{2,1,0:T(8,128)(2,1)S(1)} %collective-permute-done.29.refs_4_, ...), custom_call_target="tpu_custom_call" | custom-call | flops 2293760 | bytes 2869444 | tf_op jit(solution)/shard_map/pallas_call | solution.py:62
  (58 shorter events, 4.3 us)
Async XLA Ops:
  0.6 1.6 collective-permute-start
  2.3 0.9 copy-start.1
  3.2 17.9 %collective-permute-start.2 = (bf16[32,4096]{1,0:T(8,128)(2,1)S(1)}, bf16[32,4096]{1,0:T(8,128)(2,1)S(1)}, u32[]{:S(2)}, u32[]{:S(2)}) collective-permute-start(bf16[32,4096]{1,0:T(8,128)(2,1)S(1)} %shard_map.112), channel_id=1, source_target_pairs={{0,8},{1,25},{2,10},{3,27},{4,12},{5,29},{6,14},{7,31},{8,16},{9,1... | collective-permute-start | bytes 786440 | tf_op jit(solution)/shard_map/ppermute | solution.py:43
  6.6 12.6 %collective-permute-start.1 = (bf16[32,4096]{1,0:T(8,128)(2,1)S(1)}, bf16[32,4096]{1,0:T(8,128)(2,1)S(1)}, u32[]{:S(2)}, u32[]{:S(2)}) collective-permute-start(bf16[32,4096]{1,0:T(8,128)(2,1)S(1)} %shard_map.112), channel_id=1, source_target_pairs={{0,4},{1,29},{2,6},{3,31},{4,8},{5,1},{6,10},{7,3},{8,12},{9,5},{1... | collective-permute-start | bytes 786440 | tf_op jit(solution)/shard_map/ppermute | solution.py:43
  21.1 9.0 %collective-permute-start.4 = (bf16[32,4096]{1,0:T(8,128)(2,1)S(1)}, bf16[32,4096]{1,0:T(8,128)(2,1)S(1)}, u32[]{:S(2)}, u32[]{:S(2)}) collective-permute-start(bf16[32,4096]{1,0:T(8,128)(2,1)S(1)} %collective-permute-done.2.refs_0_.refs_3_), channel_id=1, source_target_pairs={{0,4},{1,29},{2,6},{3,31},{4,8},{5,1},{6,10},{7,3},{8,12},{9,5},{1... | collective-permute-start | bytes 786440 | tf_op jit(solution)/shard_map/ppermute | solution.py:43
  21.2 9.0 %collective-permute-start.3 = (bf16[16,4096]{1,0:T(8,128)(2,1)S(1)}, bf16[16,4096]{1,0:T(8,128)(2,1)S(1)}, u32[]{:S(2)}, u32[]{:S(2)}) collective-permute-start(bf16[16,4096]{1,0:T(8,128)(2,1)S(1)} %shard_map.115), channel_id=1, source_target_pairs={{0,8},{1,25},{2,10},{3,27},{4,12},{5,29},{6,14},{7,31},{8,16},{9,1... | collective-permute-start | bytes 393224 | tf_op jit(solution)/shard_map/ppermute | solution.py:43
  25.1 0.9 copy-start.3
  26.0 4.1 %copy-start.2 = (bf16[16,4096]{1,0:T(8,128)(2,1)S(1)}, bf16[16,4096]{1,0:T(8,128)(2,1)}, u32[]{:S(2)}) copy-start(bf16[16,4096]{1,0:T(8,128)(2,1)} %refs_0_.3) | copy-start | bytes 393220
  29.4 28.2 %copy-start = (bf16[512,896]{1,0:T(8,128)(2,1)S(1)}, bf16[512,896]{1,0:T(8,128)(2,1)}, u32[]{:S(2)}) copy-start(bf16[512,896]{1,0:T(8,128)(2,1)} %param.12) | copy-start | bytes 2752516
  30.2 27.4 %collective-permute-start.5 = (bf16[128,4096]{1,0:T(8,128)(2,1)S(1)}, bf16[128,4096]{1,0:T(8,128)(2,1)S(1)}, u32[]{:S(2)}, u32[]{:S(2)}) collective-permute-start(bf16[128,4096]{1,0:T(8,128)(2,1)S(1)} %shard_map.118.refs_1_.refs_5_), channel_id=1, source_target_pairs={{0,1},{1,0},{2,3},{3,2},{4,5},{5,4},{6,7},{7,6},{8,9},{9,8},{10,11... | collective-permute-start | bytes 3145736 | tf_op jit(solution)/shard_map/ppermute | solution.py:43
  30.3 8.0 %collective-permute-start.6 = (bf16[16,4096]{1,0:T(8,128)(2,1)S(1)}, bf16[16,4096]{1,0:T(8,128)(2,1)S(1)}, u32[]{:S(2)}, u32[]{:S(2)}) collective-permute-start(bf16[16,4096]{1,0:T(8,128)(2,1)S(1)} %copy-done.2), channel_id=1, source_target_pairs={{0,2},{1,3},{2,0},{3,1},{4,6},{5,7},{6,4},{7,5},{8,10},{9,11},{10,... | collective-permute-start | bytes 393224 | tf_op jit(solution)/shard_map/ppermute | solution.py:43
  32.5 24.9 %collective-permute-start.9 = (bf16[32,4096]{1,0:T(8,128)(2,1)S(1)}, bf16[32,4096]{1,0:T(8,128)(2,1)S(1)}, u32[]{:S(2)}, u32[]{:S(2)}) collective-permute-start(bf16[32,4096]{1,0:T(8,128)(2,1)S(1)} %collective-permute-done.2.refs_0_.refs_3_), channel_id=1, source_target_pairs={{0,2},{1,3},{2,0},{3,1},{4,6},{5,7},{6,4},{7,5},{8,10},{9,11},{10,... | collective-permute-start | bytes 786440 | tf_op jit(solution)/shard_map/ppermute | solution.py:43
  33.9 23.5 %collective-permute-start.8 = (bf16[32,4096]{1,0:T(8,128)(2,1)S(1)}, bf16[32,4096]{1,0:T(8,128)(2,1)S(1)}, u32[]{:S(2)}, u32[]{:S(2)}) collective-permute-start(bf16[32,4096]{1,0:T(8,128)(2,1)S(1)} %collective-permute-done.1.refs_2_), channel_id=1, source_target_pairs={{0,2},{1,3},{2,0},{3,1},{4,6},{5,7},{6,4},{7,5},{8,10},{9,11},{10,... | collective-permute-start | bytes 786440 | tf_op jit(solution)/shard_map/ppermute | solution.py:43
  36.0 21.3 %collective-permute-start.10 = (bf16[32,4096]{1,0:T(8,128)(2,1)S(1)}, bf16[32,4096]{1,0:T(8,128)(2,1)S(1)}, u32[]{:S(2)}, u32[]{:S(2)}) collective-permute-start(bf16[32,4096]{1,0:T(8,128)(2,1)S(1)} %collective-permute-done.4.refs_4_), channel_id=1, source_target_pairs={{0,2},{1,3},{2,0},{3,1},{4,6},{5,7},{6,4},{7,5},{8,10},{9,11},{10,... | collective-permute-start | bytes 786440 | tf_op jit(solution)/shard_map/ppermute | solution.py:43
  38.3 19.1 %collective-permute-start.7 = (bf16[16,4096]{1,0:T(8,128)(2,1)S(1)}, bf16[16,4096]{1,0:T(8,128)(2,1)S(1)}, u32[]{:S(2)}, u32[]{:S(2)}) collective-permute-start(bf16[16,4096]{1,0:T(8,128)(2,1)S(1)} %collective-permute-done.3.refs_1_), channel_id=1, source_target_pairs={{0,2},{1,3},{2,0},{3,1},{4,6},{5,7},{6,4},{7,5},{8,10},{9,11},{10,... | collective-permute-start | bytes 393224 | tf_op jit(solution)/shard_map/ppermute | solution.py:43
  57.5 8.5 %collective-permute-start.11 = (bf16[128,4096]{1,0:T(8,128)(2,1)S(1)}, bf16[128,4096]{1,0:T(8,128)(2,1)S(1)}, u32[]{:S(2)}, u32[]{:S(2)}) collective-permute-start(bf16[128,4096]{1,0:T(8,128)(2,1)S(1)} %shard_map.121.refs_1_.refs_6_), channel_id=1, source_target_pairs={{0,1},{1,0},{2,3},{3,2},{4,5},{5,4},{6,7},{7,6},{8,9},{9,8},{10,11... | collective-permute-start | bytes 3145736 | tf_op jit(solution)/shard_map/ppermute | solution.py:43
  65.2 9.1 %collective-permute-start.12 = (bf16[128,4096]{1,0:T(8,128)(2,1)S(1)}, bf16[128,4096]{1,0:T(8,128)(2,1)S(1)}, u32[]{:S(2)}, u32[]{:S(2)}) collective-permute-start(bf16[128,4096]{1,0:T(8,128)(2,1)S(1)} %get-tuple-element.70.refs_5_.refs_9_), channel_id=1, source_target_pairs={{0,1},{1,0},{2,3},{3,2},{4,5},{5,4},{6,7},{7,6},{8,9},{9,8},{10,11... | collective-permute-start | bytes 3145736 | tf_op jit(solution)/shard_map/ppermute | solution.py:43
  78.4 6.1 %collective-permute-start.13 = (bf16[128,4096]{1,0:T(8,128)(2,1)S(1)}, bf16[128,4096]{1,0:T(8,128)(2,1)S(1)}, u32[]{:S(2)}, u32[]{:S(2)}) collective-permute-start(bf16[128,4096]{1,0:T(8,128)(2,1)S(1)} %get-tuple-element.81.refs_9_), channel_id=1, source_target_pairs={{0,1},{1,0},{2,3},{3,2},{4,5},{5,4},{6,7},{7,6},{8,9},{9,8},{10,11... | collective-permute-start | bytes 3145736 | tf_op jit(solution)/shard_map/ppermute | solution.py:43
  78.6 17.5 %collective-permute-start.16 = (bf16[32,4096]{1,0:T(8,128)(2,1)S(1)}, bf16[32,4096]{1,0:T(8,128)(2,1)S(1)}, u32[]{:S(2)}, u32[]{:S(2)}) collective-permute-start(bf16[32,4096]{1,0:T(8,128)(2,1)S(1)} %get-tuple-element.87), channel_id=1, source_target_pairs={{0,28},{1,5},{2,30},{3,7},{4,0},{5,9},{6,2},{7,11},{8,4},{9,13},{1... | collective-permute-start | bytes 786440 | tf_op jit(solution)/shard_map/ppermute | solution.py:43
  84.7 21.9 %collective-permute-start.14 = (bf16[32,4096]{1,0:T(8,128)(2,1)S(1)}, bf16[32,4096]{1,0:T(8,128)(2,1)S(1)}, u32[]{:S(2)}, u32[]{:S(2)}) collective-permute-start(bf16[32,4096]{1,0:T(8,128)(2,1)S(1)} %get-tuple-element.84), channel_id=1, source_target_pairs={{0,28},{1,5},{2,30},{3,7},{4,0},{5,9},{6,2},{7,11},{8,4},{9,13},{1... | collective-permute-start | bytes 786440 | tf_op jit(solution)/shard_map/ppermute | solution.py:43
  86.1 24.4 %collective-permute-start.20 = (bf16[32,4096]{1,0:T(8,128)(2,1)S(1)}, bf16[32,4096]{1,0:T(8,128)(2,1)S(1)}, u32[]{:S(2)}, u32[]{:S(2)}) collective-permute-start(bf16[32,4096]{1,0:T(8,128)(2,1)S(1)} %get-tuple-element.93), channel_id=1, source_target_pairs={{0,28},{1,5},{2,30},{3,7},{4,0},{5,9},{6,2},{7,11},{8,4},{9,13},{1... | collective-permute-start | bytes 786440 | tf_op jit(solution)/shard_map/ppermute | solution.py:43
  89.2 6.5 %collective-permute-start.17 = (bf16[16,4096]{1,0:T(8,128)(2,1)S(1)}, bf16[16,4096]{1,0:T(8,128)(2,1)S(1)}, u32[]{:S(2)}, u32[]{:S(2)}) collective-permute-start(bf16[16,4096]{1,0:T(8,128)(2,1)S(1)} %get-tuple-element.79.refs_2_), channel_id=1, source_target_pairs={{0,24},{1,9},{2,26},{3,11},{4,28},{5,13},{6,30},{7,15},{8,0},{9,17... | collective-permute-start | bytes 393224 | tf_op jit(solution)/shard_map/ppermute | solution.py:43
  89.2 13.2 %collective-permute-start.15 = (bf16[16,4096]{1,0:T(8,128)(2,1)S(1)}, bf16[16,4096]{1,0:T(8,128)(2,1)S(1)}, u32[]{:S(2)}, u32[]{:S(2)}) collective-permute-start(bf16[16,4096]{1,0:T(8,128)(2,1)S(1)} %get-tuple-element.85.refs_3_), channel_id=1, source_target_pairs={{0,24},{1,9},{2,26},{3,11},{4,28},{5,13},{6,30},{7,15},{8,0},{9,17... | collective-permute-start | bytes 393224 | tf_op jit(solution)/shard_map/ppermute | solution.py:43
  95.8 27.5 %collective-permute-start.24 = (bf16[35,64,128]{2,1,0:T(8,128)(2,1)S(1)}, bf16[35,64,128]{2,1,0:T(8,128)(2,1)S(1)}, u32[]{:S(2)}, u32[]{:S(2)}) collective-permute-start(bf16[35,64,128]{2,1,0:T(8,128)(2,1)S(1)} %shard_map.124.refs_9_), channel_id=1, source_target_pairs={{0,160},{32,192},{64,224},{96,128},{128,32},{160,64},{192,96},{224... | collective-permute-start | bytes 1720328 | tf_op jit(solution)/shard_map/ppermute | solution.py:47
  96.1 30.3 %collective-permute-start.26 = (bf16[35,64,128]{2,1,0:T(8,128)(2,1)S(1)}, bf16[35,64,128]{2,1,0:T(8,128)(2,1)S(1)}, u32[]{:S(2)}, u32[]{:S(2)}) collective-permute-start(bf16[35,64,128]{2,1,0:T(8,128)(2,1)S(1)} %get-tuple-element.99), channel_id=1, source_target_pairs={{0,192},{32,224},{64,128},{96,160},{128,64},{160,96},{192,0},{224,... | collective-permute-start | bytes 1720328 | tf_op jit(solution)/shard_map/ppermute | solution.py:47
  102.5 10.9 %collective-permute-start.19 = (bf16[32,4096]{1,0:T(8,128)(2,1)S(1)}, bf16[32,4096]{1,0:T(8,128)(2,1)S(1)}, u32[]{:S(2)}, u32[]{:S(2)}) collective-permute-start(bf16[32,4096]{1,0:T(8,128)(2,1)S(1)} %shard_map.130.refs_9_), channel_id=1, source_target_pairs={{0,24},{1,9},{2,26},{3,11},{4,28},{5,13},{6,30},{7,15},{8,0},{9,17... | collective-permute-start | bytes 786440 | tf_op jit(solution)/shard_map/ppermute | solution.py:43
  106.7 11.2 %collective-permute-start.18 = (bf16[32,4096]{1,0:T(8,128)(2,1)S(1)}, bf16[32,4096]{1,0:T(8,128)(2,1)S(1)}, u32[]{:S(2)}, u32[]{:S(2)}) collective-permute-start(bf16[32,4096]{1,0:T(8,128)(2,1)S(1)} %get-tuple-element.91), channel_id=1, source_target_pairs={{0,28},{1,5},{2,30},{3,7},{4,0},{5,9},{6,2},{7,11},{8,4},{9,13},{1... | collective-permute-start | bytes 786440 | tf_op jit(solution)/shard_map/ppermute | solution.py:43
  110.5 11.3 %collective-permute-start.21 = (bf16[32,4096]{1,0:T(8,128)(2,1)S(1)}, bf16[32,4096]{1,0:T(8,128)(2,1)S(1)}, u32[]{:S(2)}, u32[]{:S(2)}) collective-permute-start(bf16[32,4096]{1,0:T(8,128)(2,1)S(1)} %shard_map.132.refs_9_), channel_id=1, source_target_pairs={{0,24},{1,9},{2,26},{3,11},{4,28},{5,13},{6,30},{7,15},{8,0},{9,17... | collective-permute-start | bytes 786440 | tf_op jit(solution)/shard_map/ppermute | solution.py:43
  122.0 5.9 %collective-permute-start.22 = (bf16[32,4096]{1,0:T(8,128)(2,1)S(1)}, bf16[32,4096]{1,0:T(8,128)(2,1)S(1)}, u32[]{:S(2)}, u32[]{:S(2)}) collective-permute-start(bf16[32,4096]{1,0:T(8,128)(2,1)S(1)} %get-tuple-element.96), channel_id=1, source_target_pairs={{0,1},{1,0},{2,3},{3,2},{4,5},{5,4},{6,7},{7,6},{8,9},{9,8},{10,11... | collective-permute-start | bytes 786440 | tf_op jit(solution)/shard_map/ppermute | solution.py:43
  122.1 29.1 %collective-permute-start.25 = (bf16[35,64,128]{2,1,0:T(8,128)(2,1)S(1)}, bf16[35,64,128]{2,1,0:T(8,128)(2,1)S(1)}, u32[]{:S(2)}, u32[]{:S(2)}) collective-permute-start(bf16[35,64,128]{2,1,0:T(8,128)(2,1)S(1)} %get-tuple-element.77.refs_2_), channel_id=1, source_target_pairs={{0,96},{32,0},{64,32},{96,64},{128,224},{160,128},{192,160},{224,1... | collective-permute-start | bytes 1720328 | tf_op jit(solution)/shard_map/ppermute | solution.py:47
  122.2 48.3 %collective-permute-start.27 = (bf16[35,64,128]{2,1,0:T(8,128)(2,1)S(1)}, bf16[35,64,128]{2,1,0:T(8,128)(2,1)S(1)}, u32[]{:S(2)}, u32[]{:S(2)}) collective-permute-start(bf16[35,64,128]{2,1,0:T(8,128)(2,1)S(1)} %get-tuple-element.82.refs_2_), channel_id=1, source_target_pairs={{0,224},{32,128},{64,160},{96,192},{128,96},{160,0},{192,32},{224,... | collective-permute-start | bytes 1720328 | tf_op jit(solution)/shard_map/ppermute | solution.py:47
  123.3 47.7 %collective-permute-start.28 = (bf16[35,64,128]{2,1,0:T(8,128)(2,1)S(1)}, bf16[35,64,128]{2,1,0:T(8,128)(2,1)S(1)}, u32[]{:S(2)}, u32[]{:S(2)}) collective-permute-start(bf16[35,64,128]{2,1,0:T(8,128)(2,1)S(1)} %get-tuple-element.101), channel_id=1, source_target_pairs={{0,32},{32,64},{64,96},{96,0},{128,160},{160,192},{192,224},{224,1... | collective-permute-start | bytes 1720328 | tf_op jit(solution)/shard_map/ppermute | solution.py:47
  126.5 44.6 %collective-permute-start.30 = (bf16[35,64,128]{2,1,0:T(8,128)(2,1)S(1)}, bf16[35,64,128]{2,1,0:T(8,128)(2,1)S(1)}, u32[]{:S(2)}, u32[]{:S(2)}) collective-permute-start(bf16[35,64,128]{2,1,0:T(8,128)(2,1)S(1)} %get-tuple-element.102), channel_id=1, source_target_pairs={{0,64},{32,96},{64,0},{96,32},{128,192},{160,224},{192,128},{224,1... | collective-permute-start | bytes 1720328 | tf_op jit(solution)/shard_map/ppermute | solution.py:47
  127.9 43.1 %collective-permute-start.29 = (bf16[35,64,128]{2,1,0:T(8,128)(2,1)S(1)}, bf16[35,64,128]{2,1,0:T(8,128)(2,1)S(1)}, u32[]{:S(2)}, u32[]{:S(2)}) collective-permute-start(bf16[35,64,128]{2,1,0:T(8,128)(2,1)S(1)} %get-tuple-element.88.refs_3_), channel_id=1, source_target_pairs={{0,128},{32,160},{64,192},{96,224},{128,0},{160,32},{192,64},{224,... | collective-permute-start | bytes 1720328 | tf_op jit(solution)/shard_map/ppermute | solution.py:47
  151.2 22.7 %collective-permute-start.23 = (bf16[16,4096]{1,0:T(8,128)(2,1)S(1)}, bf16[16,4096]{1,0:T(8,128)(2,1)S(1)}, u32[]{:S(2)}, u32[]{:S(2)}) collective-permute-start(bf16[16,4096]{1,0:T(8,128)(2,1)S(1)} %get-tuple-element.98), channel_id=1, source_target_pairs={{0,2},{1,3},{2,0},{3,1},{4,6},{5,7},{6,4},{7,5},{8,10},{9,11},{10,... | collective-permute-start | bytes 393224 | tf_op jit(solution)/shard_map/ppermute | solution.py:43

commit v8 on v7

--- a/solution.py
+++ b/solution.py
@@ -125,7 +125,7 @@
 
 def forward_kernel(first, idx_ref, xa, xb, w_ref, g_ref, act_ref, p_ref, acc_ref):
     d = w_ref.shape[0]
-    kb = 1024
+    kb = 2048
 
     def product(s):
         cols = pl.ds(pl.multiple_of(s * kb, kb), kb)
@@ -147,7 +147,7 @@
         p_ref[rows, :] = grad.astype(BF16)
         return carry
 
-    lax.fori_loop(0, act_ref.shape[0], finish, 0, unroll=2)
+    lax.fori_loop(0, act_ref.shape[0], finish, 0, unroll=4)
 
 
 def forward(first, idx, xa, xb, masked, act_grad, after=()):
@@ -391,7 +391,8 @@
 
     partner = move(tokens, dc=1)
     home = move(tokens, dx=1)
-    chip = join(tokens, partner)
+    lifted = call(head_kernel, 0, jax.ShapeDtypeStruct(tokens.shape, BF16), (tokens,), 0)
+    chip = join(lifted, partner)
     t, g, chip = lax.optimization_barrier((t, g, chip))
     z, xh, core = t >> 2, (t >> 1) & 1, t & 1
     xl, y = g >> 2, g & 3
@@ -441,7 +442,7 @@
     near3, masked = lax.optimization_barrier((near3, masked))
 
     cross = [move(v, dx=1) for v in (near1, near2, near3, far)]
-    x0 = join(tokens, far, near1, near2, near3)
+    x0 = join(lifted, far, near1, near2, near3)
     x2 = move(x0, dc=1)
     x1 = join(home, cross[3], *cross[:3])
     x3 = move(x1, dc=1)

time: 175 us -> 173 us (0.989)
    pallas_call x28 -> x29, Pallas kernels: 37.4 us -> 36.3 us  [call(): pl.pallas_call(run, out_shape=out_shape, in_specs=[SMEM] * n_scalar + [sp...]
  transfers between devices with their start and end apart: 31 -> 31, of which waited for: 10 -> 10; matrix products, arithmetic and copies ran while one was open for 3% -> 3% of each run, Pallas kernels for 19% -> 18%
where the time goes in v8:
time: 173 us
  starting transfers between devices  64.6 us (37%)
  waiting for transfers between devices  64.3 us (37%)
  Pallas kernels  36.3 us (21%)
  other arithmetic  3.53 us (2%)
  local copies, waits for them, and re-layouts  1.98 us (1%)
    ppermute x24, starting transfers between devices, move(): return lax.ppermute(x, 'tensor', tensor_perm(dz, dx, dc, split=True))  52.7 us
    ppermute x24, waiting for transfers between devices, move(): return lax.ppermute(x, 'tensor', tensor_perm(dz, dx, dc, split=True))  43.5 us
    pallas_call x29, Pallas kernels, call(): pl.pallas_call(run, out_shape=out_shape, in_specs=[SMEM] * n_scalar + [sp...  36.3 us
    ppermute x7, waiting for transfers between devices, move_dp(): return lax.ppermute(x, 'dp', dp_perm(dx, dy))  20.8 us
    ppermute x7, starting transfers between devices, move_dp(): return lax.ppermute(x, 'dp', dp_perm(dx, dy))  11.9 us
  transfers between devices with their start and end apart: 31, of which 10 were waited for; matrix products, arithmetic and copies ran while one was open for 3% of the time, Pallas kernels for 18%

profile of v8, /device:TPU:26, one launch (start us, length us, event | category | flops | bytes accessed | tf_op | source)
XLA Modules:
  0.0 172.8 jit_solution(7044538548481837778)
XLA Ops:
  0.8 0.9 copy-done.2
  2.3 3.3 %collective-permute-start.2 = (bf16[32,4096]{1,0:T(8,128)(2,1)S(1)}, bf16[32,4096]{1,0:T(8,128)(2,1)S(1)}, u32[]{:S(2)}, u32[]{:S(2)}) collective-permute-start(bf16[32,4096]{1,0:T(8,128)(2,1)S(1)} %shard_map.113), channel_id=1, source_target_pairs={{0,8},{1,25},{2,10},{3,27},{4,12},{5,29},{6,14},{7,31},{8,16},{9,1... | collective-permute-start | bytes 786440 | tf_op jit(solution)/shard_map/ppermute | solution.py:43
  5.6 1.9 %collective-permute-start.1 = (bf16[32,4096]{1,0:T(8,128)(2,1)S(1)}, bf16[32,4096]{1,0:T(8,128)(2,1)S(1)}, u32[]{:S(2)}, u32[]{:S(2)}) collective-permute-start(bf16[32,4096]{1,0:T(8,128)(2,1)S(1)} %shard_map.113), channel_id=1, source_target_pairs={{0,4},{1,29},{2,6},{3,31},{4,8},{5,1},{6,10},{7,3},{8,12},{9,5},{1... | collective-permute-start | bytes 786440 | tf_op jit(solution)/shard_map/ppermute | solution.py:43
  7.6 0.9 dynamic-slice_compare_fusion
  9.3 1.0 convert_reduce_fusion
  10.3 7.9 %collective-permute-done.1.refs_2_ = bf16[32,4096]{1,0:T(8,128)(2,1)S(1)} collective-permute-done((bf16[32,4096]{1,0:T(8,128)(2,1)S(1)}, bf16[32,4096]{1,0:T(8,128)(2,1)S(1)}, u32[]{:S(2)}, u32[]{:S(2)}) %collective-permute-start.1) | collective-permute-done | bytes 262176 | tf_op jit(solution)/shard_map/ppermute | solution.py:43
  18.2 1.9 %select_reduce_fusion = s32[8,70]{0,1:T(8,128)S(1)} fusion(s32[112]{0:T(128)} %constant.79, s32[8,112]{1,0:T(8,128)S(1)} %get-tuple-element.59), kind=kLoop, calls=%fused_computation.2 | loop fusion | flops 187600 | bytes 6272 | tf_op jit(solution)/shard_map/reduce_sum | solution.py:384
  20.3 3.9 %collective-permute-start.3 = (bf16[16,4096]{1,0:T(8,128)(2,1)S(1)}, bf16[16,4096]{1,0:T(8,128)(2,1)S(1)}, u32[]{:S(2)}, u32[]{:S(2)}) collective-permute-start(bf16[16,4096]{1,0:T(8,128)(2,1)S(1)} %shard_map.116), channel_id=1, source_target_pairs={{0,8},{1,25},{2,10},{3,27},{4,12},{5,29},{6,14},{7,31},{8,16},{9,1... | collective-permute-start | bytes 393224 | tf_op jit(solution)/shard_map/ppermute | solution.py:43
  24.2 0.9 copy-done.1
  25.1 3.4 %shard_map.118.refs_3_.refs_1_ = bf16[4096,896]{1,0:T(8,128)(2,1)S(1)} custom-call(s32[1]{0:T(128)} %bitcast.refs_0_, bf16[4096,896]{1,0:T(8,128)(2,1)} %refs_1_.1, s32[64,448]{1,0:T(8,128)S(1)} %copy-done.1), custom_call_target="tpu_custom_call" | custom-call | flops 3670016 | bytes 7454724 | tf_op jit(solution)/shard_map/pallas_call | solution.py:62
  28.5 0.7 collective-permute-done.4.refs_4_
  29.4 2.2 %collective-permute-start.6 = (bf16[16,4096]{1,0:T(8,128)(2,1)S(1)}, bf16[16,4096]{1,0:T(8,128)(2,1)S(1)}, u32[]{:S(2)}, u32[]{:S(2)}) collective-permute-start(bf16[16,4096]{1,0:T(8,128)(2,1)S(1)} %copy-done.3), channel_id=1, source_target_pairs={{0,2},{1,3},{2,0},{3,1},{4,6},{5,7},{6,4},{7,5},{8,10},{9,11},{10,... | collective-permute-start | bytes 393224 | tf_op jit(solution)/shard_map/ppermute | solution.py:43
  31.6 1.4 collective-permute-start.9
  33.0 2.1 %collective-permute-start.8 = (bf16[32,4096]{1,0:T(8,128)(2,1)S(1)}, bf16[32,4096]{1,0:T(8,128)(2,1)S(1)}, u32[]{:S(2)}, u32[]{:S(2)}) collective-permute-start(bf16[32,4096]{1,0:T(8,128)(2,1)S(1)} %collective-permute-done.1.refs_2_), channel_id=1, source_target_pairs={{0,2},{1,3},{2,0},{3,1},{4,6},{5,7},{6,4},{7,5},{8,10},{9,11},{10,... | collective-permute-start | bytes 786440 | tf_op jit(solution)/shard_map/ppermute | solution.py:43
  35.2 1.4 collective-permute-start.10
  36.6 0.8 collective-permute-done.6.refs_0_
  37.4 2.1 %collective-permute-start.7 = (bf16[16,4096]{1,0:T(8,128)(2,1)S(1)}, bf16[16,4096]{1,0:T(8,128)(2,1)S(1)}, u32[]{:S(2)}, u32[]{:S(2)}) collective-permute-start(bf16[16,4096]{1,0:T(8,128)(2,1)S(1)} %collective-permute-done.3.refs_1_), channel_id=1, source_target_pairs={{0,2},{1,3},{2,0},{3,1},{4,6},{5,7},{6,4},{7,5},{8,10},{9,11},{10,... | collective-permute-start | bytes 393224 | tf_op jit(solution)/shard_map/ppermute | solution.py:43
  39.5 17.0 %collective-permute-done.7.refs_1_ = bf16[16,4096]{1,0:T(8,128)(2,1)S(1)} collective-permute-done((bf16[16,4096]{1,0:T(8,128)(2,1)S(1)}, bf16[16,4096]{1,0:T(8,128)(2,1)S(1)}, u32[]{:S(2)}, u32[]{:S(2)}) %collective-permute-start.7) | collective-permute-done | bytes 131104 | tf_op jit(solution)/shard_map/ppermute | solution.py:43
  56.7 3.3 %shard_map.121 = (bf16[16,16,896]{2,1,0:T(8,128)(2,1)S(1)}, bf16[256,896]{1,0:T(8,128)(2,1)S(1)}) custom-call(s32[32]{0:T(128)S(1)} %fusion.8.refs_0_, bf16[128,4096]{1,0:T(8,128)(2,1)S(1)} %shard_map.119.refs_1_.refs_5_, bf16[128,4096]{1,0:T(8,128)(2,1)S(1)} %collective-permute-done.5.refs_2_.refs_7_, bf16[4096,896]{1,0:T(8,128)(2,1)S(1)} %shard_map.118.refs_3_.refs_1_, ...), custom_call_target="tpu_custom_call" | custom-call | flops 1879048192 | bytes 10354816 | tf_op jit(solution)/shard_map/pallas_call | solution.py:62
  60.0 3.8 %shard_map.123 = (f32[128,4096]{1,0:T(8,128)S(1)}, bf16[128,4096]{1,0:T(8,128)(2,1)S(1)}) custom-call(bf16[256,896]{1,0:T(8,128)(2,1)S(1)} %get-tuple-element.69.refs_0_.refs_3_, bf16[4096,896]{1,0:T(8,128)(2,1)S(1)} %shard_map.118.refs_3_.refs_1_), custom_call_target="tpu_custom_call" | custom-call | flops 1879048192 | bytes 7798784 | tf_op jit(solution)/shard_map/pallas_call | solution.py:62
  63.8 0.7 collective-permute-start.12
  64.5 3.3 %shard_map.124 = (bf16[16,16,896]{2,1,0:T(8,128)(2,1)S(1)}, bf16[256,896]{1,0:T(8,128)(2,1)S(1)}) custom-call(s32[32]{0:T(128)S(1)} %fusion.8.refs_0_, bf16[128,4096]{1,0:T(8,128)(2,1)S(1)} %shard_map.122.refs_1_.refs_6_, bf16[128,4096]{1,0:T(8,128)(2,1)S(1)} %collective-permute-done.11.refs_2_.refs_8_, bf16[4096,896]{1,0:T(8,128)(2,1)S(1)} %shard_map.118.refs_3_.refs_1_, ...), custom_call_target="tpu_custom_call" | custom-call | flops 1879048192 | bytes 10354816 | tf_op jit(solution)/shard_map/pallas_call | solution.py:62
  67.8 1.7 shard_map.125.refs_9_
  69.5 2.8 %shard_map.126 = (bf16[35,64,128]{2,1,0:T(8,128)(2,1)S(1)}, bf16[35,64,128]{2,1,0:T(8,128)(2,1)S(1)}) custom-call(s32[8]{0:T(128)S(1)} %and_add_fusion.refs_0_, s32[8,70]{1,0:T(8,128)S(1)} %broadcast_add_fusion.refs_1_, s32[8]{0:T(128)S(1)} %get-tuple-element.74.refs_2_, bf16[256,896]{1,0:T(8,128)(2,1)S(1)} %get-tuple-element.69.refs_0_.refs_3_, ...), custom_call_target="tpu_custom_call" | custom-call | flops 939524096 | bytes 5114112 | tf_op jit(solution)/shard_map/pallas_call | solution.py:62
  72.6 3.8 %shard_map.128 = (f32[128,4096]{1,0:T(8,128)S(1)}, bf16[128,4096]{1,0:T(8,128)(2,1)S(1)}) custom-call(bf16[256,896]{1,0:T(8,128)(2,1)S(1)} %get-tuple-element.75.refs_4_.refs_0_, bf16[4096,896]{1,0:T(8,128)(2,1)S(1)} %shard_map.118.refs_3_.refs_1_, bf16[16,4096]{1,0:T(8,128)(2,1)S(1)} %get-tuple-element.79.refs_2_), custom_call_target="tpu_custom_call" | custom-call | flops 1879048192 | bytes 7798784 | tf_op jit(solution)/shard_map/pallas_call | solution.py:62
  76.6 3.1 %collective-permute-start.16 = (bf16[32,4096]{1,0:T(8,128)(2,1)S(1)}, bf16[32,4096]{1,0:T(8,128)(2,1)S(1)}, u32[]{:S(2)}, u32[]{:S(2)}) collective-permute-start(bf16[32,4096]{1,0:T(8,128)(2,1)S(1)} %get-tuple-element.87), channel_id=1, source_target_pairs={{0,28},{1,5},{2,30},{3,7},{4,0},{5,9},{6,2},{7,11},{8,4},{9,13},{1... | collective-permute-start | bytes 786440 | tf_op jit(solution)/shard_map/ppermute | solution.py:43
  79.6 2.8 %shard_map.129 = (bf16[35,64,128]{2,1,0:T(8,128)(2,1)S(1)}, bf16[35,64,128]{2,1,0:T(8,128)(2,1)S(1)}) custom-call(s32[8]{0:T(128)S(1)} %and_add_fusion.refs_0_, s32[8,70]{1,0:T(8,128)S(1)} %broadcast_add_fusion.refs_1_, s32[8]{0:T(128)S(1)} %get-tuple-element.74.refs_2_, bf16[256,896]{1,0:T(8,128)(2,1)S(1)} %get-tuple-element.69.refs_0_.refs_3_, ...), custom_call_target="tpu_custom_call" | custom-call | flops 939524096 | bytes 5114112 | tf_op jit(solution)/shard_map/pallas_call | solution.py:62
  82.7 1.5 collective-permute-start.14
  84.2 3.1 %collective-permute-start.20 = (bf16[32,4096]{1,0:T(8,128)(2,1)S(1)}, bf16[32,4096]{1,0:T(8,128)(2,1)S(1)}, u32[]{:S(2)}, u32[]{:S(2)}) collective-permute-start(bf16[32,4096]{1,0:T(8,128)(2,1)S(1)} %get-tuple-element.93), channel_id=1, source_target_pairs={{0,28},{1,5},{2,30},{3,7},{4,0},{5,9},{6,2},{7,11},{8,4},{9,13},{1... | collective-permute-start | bytes 786440 | tf_op jit(solution)/shard_map/ppermute | solution.py:43
  87.2 1.5 collective-permute-start.15
  88.7 5.1 %collective-permute-done.17.refs_2_ = bf16[16,4096]{1,0:T(8,128)(2,1)S(1)} collective-permute-done((bf16[16,4096]{1,0:T(8,128)(2,1)S(1)}, bf16[16,4096]{1,0:T(8,128)(2,1)S(1)}, u32[]{:S(2)}, u32[]{:S(2)}) %collective-permute-start.17) | collective-permute-done | bytes 131104 | tf_op jit(solution)/shard_map/ppermute | solution.py:43
  94.1 3.4 %collective-permute-start.26 = (bf16[35,64,128]{2,1,0:T(8,128)(2,1)S(1)}, bf16[35,64,128]{2,1,0:T(8,128)(2,1)S(1)}, u32[]{:S(2)}, u32[]{:S(2)}) collective-permute-start(bf16[35,64,128]{2,1,0:T(8,128)(2,1)S(1)} %get-tuple-element.99), channel_id=1, source_target_pairs={{0,192},{32,224},{64,128},{96,160},{128,64},{160,96},{192,0},{224,... | collective-permute-start | bytes 1720328 | tf_op jit(solution)/shard_map/ppermute | solution.py:47
  97.6 2.8 %shard_map.132 = (bf16[35,64,128]{2,1,0:T(8,128)(2,1)S(1)}, bf16[35,64,128]{2,1,0:T(8,128)(2,1)S(1)}) custom-call(s32[8]{0:T(128)S(1)} %and_add_fusion.refs_0_, s32[8,70]{1,0:T(8,128)S(1)} %broadcast_add_fusion.refs_1_, s32[8]{0:T(128)S(1)} %get-tuple-element.74.refs_2_, bf16[256,896]{1,0:T(8,128)(2,1)S(1)} %get-tuple-element.69.refs_0_.refs_3_, ...), custom_call_target="tpu_custom_call" | custom-call | flops 939524096 | bytes 5114112 | tf_op jit(solution)/shard_map/pallas_call | solution.py:62
  100.5 4.4 %collective-permute-start.19 = (bf16[32,4096]{1,0:T(8,128)(2,1)S(1)}, bf16[32,4096]{1,0:T(8,128)(2,1)S(1)}, u32[]{:S(2)}, u32[]{:S(2)}) collective-permute-start(bf16[32,4096]{1,0:T(8,128)(2,1)S(1)} %shard_map.131.refs_9_), channel_id=1, source_target_pairs={{0,24},{1,9},{2,26},{3,11},{4,28},{5,13},{6,30},{7,15},{8,0},{9,17... | collective-permute-start | bytes 786440 | tf_op jit(solution)/shard_map/ppermute | solution.py:43
  104.9 3.5 %collective-permute-start.18 = (bf16[32,4096]{1,0:T(8,128)(2,1)S(1)}, bf16[32,4096]{1,0:T(8,128)(2,1)S(1)}, u32[]{:S(2)}, u32[]{:S(2)}) collective-permute-start(bf16[32,4096]{1,0:T(8,128)(2,1)S(1)} %get-tuple-element.91), channel_id=1, source_target_pairs={{0,28},{1,5},{2,30},{3,7},{4,0},{5,9},{6,2},{7,11},{8,4},{9,13},{1... | collective-permute-start | bytes 786440 | tf_op jit(solution)/shard_map/ppermute | solution.py:43
  108.5 3.0 %collective-permute-done.19.refs_1_ = bf16[32,4096]{1,0:T(8,128)(2,1)S(1)} collective-permute-done((bf16[32,4096]{1,0:T(8,128)(2,1)S(1)}, bf16[32,4096]{1,0:T(8,128)(2,1)S(1)}, u32[]{:S(2)}, u32[]{:S(2)}) %collective-permute-start.19) | collective-permute-done | bytes 262176 | tf_op jit(solution)/shard_map/ppermute | solution.py:43
  111.6 4.4 %collective-permute-done.18.refs_0_ = bf16[32,4096]{1,0:T(8,128)(2,1)S(1)} collective-permute-done((bf16[32,4096]{1,0:T(8,128)(2,1)S(1)}, bf16[32,4096]{1,0:T(8,128)(2,1)S(1)}, u32[]{:S(2)}, u32[]{:S(2)}) %collective-permute-start.18) | collective-permute-done | bytes 262176 | tf_op jit(solution)/shard_map/ppermute | solution.py:43
  115.9 4.0 %collective-permute-done.21.refs_4_ = bf16[32,4096]{1,0:T(8,128)(2,1)S(1)} collective-permute-done((bf16[32,4096]{1,0:T(8,128)(2,1)S(1)}, bf16[32,4096]{1,0:T(8,128)(2,1)S(1)}, u32[]{:S(2)}, u32[]{:S(2)}) %collective-permute-start.21) | collective-permute-done | bytes 262176 | tf_op jit(solution)/shard_map/ppermute | solution.py:43
  120.4 1.2 collective-permute-start.27
  121.5 3.1 %collective-permute-start.28 = (bf16[35,64,128]{2,1,0:T(8,128)(2,1)S(1)}, bf16[35,64,128]{2,1,0:T(8,128)(2,1)S(1)}, u32[]{:S(2)}, u32[]{:S(2)}) collective-permute-start(bf16[35,64,128]{2,1,0:T(8,128)(2,1)S(1)} %get-tuple-element.101), channel_id=1, source_target_pairs={{0,32},{32,64},{64,96},{96,0},{128,160},{160,192},{192,224},{224,1... | collective-permute-start | bytes 1720328 | tf_op jit(solution)/shard_map/ppermute | solution.py:47
  124.7 1.4 collective-permute-start.30
  126.1 2.4 %collective-permute-start.29 = (bf16[35,64,128]{2,1,0:T(8,128)(2,1)S(1)}, bf16[35,64,128]{2,1,0:T(8,128)(2,1)S(1)}, u32[]{:S(2)}, u32[]{:S(2)}) collective-permute-start(bf16[35,64,128]{2,1,0:T(8,128)(2,1)S(1)} %get-tuple-element.88.refs_3_), channel_id=1, source_target_pairs={{0,128},{32,160},{64,192},{96,224},{128,0},{160,32},{192,64},{224,... | collective-permute-start | bytes 1720328 | tf_op jit(solution)/shard_map/ppermute | solution.py:47
  128.6 20.8 %collective-permute-done.25.refs_2_ = bf16[35,64,128]{2,1,0:T(8,128)(2,1)S(1)} collective-permute-done((bf16[35,64,128]{2,1,0:T(8,128)(2,1)S(1)}, bf16[35,64,128]{2,1,0:T(8,128)(2,1)S(1)}, u32[]{:S(2)}, u32[]{:S(2)}) %collective-permute-start.25) | collective-permute-done | bytes 573472 | tf_op jit(solution)/shard_map/ppermute | solution.py:47
  149.4 15.8 %collective-permute-start.23 = (bf16[16,4096]{1,0:T(8,128)(2,1)S(1)}, bf16[16,4096]{1,0:T(8,128)(2,1)S(1)}, u32[]{:S(2)}, u32[]{:S(2)}) collective-permute-start(bf16[16,4096]{1,0:T(8,128)(2,1)S(1)} %get-tuple-element.98), channel_id=1, source_target_pairs={{0,2},{1,3},{2,0},{3,1},{4,6},{5,7},{6,4},{7,5},{8,10},{9,11},{10,... | collective-permute-start | bytes 393224 | tf_op jit(solution)/shard_map/ppermute | solution.py:43
  165.2 1.9 %shard_map.134.refs_3_.refs_0_ = bf16[35,64,128]{2,1,0:T(8,128)(2,1)S(1)} custom-call(s32[8]{0:T(128)S(1)} %and_add_fusion.refs_0_, s32[8,70]{1,0:T(8,128)S(1)} %broadcast_add_fusion.refs_1_, s32[8]{0:T(128)S(1)} %get-tuple-element.74.refs_2_, bf16[256,896]{1,0:T(8,128)(2,1)S(1)} %get-tuple-element.69.refs_0_.refs_3_, ...), custom_call_target="tpu_custom_call" | custom-call | flops 469762048 | bytes 5114112 | tf_op jit(solution)/shard_map/pallas_call | solution.py:62
  167.1 1.6 shard_map.135
  169.2 2.8 %shard_map.140 = f32[512,896]{1,0:T(8,128)} custom-call(s32[1]{0:T(128)} %bitcast.3.refs_0_, s32[8,70]{1,0:T(8,128)S(1)} %broadcast_add_fusion.refs_1_, f32[35,64,128]{2,1,0:T(8,128)S(1)} %shard_map.139.refs_2_, bf16[35,64,128]{2,1,0:T(8,128)(2,1)S(1)} %collective-permute-done.28.refs_3_, bf16[35,64,128]{2,1,0:T(8,128)(2,1)S(1)} %collective-permute-done.29.refs_4_, ...), custom_call_target="tpu_custom_call" | custom-call | flops 2293760 | bytes 2869444 | tf_op jit(solution)/shard_map/pallas_call | solution.py:62
  172.1 0.7 shard_map.138
  (59 shorter events, 4.2 us)
Async XLA Ops:
  0.6 1.6 collective-permute-start
  0.8 0.9 copy-start.2
  2.3 17.9 %collective-permute-start.2 = (bf16[32,4096]{1,0:T(8,128)(2,1)S(1)}, bf16[32,4096]{1,0:T(8,128)(2,1)S(1)}, u32[]{:S(2)}, u32[]{:S(2)}) collective-permute-start(bf16[32,4096]{1,0:T(8,128)(2,1)S(1)} %shard_map.113), channel_id=1, source_target_pairs={{0,8},{1,25},{2,10},{3,27},{4,12},{5,29},{6,14},{7,31},{8,16},{9,1... | collective-permute-start | bytes 786440 | tf_op jit(solution)/shard_map/ppermute | solution.py:43
  5.6 12.6 %collective-permute-start.1 = (bf16[32,4096]{1,0:T(8,128)(2,1)S(1)}, bf16[32,4096]{1,0:T(8,128)(2,1)S(1)}, u32[]{:S(2)}, u32[]{:S(2)}) collective-permute-start(bf16[32,4096]{1,0:T(8,128)(2,1)S(1)} %shard_map.113), channel_id=1, source_target_pairs={{0,4},{1,29},{2,6},{3,31},{4,8},{5,1},{6,10},{7,3},{8,12},{9,5},{1... | collective-permute-start | bytes 786440 | tf_op jit(solution)/shard_map/ppermute | solution.py:43
  20.2 9.0 %collective-permute-start.4 = (bf16[32,4096]{1,0:T(8,128)(2,1)S(1)}, bf16[32,4096]{1,0:T(8,128)(2,1)S(1)}, u32[]{:S(2)}, u32[]{:S(2)}) collective-permute-start(bf16[32,4096]{1,0:T(8,128)(2,1)S(1)} %collective-permute-done.2.refs_0_.refs_3_), channel_id=1, source_target_pairs={{0,4},{1,29},{2,6},{3,31},{4,8},{5,1},{6,10},{7,3},{8,12},{9,5},{1... | collective-permute-start | bytes 786440 | tf_op jit(solution)/shard_map/ppermute | solution.py:43
  20.3 9.0 %collective-permute-start.3 = (bf16[16,4096]{1,0:T(8,128)(2,1)S(1)}, bf16[16,4096]{1,0:T(8,128)(2,1)S(1)}, u32[]{:S(2)}, u32[]{:S(2)}) collective-permute-start(bf16[16,4096]{1,0:T(8,128)(2,1)S(1)} %shard_map.116), channel_id=1, source_target_pairs={{0,8},{1,25},{2,10},{3,27},{4,12},{5,29},{6,14},{7,31},{8,16},{9,1... | collective-permute-start | bytes 393224 | tf_op jit(solution)/shard_map/ppermute | solution.py:43
  24.2 0.9 copy-start.1
  28.5 0.9 copy-start.3
  28.5 28.2 %copy-start = (bf16[512,896]{1,0:T(8,128)(2,1)S(1)}, bf16[512,896]{1,0:T(8,128)(2,1)}, u32[]{:S(2)}) copy-start(bf16[512,896]{1,0:T(8,128)(2,1)} %param.12) | copy-start | bytes 2752516
  29.3 27.4 %collective-permute-start.5 = (bf16[128,4096]{1,0:T(8,128)(2,1)S(1)}, bf16[128,4096]{1,0:T(8,128)(2,1)S(1)}, u32[]{:S(2)}, u32[]{:S(2)}) collective-permute-start(bf16[128,4096]{1,0:T(8,128)(2,1)S(1)} %shard_map.119.refs_1_.refs_5_), channel_id=1, source_target_pairs={{0,1},{1,0},{2,3},{3,2},{4,5},{5,4},{6,7},{7,6},{8,9},{9,8},{10,11... | collective-permute-start | bytes 3145736 | tf_op jit(solution)/shard_map/ppermute | solution.py:43
  29.4 8.0 %collective-permute-start.6 = (bf16[16,4096]{1,0:T(8,128)(2,1)S(1)}, bf16[16,4096]{1,0:T(8,128)(2,1)S(1)}, u32[]{:S(2)}, u32[]{:S(2)}) collective-permute-start(bf16[16,4096]{1,0:T(8,128)(2,1)S(1)} %copy-done.3), channel_id=1, source_target_pairs={{0,2},{1,3},{2,0},{3,1},{4,6},{5,7},{6,4},{7,5},{8,10},{9,11},{10,... | collective-permute-start | bytes 393224 | tf_op jit(solution)/shard_map/ppermute | solution.py:43
  31.6 24.8 %collective-permute-start.9 = (bf16[32,4096]{1,0:T(8,128)(2,1)S(1)}, bf16[32,4096]{1,0:T(8,128)(2,1)S(1)}, u32[]{:S(2)}, u32[]{:S(2)}) collective-permute-start(bf16[32,4096]{1,0:T(8,128)(2,1)S(1)} %collective-permute-done.2.refs_0_.refs_3_), channel_id=1, source_target_pairs={{0,2},{1,3},{2,0},{3,1},{4,6},{5,7},{6,4},{7,5},{8,10},{9,11},{10,... | collective-permute-start | bytes 786440 | tf_op jit(solution)/shard_map/ppermute | solution.py:43
  33.0 23.4 %collective-permute-start.8 = (bf16[32,4096]{1,0:T(8,128)(2,1)S(1)}, bf16[32,4096]{1,0:T(8,128)(2,1)S(1)}, u32[]{:S(2)}, u32[]{:S(2)}) collective-permute-start(bf16[32,4096]{1,0:T(8,128)(2,1)S(1)} %collective-permute-done.1.refs_2_), channel_id=1, source_target_pairs={{0,2},{1,3},{2,0},{3,1},{4,6},{5,7},{6,4},{7,5},{8,10},{9,11},{10,... | collective-permute-start | bytes 786440 | tf_op jit(solution)/shard_map/ppermute | solution.py:43
  35.2 21.3 %collective-permute-start.10 = (bf16[32,4096]{1,0:T(8,128)(2,1)S(1)}, bf16[32,4096]{1,0:T(8,128)(2,1)S(1)}, u32[]{:S(2)}, u32[]{:S(2)}) collective-permute-start(bf16[32,4096]{1,0:T(8,128)(2,1)S(1)} %collective-permute-done.4.refs_4_), channel_id=1, source_target_pairs={{0,2},{1,3},{2,0},{3,1},{4,6},{5,7},{6,4},{7,5},{8,10},{9,11},{10,... | collective-permute-start | bytes 786440 | tf_op jit(solution)/shard_map/ppermute | solution.py:43
  37.4 19.1 %collective-permute-start.7 = (bf16[16,4096]{1,0:T(8,128)(2,1)S(1)}, bf16[16,4096]{1,0:T(8,128)(2,1)S(1)}, u32[]{:S(2)}, u32[]{:S(2)}) collective-permute-start(bf16[16,4096]{1,0:T(8,128)(2,1)S(1)} %collective-permute-done.3.refs_1_), channel_id=1, source_target_pairs={{0,2},{1,3},{2,0},{3,1},{4,6},{5,7},{6,4},{7,5},{8,10},{9,11},{10,... | collective-permute-start | bytes 393224 | tf_op jit(solution)/shard_map/ppermute | solution.py:43
  56.6 7.9 %collective-permute-start.11 = (bf16[128,4096]{1,0:T(8,128)(2,1)S(1)}, bf16[128,4096]{1,0:T(8,128)(2,1)S(1)}, u32[]{:S(2)}, u32[]{:S(2)}) collective-permute-start(bf16[128,4096]{1,0:T(8,128)(2,1)S(1)} %shard_map.122.refs_1_.refs_6_), channel_id=1, source_target_pairs={{0,1},{1,0},{2,3},{3,2},{4,5},{5,4},{6,7},{7,6},{8,9},{9,8},{10,11... | collective-permute-start | bytes 3145736 | tf_op jit(solution)/shard_map/ppermute | solution.py:43
  63.8 8.6 %collective-permute-start.12 = (bf16[128,4096]{1,0:T(8,128)(2,1)S(1)}, bf16[128,4096]{1,0:T(8,128)(2,1)S(1)}, u32[]{:S(2)}, u32[]{:S(2)}) collective-permute-start(bf16[128,4096]{1,0:T(8,128)(2,1)S(1)} %get-tuple-element.70.refs_5_.refs_9_), channel_id=1, source_target_pairs={{0,1},{1,0},{2,3},{3,2},{4,5},{5,4},{6,7},{7,6},{8,9},{9,8},{10,11... | collective-permute-start | bytes 3145736 | tf_op jit(solution)/shard_map/ppermute | solution.py:43
  76.4 6.1 %collective-permute-start.13 = (bf16[128,4096]{1,0:T(8,128)(2,1)S(1)}, bf16[128,4096]{1,0:T(8,128)(2,1)S(1)}, u32[]{:S(2)}, u32[]{:S(2)}) collective-permute-start(bf16[128,4096]{1,0:T(8,128)(2,1)S(1)} %get-tuple-element.81.refs_9_), channel_id=1, source_target_pairs={{0,1},{1,0},{2,3},{3,2},{4,5},{5,4},{6,7},{7,6},{8,9},{9,8},{10,11... | collective-permute-start | bytes 3145736 | tf_op jit(solution)/shard_map/ppermute | solution.py:43
  76.6 17.6 %collective-permute-start.16 = (bf16[32,4096]{1,0:T(8,128)(2,1)S(1)}, bf16[32,4096]{1,0:T(8,128)(2,1)S(1)}, u32[]{:S(2)}, u32[]{:S(2)}) collective-permute-start(bf16[32,4096]{1,0:T(8,128)(2,1)S(1)} %get-tuple-element.87), channel_id=1, source_target_pairs={{0,28},{1,5},{2,30},{3,7},{4,0},{5,9},{6,2},{7,11},{8,4},{9,13},{1... | collective-permute-start | bytes 786440 | tf_op jit(solution)/shard_map/ppermute | solution.py:43
  82.7 22.1 %collective-permute-start.14 = (bf16[32,4096]{1,0:T(8,128)(2,1)S(1)}, bf16[32,4096]{1,0:T(8,128)(2,1)S(1)}, u32[]{:S(2)}, u32[]{:S(2)}) collective-permute-start(bf16[32,4096]{1,0:T(8,128)(2,1)S(1)} %get-tuple-element.84), channel_id=1, source_target_pairs={{0,28},{1,5},{2,30},{3,7},{4,0},{5,9},{6,2},{7,11},{8,4},{9,13},{1... | collective-permute-start | bytes 786440 | tf_op jit(solution)/shard_map/ppermute | solution.py:43
  84.2 24.3 %collective-permute-start.20 = (bf16[32,4096]{1,0:T(8,128)(2,1)S(1)}, bf16[32,4096]{1,0:T(8,128)(2,1)S(1)}, u32[]{:S(2)}, u32[]{:S(2)}) collective-permute-start(bf16[32,4096]{1,0:T(8,128)(2,1)S(1)} %get-tuple-element.93), channel_id=1, source_target_pairs={{0,28},{1,5},{2,30},{3,7},{4,0},{5,9},{6,2},{7,11},{8,4},{9,13},{1... | collective-permute-start | bytes 786440 | tf_op jit(solution)/shard_map/ppermute | solution.py:43
  87.2 6.5 %collective-permute-start.17 = (bf16[16,4096]{1,0:T(8,128)(2,1)S(1)}, bf16[16,4096]{1,0:T(8,128)(2,1)S(1)}, u32[]{:S(2)}, u32[]{:S(2)}) collective-permute-start(bf16[16,4096]{1,0:T(8,128)(2,1)S(1)} %get-tuple-element.79.refs_2_), channel_id=1, source_target_pairs={{0,24},{1,9},{2,26},{3,11},{4,28},{5,13},{6,30},{7,15},{8,0},{9,17... | collective-permute-start | bytes 393224 | tf_op jit(solution)/shard_map/ppermute | solution.py:43
  87.2 13.2 %collective-permute-start.15 = (bf16[16,4096]{1,0:T(8,128)(2,1)S(1)}, bf16[16,4096]{1,0:T(8,128)(2,1)S(1)}, u32[]{:S(2)}, u32[]{:S(2)}) collective-permute-start(bf16[16,4096]{1,0:T(8,128)(2,1)S(1)} %get-tuple-element.85.refs_3_), channel_id=1, source_target_pairs={{0,24},{1,9},{2,26},{3,11},{4,28},{5,13},{6,30},{7,15},{8,0},{9,17... | collective-permute-start | bytes 393224 | tf_op jit(solution)/shard_map/ppermute | solution.py:43
  93.8 27.7 %collective-permute-start.24 = (bf16[35,64,128]{2,1,0:T(8,128)(2,1)S(1)}, bf16[35,64,128]{2,1,0:T(8,128)(2,1)S(1)}, u32[]{:S(2)}, u32[]{:S(2)}) collective-permute-start(bf16[35,64,128]{2,1,0:T(8,128)(2,1)S(1)} %shard_map.125.refs_9_), channel_id=1, source_target_pairs={{0,160},{32,192},{64,224},{96,128},{128,32},{160,64},{192,96},{224... | collective-permute-start | bytes 1720328 | tf_op jit(solution)/shard_map/ppermute | solution.py:47
  94.1 30.6 %collective-permute-start.26 = (bf16[35,64,128]{2,1,0:T(8,128)(2,1)S(1)}, bf16[35,64,128]{2,1,0:T(8,128)(2,1)S(1)}, u32[]{:S(2)}, u32[]{:S(2)}) collective-permute-start(bf16[35,64,128]{2,1,0:T(8,128)(2,1)S(1)} %get-tuple-element.99), channel_id=1, source_target_pairs={{0,192},{32,224},{64,128},{96,160},{128,64},{160,96},{192,0},{224,... | collective-permute-start | bytes 1720328 | tf_op jit(solution)/shard_map/ppermute | solution.py:47
  100.5 11.1 %collective-permute-start.19 = (bf16[32,4096]{1,0:T(8,128)(2,1)S(1)}, bf16[32,4096]{1,0:T(8,128)(2,1)S(1)}, u32[]{:S(2)}, u32[]{:S(2)}) collective-permute-start(bf16[32,4096]{1,0:T(8,128)(2,1)S(1)} %shard_map.131.refs_9_), channel_id=1, source_target_pairs={{0,24},{1,9},{2,26},{3,11},{4,28},{5,13},{6,30},{7,15},{8,0},{9,17... | collective-permute-start | bytes 786440 | tf_op jit(solution)/shard_map/ppermute | solution.py:43
  104.9 11.0 %collective-permute-start.18 = (bf16[32,4096]{1,0:T(8,128)(2,1)S(1)}, bf16[32,4096]{1,0:T(8,128)(2,1)S(1)}, u32[]{:S(2)}, u32[]{:S(2)}) collective-permute-start(bf16[32,4096]{1,0:T(8,128)(2,1)S(1)} %get-tuple-element.91), channel_id=1, source_target_pairs={{0,28},{1,5},{2,30},{3,7},{4,0},{5,9},{6,2},{7,11},{8,4},{9,13},{1... | collective-permute-start | bytes 786440 | tf_op jit(solution)/shard_map/ppermute | solution.py:43
  108.5 11.5 %collective-permute-start.21 = (bf16[32,4096]{1,0:T(8,128)(2,1)S(1)}, bf16[32,4096]{1,0:T(8,128)(2,1)S(1)}, u32[]{:S(2)}, u32[]{:S(2)}) collective-permute-start(bf16[32,4096]{1,0:T(8,128)(2,1)S(1)} %shard_map.133.refs_9_), channel_id=1, source_target_pairs={{0,24},{1,9},{2,26},{3,11},{4,28},{5,13},{6,30},{7,15},{8,0},{9,17... | collective-permute-start | bytes 786440 | tf_op jit(solution)/shard_map/ppermute | solution.py:43
  120.2 5.9 %collective-permute-start.22 = (bf16[32,4096]{1,0:T(8,128)(2,1)S(1)}, bf16[32,4096]{1,0:T(8,128)(2,1)S(1)}, u32[]{:S(2)}, u32[]{:S(2)}) collective-permute-start(bf16[32,4096]{1,0:T(8,128)(2,1)S(1)} %get-tuple-element.96), channel_id=1, source_target_pairs={{0,1},{1,0},{2,3},{3,2},{4,5},{5,4},{6,7},{7,6},{8,9},{9,8},{10,11... | collective-permute-start | bytes 786440 | tf_op jit(solution)/shard_map/ppermute | solution.py:43
  120.3 29.1 %collective-permute-start.25 = (bf16[35,64,128]{2,1,0:T(8,128)(2,1)S(1)}, bf16[35,64,128]{2,1,0:T(8,128)(2,1)S(1)}, u32[]{:S(2)}, u32[]{:S(2)}) collective-permute-start(bf16[35,64,128]{2,1,0:T(8,128)(2,1)S(1)} %get-tuple-element.77.refs_2_), channel_id=1, source_target_pairs={{0,96},{32,0},{64,32},{96,64},{128,224},{160,128},{192,160},{224,1... | collective-permute-start | bytes 1720328 | tf_op jit(solution)/shard_map/ppermute | solution.py:47
  120.4 48.3 %collective-permute-start.27 = (bf16[35,64,128]{2,1,0:T(8,128)(2,1)S(1)}, bf16[35,64,128]{2,1,0:T(8,128)(2,1)S(1)}, u32[]{:S(2)}, u32[]{:S(2)}) collective-permute-start(bf16[35,64,128]{2,1,0:T(8,128)(2,1)S(1)} %get-tuple-element.82.refs_2_), channel_id=1, source_target_pairs={{0,224},{32,128},{64,160},{96,192},{128,96},{160,0},{192,32},{224,... | collective-permute-start | bytes 1720328 | tf_op jit(solution)/shard_map/ppermute | solution.py:47
  121.5 47.7 %collective-permute-start.28 = (bf16[35,64,128]{2,1,0:T(8,128)(2,1)S(1)}, bf16[35,64,128]{2,1,0:T(8,128)(2,1)S(1)}, u32[]{:S(2)}, u32[]{:S(2)}) collective-permute-start(bf16[35,64,128]{2,1,0:T(8,128)(2,1)S(1)} %get-tuple-element.101), channel_id=1, source_target_pairs={{0,32},{32,64},{64,96},{96,0},{128,160},{160,192},{192,224},{224,1... | collective-permute-start | bytes 1720328 | tf_op jit(solution)/shard_map/ppermute | solution.py:47
  124.7 44.5 %collective-permute-start.30 = (bf16[35,64,128]{2,1,0:T(8,128)(2,1)S(1)}, bf16[35,64,128]{2,1,0:T(8,128)(2,1)S(1)}, u32[]{:S(2)}, u32[]{:S(2)}) collective-permute-start(bf16[35,64,128]{2,1,0:T(8,128)(2,1)S(1)} %get-tuple-element.102), channel_id=1, source_target_pairs={{0,64},{32,96},{64,0},{96,32},{128,192},{160,224},{192,128},{224,1... | collective-permute-start | bytes 1720328 | tf_op jit(solution)/shard_map/ppermute | solution.py:47
  126.1 43.1 %collective-permute-start.29 = (bf16[35,64,128]{2,1,0:T(8,128)(2,1)S(1)}, bf16[35,64,128]{2,1,0:T(8,128)(2,1)S(1)}, u32[]{:S(2)}, u32[]{:S(2)}) collective-permute-start(bf16[35,64,128]{2,1,0:T(8,128)(2,1)S(1)} %get-tuple-element.88.refs_3_), channel_id=1, source_target_pairs={{0,128},{32,160},{64,192},{96,224},{128,0},{160,32},{192,64},{224,... | collective-permute-start | bytes 1720328 | tf_op jit(solution)/shard_map/ppermute | solution.py:47
  149.4 22.7 %collective-permute-start.23 = (bf16[16,4096]{1,0:T(8,128)(2,1)S(1)}, bf16[16,4096]{1,0:T(8,128)(2,1)S(1)}, u32[]{:S(2)}, u32[]{:S(2)}) collective-permute-start(bf16[16,4096]{1,0:T(8,128)(2,1)S(1)} %get-tuple-element.98), channel_id=1, source_target_pairs={{0,2},{1,3},{2,0},{3,1},{4,6},{5,7},{6,4},{7,5},{8,10},{9,11},{10,... | collective-permute-start | bytes 393224 | tf_op jit(solution)/shard_map/ppermute | solution.py:43

commit v9 on v8

--- a/solution.py
+++ b/solution.py
@@ -404,7 +404,7 @@
     gather_core = core ^ ((n >> 3) & 1)
     zk = (z - (1 - 2 * gather_core) * dist) & (NZ - 1)
     idx = zk * 4 + (xh ^ (n >> 4)) * 2 + (gather_core ^ flip)
-    order = [(1, 1), (0, 3), (1, 2), (1, 3), (0, 1), (1, 0), (0, 2), (0, 0)]
+    order = [(1, 1), (0, 3), (1, 2), (0, 1), (1, 3), (1, 0), (0, 2), (0, 0)]
     dx = jnp.array([o[0] for o in order], jnp.int32)
     dy = jnp.array([o[1] for o in order], jnp.int32)
     dests = (xl ^ dx) * NY + ((y + dy) & (NY - 1))
@@ -465,18 +465,17 @@
     def back(x, hops):
         return move(x, dz=NZ - hops)
 
-    done = pack(0, 1, other_a)
-    done = pack(1, 2, done)
+    done = pack(0, 2, other_a)
+    done = pack(2, 2, done)
     a1, a2, a3, a4, home_a = mix(own_a, received_a, (done,))
     from_a3, from_a4 = back(a3, 1), back(a4, 2)
     own_b, other_b = xgrad(pb, masked, (a4,))
     received_b = move(other_b, dc=1)
-    done = pack(3, 2, other_b)
+    done = pack(4, 3, other_b)
     b1, b2, b3, b4, home_b = mix(own_b, received_b, (done,))
     from_b3, from_b4, from_b1 = back(b3, 1), back(b4, 2), back(b1, 1)
     done = hop(a2, from_a3, from_a4, (b4,))
     from_a2 = back(done, 2)
-    done = pack(5, 2, done)
     done = hop(b2, from_b3, from_b4, (done,))
     a1, done = lax.optimization_barrier((a1, done))
     from_b2, from_a1 = back(done, 2), back(a1, 1)

time: 173 us -> 171 us (0.988)
  the two profiles are of different devices: /device:TPU:26 before, /device:TPU:8 now
where the time goes in v9:
time: 171 us; the launch traced here: 168 us
  waiting for transfers between devices  71.8 us (42%)
  starting transfers between devices  53.3 us (31%)
  Pallas kernels  35.7 us (21%)
  other arithmetic  3.53 us (2%)
  local copies, waits for them, and re-layouts  1.98 us (1%)
    ppermute x24, waiting for transfers between devices, move(): return lax.ppermute(x, 'tensor', tensor_perm(dz, dx, dc, split=True))  42.9 us
    ppermute x24, starting transfers between devices, move(): return lax.ppermute(x, 'tensor', tensor_perm(dz, dx, dc, split=True))  42.7 us
    pallas_call x28, Pallas kernels, call(): pl.pallas_call(run, out_shape=out_shape, in_specs=[SMEM] * n_scalar + [sp...  35.7 us
    ppermute x7, waiting for transfers between devices, move_dp(): return lax.ppermute(x, 'dp', dp_perm(dx, dy))  28.9 us
    ppermute x7, starting transfers between devices, move_dp(): return lax.ppermute(x, 'dp', dp_perm(dx, dy))  10.6 us
  transfers between devices with their start and end apart: 31, of which 14 were waited for; matrix products, arithmetic and copies ran while one was open for 3% of the time, Pallas kernels for 18%

profile of v9, /device:TPU:8, one launch (start us, length us, event | category | flops | bytes accessed | tf_op | source)
XLA Modules:
  0.0 168.3 jit_solution(17974634510465701965)
XLA Ops:
  0.8 0.9 copy-done.2
  2.3 3.3 %collective-permute-start.2 = (bf16[32,4096]{1,0:T(8,128)(2,1)S(1)}, bf16[32,4096]{1,0:T(8,128)(2,1)S(1)}, u32[]{:S(2)}, u32[]{:S(2)}) collective-permute-start(bf16[32,4096]{1,0:T(8,128)(2,1)S(1)} %shard_map.113), channel_id=1, source_target_pairs={{0,8},{1,25},{2,10},{3,27},{4,12},{5,29},{6,14},{7,31},{8,16},{9,1... | collective-permute-start | bytes 786440 | tf_op jit(solution)/shard_map/ppermute | solution.py:43
  5.6 1.9 %collective-permute-start.1 = (bf16[32,4096]{1,0:T(8,128)(2,1)S(1)}, bf16[32,4096]{1,0:T(8,128)(2,1)S(1)}, u32[]{:S(2)}, u32[]{:S(2)}) collective-permute-start(bf16[32,4096]{1,0:T(8,128)(2,1)S(1)} %shard_map.113), channel_id=1, source_target_pairs={{0,4},{1,29},{2,6},{3,31},{4,8},{5,1},{6,10},{7,3},{8,12},{9,5},{1... | collective-permute-start | bytes 786440 | tf_op jit(solution)/shard_map/ppermute | solution.py:43
  7.6 0.9 dynamic-slice_compare_fusion
  9.3 1.0 convert_reduce_fusion
  10.3 7.9 %collective-permute-done.1.refs_2_ = bf16[32,4096]{1,0:T(8,128)(2,1)S(1)} collective-permute-done((bf16[32,4096]{1,0:T(8,128)(2,1)S(1)}, bf16[32,4096]{1,0:T(8,128)(2,1)S(1)}, u32[]{:S(2)}, u32[]{:S(2)}) %collective-permute-start.1) | collective-permute-done | bytes 262176 | tf_op jit(solution)/shard_map/ppermute | solution.py:43
  18.2 1.9 %select_reduce_fusion = s32[8,70]{0,1:T(8,128)S(1)} fusion(s32[112]{0:T(128)} %constant.79, s32[8,112]{1,0:T(8,128)S(1)} %get-tuple-element.60), kind=kLoop, calls=%fused_computation.2 | loop fusion | flops 187600 | bytes 6272 | tf_op jit(solution)/shard_map/reduce_sum | solution.py:384
  20.3 3.9 %collective-permute-start.3 = (bf16[16,4096]{1,0:T(8,128)(2,1)S(1)}, bf16[16,4096]{1,0:T(8,128)(2,1)S(1)}, u32[]{:S(2)}, u32[]{:S(2)}) collective-permute-start(bf16[16,4096]{1,0:T(8,128)(2,1)S(1)} %shard_map.116), channel_id=1, source_target_pairs={{0,8},{1,25},{2,10},{3,27},{4,12},{5,29},{6,14},{7,31},{8,16},{9,1... | collective-permute-start | bytes 393224 | tf_op jit(solution)/shard_map/ppermute | solution.py:43
  24.2 0.9 copy-done.1
  25.1 3.4 %shard_map.118.refs_3_.refs_1_ = bf16[4096,896]{1,0:T(8,128)(2,1)S(1)} custom-call(s32[1]{0:T(128)} %bitcast.refs_0_, bf16[4096,896]{1,0:T(8,128)(2,1)} %refs_1_.1, s32[64,448]{1,0:T(8,128)S(1)} %copy-done.1), custom_call_target="tpu_custom_call" | custom-call | flops 3670016 | bytes 7454724 | tf_op jit(solution)/shard_map/pallas_call | solution.py:62
  28.5 0.7 collective-permute-done.4.refs_4_
  29.4 3.1 %collective-permute-start.6 = (bf16[16,4096]{1,0:T(8,128)(2,1)S(1)}, bf16[16,4096]{1,0:T(8,128)(2,1)S(1)}, u32[]{:S(2)}, u32[]{:S(2)}) collective-permute-start(bf16[16,4096]{1,0:T(8,128)(2,1)S(1)} %copy-done.3), channel_id=1, source_target_pairs={{0,2},{1,3},{2,0},{3,1},{4,6},{5,7},{6,4},{7,5},{8,10},{9,11},{10,... | collective-permute-start | bytes 393224 | tf_op jit(solution)/shard_map/ppermute | solution.py:43
  33.0 3.0 %collective-permute-start.8 = (bf16[32,4096]{1,0:T(8,128)(2,1)S(1)}, bf16[32,4096]{1,0:T(8,128)(2,1)S(1)}, u32[]{:S(2)}, u32[]{:S(2)}) collective-permute-start(bf16[32,4096]{1,0:T(8,128)(2,1)S(1)} %collective-permute-done.1.refs_2_), channel_id=1, source_target_pairs={{0,2},{1,3},{2,0},{3,1},{4,6},{5,7},{6,4},{7,5},{8,10},{9,11},{10,... | collective-permute-start | bytes 786440 | tf_op jit(solution)/shard_map/ppermute | solution.py:43
  36.9 3.5 %collective-permute-start.7 = (bf16[16,4096]{1,0:T(8,128)(2,1)S(1)}, bf16[16,4096]{1,0:T(8,128)(2,1)S(1)}, u32[]{:S(2)}, u32[]{:S(2)}) collective-permute-start(bf16[16,4096]{1,0:T(8,128)(2,1)S(1)} %collective-permute-done.3.refs_1_), channel_id=1, source_target_pairs={{0,2},{1,3},{2,0},{3,1},{4,6},{5,7},{6,4},{7,5},{8,10},{9,11},{10,... | collective-permute-start | bytes 393224 | tf_op jit(solution)/shard_map/ppermute | solution.py:43
  40.4 16.1 %collective-permute-done.7.refs_1_ = bf16[16,4096]{1,0:T(8,128)(2,1)S(1)} collective-permute-done((bf16[16,4096]{1,0:T(8,128)(2,1)S(1)}, bf16[16,4096]{1,0:T(8,128)(2,1)S(1)}, u32[]{:S(2)}, u32[]{:S(2)}) %collective-permute-start.7) | collective-permute-done | bytes 131104 | tf_op jit(solution)/shard_map/ppermute | solution.py:43
  56.7 3.3 %shard_map.121 = (bf16[16,16,896]{2,1,0:T(8,128)(2,1)S(1)}, bf16[256,896]{1,0:T(8,128)(2,1)S(1)}) custom-call(s32[32]{0:T(128)S(1)} %fusion.8.refs_0_, bf16[128,4096]{1,0:T(8,128)(2,1)S(1)} %shard_map.119.refs_1_.refs_5_, bf16[128,4096]{1,0:T(8,128)(2,1)S(1)} %collective-permute-done.5.refs_2_.refs_7_, bf16[4096,896]{1,0:T(8,128)(2,1)S(1)} %shard_map.118.refs_3_.refs_1_, ...), custom_call_target="tpu_custom_call" | custom-call | flops 1879048192 | bytes 10354816 | tf_op jit(solution)/shard_map/pallas_call | solution.py:62
  60.0 3.8 %shard_map.123 = (f32[128,4096]{1,0:T(8,128)S(1)}, bf16[128,4096]{1,0:T(8,128)(2,1)S(1)}) custom-call(bf16[256,896]{1,0:T(8,128)(2,1)S(1)} %get-tuple-element.70.refs_0_.refs_3_, bf16[4096,896]{1,0:T(8,128)(2,1)S(1)} %shard_map.118.refs_3_.refs_1_), custom_call_target="tpu_custom_call" | custom-call | flops 1879048192 | bytes 7798784 | tf_op jit(solution)/shard_map/pallas_call | solution.py:62
  63.8 0.7 collective-permute-start.12
  64.5 3.3 %shard_map.124 = (bf16[16,16,896]{2,1,0:T(8,128)(2,1)S(1)}, bf16[256,896]{1,0:T(8,128)(2,1)S(1)}) custom-call(s32[32]{0:T(128)S(1)} %fusion.8.refs_0_, bf16[128,4096]{1,0:T(8,128)(2,1)S(1)} %shard_map.122.refs_1_.refs_6_, bf16[128,4096]{1,0:T(8,128)(2,1)S(1)} %collective-permute-done.11.refs_2_.refs_8_, bf16[4096,896]{1,0:T(8,128)(2,1)S(1)} %shard_map.118.refs_3_.refs_1_, ...), custom_call_target="tpu_custom_call" | custom-call | flops 1879048192 | bytes 10354816 | tf_op jit(solution)/shard_map/pallas_call | solution.py:62
  67.8 2.8 %shard_map.125 = (bf16[35,64,128]{2,1,0:T(8,128)(2,1)S(1)}, bf16[35,64,128]{2,1,0:T(8,128)(2,1)S(1)}) custom-call(s32[8]{0:T(128)S(1)} %and_add_fusion.refs_0_, s32[8,70]{1,0:T(8,128)S(1)} %broadcast_add_fusion.refs_1_, s32[8]{0:T(128)S(1)} %get-tuple-element.75.refs_2_, bf16[256,896]{1,0:T(8,128)(2,1)S(1)} %get-tuple-element.70.refs_0_.refs_3_, ...), custom_call_target="tpu_custom_call" | custom-call | flops 939524096 | bytes 5114112 | tf_op jit(solution)/shard_map/pallas_call | solution.py:62
  70.6 3.0 %shard_map.126 = (bf16[35,64,128]{2,1,0:T(8,128)(2,1)S(1)}, bf16[35,64,128]{2,1,0:T(8,128)(2,1)S(1)}) custom-call(s32[8]{0:T(128)S(1)} %and_add_fusion.refs_0_, s32[8,70]{1,0:T(8,128)S(1)} %broadcast_add_fusion.refs_1_, s32[8]{0:T(128)S(1)} %get-tuple-element.75.refs_2_, bf16[256,896]{1,0:T(8,128)(2,1)S(1)} %get-tuple-element.70.refs_0_.refs_3_, ...), custom_call_target="tpu_custom_call" | custom-call | flops 939524096 | bytes 5114112 | tf_op jit(solution)/shard_map/pallas_call | solution.py:62
  73.8 3.8 %shard_map.128 = (f32[128,4096]{1,0:T(8,128)S(1)}, bf16[128,4096]{1,0:T(8,128)(2,1)S(1)}) custom-call(bf16[256,896]{1,0:T(8,128)(2,1)S(1)} %get-tuple-element.76.refs_4_.refs_0_, bf16[4096,896]{1,0:T(8,128)(2,1)S(1)} %shard_map.118.refs_3_.refs_1_, bf16[16,4096]{1,0:T(8,128)(2,1)S(1)} %get-tuple-element.81.refs_2_), custom_call_target="tpu_custom_call" | custom-call | flops 1879048192 | bytes 7798784 | tf_op jit(solution)/shard_map/pallas_call | solution.py:62
  77.7 3.0 %collective-permute-start.16 = (bf16[32,4096]{1,0:T(8,128)(2,1)S(1)}, bf16[32,4096]{1,0:T(8,128)(2,1)S(1)}, u32[]{:S(2)}, u32[]{:S(2)}) collective-permute-start(bf16[32,4096]{1,0:T(8,128)(2,1)S(1)} %get-tuple-element.89), channel_id=1, source_target_pairs={{0,28},{1,5},{2,30},{3,7},{4,0},{5,9},{6,2},{7,11},{8,4},{9,13},{1... | collective-permute-start | bytes 786440 | tf_op jit(solution)/shard_map/ppermute | solution.py:43
  80.7 3.9 %shard_map.129 = (bf16[35,64,128]{2,1,0:T(8,128)(2,1)S(1)}, bf16[35,64,128]{2,1,0:T(8,128)(2,1)S(1)}, bf16[35,64,128]{2,1,0:T(8,128)(2,1)S(1)}) custom-call(s32[8]{0:T(128)S(1)} %and_add_fusion.refs_0_, s32[8,70]{1,0:T(8,128)S(1)} %broadcast_add_fusion.refs_1_, s32[8]{0:T(128)S(1)} %get-tuple-element.75.refs_2_, ...), custom_call_target="tpu_custom_call" | custom-call | flops 1409286144 | bytes 5114112 | tf_op jit(solution)/shard_map/pallas_call | solution.py:62
  84.9 1.1 collective-permute-start.14
  86.0 3.6 %collective-permute-start.20 = (bf16[32,4096]{1,0:T(8,128)(2,1)S(1)}, bf16[32,4096]{1,0:T(8,128)(2,1)S(1)}, u32[]{:S(2)}, u32[]{:S(2)}) collective-permute-start(bf16[32,4096]{1,0:T(8,128)(2,1)S(1)} %get-tuple-element.94), channel_id=1, source_target_pairs={{0,28},{1,5},{2,30},{3,7},{4,0},{5,9},{6,2},{7,11},{8,4},{9,13},{1... | collective-permute-start | bytes 786440 | tf_op jit(solution)/shard_map/ppermute | solution.py:43
  89.6 1.4 collective-permute-start.15
  91.0 5.0 %collective-permute-done.17.refs_2_ = bf16[16,4096]{1,0:T(8,128)(2,1)S(1)} collective-permute-done((bf16[16,4096]{1,0:T(8,128)(2,1)S(1)}, bf16[16,4096]{1,0:T(8,128)(2,1)S(1)}, u32[]{:S(2)}, u32[]{:S(2)}) %collective-permute-start.17) | collective-permute-done | bytes 131104 | tf_op jit(solution)/shard_map/ppermute | solution.py:43
  96.6 2.1 %collective-permute-start.24 = (bf16[35,64,128]{2,1,0:T(8,128)(2,1)S(1)}, bf16[35,64,128]{2,1,0:T(8,128)(2,1)S(1)}, u32[]{:S(2)}, u32[]{:S(2)}) collective-permute-start(bf16[35,64,128]{2,1,0:T(8,128)(2,1)S(1)} %get-tuple-element.78.refs_9_), channel_id=1, source_target_pairs={{0,160},{32,192},{64,224},{96,128},{128,32},{160,64},{192,96},{224... | collective-permute-start | bytes 1720328 | tf_op jit(solution)/shard_map/ppermute | solution.py:47
  99.1 4.7 %collective-permute-start.19 = (bf16[32,4096]{1,0:T(8,128)(2,1)S(1)}, bf16[32,4096]{1,0:T(8,128)(2,1)S(1)}, u32[]{:S(2)}, u32[]{:S(2)}) collective-permute-start(bf16[32,4096]{1,0:T(8,128)(2,1)S(1)} %shard_map.131.refs_3_), channel_id=1, source_target_pairs={{0,24},{1,9},{2,26},{3,11},{4,28},{5,13},{6,30},{7,15},{8,0},{9,17... | collective-permute-start | bytes 786440 | tf_op jit(solution)/shard_map/ppermute | solution.py:43
  103.9 3.1 %collective-permute-start.18 = (bf16[32,4096]{1,0:T(8,128)(2,1)S(1)}, bf16[32,4096]{1,0:T(8,128)(2,1)S(1)}, u32[]{:S(2)}, u32[]{:S(2)}) collective-permute-start(bf16[32,4096]{1,0:T(8,128)(2,1)S(1)} %get-tuple-element.92), channel_id=1, source_target_pairs={{0,28},{1,5},{2,30},{3,7},{4,0},{5,9},{6,2},{7,11},{8,4},{9,13},{1... | collective-permute-start | bytes 786440 | tf_op jit(solution)/shard_map/ppermute | solution.py:43
  107.1 1.0 collective-permute-start.21
  108.1 2.4 %collective-permute-done.19.refs_1_ = bf16[32,4096]{1,0:T(8,128)(2,1)S(1)} collective-permute-done((bf16[32,4096]{1,0:T(8,128)(2,1)S(1)}, bf16[32,4096]{1,0:T(8,128)(2,1)S(1)}, u32[]{:S(2)}, u32[]{:S(2)}) %collective-permute-start.19) | collective-permute-done | bytes 262176 | tf_op jit(solution)/shard_map/ppermute | solution.py:43
  110.5 4.6 %collective-permute-done.18.refs_0_ = bf16[32,4096]{1,0:T(8,128)(2,1)S(1)} collective-permute-done((bf16[32,4096]{1,0:T(8,128)(2,1)S(1)}, bf16[32,4096]{1,0:T(8,128)(2,1)S(1)}, u32[]{:S(2)}, u32[]{:S(2)}) %collective-permute-start.18) | collective-permute-done | bytes 262176 | tf_op jit(solution)/shard_map/ppermute | solution.py:43
  115.1 3.8 %collective-permute-done.21.refs_4_ = bf16[32,4096]{1,0:T(8,128)(2,1)S(1)} collective-permute-done((bf16[32,4096]{1,0:T(8,128)(2,1)S(1)}, bf16[32,4096]{1,0:T(8,128)(2,1)S(1)}, u32[]{:S(2)}, u32[]{:S(2)}) %collective-permute-start.21) | collective-permute-done | bytes 262176 | tf_op jit(solution)/shard_map/ppermute | solution.py:43
  119.3 1.6 collective-permute-start.27
  120.9 1.9 %collective-permute-start.26 = (bf16[35,64,128]{2,1,0:T(8,128)(2,1)S(1)}, bf16[35,64,128]{2,1,0:T(8,128)(2,1)S(1)}, u32[]{:S(2)}, u32[]{:S(2)}) collective-permute-start(bf16[35,64,128]{2,1,0:T(8,128)(2,1)S(1)} %get-tuple-element.79.refs_2_), channel_id=1, source_target_pairs={{0,192},{32,224},{64,128},{96,160},{128,64},{160,96},{192,0},{224,... | collective-permute-start | bytes 1720328 | tf_op jit(solution)/shard_map/ppermute | solution.py:47
  122.8 0.9 collective-permute-start.29
  123.7 2.2 %collective-permute-start.30 = (bf16[35,64,128]{2,1,0:T(8,128)(2,1)S(1)}, bf16[35,64,128]{2,1,0:T(8,128)(2,1)S(1)}, u32[]{:S(2)}, u32[]{:S(2)}) collective-permute-start(bf16[35,64,128]{2,1,0:T(8,128)(2,1)S(1)} %get-tuple-element.104), channel_id=1, source_target_pairs={{0,64},{32,96},{64,0},{96,32},{128,192},{160,224},{192,128},{224,1... | collective-permute-start | bytes 1720328 | tf_op jit(solution)/shard_map/ppermute | solution.py:47
  125.9 1.3 collective-permute-start.28
  127.2 20.3 %collective-permute-done.27.refs_4_ = bf16[35,64,128]{2,1,0:T(8,128)(2,1)S(1)} collective-permute-done((bf16[35,64,128]{2,1,0:T(8,128)(2,1)S(1)}, bf16[35,64,128]{2,1,0:T(8,128)(2,1)S(1)}, u32[]{:S(2)}, u32[]{:S(2)}) %collective-permute-start.27) | collective-permute-done | bytes 573472 | tf_op jit(solution)/shard_map/ppermute | solution.py:47
  147.5 3.7 %collective-permute-start.23 = (bf16[16,4096]{1,0:T(8,128)(2,1)S(1)}, bf16[16,4096]{1,0:T(8,128)(2,1)S(1)}, u32[]{:S(2)}, u32[]{:S(2)}) collective-permute-start(bf16[16,4096]{1,0:T(8,128)(2,1)S(1)} %get-tuple-element.99), channel_id=1, source_target_pairs={{0,2},{1,3},{2,0},{3,1},{4,6},{5,7},{6,4},{7,5},{8,10},{9,11},{10,... | collective-permute-start | bytes 393224 | tf_op jit(solution)/shard_map/ppermute | solution.py:43
  151.2 1.7 %shard_map.133.refs_3_.refs_0_ = bf16[35,64,128]{2,1,0:T(8,128)(2,1)S(1)} custom-call(s32[8]{0:T(128)S(1)} %and_add_fusion.refs_0_, s32[8,70]{1,0:T(8,128)S(1)} %broadcast_add_fusion.refs_1_, s32[8]{0:T(128)S(1)} %get-tuple-element.75.refs_2_, bf16[256,896]{1,0:T(8,128)(2,1)S(1)} %get-tuple-element.70.refs_0_.refs_3_, ...), custom_call_target="tpu_custom_call" | custom-call | flops 469762048 | bytes 5114112 | tf_op jit(solution)/shard_map/pallas_call | solution.py:62
  152.9 1.6 shard_map.134
  155.0 7.3 %collective-permute-done.30.refs_5_ = bf16[35,64,128]{2,1,0:T(8,128)(2,1)S(1)} collective-permute-done((bf16[35,64,128]{2,1,0:T(8,128)(2,1)S(1)}, bf16[35,64,128]{2,1,0:T(8,128)(2,1)S(1)}, u32[]{:S(2)}, u32[]{:S(2)}) %collective-permute-start.30) | collective-permute-done | bytes 573472 | tf_op jit(solution)/shard_map/ppermute | solution.py:47
  162.3 1.3 collective-permute-done.28.refs_3_
  163.6 2.8 %shard_map.139 = f32[512,896]{1,0:T(8,128)} custom-call(s32[1]{0:T(128)} %bitcast.3.refs_0_, s32[8,70]{1,0:T(8,128)S(1)} %broadcast_add_fusion.refs_1_, f32[35,64,128]{2,1,0:T(8,128)S(1)} %shard_map.138.refs_2_, bf16[35,64,128]{2,1,0:T(8,128)(2,1)S(1)} %collective-permute-done.28.refs_3_, bf16[35,64,128]{2,1,0:T(8,128)(2,1)S(1)} %collective-permute-done.29.refs_4_, ...), custom_call_target="tpu_custom_call" | custom-call | flops 2293760 | bytes 2869444 | tf_op jit(solution)/shard_map/pallas_call | solution.py:62
  166.5 1.1 collective-permute-done.23.refs_1_
  (58 shorter events, 6.6 us)
Async XLA Ops:
  0.6 1.6 collective-permute-start
  0.8 0.9 copy-start.2
  2.3 17.9 %collective-permute-start.2 = (bf16[32,4096]{1,0:T(8,128)(2,1)S(1)}, bf16[32,4096]{1,0:T(8,128)(2,1)S(1)}, u32[]{:S(2)}, u32[]{:S(2)}) collective-permute-start(bf16[32,4096]{1,0:T(8,128)(2,1)S(1)} %shard_map.113), channel_id=1, source_target_pairs={{0,8},{1,25},{2,10},{3,27},{4,12},{5,29},{6,14},{7,31},{8,16},{9,1... | collective-permute-start | bytes 786440 | tf_op jit(solution)/shard_map/ppermute | solution.py:43
  5.6 12.6 %collective-permute-start.1 = (bf16[32,4096]{1,0:T(8,128)(2,1)S(1)}, bf16[32,4096]{1,0:T(8,128)(2,1)S(1)}, u32[]{:S(2)}, u32[]{:S(2)}) collective-permute-start(bf16[32,4096]{1,0:T(8,128)(2,1)S(1)} %shard_map.113), channel_id=1, source_target_pairs={{0,4},{1,29},{2,6},{3,31},{4,8},{5,1},{6,10},{7,3},{8,12},{9,5},{1... | collective-permute-start | bytes 786440 | tf_op jit(solution)/shard_map/ppermute | solution.py:43
  20.2 9.0 %collective-permute-start.4 = (bf16[32,4096]{1,0:T(8,128)(2,1)S(1)}, bf16[32,4096]{1,0:T(8,128)(2,1)S(1)}, u32[]{:S(2)}, u32[]{:S(2)}) collective-permute-start(bf16[32,4096]{1,0:T(8,128)(2,1)S(1)} %collective-permute-done.2.refs_0_.refs_3_), channel_id=1, source_target_pairs={{0,4},{1,29},{2,6},{3,31},{4,8},{5,1},{6,10},{7,3},{8,12},{9,5},{1... | collective-permute-start | bytes 786440 | tf_op jit(solution)/shard_map/ppermute | solution.py:43
  20.3 9.0 %collective-permute-start.3 = (bf16[16,4096]{1,0:T(8,128)(2,1)S(1)}, bf16[16,4096]{1,0:T(8,128)(2,1)S(1)}, u32[]{:S(2)}, u32[]{:S(2)}) collective-permute-start(bf16[16,4096]{1,0:T(8,128)(2,1)S(1)} %shard_map.116), channel_id=1, source_target_pairs={{0,8},{1,25},{2,10},{3,27},{4,12},{5,29},{6,14},{7,31},{8,16},{9,1... | collective-permute-start | bytes 393224 | tf_op jit(solution)/shard_map/ppermute | solution.py:43
  24.2 0.9 copy-start.1
  28.5 0.9 copy-start.3
  28.5 28.2 %copy-start = (bf16[512,896]{1,0:T(8,128)(2,1)S(1)}, bf16[512,896]{1,0:T(8,128)(2,1)}, u32[]{:S(2)}) copy-start(bf16[512,896]{1,0:T(8,128)(2,1)} %param.12) | copy-start | bytes 2752516
  29.3 27.4 %collective-permute-start.5 = (bf16[128,4096]{1,0:T(8,128)(2,1)S(1)}, bf16[128,4096]{1,0:T(8,128)(2,1)S(1)}, u32[]{:S(2)}, u32[]{:S(2)}) collective-permute-start(bf16[128,4096]{1,0:T(8,128)(2,1)S(1)} %shard_map.119.refs_1_.refs_5_), channel_id=1, source_target_pairs={{0,1},{1,0},{2,3},{3,2},{4,5},{5,4},{6,7},{7,6},{8,9},{9,8},{10,11... | collective-permute-start | bytes 3145736 | tf_op jit(solution)/shard_map/ppermute | solution.py:43
  29.4 7.5 %collective-permute-start.6 = (bf16[16,4096]{1,0:T(8,128)(2,1)S(1)}, bf16[16,4096]{1,0:T(8,128)(2,1)S(1)}, u32[]{:S(2)}, u32[]{:S(2)}) collective-permute-start(bf16[16,4096]{1,0:T(8,128)(2,1)S(1)} %copy-done.3), channel_id=1, source_target_pairs={{0,2},{1,3},{2,0},{3,1},{4,6},{5,7},{6,4},{7,5},{8,10},{9,11},{10,... | collective-permute-start | bytes 393224 | tf_op jit(solution)/shard_map/ppermute | solution.py:43
  32.5 23.9 %collective-permute-start.9 = (bf16[32,4096]{1,0:T(8,128)(2,1)S(1)}, bf16[32,4096]{1,0:T(8,128)(2,1)S(1)}, u32[]{:S(2)}, u32[]{:S(2)}) collective-permute-start(bf16[32,4096]{1,0:T(8,128)(2,1)S(1)} %collective-permute-done.2.refs_0_.refs_3_), channel_id=1, source_target_pairs={{0,2},{1,3},{2,0},{3,1},{4,6},{5,7},{6,4},{7,5},{8,10},{9,11},{10,... | collective-permute-start | bytes 786440 | tf_op jit(solution)/shard_map/ppermute | solution.py:43
  33.0 23.4 %collective-permute-start.8 = (bf16[32,4096]{1,0:T(8,128)(2,1)S(1)}, bf16[32,4096]{1,0:T(8,128)(2,1)S(1)}, u32[]{:S(2)}, u32[]{:S(2)}) collective-permute-start(bf16[32,4096]{1,0:T(8,128)(2,1)S(1)} %collective-permute-done.1.refs_2_), channel_id=1, source_target_pairs={{0,2},{1,3},{2,0},{3,1},{4,6},{5,7},{6,4},{7,5},{8,10},{9,11},{10,... | collective-permute-start | bytes 786440 | tf_op jit(solution)/shard_map/ppermute | solution.py:43
  36.1 20.4 %collective-permute-start.10 = (bf16[32,4096]{1,0:T(8,128)(2,1)S(1)}, bf16[32,4096]{1,0:T(8,128)(2,1)S(1)}, u32[]{:S(2)}, u32[]{:S(2)}) collective-permute-start(bf16[32,4096]{1,0:T(8,128)(2,1)S(1)} %collective-permute-done.4.refs_4_), channel_id=1, source_target_pairs={{0,2},{1,3},{2,0},{3,1},{4,6},{5,7},{6,4},{7,5},{8,10},{9,11},{10,... | collective-permute-start | bytes 786440 | tf_op jit(solution)/shard_map/ppermute | solution.py:43
  36.9 19.6 %collective-permute-start.7 = (bf16[16,4096]{1,0:T(8,128)(2,1)S(1)}, bf16[16,4096]{1,0:T(8,128)(2,1)S(1)}, u32[]{:S(2)}, u32[]{:S(2)}) collective-permute-start(bf16[16,4096]{1,0:T(8,128)(2,1)S(1)} %collective-permute-done.3.refs_1_), channel_id=1, source_target_pairs={{0,2},{1,3},{2,0},{3,1},{4,6},{5,7},{6,4},{7,5},{8,10},{9,11},{10,... | collective-permute-start | bytes 393224 | tf_op jit(solution)/shard_map/ppermute | solution.py:43
  56.6 7.9 %collective-permute-start.11 = (bf16[128,4096]{1,0:T(8,128)(2,1)S(1)}, bf16[128,4096]{1,0:T(8,128)(2,1)S(1)}, u32[]{:S(2)}, u32[]{:S(2)}) collective-permute-start(bf16[128,4096]{1,0:T(8,128)(2,1)S(1)} %shard_map.122.refs_1_.refs_6_), channel_id=1, source_target_pairs={{0,1},{1,0},{2,3},{3,2},{4,5},{5,4},{6,7},{7,6},{8,9},{9,8},{10,11... | collective-permute-start | bytes 3145736 | tf_op jit(solution)/shard_map/ppermute | solution.py:43
  63.8 9.8 %collective-permute-start.12 = (bf16[128,4096]{1,0:T(8,128)(2,1)S(1)}, bf16[128,4096]{1,0:T(8,128)(2,1)S(1)}, u32[]{:S(2)}, u32[]{:S(2)}) collective-permute-start(bf16[128,4096]{1,0:T(8,128)(2,1)S(1)} %get-tuple-element.71.refs_5_.refs_9_), channel_id=1, source_target_pairs={{0,1},{1,0},{2,3},{3,2},{4,5},{5,4},{6,7},{7,6},{8,9},{9,8},{10,11... | collective-permute-start | bytes 3145736 | tf_op jit(solution)/shard_map/ppermute | solution.py:43
  77.6 7.0 %collective-permute-start.13 = (bf16[128,4096]{1,0:T(8,128)(2,1)S(1)}, bf16[128,4096]{1,0:T(8,128)(2,1)S(1)}, u32[]{:S(2)}, u32[]{:S(2)}) collective-permute-start(bf16[128,4096]{1,0:T(8,128)(2,1)S(1)} %get-tuple-element.83.refs_9_), channel_id=1, source_target_pairs={{0,1},{1,0},{2,3},{3,2},{4,5},{5,4},{6,7},{7,6},{8,9},{9,8},{10,11... | collective-permute-start | bytes 3145736 | tf_op jit(solution)/shard_map/ppermute | solution.py:43
  77.7 18.9 %collective-permute-start.16 = (bf16[32,4096]{1,0:T(8,128)(2,1)S(1)}, bf16[32,4096]{1,0:T(8,128)(2,1)S(1)}, u32[]{:S(2)}, u32[]{:S(2)}) collective-permute-start(bf16[32,4096]{1,0:T(8,128)(2,1)S(1)} %get-tuple-element.89), channel_id=1, source_target_pairs={{0,28},{1,5},{2,30},{3,7},{4,0},{5,9},{6,2},{7,11},{8,4},{9,13},{1... | collective-permute-start | bytes 786440 | tf_op jit(solution)/shard_map/ppermute | solution.py:43
  84.9 18.9 %collective-permute-start.14 = (bf16[32,4096]{1,0:T(8,128)(2,1)S(1)}, bf16[32,4096]{1,0:T(8,128)(2,1)S(1)}, u32[]{:S(2)}, u32[]{:S(2)}) collective-permute-start(bf16[32,4096]{1,0:T(8,128)(2,1)S(1)} %get-tuple-element.86), channel_id=1, source_target_pairs={{0,28},{1,5},{2,30},{3,7},{4,0},{5,9},{6,2},{7,11},{8,4},{9,13},{1... | collective-permute-start | bytes 786440 | tf_op jit(solution)/shard_map/ppermute | solution.py:43
  86.0 21.1 %collective-permute-start.20 = (bf16[32,4096]{1,0:T(8,128)(2,1)S(1)}, bf16[32,4096]{1,0:T(8,128)(2,1)S(1)}, u32[]{:S(2)}, u32[]{:S(2)}) collective-permute-start(bf16[32,4096]{1,0:T(8,128)(2,1)S(1)} %get-tuple-element.94), channel_id=1, source_target_pairs={{0,28},{1,5},{2,30},{3,7},{4,0},{5,9},{6,2},{7,11},{8,4},{9,13},{1... | collective-permute-start | bytes 786440 | tf_op jit(solution)/shard_map/ppermute | solution.py:43
  89.6 6.4 %collective-permute-start.17 = (bf16[16,4096]{1,0:T(8,128)(2,1)S(1)}, bf16[16,4096]{1,0:T(8,128)(2,1)S(1)}, u32[]{:S(2)}, u32[]{:S(2)}) collective-permute-start(bf16[16,4096]{1,0:T(8,128)(2,1)S(1)} %get-tuple-element.81.refs_2_), channel_id=1, source_target_pairs={{0,24},{1,9},{2,26},{3,11},{4,28},{5,13},{6,30},{7,15},{8,0},{9,17... | collective-permute-start | bytes 393224 | tf_op jit(solution)/shard_map/ppermute | solution.py:43
  89.6 9.5 %collective-permute-start.15 = (bf16[16,4096]{1,0:T(8,128)(2,1)S(1)}, bf16[16,4096]{1,0:T(8,128)(2,1)S(1)}, u32[]{:S(2)}, u32[]{:S(2)}) collective-permute-start(bf16[16,4096]{1,0:T(8,128)(2,1)S(1)} %get-tuple-element.87.refs_3_), channel_id=1, source_target_pairs={{0,24},{1,9},{2,26},{3,11},{4,28},{5,13},{6,30},{7,15},{8,0},{9,17... | collective-permute-start | bytes 393224 | tf_op jit(solution)/shard_map/ppermute | solution.py:43
  96.0 26.8 %collective-permute-start.25 = (bf16[35,64,128]{2,1,0:T(8,128)(2,1)S(1)}, bf16[35,64,128]{2,1,0:T(8,128)(2,1)S(1)}, u32[]{:S(2)}, u32[]{:S(2)}) collective-permute-start(bf16[35,64,128]{2,1,0:T(8,128)(2,1)S(1)} %get-tuple-element.100), channel_id=1, source_target_pairs={{0,96},{32,0},{64,32},{96,64},{128,224},{160,128},{192,160},{224,1... | collective-permute-start | bytes 1720328 | tf_op jit(solution)/shard_map/ppermute | solution.py:47
  96.6 27.1 %collective-permute-start.24 = (bf16[35,64,128]{2,1,0:T(8,128)(2,1)S(1)}, bf16[35,64,128]{2,1,0:T(8,128)(2,1)S(1)}, u32[]{:S(2)}, u32[]{:S(2)}) collective-permute-start(bf16[35,64,128]{2,1,0:T(8,128)(2,1)S(1)} %get-tuple-element.78.refs_9_), channel_id=1, source_target_pairs={{0,160},{32,192},{64,224},{96,128},{128,32},{160,64},{192,96},{224... | collective-permute-start | bytes 1720328 | tf_op jit(solution)/shard_map/ppermute | solution.py:47
  99.1 11.4 %collective-permute-start.19 = (bf16[32,4096]{1,0:T(8,128)(2,1)S(1)}, bf16[32,4096]{1,0:T(8,128)(2,1)S(1)}, u32[]{:S(2)}, u32[]{:S(2)}) collective-permute-start(bf16[32,4096]{1,0:T(8,128)(2,1)S(1)} %shard_map.131.refs_3_), channel_id=1, source_target_pairs={{0,24},{1,9},{2,26},{3,11},{4,28},{5,13},{6,30},{7,15},{8,0},{9,17... | collective-permute-start | bytes 786440 | tf_op jit(solution)/shard_map/ppermute | solution.py:43
  103.9 11.2 %collective-permute-start.18 = (bf16[32,4096]{1,0:T(8,128)(2,1)S(1)}, bf16[32,4096]{1,0:T(8,128)(2,1)S(1)}, u32[]{:S(2)}, u32[]{:S(2)}) collective-permute-start(bf16[32,4096]{1,0:T(8,128)(2,1)S(1)} %get-tuple-element.92), channel_id=1, source_target_pairs={{0,28},{1,5},{2,30},{3,7},{4,0},{5,9},{6,2},{7,11},{8,4},{9,13},{1... | collective-permute-start | bytes 786440 | tf_op jit(solution)/shard_map/ppermute | solution.py:43
  107.1 11.9 %collective-permute-start.21 = (bf16[32,4096]{1,0:T(8,128)(2,1)S(1)}, bf16[32,4096]{1,0:T(8,128)(2,1)S(1)}, u32[]{:S(2)}, u32[]{:S(2)}) collective-permute-start(bf16[32,4096]{1,0:T(8,128)(2,1)S(1)} %shard_map.132.refs_9_), channel_id=1, source_target_pairs={{0,24},{1,9},{2,26},{3,11},{4,28},{5,13},{6,30},{7,15},{8,0},{9,17... | collective-permute-start | bytes 786440 | tf_op jit(solution)/shard_map/ppermute | solution.py:43
  119.2 6.7 %collective-permute-start.22 = (bf16[32,4096]{1,0:T(8,128)(2,1)S(1)}, bf16[32,4096]{1,0:T(8,128)(2,1)S(1)}, u32[]{:S(2)}, u32[]{:S(2)}) collective-permute-start(bf16[32,4096]{1,0:T(8,128)(2,1)S(1)} %get-tuple-element.97), channel_id=1, source_target_pairs={{0,1},{1,0},{2,3},{3,2},{4,5},{5,4},{6,7},{7,6},{8,9},{9,8},{10,11... | collective-permute-start | bytes 786440 | tf_op jit(solution)/shard_map/ppermute | solution.py:43
  119.3 28.2 %collective-permute-start.27 = (bf16[35,64,128]{2,1,0:T(8,128)(2,1)S(1)}, bf16[35,64,128]{2,1,0:T(8,128)(2,1)S(1)}, u32[]{:S(2)}, u32[]{:S(2)}) collective-permute-start(bf16[35,64,128]{2,1,0:T(8,128)(2,1)S(1)} %get-tuple-element.101), channel_id=1, source_target_pairs={{0,32},{32,64},{64,96},{96,0},{128,160},{160,192},{192,224},{224,1... | collective-permute-start | bytes 1720328 | tf_op jit(solution)/shard_map/ppermute | solution.py:47
  120.9 33.6 %collective-permute-start.26 = (bf16[35,64,128]{2,1,0:T(8,128)(2,1)S(1)}, bf16[35,64,128]{2,1,0:T(8,128)(2,1)S(1)}, u32[]{:S(2)}, u32[]{:S(2)}) collective-permute-start(bf16[35,64,128]{2,1,0:T(8,128)(2,1)S(1)} %get-tuple-element.79.refs_2_), channel_id=1, source_target_pairs={{0,192},{32,224},{64,128},{96,160},{128,64},{160,96},{192,0},{224,... | collective-permute-start | bytes 1720328 | tf_op jit(solution)/shard_map/ppermute | solution.py:47
  122.8 32.2 %collective-permute-start.29 = (bf16[35,64,128]{2,1,0:T(8,128)(2,1)S(1)}, bf16[35,64,128]{2,1,0:T(8,128)(2,1)S(1)}, u32[]{:S(2)}, u32[]{:S(2)}) collective-permute-start(bf16[35,64,128]{2,1,0:T(8,128)(2,1)S(1)} %get-tuple-element.103), channel_id=1, source_target_pairs={{0,128},{32,160},{64,192},{96,224},{128,0},{160,32},{192,64},{224,... | collective-permute-start | bytes 1720328 | tf_op jit(solution)/shard_map/ppermute | solution.py:47
  123.7 38.6 %collective-permute-start.30 = (bf16[35,64,128]{2,1,0:T(8,128)(2,1)S(1)}, bf16[35,64,128]{2,1,0:T(8,128)(2,1)S(1)}, u32[]{:S(2)}, u32[]{:S(2)}) collective-permute-start(bf16[35,64,128]{2,1,0:T(8,128)(2,1)S(1)} %get-tuple-element.104), channel_id=1, source_target_pairs={{0,64},{32,96},{64,0},{96,32},{128,192},{160,224},{192,128},{224,1... | collective-permute-start | bytes 1720328 | tf_op jit(solution)/shard_map/ppermute | solution.py:47
  125.9 37.7 %collective-permute-start.28 = (bf16[35,64,128]{2,1,0:T(8,128)(2,1)S(1)}, bf16[35,64,128]{2,1,0:T(8,128)(2,1)S(1)}, u32[]{:S(2)}, u32[]{:S(2)}) collective-permute-start(bf16[35,64,128]{2,1,0:T(8,128)(2,1)S(1)} %get-tuple-element.84.refs_2_), channel_id=1, source_target_pairs={{0,224},{32,128},{64,160},{96,192},{128,96},{160,0},{192,32},{224,... | collective-permute-start | bytes 1720328 | tf_op jit(solution)/shard_map/ppermute | solution.py:47
  147.5 20.1 %collective-permute-start.23 = (bf16[16,4096]{1,0:T(8,128)(2,1)S(1)}, bf16[16,4096]{1,0:T(8,128)(2,1)S(1)}, u32[]{:S(2)}, u32[]{:S(2)}) collective-permute-start(bf16[16,4096]{1,0:T(8,128)(2,1)S(1)} %get-tuple-element.99), channel_id=1, source_target_pairs={{0,2},{1,3},{2,0},{3,1},{4,6},{5,7},{6,4},{7,5},{8,10},{9,11},{10,... | collective-permute-start | bytes 393224 | tf_op jit(solution)/shard_map/ppermute | solution.py:43

commit v10 on v5

--- a/solution.py
+++ b/solution.py
@@ -125,7 +125,7 @@
 
 def forward_kernel(first, idx_ref, xa, xb, w_ref, g_ref, act_ref, p_ref, acc_ref):
     d = w_ref.shape[0]
-    kb = 1024
+    kb = 2048
 
     def product(s):
         cols = pl.ds(pl.multiple_of(s * kb, kb), kb)
@@ -147,7 +147,7 @@
         p_ref[rows, :] = grad.astype(BF16)
         return carry
 
-    lax.fori_loop(0, act_ref.shape[0], finish, 0, unroll=2)
+    lax.fori_loop(0, act_ref.shape[0], finish, 0, unroll=4)
 
 
 def forward(first, idx, xa, xb, masked, act_grad, after=()):
@@ -392,7 +392,8 @@
 
     partner = move(tokens, dc=1)
     home = move(tokens, dx=1)
-    chip = join(tokens, partner)
+    lifted = call(head_kernel, 0, jax.ShapeDtypeStruct(tokens.shape, BF16), (tokens,), 0)
+    chip = join(lifted, partner)
     t, g, chip = lax.optimization_barrier((t, g, chip))
     z, xh, core = t >> 2, (t >> 1) & 1, t & 1
     xl, y = g >> 2, g & 3
@@ -442,7 +443,7 @@
     near3, masked = lax.optimization_barrier((near3, masked))
 
     cross = [move(v, dx=1) for v in (near1, near2, near3, far)]
-    x0 = join(tokens, far, near1, near2, near3)
+    x0 = join(lifted, far, near1, near2, near3)
     x2 = move(x0, dc=1)
     x1 = join(home, cross[3], *cross[:3])
     x3 = move(x1, dc=1)

time: 175 us -> 173 us (0.989)
    pallas_call x28 -> x29, Pallas kernels: 37.6 us -> 36.5 us  [call(): pl.pallas_call(run, out_shape=out_shape, in_specs=[SMEM] * n_scalar + [sp...]
  transfers between devices with their start and end apart: 31 -> 31, of which waited for: 10 -> 10; matrix products, arithmetic and copies ran while one was open for 3% -> 3% of each run, Pallas kernels for 18% -> 17%
where the time goes in v10:
time: 173 us
  waiting for transfers between devices  81.4 us (47%)
  starting transfers between devices  47.6 us (28%)
  Pallas kernels  36.5 us (21%)
  other arithmetic  3.53 us (2%)
  local copies, waits for them, and re-layouts  1.98 us (1%)
    ppermute x24, waiting for transfers between devices, move(): return lax.ppermute(x, 'tensor', tensor_perm(dz, dx, dc, split=True))  46.9 us
    ppermute x24, starting transfers between devices, move(): return lax.ppermute(x, 'tensor', tensor_perm(dz, dx, dc, split=True))  36.9 us
    pallas_call x29, Pallas kernels, call(): pl.pallas_call(run, out_shape=out_shape, in_specs=[SMEM] * n_scalar + [sp...  36.5 us
    ppermute x7, waiting for transfers between devices, move_dp(): return lax.ppermute(x, 'dp', dp_perm(dx, dy))  34.5 us
    ppermute x7, starting transfers between devices, move_dp(): return lax.ppermute(x, 'dp', dp_perm(dx, dy))  10.7 us
  transfers between devices with their start and end apart: 31, of which 10 were waited for; matrix products, arithmetic and copies ran while one was open for 3% of the time, Pallas kernels for 17%

profile of v10, /device:TPU:30, one launch (start us, length us, event | category | flops | bytes accessed | tf_op | source)
XLA Modules:
  0.0 173.3 jit_solution(5206091794967504697)
XLA Ops:
  0.8 0.9 copy-done.2
  2.3 3.3 %collective-permute-start.2 = (bf16[32,4096]{1,0:T(8,128)(2,1)S(1)}, bf16[32,4096]{1,0:T(8,128)(2,1)S(1)}, u32[]{:S(2)}, u32[]{:S(2)}) collective-permute-start(bf16[32,4096]{1,0:T(8,128)(2,1)S(1)} %shard_map.113), channel_id=1, source_target_pairs={{0,8},{1,25},{2,10},{3,27},{4,12},{5,29},{6,14},{7,31},{8,16},{9,1... | collective-permute-start | bytes 786440 | tf_op jit(solution)/shard_map/ppermute | solution.py:43
  5.6 1.9 %collective-permute-start.1 = (bf16[32,4096]{1,0:T(8,128)(2,1)S(1)}, bf16[32,4096]{1,0:T(8,128)(2,1)S(1)}, u32[]{:S(2)}, u32[]{:S(2)}) collective-permute-start(bf16[32,4096]{1,0:T(8,128)(2,1)S(1)} %shard_map.113), channel_id=1, source_target_pairs={{0,4},{1,29},{2,6},{3,31},{4,8},{5,1},{6,10},{7,3},{8,12},{9,5},{1... | collective-permute-start | bytes 786440 | tf_op jit(solution)/shard_map/ppermute | solution.py:43
  7.6 0.9 dynamic-slice_compare_fusion
  8.5 0.7 and_add_fusion.refs_0_
  9.3 1.0 convert_reduce_fusion
  10.3 7.9 %collective-permute-done.1.refs_2_ = bf16[32,4096]{1,0:T(8,128)(2,1)S(1)} collective-permute-done((bf16[32,4096]{1,0:T(8,128)(2,1)S(1)}, bf16[32,4096]{1,0:T(8,128)(2,1)S(1)}, u32[]{:S(2)}, u32[]{:S(2)}) %collective-permute-start.1) | collective-permute-done | bytes 262176 | tf_op jit(solution)/shard_map/ppermute | solution.py:43
  18.2 1.9 %select_reduce_fusion = s32[8,70]{0,1:T(8,128)S(1)} fusion(s32[112]{0:T(128)} %constant.79, s32[8,112]{1,0:T(8,128)S(1)} %get-tuple-element.61), kind=kLoop, calls=%fused_computation.2 | loop fusion | flops 187600 | bytes 6272 | tf_op jit(solution)/shard_map/reduce_sum | solution.py:385
  20.3 3.9 %collective-permute-start.3 = (bf16[16,4096]{1,0:T(8,128)(2,1)S(1)}, bf16[16,4096]{1,0:T(8,128)(2,1)S(1)}, u32[]{:S(2)}, u32[]{:S(2)}) collective-permute-start(bf16[16,4096]{1,0:T(8,128)(2,1)S(1)} %shard_map.116), channel_id=1, source_target_pairs={{0,8},{1,25},{2,10},{3,27},{4,12},{5,29},{6,14},{7,31},{8,16},{9,1... | collective-permute-start | bytes 393224 | tf_op jit(solution)/shard_map/ppermute | solution.py:43
  24.2 0.9 copy-done.1
  25.1 3.4 %shard_map.118.refs_3_.refs_1_ = bf16[4096,896]{1,0:T(8,128)(2,1)S(1)} custom-call(s32[1]{0:T(128)} %bitcast.refs_0_, bf16[4096,896]{1,0:T(8,128)(2,1)} %refs_1_.1, s32[64,448]{1,0:T(8,128)S(1)} %copy-done.1), custom_call_target="tpu_custom_call" | custom-call | flops 3670016 | bytes 7454724 | tf_op jit(solution)/shard_map/pallas_call | solution.py:62
  28.5 0.7 collective-permute-done.4.refs_4_
  29.4 1.5 collective-permute-start.6
  30.9 2.1 %collective-permute-start.9 = (bf16[32,4096]{1,0:T(8,128)(2,1)S(1)}, bf16[32,4096]{1,0:T(8,128)(2,1)S(1)}, u32[]{:S(2)}, u32[]{:S(2)}) collective-permute-start(bf16[32,4096]{1,0:T(8,128)(2,1)S(1)} %collective-permute-done.2.refs_0_.refs_3_), channel_id=1, source_target_pairs={{0,2},{1,3},{2,0},{3,1},{4,6},{5,7},{6,4},{7,5},{8,10},{9,11},{10,... | collective-permute-start | bytes 786440 | tf_op jit(solution)/shard_map/ppermute | solution.py:43
  33.0 1.4 collective-permute-start.8
  34.4 2.1 %collective-permute-start.10 = (bf16[32,4096]{1,0:T(8,128)(2,1)S(1)}, bf16[32,4096]{1,0:T(8,128)(2,1)S(1)}, u32[]{:S(2)}, u32[]{:S(2)}) collective-permute-start(bf16[32,4096]{1,0:T(8,128)(2,1)S(1)} %collective-permute-done.4.refs_4_), channel_id=1, source_target_pairs={{0,2},{1,3},{2,0},{3,1},{4,6},{5,7},{6,4},{7,5},{8,10},{9,11},{10,... | collective-permute-start | bytes 786440 | tf_op jit(solution)/shard_map/ppermute | solution.py:43
  36.6 0.8 collective-permute-done.6.refs_0_
  37.4 1.4 collective-permute-start.7
  38.8 17.7 %collective-permute-done.7.refs_1_ = bf16[16,4096]{1,0:T(8,128)(2,1)S(1)} collective-permute-done((bf16[16,4096]{1,0:T(8,128)(2,1)S(1)}, bf16[16,4096]{1,0:T(8,128)(2,1)S(1)}, u32[]{:S(2)}, u32[]{:S(2)}) %collective-permute-start.7) | collective-permute-done | bytes 131104 | tf_op jit(solution)/shard_map/ppermute | solution.py:43
  56.7 3.3 %shard_map.121 = (bf16[16,16,896]{2,1,0:T(8,128)(2,1)S(1)}, bf16[256,896]{1,0:T(8,128)(2,1)S(1)}) custom-call(s32[32]{0:T(128)S(1)} %fusion.8.refs_0_, bf16[128,4096]{1,0:T(8,128)(2,1)S(1)} %shard_map.119.refs_1_.refs_5_, bf16[128,4096]{1,0:T(8,128)(2,1)S(1)} %collective-permute-done.5.refs_2_.refs_7_, bf16[4096,896]{1,0:T(8,128)(2,1)S(1)} %shard_map.118.refs_3_.refs_1_, ...), custom_call_target="tpu_custom_call" | custom-call | flops 1879048192 | bytes 10354816 | tf_op jit(solution)/shard_map/pallas_call | solution.py:62
  60.0 3.8 %shard_map.123 = (f32[128,4096]{1,0:T(8,128)S(1)}, bf16[128,4096]{1,0:T(8,128)(2,1)S(1)}) custom-call(bf16[256,896]{1,0:T(8,128)(2,1)S(1)} %get-tuple-element.71.refs_0_.refs_3_, bf16[4096,896]{1,0:T(8,128)(2,1)S(1)} %shard_map.118.refs_3_.refs_1_), custom_call_target="tpu_custom_call" | custom-call | flops 1879048192 | bytes 7798784 | tf_op jit(solution)/shard_map/pallas_call | solution.py:62
  63.8 0.7 collective-permute-start.12
  64.5 3.3 %shard_map.124 = (bf16[16,16,896]{2,1,0:T(8,128)(2,1)S(1)}, bf16[256,896]{1,0:T(8,128)(2,1)S(1)}) custom-call(s32[32]{0:T(128)S(1)} %fusion.8.refs_0_, bf16[128,4096]{1,0:T(8,128)(2,1)S(1)} %shard_map.122.refs_1_.refs_6_, bf16[128,4096]{1,0:T(8,128)(2,1)S(1)} %collective-permute-done.11.refs_2_.refs_8_, bf16[4096,896]{1,0:T(8,128)(2,1)S(1)} %shard_map.118.refs_3_.refs_1_, ...), custom_call_target="tpu_custom_call" | custom-call | flops 1879048192 | bytes 10354816 | tf_op jit(solution)/shard_map/pallas_call | solution.py:62
  67.8 1.7 shard_map.125.refs_9_
  69.5 3.2 %shard_map.126 = (bf16[35,64,128]{2,1,0:T(8,128)(2,1)S(1)}, bf16[35,64,128]{2,1,0:T(8,128)(2,1)S(1)}) custom-call(s32[8]{0:T(128)S(1)} %and_add_fusion.refs_0_, s32[8,70]{1,0:T(8,128)S(1)} %broadcast_add_fusion.refs_1_, s32[8]{0:T(128)S(1)} %get-tuple-element.76.refs_2_, bf16[256,896]{1,0:T(8,128)(2,1)S(1)} %get-tuple-element.71.refs_0_.refs_3_, ...), custom_call_target="tpu_custom_call" | custom-call | flops 939524096 | bytes 5114112 | tf_op jit(solution)/shard_map/pallas_call | solution.py:62
  73.0 3.8 %shard_map.128 = (f32[128,4096]{1,0:T(8,128)S(1)}, bf16[128,4096]{1,0:T(8,128)(2,1)S(1)}) custom-call(bf16[256,896]{1,0:T(8,128)(2,1)S(1)} %get-tuple-element.77.refs_4_.refs_0_, bf16[4096,896]{1,0:T(8,128)(2,1)S(1)} %shard_map.118.refs_3_.refs_1_, bf16[16,4096]{1,0:T(8,128)(2,1)S(1)} %get-tuple-element.81.refs_2_), custom_call_target="tpu_custom_call" | custom-call | flops 1879048192 | bytes 7798784 | tf_op jit(solution)/shard_map/pallas_call | solution.py:62
  76.9 3.0 %collective-permute-start.16 = (bf16[32,4096]{1,0:T(8,128)(2,1)S(1)}, bf16[32,4096]{1,0:T(8,128)(2,1)S(1)}, u32[]{:S(2)}, u32[]{:S(2)}) collective-permute-start(bf16[32,4096]{1,0:T(8,128)(2,1)S(1)} %get-tuple-element.89), channel_id=1, source_target_pairs={{0,28},{1,5},{2,30},{3,7},{4,0},{5,9},{6,2},{7,11},{8,4},{9,13},{1... | collective-permute-start | bytes 786440 | tf_op jit(solution)/shard_map/ppermute | solution.py:43
  79.9 2.8 %shard_map.129 = (bf16[35,64,128]{2,1,0:T(8,128)(2,1)S(1)}, bf16[35,64,128]{2,1,0:T(8,128)(2,1)S(1)}) custom-call(s32[8]{0:T(128)S(1)} %and_add_fusion.refs_0_, s32[8,70]{1,0:T(8,128)S(1)} %broadcast_add_fusion.refs_1_, s32[8]{0:T(128)S(1)} %get-tuple-element.76.refs_2_, bf16[256,896]{1,0:T(8,128)(2,1)S(1)} %get-tuple-element.71.refs_0_.refs_3_, ...), custom_call_target="tpu_custom_call" | custom-call | flops 939524096 | bytes 5114112 | tf_op jit(solution)/shard_map/pallas_call | solution.py:62
  82.9 0.8 collective-permute-start.14
  83.7 3.6 %collective-permute-start.20 = (bf16[32,4096]{1,0:T(8,128)(2,1)S(1)}, bf16[32,4096]{1,0:T(8,128)(2,1)S(1)}, u32[]{:S(2)}, u32[]{:S(2)}) collective-permute-start(bf16[32,4096]{1,0:T(8,128)(2,1)S(1)} %get-tuple-element.95), channel_id=1, source_target_pairs={{0,28},{1,5},{2,30},{3,7},{4,0},{5,9},{6,2},{7,11},{8,4},{9,13},{1... | collective-permute-start | bytes 786440 | tf_op jit(solution)/shard_map/ppermute | solution.py:43
  87.3 1.5 collective-permute-start.15
  88.7 5.1 %collective-permute-done.17.refs_2_ = bf16[16,4096]{1,0:T(8,128)(2,1)S(1)} collective-permute-done((bf16[16,4096]{1,0:T(8,128)(2,1)S(1)}, bf16[16,4096]{1,0:T(8,128)(2,1)S(1)}, u32[]{:S(2)}, u32[]{:S(2)}) %collective-permute-start.17) | collective-permute-done | bytes 131104 | tf_op jit(solution)/shard_map/ppermute | solution.py:43
  94.5 3.5 %collective-permute-start.26 = (bf16[35,64,128]{2,1,0:T(8,128)(2,1)S(1)}, bf16[35,64,128]{2,1,0:T(8,128)(2,1)S(1)}, u32[]{:S(2)}, u32[]{:S(2)}) collective-permute-start(bf16[35,64,128]{2,1,0:T(8,128)(2,1)S(1)} %get-tuple-element.102), channel_id=1, source_target_pairs={{0,192},{32,224},{64,128},{96,160},{128,64},{160,96},{192,0},{224,... | collective-permute-start | bytes 1720328 | tf_op jit(solution)/shard_map/ppermute | solution.py:47
  98.1 2.8 %shard_map.132 = (bf16[35,64,128]{2,1,0:T(8,128)(2,1)S(1)}, bf16[35,64,128]{2,1,0:T(8,128)(2,1)S(1)}) custom-call(s32[8]{0:T(128)S(1)} %and_add_fusion.refs_0_, s32[8,70]{1,0:T(8,128)S(1)} %broadcast_add_fusion.refs_1_, s32[8]{0:T(128)S(1)} %get-tuple-element.76.refs_2_, bf16[256,896]{1,0:T(8,128)(2,1)S(1)} %get-tuple-element.71.refs_0_.refs_3_, ...), custom_call_target="tpu_custom_call" | custom-call | flops 939524096 | bytes 5114112 | tf_op jit(solution)/shard_map/pallas_call | solution.py:62
  100.9 3.5 %collective-permute-start.19 = (bf16[32,4096]{1,0:T(8,128)(2,1)S(1)}, bf16[32,4096]{1,0:T(8,128)(2,1)S(1)}, u32[]{:S(2)}, u32[]{:S(2)}) collective-permute-start(bf16[32,4096]{1,0:T(8,128)(2,1)S(1)} %shard_map.131.refs_9_), channel_id=1, source_target_pairs={{0,24},{1,9},{2,26},{3,11},{4,28},{5,13},{6,30},{7,15},{8,0},{9,17... | collective-permute-start | bytes 786440 | tf_op jit(solution)/shard_map/ppermute | solution.py:43
  104.6 4.3 %collective-permute-start.18 = (bf16[32,4096]{1,0:T(8,128)(2,1)S(1)}, bf16[32,4096]{1,0:T(8,128)(2,1)S(1)}, u32[]{:S(2)}, u32[]{:S(2)}) collective-permute-start(bf16[32,4096]{1,0:T(8,128)(2,1)S(1)} %get-tuple-element.93), channel_id=1, source_target_pairs={{0,28},{1,5},{2,30},{3,7},{4,0},{5,9},{6,2},{7,11},{8,4},{9,13},{1... | collective-permute-start | bytes 786440 | tf_op jit(solution)/shard_map/ppermute | solution.py:43
  108.9 1.2 collective-permute-start.21
  110.2 5.4 %collective-permute-done.18.refs_0_ = bf16[32,4096]{1,0:T(8,128)(2,1)S(1)} collective-permute-done((bf16[32,4096]{1,0:T(8,128)(2,1)S(1)}, bf16[32,4096]{1,0:T(8,128)(2,1)S(1)}, u32[]{:S(2)}, u32[]{:S(2)}) %collective-permute-start.18) | collective-permute-done | bytes 262176 | tf_op jit(solution)/shard_map/ppermute | solution.py:43
  115.6 6.0 %collective-permute-done.21.refs_4_ = bf16[32,4096]{1,0:T(8,128)(2,1)S(1)} collective-permute-done((bf16[32,4096]{1,0:T(8,128)(2,1)S(1)}, bf16[32,4096]{1,0:T(8,128)(2,1)S(1)}, u32[]{:S(2)}, u32[]{:S(2)}) %collective-permute-start.21) | collective-permute-done | bytes 262176 | tf_op jit(solution)/shard_map/ppermute | solution.py:43
  122.0 0.9 collective-permute-start.27
  122.9 2.3 %collective-permute-start.28 = (bf16[35,64,128]{2,1,0:T(8,128)(2,1)S(1)}, bf16[35,64,128]{2,1,0:T(8,128)(2,1)S(1)}, u32[]{:S(2)}, u32[]{:S(2)}) collective-permute-start(bf16[35,64,128]{2,1,0:T(8,128)(2,1)S(1)} %get-tuple-element.104), channel_id=1, source_target_pairs={{0,32},{32,64},{64,96},{96,0},{128,160},{160,192},{192,224},{224,1... | collective-permute-start | bytes 1720328 | tf_op jit(solution)/shard_map/ppermute | solution.py:47
  125.2 2.1 %collective-permute-start.30 = (bf16[35,64,128]{2,1,0:T(8,128)(2,1)S(1)}, bf16[35,64,128]{2,1,0:T(8,128)(2,1)S(1)}, u32[]{:S(2)}, u32[]{:S(2)}) collective-permute-start(bf16[35,64,128]{2,1,0:T(8,128)(2,1)S(1)} %get-tuple-element.105), channel_id=1, source_target_pairs={{0,64},{32,96},{64,0},{96,32},{128,192},{160,224},{192,128},{224,1... | collective-permute-start | bytes 1720328 | tf_op jit(solution)/shard_map/ppermute | solution.py:47
  127.4 1.1 collective-permute-start.29
  128.6 34.5 %collective-permute-done.25.refs_2_ = bf16[35,64,128]{2,1,0:T(8,128)(2,1)S(1)} collective-permute-done((bf16[35,64,128]{2,1,0:T(8,128)(2,1)S(1)}, bf16[35,64,128]{2,1,0:T(8,128)(2,1)S(1)}, u32[]{:S(2)}, u32[]{:S(2)}) %collective-permute-start.25) | collective-permute-done | bytes 573472 | tf_op jit(solution)/shard_map/ppermute | solution.py:47
  163.1 1.7 shard_map.134.refs_3_.refs_0_
  164.8 1.6 shard_map.135
  166.9 2.6 %collective-permute-done.23.refs_1_ = bf16[16,4096]{1,0:T(8,128)(2,1)S(1)} collective-permute-done((bf16[16,4096]{1,0:T(8,128)(2,1)S(1)}, bf16[16,4096]{1,0:T(8,128)(2,1)S(1)}, u32[]{:S(2)}, u32[]{:S(2)}) %collective-permute-start.23) | collective-permute-done | bytes 131104 | tf_op jit(solution)/shard_map/ppermute | solution.py:43
  170.2 2.8 %shard_map.140 = f32[512,896]{1,0:T(8,128)} custom-call(s32[1]{0:T(128)} %bitcast.3.refs_0_, s32[8,70]{1,0:T(8,128)S(1)} %broadcast_add_fusion.refs_1_, f32[35,64,128]{2,1,0:T(8,128)S(1)} %shard_map.139.refs_2_, bf16[35,64,128]{2,1,0:T(8,128)(2,1)S(1)} %collective-permute-done.28.refs_3_, bf16[35,64,128]{2,1,0:T(8,128)(2,1)S(1)} %collective-permute-done.29.refs_4_, ...), custom_call_target="tpu_custom_call" | custom-call | flops 2293760 | bytes 2869444 | tf_op jit(solution)/shard_map/pallas_call | solution.py:62
  (59 shorter events, 4.4 us)
Async XLA Ops:
  0.6 1.6 collective-permute-start
  0.8 0.9 copy-start.2
  2.3 17.9 %collective-permute-start.2 = (bf16[32,4096]{1,0:T(8,128)(2,1)S(1)}, bf16[32,4096]{1,0:T(8,128)(2,1)S(1)}, u32[]{:S(2)}, u32[]{:S(2)}) collective-permute-start(bf16[32,4096]{1,0:T(8,128)(2,1)S(1)} %shard_map.113), channel_id=1, source_target_pairs={{0,8},{1,25},{2,10},{3,27},{4,12},{5,29},{6,14},{7,31},{8,16},{9,1... | collective-permute-start | bytes 786440 | tf_op jit(solution)/shard_map/ppermute | solution.py:43
  5.6 12.6 %collective-permute-start.1 = (bf16[32,4096]{1,0:T(8,128)(2,1)S(1)}, bf16[32,4096]{1,0:T(8,128)(2,1)S(1)}, u32[]{:S(2)}, u32[]{:S(2)}) collective-permute-start(bf16[32,4096]{1,0:T(8,128)(2,1)S(1)} %shard_map.113), channel_id=1, source_target_pairs={{0,4},{1,29},{2,6},{3,31},{4,8},{5,1},{6,10},{7,3},{8,12},{9,5},{1... | collective-permute-start | bytes 786440 | tf_op jit(solution)/shard_map/ppermute | solution.py:43
  20.2 9.0 %collective-permute-start.4 = (bf16[32,4096]{1,0:T(8,128)(2,1)S(1)}, bf16[32,4096]{1,0:T(8,128)(2,1)S(1)}, u32[]{:S(2)}, u32[]{:S(2)}) collective-permute-start(bf16[32,4096]{1,0:T(8,128)(2,1)S(1)} %collective-permute-done.2.refs_0_.refs_3_), channel_id=1, source_target_pairs={{0,4},{1,29},{2,6},{3,31},{4,8},{5,1},{6,10},{7,3},{8,12},{9,5},{1... | collective-permute-start | bytes 786440 | tf_op jit(solution)/shard_map/ppermute | solution.py:43
  20.3 9.0 %collective-permute-start.3 = (bf16[16,4096]{1,0:T(8,128)(2,1)S(1)}, bf16[16,4096]{1,0:T(8,128)(2,1)S(1)}, u32[]{:S(2)}, u32[]{:S(2)}) collective-permute-start(bf16[16,4096]{1,0:T(8,128)(2,1)S(1)} %shard_map.116), channel_id=1, source_target_pairs={{0,8},{1,25},{2,10},{3,27},{4,12},{5,29},{6,14},{7,31},{8,16},{9,1... | collective-permute-start | bytes 393224 | tf_op jit(solution)/shard_map/ppermute | solution.py:43
  24.2 0.9 copy-start.1
  28.5 0.9 copy-start.3
  28.5 28.2 %copy-start = (bf16[512,896]{1,0:T(8,128)(2,1)S(1)}, bf16[512,896]{1,0:T(8,128)(2,1)}, u32[]{:S(2)}) copy-start(bf16[512,896]{1,0:T(8,128)(2,1)} %param.12) | copy-start | bytes 2752516
  29.3 27.4 %collective-permute-start.5 = (bf16[128,4096]{1,0:T(8,128)(2,1)S(1)}, bf16[128,4096]{1,0:T(8,128)(2,1)S(1)}, u32[]{:S(2)}, u32[]{:S(2)}) collective-permute-start(bf16[128,4096]{1,0:T(8,128)(2,1)S(1)} %shard_map.119.refs_1_.refs_5_), channel_id=1, source_target_pairs={{0,1},{1,0},{2,3},{3,2},{4,5},{5,4},{6,7},{7,6},{8,9},{9,8},{10,11... | collective-permute-start | bytes 3145736 | tf_op jit(solution)/shard_map/ppermute | solution.py:43
  29.4 8.0 %collective-permute-start.6 = (bf16[16,4096]{1,0:T(8,128)(2,1)S(1)}, bf16[16,4096]{1,0:T(8,128)(2,1)S(1)}, u32[]{:S(2)}, u32[]{:S(2)}) collective-permute-start(bf16[16,4096]{1,0:T(8,128)(2,1)S(1)} %copy-done.3), channel_id=1, source_target_pairs={{0,2},{1,3},{2,0},{3,1},{4,6},{5,7},{6,4},{7,5},{8,10},{9,11},{10,... | collective-permute-start | bytes 393224 | tf_op jit(solution)/shard_map/ppermute | solution.py:43
  30.9 25.6 %collective-permute-start.9 = (bf16[32,4096]{1,0:T(8,128)(2,1)S(1)}, bf16[32,4096]{1,0:T(8,128)(2,1)S(1)}, u32[]{:S(2)}, u32[]{:S(2)}) collective-permute-start(bf16[32,4096]{1,0:T(8,128)(2,1)S(1)} %collective-permute-done.2.refs_0_.refs_3_), channel_id=1, source_target_pairs={{0,2},{1,3},{2,0},{3,1},{4,6},{5,7},{6,4},{7,5},{8,10},{9,11},{10,... | collective-permute-start | bytes 786440 | tf_op jit(solution)/shard_map/ppermute | solution.py:43
  33.0 23.4 %collective-permute-start.8 = (bf16[32,4096]{1,0:T(8,128)(2,1)S(1)}, bf16[32,4096]{1,0:T(8,128)(2,1)S(1)}, u32[]{:S(2)}, u32[]{:S(2)}) collective-permute-start(bf16[32,4096]{1,0:T(8,128)(2,1)S(1)} %collective-permute-done.1.refs_2_), channel_id=1, source_target_pairs={{0,2},{1,3},{2,0},{3,1},{4,6},{5,7},{6,4},{7,5},{8,10},{9,11},{10,... | collective-permute-start | bytes 786440 | tf_op jit(solution)/shard_map/ppermute | solution.py:43
  34.4 22.0 %collective-permute-start.10 = (bf16[32,4096]{1,0:T(8,128)(2,1)S(1)}, bf16[32,4096]{1,0:T(8,128)(2,1)S(1)}, u32[]{:S(2)}, u32[]{:S(2)}) collective-permute-start(bf16[32,4096]{1,0:T(8,128)(2,1)S(1)} %collective-permute-done.4.refs_4_), channel_id=1, source_target_pairs={{0,2},{1,3},{2,0},{3,1},{4,6},{5,7},{6,4},{7,5},{8,10},{9,11},{10,... | collective-permute-start | bytes 786440 | tf_op jit(solution)/shard_map/ppermute | solution.py:43
  37.4 19.1 %collective-permute-start.7 = (bf16[16,4096]{1,0:T(8,128)(2,1)S(1)}, bf16[16,4096]{1,0:T(8,128)(2,1)S(1)}, u32[]{:S(2)}, u32[]{:S(2)}) collective-permute-start(bf16[16,4096]{1,0:T(8,128)(2,1)S(1)} %collective-permute-done.3.refs_1_), channel_id=1, source_target_pairs={{0,2},{1,3},{2,0},{3,1},{4,6},{5,7},{6,4},{7,5},{8,10},{9,11},{10,... | collective-permute-start | bytes 393224 | tf_op jit(solution)/shard_map/ppermute | solution.py:43
  56.6 7.9 %collective-permute-start.11 = (bf16[128,4096]{1,0:T(8,128)(2,1)S(1)}, bf16[128,4096]{1,0:T(8,128)(2,1)S(1)}, u32[]{:S(2)}, u32[]{:S(2)}) collective-permute-start(bf16[128,4096]{1,0:T(8,128)(2,1)S(1)} %shard_map.122.refs_1_.refs_6_), channel_id=1, source_target_pairs={{0,1},{1,0},{2,3},{3,2},{4,5},{5,4},{6,7},{7,6},{8,9},{9,8},{10,11... | collective-permute-start | bytes 3145736 | tf_op jit(solution)/shard_map/ppermute | solution.py:43
  63.8 9.0 %collective-permute-start.12 = (bf16[128,4096]{1,0:T(8,128)(2,1)S(1)}, bf16[128,4096]{1,0:T(8,128)(2,1)S(1)}, u32[]{:S(2)}, u32[]{:S(2)}) collective-permute-start(bf16[128,4096]{1,0:T(8,128)(2,1)S(1)} %get-tuple-element.72.refs_5_.refs_9_), channel_id=1, source_target_pairs={{0,1},{1,0},{2,3},{3,2},{4,5},{5,4},{6,7},{7,6},{8,9},{9,8},{10,11... | collective-permute-start | bytes 3145736 | tf_op jit(solution)/shard_map/ppermute | solution.py:43
  76.8 5.9 %collective-permute-start.13 = (bf16[128,4096]{1,0:T(8,128)(2,1)S(1)}, bf16[128,4096]{1,0:T(8,128)(2,1)S(1)}, u32[]{:S(2)}, u32[]{:S(2)}) collective-permute-start(bf16[128,4096]{1,0:T(8,128)(2,1)S(1)} %get-tuple-element.83.refs_9_), channel_id=1, source_target_pairs={{0,1},{1,0},{2,3},{3,2},{4,5},{5,4},{6,7},{7,6},{8,9},{9,8},{10,11... | collective-permute-start | bytes 3145736 | tf_op jit(solution)/shard_map/ppermute | solution.py:43
  76.9 17.6 %collective-permute-start.16 = (bf16[32,4096]{1,0:T(8,128)(2,1)S(1)}, bf16[32,4096]{1,0:T(8,128)(2,1)S(1)}, u32[]{:S(2)}, u32[]{:S(2)}) collective-permute-start(bf16[32,4096]{1,0:T(8,128)(2,1)S(1)} %get-tuple-element.89), channel_id=1, source_target_pairs={{0,28},{1,5},{2,30},{3,7},{4,0},{5,9},{6,2},{7,11},{8,4},{9,13},{1... | collective-permute-start | bytes 786440 | tf_op jit(solution)/shard_map/ppermute | solution.py:43
  82.9 21.6 %collective-permute-start.14 = (bf16[32,4096]{1,0:T(8,128)(2,1)S(1)}, bf16[32,4096]{1,0:T(8,128)(2,1)S(1)}, u32[]{:S(2)}, u32[]{:S(2)}) collective-permute-start(bf16[32,4096]{1,0:T(8,128)(2,1)S(1)} %get-tuple-element.86), channel_id=1, source_target_pairs={{0,28},{1,5},{2,30},{3,7},{4,0},{5,9},{6,2},{7,11},{8,4},{9,13},{1... | collective-permute-start | bytes 786440 | tf_op jit(solution)/shard_map/ppermute | solution.py:43
  83.7 25.3 %collective-permute-start.20 = (bf16[32,4096]{1,0:T(8,128)(2,1)S(1)}, bf16[32,4096]{1,0:T(8,128)(2,1)S(1)}, u32[]{:S(2)}, u32[]{:S(2)}) collective-permute-start(bf16[32,4096]{1,0:T(8,128)(2,1)S(1)} %get-tuple-element.95), channel_id=1, source_target_pairs={{0,28},{1,5},{2,30},{3,7},{4,0},{5,9},{6,2},{7,11},{8,4},{9,13},{1... | collective-permute-start | bytes 786440 | tf_op jit(solution)/shard_map/ppermute | solution.py:43
  87.3 6.6 %collective-permute-start.17 = (bf16[16,4096]{1,0:T(8,128)(2,1)S(1)}, bf16[16,4096]{1,0:T(8,128)(2,1)S(1)}, u32[]{:S(2)}, u32[]{:S(2)}) collective-permute-start(bf16[16,4096]{1,0:T(8,128)(2,1)S(1)} %get-tuple-element.81.refs_2_), channel_id=1, source_target_pairs={{0,24},{1,9},{2,26},{3,11},{4,28},{5,13},{6,30},{7,15},{8,0},{9,17... | collective-permute-start | bytes 393224 | tf_op jit(solution)/shard_map/ppermute | solution.py:43
  87.3 13.7 %collective-permute-start.15 = (bf16[16,4096]{1,0:T(8,128)(2,1)S(1)}, bf16[16,4096]{1,0:T(8,128)(2,1)S(1)}, u32[]{:S(2)}, u32[]{:S(2)}) collective-permute-start(bf16[16,4096]{1,0:T(8,128)(2,1)S(1)} %get-tuple-element.87.refs_3_), channel_id=1, source_target_pairs={{0,24},{1,9},{2,26},{3,11},{4,28},{5,13},{6,30},{7,15},{8,0},{9,17... | collective-permute-start | bytes 393224 | tf_op jit(solution)/shard_map/ppermute | solution.py:43
  93.8 29.1 %collective-permute-start.24 = (bf16[35,64,128]{2,1,0:T(8,128)(2,1)S(1)}, bf16[35,64,128]{2,1,0:T(8,128)(2,1)S(1)}, u32[]{:S(2)}, u32[]{:S(2)}) collective-permute-start(bf16[35,64,128]{2,1,0:T(8,128)(2,1)S(1)} %shard_map.125.refs_9_), channel_id=1, source_target_pairs={{0,160},{32,192},{64,224},{96,128},{128,32},{160,64},{192,96},{224... | collective-permute-start | bytes 1720328 | tf_op jit(solution)/shard_map/ppermute | solution.py:47
  94.5 30.8 %collective-permute-start.26 = (bf16[35,64,128]{2,1,0:T(8,128)(2,1)S(1)}, bf16[35,64,128]{2,1,0:T(8,128)(2,1)S(1)}, u32[]{:S(2)}, u32[]{:S(2)}) collective-permute-start(bf16[35,64,128]{2,1,0:T(8,128)(2,1)S(1)} %get-tuple-element.102), channel_id=1, source_target_pairs={{0,192},{32,224},{64,128},{96,160},{128,64},{160,96},{192,0},{224,... | collective-permute-start | bytes 1720328 | tf_op jit(solution)/shard_map/ppermute | solution.py:47
  100.9 9.2 %collective-permute-start.19 = (bf16[32,4096]{1,0:T(8,128)(2,1)S(1)}, bf16[32,4096]{1,0:T(8,128)(2,1)S(1)}, u32[]{:S(2)}, u32[]{:S(2)}) collective-permute-start(bf16[32,4096]{1,0:T(8,128)(2,1)S(1)} %shard_map.131.refs_9_), channel_id=1, source_target_pairs={{0,24},{1,9},{2,26},{3,11},{4,28},{5,13},{6,30},{7,15},{8,0},{9,17... | collective-permute-start | bytes 786440 | tf_op jit(solution)/shard_map/ppermute | solution.py:43
  104.6 11.0 %collective-permute-start.18 = (bf16[32,4096]{1,0:T(8,128)(2,1)S(1)}, bf16[32,4096]{1,0:T(8,128)(2,1)S(1)}, u32[]{:S(2)}, u32[]{:S(2)}) collective-permute-start(bf16[32,4096]{1,0:T(8,128)(2,1)S(1)} %get-tuple-element.93), channel_id=1, source_target_pairs={{0,28},{1,5},{2,30},{3,7},{4,0},{5,9},{6,2},{7,11},{8,4},{9,13},{1... | collective-permute-start | bytes 786440 | tf_op jit(solution)/shard_map/ppermute | solution.py:43
  108.9 12.7 %collective-permute-start.21 = (bf16[32,4096]{1,0:T(8,128)(2,1)S(1)}, bf16[32,4096]{1,0:T(8,128)(2,1)S(1)}, u32[]{:S(2)}, u32[]{:S(2)}) collective-permute-start(bf16[32,4096]{1,0:T(8,128)(2,1)S(1)} %shard_map.133.refs_9_), channel_id=1, source_target_pairs={{0,24},{1,9},{2,26},{3,11},{4,28},{5,13},{6,30},{7,15},{8,0},{9,17... | collective-permute-start | bytes 786440 | tf_op jit(solution)/shard_map/ppermute | solution.py:43
  121.8 5.6 %collective-permute-start.22 = (bf16[32,4096]{1,0:T(8,128)(2,1)S(1)}, bf16[32,4096]{1,0:T(8,128)(2,1)S(1)}, u32[]{:S(2)}, u32[]{:S(2)}) collective-permute-start(bf16[32,4096]{1,0:T(8,128)(2,1)S(1)} %get-tuple-element.98), channel_id=1, source_target_pairs={{0,1},{1,0},{2,3},{3,2},{4,5},{5,4},{6,7},{7,6},{8,9},{9,8},{10,11... | collective-permute-start | bytes 786440 | tf_op jit(solution)/shard_map/ppermute | solution.py:43
  121.9 41.2 %collective-permute-start.25 = (bf16[35,64,128]{2,1,0:T(8,128)(2,1)S(1)}, bf16[35,64,128]{2,1,0:T(8,128)(2,1)S(1)}, u32[]{:S(2)}, u32[]{:S(2)}) collective-permute-start(bf16[35,64,128]{2,1,0:T(8,128)(2,1)S(1)} %get-tuple-element.79.refs_2_), channel_id=1, source_target_pairs={{0,96},{32,0},{64,32},{96,64},{128,224},{160,128},{192,160},{224,1... | collective-permute-start | bytes 1720328 | tf_op jit(solution)/shard_map/ppermute | solution.py:47
  122.0 44.4 %collective-permute-start.27 = (bf16[35,64,128]{2,1,0:T(8,128)(2,1)S(1)}, bf16[35,64,128]{2,1,0:T(8,128)(2,1)S(1)}, u32[]{:S(2)}, u32[]{:S(2)}) collective-permute-start(bf16[35,64,128]{2,1,0:T(8,128)(2,1)S(1)} %get-tuple-element.84.refs_2_), channel_id=1, source_target_pairs={{0,224},{32,128},{64,160},{96,192},{128,96},{160,0},{192,32},{224,... | collective-permute-start | bytes 1720328 | tf_op jit(solution)/shard_map/ppermute | solution.py:47
  122.9 47.3 %collective-permute-start.28 = (bf16[35,64,128]{2,1,0:T(8,128)(2,1)S(1)}, bf16[35,64,128]{2,1,0:T(8,128)(2,1)S(1)}, u32[]{:S(2)}, u32[]{:S(2)}) collective-permute-start(bf16[35,64,128]{2,1,0:T(8,128)(2,1)S(1)} %get-tuple-element.104), channel_id=1, source_target_pairs={{0,32},{32,64},{64,96},{96,0},{128,160},{160,192},{192,224},{224,1... | collective-permute-start | bytes 1720328 | tf_op jit(solution)/shard_map/ppermute | solution.py:47
  125.2 45.0 %collective-permute-start.30 = (bf16[35,64,128]{2,1,0:T(8,128)(2,1)S(1)}, bf16[35,64,128]{2,1,0:T(8,128)(2,1)S(1)}, u32[]{:S(2)}, u32[]{:S(2)}) collective-permute-start(bf16[35,64,128]{2,1,0:T(8,128)(2,1)S(1)} %get-tuple-element.105), channel_id=1, source_target_pairs={{0,64},{32,96},{64,0},{96,32},{128,192},{160,224},{192,128},{224,1... | collective-permute-start | bytes 1720328 | tf_op jit(solution)/shard_map/ppermute | solution.py:47
  127.4 42.9 %collective-permute-start.29 = (bf16[35,64,128]{2,1,0:T(8,128)(2,1)S(1)}, bf16[35,64,128]{2,1,0:T(8,128)(2,1)S(1)}, u32[]{:S(2)}, u32[]{:S(2)}) collective-permute-start(bf16[35,64,128]{2,1,0:T(8,128)(2,1)S(1)} %get-tuple-element.90.refs_3_), channel_id=1, source_target_pairs={{0,128},{32,160},{64,192},{96,224},{128,0},{160,32},{192,64},{224,... | collective-permute-start | bytes 1720328 | tf_op jit(solution)/shard_map/ppermute | solution.py:47
  163.1 6.5 %collective-permute-start.23 = (bf16[16,4096]{1,0:T(8,128)(2,1)S(1)}, bf16[16,4096]{1,0:T(8,128)(2,1)S(1)}, u32[]{:S(2)}, u32[]{:S(2)}) collective-permute-start(bf16[16,4096]{1,0:T(8,128)(2,1)S(1)} %get-tuple-element.100), channel_id=1, source_target_pairs={{0,2},{1,3},{2,0},{3,1},{4,6},{5,7},{6,4},{7,5},{8,10},{9,11},{10,... | collective-permute-start | bytes 393224 | tf_op jit(solution)/shard_map/ppermute | solution.py:43
